TPU v7x, 128 devices: a whole 4x4x4 slice. The times are simulated.
128 devices in a mesh: layer: 4 (over x), node: 32 (over y, z, core).
Axes of the slice: x: 4, y: 4, z: 4, core: 2. Of those that a mesh axis runs over, the one named last changes fastest.
Arguments:
- features: bfloat16 [4, 8192, 512], P(None, 'node'), may hold values from -6 to 6
- w_self: bfloat16 [4, 512, 512], P('layer'), may hold values from -0.1875 to 0.1875
- w_neigh: bfloat16 [4, 512, 512], P('layer'), may hold values from -0.1875 to 0.1875
- w_out: bfloat16 [512, 172], replicated, may hold values from -0.25 to 0.25
- labels: int32 [4, 8192], P(None, 'node'), may hold values from 0 to 171
- train_mask: int32 [4, 8192], P(None, 'node'), may hold values 0 or 1
- tile_cols: int32 [4, 32, 2, 4], P(None, 'node'), may hold values from 0 to 3
- tile_vals: bfloat16 [4, 32, 2, 4, 128, 128], P(None, 'node'), may hold values from -0.25 to 0.25
- send_rows: int32 [4, 32, 32, 8], P(None, 'node'), may hold values from 0 to 255
- send_counts: int32 [4, 32, 32], P(None, 'node'), may hold values from 0 to 8, as said below
Outputs:
- layer_acts: bfloat16 [4, 4, 8192, 512], P('layer', None, 'node')
- act_grads: bfloat16 [4, 4, 8192, 512], P('layer', None, 'node')
- grad_self: float32 [4, 512, 512], P('layer')
- grad_neigh: float32 [4, 512, 512], P('layer')
Inputs may be any that keep to these rules, and one draw needn't show every extreme that they name: `send_counts`: in every span one partition, drawn per span, gets 8 rows from every partition, itself included; the other counts are at most 4. `send_rows`: entries of slots at or past the count are ignored; rows may repeat. `tile_cols`: A value below 2 is a tile of the partition's own rows; larger values are tiles of the received rows in source order, 8 slots per source, then zero rows; tiles of a row tile may repeat.
All inputs are finite; a program needn't handle non-finite values. No bound on the sum of `train_mask` on one device may be relied on, other than what follows from the above.
Results may differ from a plain program's by a relative error of at most 0.03.
Values may be sent and summed in bfloat16 or wider, within the bound.
No kernel may reach another device: no remote copies, remote signals or barrier semaphores. Data moves between devices by JAX's collectives and lax.ppermute only.
A program may use at most 128 MiB of HBM per device.

v0:
```python
import jax
import jax.numpy as jnp
from jax import lax
from jax.sharding import PartitionSpec as P


def from_behind(value, axis, steps):
    count = lax.axis_size(axis)
    first, last = (max(0, -steps), min(count, count - steps))
    return lax.ppermute(value, axis, [(source, source + steps) for source in range(first, last)])


def silu_slope(preact):
    sigma = jax.nn.sigmoid(preact)
    return sigma * (1.0 + preact * (1.0 - sigma))


def pick(array, index):
    return lax.dynamic_index_in_dim(array, index, 0, keepdims=False)


def put_row(buffer, value, index, valid):
    current = pick(buffer, index)
    return lax.dynamic_update_index_in_dim(buffer, jnp.where(valid, value, current), index, 0)


def live_slots(send_list, counts):
    return jnp.arange(send_list.shape[1])[None, :] < counts[:, None]


def layer_forward(hidden_in, weight_self, weight_neigh, col_tiles, values, send_list, counts):
    feat_dim = hidden_in.shape[1]
    tile_size = values.shape[-1]
    is_live = live_slots(send_list, counts)
    outgoing = jnp.where(
        is_live[:, :, None], jnp.take(hidden_in, send_list, axis=0), jnp.zeros((), hidden_in.dtype)
    )
    arrived = lax.all_to_all(outgoing, "node", split_axis=0, concat_axis=0, tiled=True)
    extended = jnp.concatenate([hidden_in, arrived.reshape(-1, feat_dim)], axis=0)
    blocks = jnp.take(extended.reshape(-1, tile_size, feat_dim), col_tiles, axis=0)
    summed = jnp.einsum("rkij,rkjd->rid", values, blocks, preferred_element_type=jnp.float32)
    aggregate = summed.reshape(hidden_in.shape).astype(jnp.bfloat16)
    preact = jnp.dot(hidden_in, weight_self, preferred_element_type=jnp.float32)
    preact = preact + jnp.dot(aggregate, weight_neigh, preferred_element_type=jnp.float32)
    return (aggregate, preact, jax.nn.silu(preact).astype(jnp.bfloat16))


def layer_backward(
    d_out,
    hidden_in,
    aggregate,
    preact,
    weight_self,
    weight_neigh,
    col_tiles,
    values,
    send_list,
    counts,
):
    node_rows, feat_dim = hidden_in.shape
    row_tiles, degree, tile_size = (values.shape[0], values.shape[1], values.shape[-1])
    peers, slot_count = send_list.shape
    d_pre = (d_out.astype(jnp.float32) * silu_slope(preact)).astype(jnp.bfloat16)
    over_rows = (((0,), (0,)), ((), ()))
    over_cols = (((1,), (1,)), ((), ()))
    g_self = lax.dot_general(hidden_in, d_pre, over_rows, preferred_element_type=jnp.float32)
    g_neigh = lax.dot_general(aggregate, d_pre, over_rows, preferred_element_type=jnp.float32)
    back_self = lax.dot_general(d_pre, weight_self, over_cols, preferred_element_type=jnp.float32)
    d_agg = lax.dot_general(
        d_pre, weight_neigh, over_cols, preferred_element_type=jnp.float32
    ).astype(jnp.bfloat16)
    pieces = jnp.einsum(
        "rkij,rid->rkjd",
        values,
        d_agg.reshape(row_tiles, tile_size, feat_dim),
        preferred_element_type=jnp.float32,
    )
    col_count = (node_rows + peers * slot_count + tile_size - 1) // tile_size
    selector = (col_tiles.reshape(-1)[None, :] == jnp.arange(col_count)[:, None]).astype(
        jnp.float32
    )
    d_ext = jnp.einsum(
        "cn,njd->cjd",
        selector,
        pieces.reshape(row_tiles * degree, tile_size, feat_dim),
        precision=lax.Precision.HIGHEST,
    )
    d_ext = d_ext.reshape(-1, feat_dim)
    local_part = d_ext[:node_rows]
    remote = (
        d_ext[node_rows : node_rows + peers * slot_count]
        .reshape(peers, slot_count, feat_dim)
        .astype(jnp.bfloat16)
    )
    returned = lax.all_to_all(remote, "node", split_axis=0, concat_axis=0, tiled=True)
    is_live = live_slots(send_list, counts)
    masked = jnp.where(
        is_live[:, :, None], returned.astype(jnp.float32), jnp.zeros((), jnp.float32)
    )
    scattered = jax.ops.segment_sum(
        masked.reshape(-1, feat_dim), send_list.reshape(-1), num_segments=node_rows
    )
    d_in = (back_self + local_part + scattered).astype(jnp.bfloat16)
    return (d_in, g_self, g_neigh)


def finish_grads(grad_pair, scale):
    summed = (
        lax.psum(grad_pair[0].astype(jnp.bfloat16), "node").astype(jnp.float32),
        lax.psum(grad_pair[1].astype(jnp.bfloat16), "node").astype(jnp.float32),
    )
    return (summed[0] * scale, summed[1] * scale)


def body(
    features,
    w_self,
    w_neigh,
    w_out,
    labels,
    train_mask,
    tile_cols,
    tile_vals,
    send_rows,
    send_counts,
):
    my_section = lax.axis_index("layer")
    sections = lax.axis_size("layer")
    spans, node_rows, feat_dim = features.shape
    classes = w_out.shape[1]
    scale = 1.0 / (spans * node_rows * lax.axis_size("node"))

    def graph_of(span_idx):
        return (
            pick(tile_cols, span_idx)[0],
            pick(tile_vals, span_idx)[0],
            pick(send_rows, span_idx)[0],
            pick(send_counts, span_idx)[0],
        )

    rows_zero = jnp.zeros((node_rows, feat_dim), jnp.bfloat16)
    block_bf = jnp.zeros((spans, node_rows, feat_dim), jnp.bfloat16)
    block_f32 = jnp.zeros((spans, node_rows, feat_dim), jnp.float32)
    square_zero = jnp.zeros((feat_dim, feat_dim), jnp.float32)
    weight_self = w_self[0]
    weight_neigh = w_neigh[0]
    steps_total = spans + sections - 1

    def forward_step(step, carry):
        incoming, saved_in, saved_agg, saved_pre, acts = carry
        span_idx = step - my_section
        valid = (span_idx >= 0) & (span_idx < spans)
        safe_idx = jnp.clip(span_idx, 0, spans - 1)
        hidden_in = jnp.where(my_section == 0, pick(features, safe_idx), incoming)
        aggregate, preact, hidden_out = layer_forward(
            hidden_in, weight_self, weight_neigh, *graph_of(safe_idx)
        )
        saved_in = put_row(saved_in, hidden_in, safe_idx, valid)
        saved_agg = put_row(saved_agg, aggregate, safe_idx, valid)
        saved_pre = put_row(saved_pre, preact, safe_idx, valid)
        acts = put_row(acts, hidden_out, safe_idx, valid)
        outgoing = from_behind(hidden_out, "layer", 1)
        return (outgoing, saved_in, saved_agg, saved_pre, acts)

    start = (rows_zero, block_bf, block_bf, block_f32, block_bf)
    fwd_done = lax.fori_loop(0, steps_total, forward_step, start)
    saved_in, saved_agg, saved_pre, acts = (fwd_done[1], fwd_done[2], fwd_done[3], fwd_done[4])
    logits = jnp.einsum("...d,dc->...c", acts, w_out, preferred_element_type=jnp.float32)
    expo = jnp.exp(logits)
    probs = expo / jnp.sum(expo, axis=-1, keepdims=True)
    onehot = (labels[..., None] == jnp.arange(classes)).astype(jnp.float32)
    g_logits = (train_mask[..., None].astype(jnp.float32) * (probs - onehot)).astype(jnp.bfloat16)
    d_top = jnp.einsum("...c,dc->...d", g_logits, w_out, preferred_element_type=jnp.float32).astype(
        jnp.bfloat16
    )

    def backward_step(step, carry):
        incoming, sum_self, sum_neigh, grads_out = carry
        span_idx = step - (sections - 1 - my_section)
        valid = (span_idx >= 0) & (span_idx < spans)
        safe_idx = jnp.clip(span_idx, 0, spans - 1)
        d_out = jnp.where(my_section == sections - 1, pick(d_top, safe_idx), incoming)
        hidden_in = pick(saved_in, safe_idx)
        graph = graph_of(safe_idx)
        aggregate = pick(saved_agg, safe_idx)
        preact = pick(saved_pre, safe_idx)
        d_in, g_self, g_neigh = layer_backward(
            d_out, hidden_in, aggregate, preact, weight_self, weight_neigh, *graph
        )
        sum_self = sum_self + jnp.where(valid, g_self, 0.0)
        sum_neigh = sum_neigh + jnp.where(valid, g_neigh, 0.0)
        grads_out = put_row(grads_out, d_in, safe_idx, valid)
        outgoing = from_behind(d_in, "layer", -1)
        return (outgoing, sum_self, sum_neigh, grads_out)

    bwd_done = lax.fori_loop(
        0, steps_total, backward_step, (rows_zero, square_zero, square_zero, block_bf)
    )
    grad_self, grad_neigh = finish_grads((bwd_done[1][None], bwd_done[2][None]), scale)
    return (acts[None], bwd_done[3][None], grad_self, grad_neigh)


def solution(mesh):
    in_specs = (
        P(None, "node", None),
        P("layer", None, None),
        P("layer", None, None),
        P(),
        P(None, "node"),
        P(None, "node"),
        P(None, "node", None, None),
        P(None, "node", None, None, None, None),
        P(None, "node", None, None),
        P(None, "node", None),
    )
    out_specs = (
        P("layer", None, "node", None),
        P("layer", None, "node", None),
        P("layer", None, None),
        P("layer", None, None),
    )
    return jax.shard_map(body, mesh=mesh, in_specs=in_specs, out_specs=out_specs, check_vma=False)
```

profile of v0, /device:TPU:0, one launch (start us, length us, event | category | flops | bytes accessed | tf_op | source)
XLA Modules:
  0.0 613.2 jit_solution(9725740799689017812)
XLA Ops:
  12.6 232.6 %while.44 = (s32[]{:T(128)}, bf16[256,512]{1,0:T(8,128)(2,1)S(1)}, bf16[4,256,512]{2,1,0:T(8,128)(2,1)}, bf16[4,256,512]{2,1,0:T(8,128)(2,1)}, f32[4,256,512]{2,...) while((s32[]{:T(128)}, bf16[256,512]{1,0:T(8,128)(2,1)S(1)}, ...), condition=%wide.region_1.2_spmd, body=%wide.region_0.1_spmd.sunk | while | flops 406065728 | bytes 27805224 | solution.py:166
  17.8 8.4 %all-to-all-start = ((bf16[32,8,512]{2,1,0:T(8,128)(2,1)}), bf16[32,8,512]{2,1,0:T(8,128)(2,1)S(1)}, u32[]{:S(2)}, u32[]{:S(2)}) async-start(bf16[32,8,512]{2,1,0:T(8,128)(2,1)} %fusion.105), calls=%async_computation | async-start | bytes 524288 | tf_op jit(solution)/shard_map/while/body/eval_jaxpr/all_to_all | solution.py:38
  28.6 6.6 %all-to-all-done = bf16[32,8,512]{2,1,0:T(8,128)(2,1)S(1)} async-done(((bf16[32,8,512]{2,1,0:T(8,128)(2,1)}), bf16[32,8,512]{2,1,0:T(8,128)(2,1)S(1)}, u32[]{:S(2)}, u32[]{:S(2)}) %all-to-all-start) | async-done | bytes 262176 | tf_op jit(solution)/shard_map/while/body/eval_jaxpr/all_to_all | solution.py:38
  39.4 3.5 collective-permute-start
  45.5 3.4 collective-permute-done
  54.1 3.9 all-to-all-start
  60.3 6.6 %all-to-all-done = bf16[32,8,512]{2,1,0:T(8,128)(2,1)S(1)} async-done(((bf16[32,8,512]{2,1,0:T(8,128)(2,1)}), bf16[32,8,512]{2,1,0:T(8,128)(2,1)S(1)}, u32[]{:S(2)}, u32[]{:S(2)}) %all-to-all-start) | async-done | bytes 262176 | tf_op jit(solution)/shard_map/while/body/eval_jaxpr/all_to_all | solution.py:38
  71.1 4.5 collective-permute-start
  78.3 3.4 collective-permute-done
  86.8 3.9 all-to-all-start
  93.0 6.6 %all-to-all-done = bf16[32,8,512]{2,1,0:T(8,128)(2,1)S(1)} async-done(((bf16[32,8,512]{2,1,0:T(8,128)(2,1)}), bf16[32,8,512]{2,1,0:T(8,128)(2,1)S(1)}, u32[]{:S(2)}, u32[]{:S(2)}) %all-to-all-start) | async-done | bytes 262176 | tf_op jit(solution)/shard_map/while/body/eval_jaxpr/all_to_all | solution.py:38
  103.8 4.5 collective-permute-start
  111.0 3.4 collective-permute-done
  119.5 3.9 all-to-all-start
  125.7 6.6 %all-to-all-done = bf16[32,8,512]{2,1,0:T(8,128)(2,1)S(1)} async-done(((bf16[32,8,512]{2,1,0:T(8,128)(2,1)}), bf16[32,8,512]{2,1,0:T(8,128)(2,1)S(1)}, u32[]{:S(2)}, u32[]{:S(2)}) %all-to-all-start) | async-done | bytes 262176 | tf_op jit(solution)/shard_map/while/body/eval_jaxpr/all_to_all | solution.py:38
  136.6 4.5 collective-permute-start
  152.2 3.9 all-to-all-start
  158.4 6.6 %all-to-all-done = bf16[32,8,512]{2,1,0:T(8,128)(2,1)S(1)} async-done(((bf16[32,8,512]{2,1,0:T(8,128)(2,1)}), bf16[32,8,512]{2,1,0:T(8,128)(2,1)S(1)}, u32[]{:S(2)}, u32[]{:S(2)}) %all-to-all-start) | async-done | bytes 262176 | tf_op jit(solution)/shard_map/while/body/eval_jaxpr/all_to_all | solution.py:38
  169.3 4.5 collective-permute-start
  184.9 3.9 all-to-all-start
  191.1 6.6 %all-to-all-done = bf16[32,8,512]{2,1,0:T(8,128)(2,1)S(1)} async-done(((bf16[32,8,512]{2,1,0:T(8,128)(2,1)}), bf16[32,8,512]{2,1,0:T(8,128)(2,1)S(1)}, u32[]{:S(2)}, u32[]{:S(2)}) %all-to-all-start) | async-done | bytes 262176 | tf_op jit(solution)/shard_map/while/body/eval_jaxpr/all_to_all | solution.py:38
  202.0 4.5 collective-permute-start
  217.6 3.9 all-to-all-start
  223.9 6.6 %all-to-all-done = bf16[32,8,512]{2,1,0:T(8,128)(2,1)S(1)} async-done(((bf16[32,8,512]{2,1,0:T(8,128)(2,1)}), bf16[32,8,512]{2,1,0:T(8,128)(2,1)S(1)}, u32[]{:S(2)}, u32[]{:S(2)}) %all-to-all-start) | async-done | bytes 262176 | tf_op jit(solution)/shard_map/while/body/eval_jaxpr/all_to_all | solution.py:38
  234.7 4.5 collective-permute-start
  249.1 247.1 %while.45 = (s32[]{:T(128)}, bf16[256,512]{1,0:T(8,128)(2,1)}, f32[512,512]{1,0:T(8,128)}, f32[512,512]{1,0:T(8,128)}, bf16[4,256,512]{2,1,0:T(8,128)(2,1)}, /*i...) while((s32[]{:T(128)}, bf16[256,512]{1,0:T(8,128)(2,1)}, ...), condition=%wide.region_5.6_spmd.clone, body=%wide.region_3.5_spmd.clone.sunk | while | flops 700186880 | bytes 31204564 | solution.py:196
  256.6 4.6 all-to-all-start.1
  265.3 4.8 all-to-all-done.1
  276.4 8.6 %collective-permute-done.1 = bf16[256,512]{1,0:T(8,128)(2,1)} collective-permute-done((bf16[256,512]{1,0:T(8,128)(2,1)S(1)}, bf16[256,512]{1,0:T(8,128)(2,1)}, u32[]{:S(2)}, u32[]{:S(2)}) %collective-permute-start.1) | collective-permute-done | bytes 262176 | tf_op jit(solution)/shard_map/while/body/eval_jaxpr/ppermute | solution.py:10
  292.5 4.6 all-to-all-start.1
  301.6 4.4 all-to-all-done.1
  312.3 7.9 %collective-permute-done.1 = bf16[256,512]{1,0:T(8,128)(2,1)} collective-permute-done((bf16[256,512]{1,0:T(8,128)(2,1)S(1)}, bf16[256,512]{1,0:T(8,128)(2,1)}, u32[]{:S(2)}, u32[]{:S(2)}) %collective-permute-start.1) | collective-permute-done | bytes 262176 | tf_op jit(solution)/shard_map/while/body/eval_jaxpr/ppermute | solution.py:10
  327.7 4.6 all-to-all-start.1
  336.8 4.4 all-to-all-done.1
  347.5 7.9 %collective-permute-done.1 = bf16[256,512]{1,0:T(8,128)(2,1)} collective-permute-done((bf16[256,512]{1,0:T(8,128)(2,1)S(1)}, bf16[256,512]{1,0:T(8,128)(2,1)}, u32[]{:S(2)}, u32[]{:S(2)}) %collective-permute-start.1) | collective-permute-done | bytes 262176 | tf_op jit(solution)/shard_map/while/body/eval_jaxpr/ppermute | solution.py:10
  362.9 4.6 all-to-all-start.1
  372.0 4.4 all-to-all-done.1
  382.7 7.9 %collective-permute-done.1 = bf16[256,512]{1,0:T(8,128)(2,1)} collective-permute-done((bf16[256,512]{1,0:T(8,128)(2,1)S(1)}, bf16[256,512]{1,0:T(8,128)(2,1)}, u32[]{:S(2)}, u32[]{:S(2)}) %collective-permute-start.1) | collective-permute-done | bytes 262176 | tf_op jit(solution)/shard_map/while/body/eval_jaxpr/ppermute | solution.py:10
  398.1 4.6 all-to-all-start.1
  407.2 4.4 all-to-all-done.1
  417.9 7.9 %collective-permute-done.1 = bf16[256,512]{1,0:T(8,128)(2,1)} collective-permute-done((bf16[256,512]{1,0:T(8,128)(2,1)S(1)}, bf16[256,512]{1,0:T(8,128)(2,1)}, u32[]{:S(2)}, u32[]{:S(2)}) %collective-permute-start.1) | collective-permute-done | bytes 262176 | tf_op jit(solution)/shard_map/while/body/eval_jaxpr/ppermute | solution.py:10
  433.3 4.6 all-to-all-start.1
  442.4 4.4 all-to-all-done.1
  453.1 7.9 %collective-permute-done.1 = bf16[256,512]{1,0:T(8,128)(2,1)} collective-permute-done((bf16[256,512]{1,0:T(8,128)(2,1)S(1)}, bf16[256,512]{1,0:T(8,128)(2,1)}, u32[]{:S(2)}, u32[]{:S(2)}) %collective-permute-start.1) | collective-permute-done | bytes 262176 | tf_op jit(solution)/shard_map/while/body/eval_jaxpr/ppermute | solution.py:10
  468.5 4.6 all-to-all-start.1
  477.6 4.4 all-to-all-done.1
  488.3 7.9 %collective-permute-done.1 = bf16[256,512]{1,0:T(8,128)(2,1)} collective-permute-done((bf16[256,512]{1,0:T(8,128)(2,1)S(1)}, bf16[256,512]{1,0:T(8,128)(2,1)}, u32[]{:S(2)}, u32[]{:S(2)}) %collective-permute-start.1) | collective-permute-done | bytes 262176 | tf_op jit(solution)/shard_map/while/body/eval_jaxpr/ppermute | solution.py:10
  498.8 103.2 %all-reduce.3.cloned.1.call-done = (bf16[1,512,512]{2,1,0:T(8,128)(2,1)}, bf16[1,512,512]{2,1,0:T(8,128)(2,1)}) async-done(((bf16[1,512,512]{2,1,0:T(8,128)(2,1)}, bf16[1,512,512]{2,1,0:T(8,128)(2,1)}), (bf16[1,512,512]{2,1,0:T(8,128)(2,1)}, bf16[1,512,512]{2,1,0:T(8,128)(2,1)})) %all-reduce.3.cloned.1.call-update) | async-done | bytes 1048592 | tf_op jit(solution)/shard_map/psum | solution.py:109
  (405 shorter events, 255.8 us)
Async XLA Ops:
  7.2 238.1 %copy-start = (bf16[512,172]{0,1:T(8,128)(2,1)S(1)}, bf16[512,172]{0,1:T(8,128)(2,1)}, u32[]{:S(2)}) copy-start(bf16[512,172]{0,1:T(8,128)(2,1)} %param.17) | copy-start | bytes 528388
  7.2 594.8 %all-reduce.3.cloned.1.call-start = ((), (), s32[]{:S(2)}) async-start(), calls=%async_computation.2 | async-start | bytes 2097152 | tf_op jit(solution)/shard_map/psum | solution.py:109
  12.6 233.2 %copy-start.9 = (s32[4,256]{1,0:T(4,128)S(1)}, s32[4,256]{1,0:T(4,128)}, u32[]{:S(2)}) copy-start(s32[4,256]{1,0:T(4,128)} %param.18) | copy-start | bytes 12292
  12.6 13.7 %copy-start.5 = (bf16[4,256,512]{2,1,0:T(8,128)(2,1)}, bf16[4,256,512]{2,1,0:T(8,128)(2,1)S(1)}, u32[]{:S(2)}) copy-start(bf16[4,256,512]{2,1,0:T(8,128)(2,1)S(1)} %get-tuple-element.1101) | copy-start | bytes 3145732 | tf_op jit(solution)/shard_map/while
  17.8 17.4 %all-to-all-start = ((bf16[32,8,512]{2,1,0:T(8,128)(2,1)}), bf16[32,8,512]{2,1,0:T(8,128)(2,1)S(1)}, u32[]{:S(2)}, u32[]{:S(2)}) async-start(bf16[32,8,512]{2,1,0:T(8,128)(2,1)} %fusion.105), calls=%async_computation | async-start | bytes 524288 | tf_op jit(solution)/shard_map/while/body/eval_jaxpr/all_to_all | solution.py:38
  39.4 9.6 %copy-start.6 = (bf16[4,256,512]{2,1,0:T(8,128)(2,1)S(1)}, bf16[4,256,512]{2,1,0:T(8,128)(2,1)}, u32[]{:S(2)}) copy-start(bf16[4,256,512]{2,1,0:T(8,128)(2,1)} %get-tuple-element.1120) | copy-start | bytes 3145732 | tf_op jit(solution)/shard_map/while
  39.4 9.6 %collective-permute-start = (bf16[256,512]{1,0:T(8,128)(2,1)S(1)}, bf16[256,512]{1,0:T(8,128)(2,1)S(1)}, u32[]{:S(2)}, u32[]{:S(2)}) collective-permute-start(bf16[256,512]{1,0:T(8,128)(2,1)S(1)} %get-tuple-element.1054), channel_id=1, source_target_pairs={{0,32},{32,64},{64,96},{1,33},{33,65},{65,97},{2,34},{34,66},{66,9... | collective-permute-start | bytes 786440 | tf_op jit(solution)/shard_map/while/body/eval_jaxpr/ppermute | solution.py:10
  49.0 9.1 %copy-start.5 = (bf16[4,256,512]{2,1,0:T(8,128)(2,1)}, bf16[4,256,512]{2,1,0:T(8,128)(2,1)S(1)}, u32[]{:S(2)}) copy-start(bf16[4,256,512]{2,1,0:T(8,128)(2,1)S(1)} %get-tuple-element.1101) | copy-start | bytes 3145732 | tf_op jit(solution)/shard_map/while
  54.1 12.8 %all-to-all-start = ((bf16[32,8,512]{2,1,0:T(8,128)(2,1)}), bf16[32,8,512]{2,1,0:T(8,128)(2,1)S(1)}, u32[]{:S(2)}, u32[]{:S(2)}) async-start(bf16[32,8,512]{2,1,0:T(8,128)(2,1)} %fusion.105), calls=%async_computation | async-start | bytes 524288 | tf_op jit(solution)/shard_map/while/body/eval_jaxpr/all_to_all | solution.py:38
  71.1 10.5 %copy-start.6 = (bf16[4,256,512]{2,1,0:T(8,128)(2,1)S(1)}, bf16[4,256,512]{2,1,0:T(8,128)(2,1)}, u32[]{:S(2)}) copy-start(bf16[4,256,512]{2,1,0:T(8,128)(2,1)} %get-tuple-element.1120) | copy-start | bytes 3145732 | tf_op jit(solution)/shard_map/while
  71.1 10.5 %collective-permute-start = (bf16[256,512]{1,0:T(8,128)(2,1)S(1)}, bf16[256,512]{1,0:T(8,128)(2,1)S(1)}, u32[]{:S(2)}, u32[]{:S(2)}) collective-permute-start(bf16[256,512]{1,0:T(8,128)(2,1)S(1)} %get-tuple-element.1054), channel_id=1, source_target_pairs={{0,32},{32,64},{64,96},{1,33},{33,65},{65,97},{2,34},{34,66},{66,9... | collective-permute-start | bytes 786440 | tf_op jit(solution)/shard_map/while/body/eval_jaxpr/ppermute | solution.py:10
  81.7 9.1 %copy-start.5 = (bf16[4,256,512]{2,1,0:T(8,128)(2,1)}, bf16[4,256,512]{2,1,0:T(8,128)(2,1)S(1)}, u32[]{:S(2)}) copy-start(bf16[4,256,512]{2,1,0:T(8,128)(2,1)S(1)} %get-tuple-element.1101) | copy-start | bytes 3145732 | tf_op jit(solution)/shard_map/while
  86.8 12.8 %all-to-all-start = ((bf16[32,8,512]{2,1,0:T(8,128)(2,1)}), bf16[32,8,512]{2,1,0:T(8,128)(2,1)S(1)}, u32[]{:S(2)}, u32[]{:S(2)}) async-start(bf16[32,8,512]{2,1,0:T(8,128)(2,1)} %fusion.105), calls=%async_computation | async-start | bytes 524288 | tf_op jit(solution)/shard_map/while/body/eval_jaxpr/all_to_all | solution.py:38
  103.8 10.6 %copy-start.6 = (bf16[4,256,512]{2,1,0:T(8,128)(2,1)S(1)}, bf16[4,256,512]{2,1,0:T(8,128)(2,1)}, u32[]{:S(2)}) copy-start(bf16[4,256,512]{2,1,0:T(8,128)(2,1)} %get-tuple-element.1120) | copy-start | bytes 3145732 | tf_op jit(solution)/shard_map/while
  103.8 10.6 %collective-permute-start = (bf16[256,512]{1,0:T(8,128)(2,1)S(1)}, bf16[256,512]{1,0:T(8,128)(2,1)S(1)}, u32[]{:S(2)}, u32[]{:S(2)}) collective-permute-start(bf16[256,512]{1,0:T(8,128)(2,1)S(1)} %get-tuple-element.1054), channel_id=1, source_target_pairs={{0,32},{32,64},{64,96},{1,33},{33,65},{65,97},{2,34},{34,66},{66,9... | collective-permute-start | bytes 786440 | tf_op jit(solution)/shard_map/while/body/eval_jaxpr/ppermute | solution.py:10
  119.5 12.8 %all-to-all-start = ((bf16[32,8,512]{2,1,0:T(8,128)(2,1)}), bf16[32,8,512]{2,1,0:T(8,128)(2,1)S(1)}, u32[]{:S(2)}, u32[]{:S(2)}) async-start(bf16[32,8,512]{2,1,0:T(8,128)(2,1)} %fusion.105), calls=%async_computation | async-start | bytes 524288 | tf_op jit(solution)/shard_map/while/body/eval_jaxpr/all_to_all | solution.py:38
  136.6 10.6 %copy-start.6 = (bf16[4,256,512]{2,1,0:T(8,128)(2,1)S(1)}, bf16[4,256,512]{2,1,0:T(8,128)(2,1)}, u32[]{:S(2)}) copy-start(bf16[4,256,512]{2,1,0:T(8,128)(2,1)} %get-tuple-element.1120) | copy-start | bytes 3145732 | tf_op jit(solution)/shard_map/while
  136.6 10.6 %collective-permute-start = (bf16[256,512]{1,0:T(8,128)(2,1)S(1)}, bf16[256,512]{1,0:T(8,128)(2,1)S(1)}, u32[]{:S(2)}, u32[]{:S(2)}) collective-permute-start(bf16[256,512]{1,0:T(8,128)(2,1)S(1)} %get-tuple-element.1054), channel_id=1, source_target_pairs={{0,32},{32,64},{64,96},{1,33},{33,65},{65,97},{2,34},{34,66},{66,9... | collective-permute-start | bytes 786440 | tf_op jit(solution)/shard_map/while/body/eval_jaxpr/ppermute | solution.py:10
  152.2 12.8 %all-to-all-start = ((bf16[32,8,512]{2,1,0:T(8,128)(2,1)}), bf16[32,8,512]{2,1,0:T(8,128)(2,1)S(1)}, u32[]{:S(2)}, u32[]{:S(2)}) async-start(bf16[32,8,512]{2,1,0:T(8,128)(2,1)} %fusion.105), calls=%async_computation | async-start | bytes 524288 | tf_op jit(solution)/shard_map/while/body/eval_jaxpr/all_to_all | solution.py:38
  169.3 10.6 %copy-start.6 = (bf16[4,256,512]{2,1,0:T(8,128)(2,1)S(1)}, bf16[4,256,512]{2,1,0:T(8,128)(2,1)}, u32[]{:S(2)}) copy-start(bf16[4,256,512]{2,1,0:T(8,128)(2,1)} %get-tuple-element.1120) | copy-start | bytes 3145732 | tf_op jit(solution)/shard_map/while
  169.3 10.6 %collective-permute-start = (bf16[256,512]{1,0:T(8,128)(2,1)S(1)}, bf16[256,512]{1,0:T(8,128)(2,1)S(1)}, u32[]{:S(2)}, u32[]{:S(2)}) collective-permute-start(bf16[256,512]{1,0:T(8,128)(2,1)S(1)} %get-tuple-element.1054), channel_id=1, source_target_pairs={{0,32},{32,64},{64,96},{1,33},{33,65},{65,97},{2,34},{34,66},{66,9... | collective-permute-start | bytes 786440 | tf_op jit(solution)/shard_map/while/body/eval_jaxpr/ppermute | solution.py:10
  184.9 12.8 %all-to-all-start = ((bf16[32,8,512]{2,1,0:T(8,128)(2,1)}), bf16[32,8,512]{2,1,0:T(8,128)(2,1)S(1)}, u32[]{:S(2)}, u32[]{:S(2)}) async-start(bf16[32,8,512]{2,1,0:T(8,128)(2,1)} %fusion.105), calls=%async_computation | async-start | bytes 524288 | tf_op jit(solution)/shard_map/while/body/eval_jaxpr/all_to_all | solution.py:38
  202.0 10.6 %copy-start.6 = (bf16[4,256,512]{2,1,0:T(8,128)(2,1)S(1)}, bf16[4,256,512]{2,1,0:T(8,128)(2,1)}, u32[]{:S(2)}) copy-start(bf16[4,256,512]{2,1,0:T(8,128)(2,1)} %get-tuple-element.1120) | copy-start | bytes 3145732 | tf_op jit(solution)/shard_map/while
  202.0 10.6 %collective-permute-start = (bf16[256,512]{1,0:T(8,128)(2,1)S(1)}, bf16[256,512]{1,0:T(8,128)(2,1)S(1)}, u32[]{:S(2)}, u32[]{:S(2)}) collective-permute-start(bf16[256,512]{1,0:T(8,128)(2,1)S(1)} %get-tuple-element.1054), channel_id=1, source_target_pairs={{0,32},{32,64},{64,96},{1,33},{33,65},{65,97},{2,34},{34,66},{66,9... | collective-permute-start | bytes 786440 | tf_op jit(solution)/shard_map/while/body/eval_jaxpr/ppermute | solution.py:10
  217.6 12.8 %all-to-all-start = ((bf16[32,8,512]{2,1,0:T(8,128)(2,1)}), bf16[32,8,512]{2,1,0:T(8,128)(2,1)S(1)}, u32[]{:S(2)}, u32[]{:S(2)}) async-start(bf16[32,8,512]{2,1,0:T(8,128)(2,1)} %fusion.105), calls=%async_computation | async-start | bytes 524288 | tf_op jit(solution)/shard_map/while/body/eval_jaxpr/all_to_all | solution.py:38
  234.7 10.6 %copy-start.6 = (bf16[4,256,512]{2,1,0:T(8,128)(2,1)S(1)}, bf16[4,256,512]{2,1,0:T(8,128)(2,1)}, u32[]{:S(2)}) copy-start(bf16[4,256,512]{2,1,0:T(8,128)(2,1)} %get-tuple-element.1120) | copy-start | bytes 3145732 | tf_op jit(solution)/shard_map/while
  234.7 10.6 %collective-permute-start = (bf16[256,512]{1,0:T(8,128)(2,1)S(1)}, bf16[256,512]{1,0:T(8,128)(2,1)S(1)}, u32[]{:S(2)}, u32[]{:S(2)}) collective-permute-start(bf16[256,512]{1,0:T(8,128)(2,1)S(1)} %get-tuple-element.1054), channel_id=1, source_target_pairs={{0,32},{32,64},{64,96},{1,33},{33,65},{65,97},{2,34},{34,66},{66,9... | collective-permute-start | bytes 786440 | tf_op jit(solution)/shard_map/while/body/eval_jaxpr/ppermute | solution.py:10
  256.6 13.5 %all-to-all-start.1 = ((bf16[32,8,512]{2,1,0:T(8,128)(2,1)}), bf16[32,8,512]{2,1,0:T(8,128)(2,1)}, u32[]{:S(2)}, u32[]{:S(2)}) async-start(bf16[32,8,512]{2,1,0:T(8,128)(2,1)} %bitcast.226), calls=%async_computation.1 | async-start | bytes 524288 | tf_op jit(solution)/shard_map/while/body/eval_jaxpr/all_to_all | solution.py:95
  265.0 10.0 %copy-start.2 = (f32[512,512]{1,0:T(8,128)S(1)}, f32[512,512]{1,0:T(8,128)}, u32[]{:S(2)}) copy-start(f32[512,512]{1,0:T(8,128)} %get-tuple-element.1159) | copy-start | bytes 3145732 | tf_op jit(solution)/shard_map/while
  273.7 11.3 %collective-permute-start.1 = (bf16[256,512]{1,0:T(8,128)(2,1)S(1)}, bf16[256,512]{1,0:T(8,128)(2,1)}, u32[]{:S(2)}, u32[]{:S(2)}) collective-permute-start(bf16[256,512]{1,0:T(8,128)(2,1)S(1)} %get-tuple-element.1075), channel_id=1, source_target_pairs={{32,0},{64,32},{96,64},{33,1},{65,33},{97,65},{34,2},{66,34},{98,6... | collective-permute-start | bytes 786440 | tf_op jit(solution)/shard_map/while/body/eval_jaxpr/ppermute | solution.py:10
  292.5 13.5 %all-to-all-start.1 = ((bf16[32,8,512]{2,1,0:T(8,128)(2,1)}), bf16[32,8,512]{2,1,0:T(8,128)(2,1)}, u32[]{:S(2)}, u32[]{:S(2)}) async-start(bf16[32,8,512]{2,1,0:T(8,128)(2,1)} %bitcast.226), calls=%async_computation.1 | async-start | bytes 524288 | tf_op jit(solution)/shard_map/while/body/eval_jaxpr/all_to_all | solution.py:95
  301.3 9.7 %copy-start.2 = (f32[512,512]{1,0:T(8,128)S(1)}, f32[512,512]{1,0:T(8,128)}, u32[]{:S(2)}) copy-start(f32[512,512]{1,0:T(8,128)} %get-tuple-element.1159) | copy-start | bytes 3145732 | tf_op jit(solution)/shard_map/while
  309.7 10.5 %collective-permute-start.1 = (bf16[256,512]{1,0:T(8,128)(2,1)S(1)}, bf16[256,512]{1,0:T(8,128)(2,1)}, u32[]{:S(2)}, u32[]{:S(2)}) collective-permute-start(bf16[256,512]{1,0:T(8,128)(2,1)S(1)} %get-tuple-element.1075), channel_id=1, source_target_pairs={{32,0},{64,32},{96,64},{33,1},{65,33},{97,65},{34,2},{66,34},{98,6... | collective-permute-start | bytes 786440 | tf_op jit(solution)/shard_map/while/body/eval_jaxpr/ppermute | solution.py:10
  327.7 13.5 %all-to-all-start.1 = ((bf16[32,8,512]{2,1,0:T(8,128)(2,1)}), bf16[32,8,512]{2,1,0:T(8,128)(2,1)}, u32[]{:S(2)}, u32[]{:S(2)}) async-start(bf16[32,8,512]{2,1,0:T(8,128)(2,1)} %bitcast.226), calls=%async_computation.1 | async-start | bytes 524288 | tf_op jit(solution)/shard_map/while/body/eval_jaxpr/all_to_all | solution.py:95
  336.5 9.7 %copy-start.2 = (f32[512,512]{1,0:T(8,128)S(1)}, f32[512,512]{1,0:T(8,128)}, u32[]{:S(2)}) copy-start(f32[512,512]{1,0:T(8,128)} %get-tuple-element.1159) | copy-start | bytes 3145732 | tf_op jit(solution)/shard_map/while
  344.9 10.5 %collective-permute-start.1 = (bf16[256,512]{1,0:T(8,128)(2,1)S(1)}, bf16[256,512]{1,0:T(8,128)(2,1)}, u32[]{:S(2)}, u32[]{:S(2)}) collective-permute-start(bf16[256,512]{1,0:T(8,128)(2,1)S(1)} %get-tuple-element.1075), channel_id=1, source_target_pairs={{32,0},{64,32},{96,64},{33,1},{65,33},{97,65},{34,2},{66,34},{98,6... | collective-permute-start | bytes 786440 | tf_op jit(solution)/shard_map/while/body/eval_jaxpr/ppermute | solution.py:10
  362.9 13.5 %all-to-all-start.1 = ((bf16[32,8,512]{2,1,0:T(8,128)(2,1)}), bf16[32,8,512]{2,1,0:T(8,128)(2,1)}, u32[]{:S(2)}, u32[]{:S(2)}) async-start(bf16[32,8,512]{2,1,0:T(8,128)(2,1)} %bitcast.226), calls=%async_computation.1 | async-start | bytes 524288 | tf_op jit(solution)/shard_map/while/body/eval_jaxpr/all_to_all | solution.py:95
  371.7 9.7 %copy-start.2 = (f32[512,512]{1,0:T(8,128)S(1)}, f32[512,512]{1,0:T(8,128)}, u32[]{:S(2)}) copy-start(f32[512,512]{1,0:T(8,128)} %get-tuple-element.1159) | copy-start | bytes 3145732 | tf_op jit(solution)/shard_map/while
  380.1 10.5 %collective-permute-start.1 = (bf16[256,512]{1,0:T(8,128)(2,1)S(1)}, bf16[256,512]{1,0:T(8,128)(2,1)}, u32[]{:S(2)}, u32[]{:S(2)}) collective-permute-start(bf16[256,512]{1,0:T(8,128)(2,1)S(1)} %get-tuple-element.1075), channel_id=1, source_target_pairs={{32,0},{64,32},{96,64},{33,1},{65,33},{97,65},{34,2},{66,34},{98,6... | collective-permute-start | bytes 786440 | tf_op jit(solution)/shard_map/while/body/eval_jaxpr/ppermute | solution.py:10
  398.1 13.5 %all-to-all-start.1 = ((bf16[32,8,512]{2,1,0:T(8,128)(2,1)}), bf16[32,8,512]{2,1,0:T(8,128)(2,1)}, u32[]{:S(2)}, u32[]{:S(2)}) async-start(bf16[32,8,512]{2,1,0:T(8,128)(2,1)} %bitcast.226), calls=%async_computation.1 | async-start | bytes 524288 | tf_op jit(solution)/shard_map/while/body/eval_jaxpr/all_to_all | solution.py:95
  406.9 9.7 %copy-start.2 = (f32[512,512]{1,0:T(8,128)S(1)}, f32[512,512]{1,0:T(8,128)}, u32[]{:S(2)}) copy-start(f32[512,512]{1,0:T(8,128)} %get-tuple-element.1159) | copy-start | bytes 3145732 | tf_op jit(solution)/shard_map/while
  415.2 10.5 %collective-permute-start.1 = (bf16[256,512]{1,0:T(8,128)(2,1)S(1)}, bf16[256,512]{1,0:T(8,128)(2,1)}, u32[]{:S(2)}, u32[]{:S(2)}) collective-permute-start(bf16[256,512]{1,0:T(8,128)(2,1)S(1)} %get-tuple-element.1075), channel_id=1, source_target_pairs={{32,0},{64,32},{96,64},{33,1},{65,33},{97,65},{34,2},{66,34},{98,6... | collective-permute-start | bytes 786440 | tf_op jit(solution)/shard_map/while/body/eval_jaxpr/ppermute | solution.py:10
  433.3 13.5 %all-to-all-start.1 = ((bf16[32,8,512]{2,1,0:T(8,128)(2,1)}), bf16[32,8,512]{2,1,0:T(8,128)(2,1)}, u32[]{:S(2)}, u32[]{:S(2)}) async-start(bf16[32,8,512]{2,1,0:T(8,128)(2,1)} %bitcast.226), calls=%async_computation.1 | async-start | bytes 524288 | tf_op jit(solution)/shard_map/while/body/eval_jaxpr/all_to_all | solution.py:95
  442.0 9.7 %copy-start.2 = (f32[512,512]{1,0:T(8,128)S(1)}, f32[512,512]{1,0:T(8,128)}, u32[]{:S(2)}) copy-start(f32[512,512]{1,0:T(8,128)} %get-tuple-element.1159) | copy-start | bytes 3145732 | tf_op jit(solution)/shard_map/while
  450.4 10.5 %collective-permute-start.1 = (bf16[256,512]{1,0:T(8,128)(2,1)S(1)}, bf16[256,512]{1,0:T(8,128)(2,1)}, u32[]{:S(2)}, u32[]{:S(2)}) collective-permute-start(bf16[256,512]{1,0:T(8,128)(2,1)S(1)} %get-tuple-element.1075), channel_id=1, source_target_pairs={{32,0},{64,32},{96,64},{33,1},{65,33},{97,65},{34,2},{66,34},{98,6... | collective-permute-start | bytes 786440 | tf_op jit(solution)/shard_map/while/body/eval_jaxpr/ppermute | solution.py:10
  468.5 13.5 %all-to-all-start.1 = ((bf16[32,8,512]{2,1,0:T(8,128)(2,1)}), bf16[32,8,512]{2,1,0:T(8,128)(2,1)}, u32[]{:S(2)}, u32[]{:S(2)}) async-start(bf16[32,8,512]{2,1,0:T(8,128)(2,1)} %bitcast.226), calls=%async_computation.1 | async-start | bytes 524288 | tf_op jit(solution)/shard_map/while/body/eval_jaxpr/all_to_all | solution.py:95
  477.2 9.7 %copy-start.2 = (f32[512,512]{1,0:T(8,128)S(1)}, f32[512,512]{1,0:T(8,128)}, u32[]{:S(2)}) copy-start(f32[512,512]{1,0:T(8,128)} %get-tuple-element.1159) | copy-start | bytes 3145732 | tf_op jit(solution)/shard_map/while
  485.6 10.5 %collective-permute-start.1 = (bf16[256,512]{1,0:T(8,128)(2,1)S(1)}, bf16[256,512]{1,0:T(8,128)(2,1)}, u32[]{:S(2)}, u32[]{:S(2)}) collective-permute-start(bf16[256,512]{1,0:T(8,128)(2,1)S(1)} %get-tuple-element.1075), channel_id=1, source_target_pairs={{32,0},{64,32},{96,64},{33,1},{65,33},{97,65},{34,2},{66,34},{98,6... | collective-permute-start | bytes 786440 | tf_op jit(solution)/shard_map/while/body/eval_jaxpr/ppermute | solution.py:10
  (22 other events, 111.0 us)
Sparse Core Ops, SparseCore 0:
  498.9 103.0 all-reduce.2
where the time goes:
time: 619 us; the launch traced here: 613 us
  waiting for transfers between devices  261 us (42%)
  starting transfers between devices  103 us (17%)
  matrix products  99.3 us (16%)
  other arithmetic  80.9 us (13%)
  local copies, waits for them, and re-layouts  53 us (9%)
  between operations  14.1 us (2%)
    psum x1, waiting for transfers between devices, finish_grads(): lax.psum(grad_pair[0].astype(jnp.bfloat16), 'node').astype(jnp.float32)  103 us
    ppermute x14, waiting for transfers between devices, from_behind(): lax.ppermute(value, axis, [(source, source + steps) for source in range(f...  79.7 us
    all_to_all x7, waiting for transfers between devices, layer_forward(): lax.all_to_all(outgoing, 'node', split_axis=0, concat_axis=0, tiled=True)  46.2 us
    ppermute x14, starting transfers between devices, from_behind(): lax.ppermute(value, axis, [(source, source + steps) for source in range(f...  39.6 us
    dynamic_update_slice x28, other arithmetic, put_row(): lax.dynamic_update_index_in_dim(buffer, jnp.where(valid, value, current),...  36.2 us
    all_to_all x7, starting transfers between devices, layer_backward(): lax.all_to_all(remote, 'node', split_axis=0, concat_axis=0, tiled=True)  32.2 us
    all_to_all x7, starting transfers between devices, layer_forward(): lax.all_to_all(outgoing, 'node', split_axis=0, concat_axis=0, tiled=True)  31.6 us
    all_to_all x7, waiting for transfers between devices, layer_backward(): lax.all_to_all(remote, 'node', split_axis=0, concat_axis=0, tiled=True)  31.5 us
  transfers between devices with their start and end apart: 29, of which 29 were waited for; matrix products, arithmetic and copies ran while one was open for 12% of the time, Pallas kernels for 0%

commit v1 on v0

v1 whole, which is shorter than its diff:
```python
import functools

import jax
import jax.numpy as jnp
from jax import lax
from jax.experimental import pallas as pl
from jax.experimental.pallas import tpu as pltpu
from jax.sharding import PartitionSpec as P

BF = jnp.bfloat16
F32 = jnp.float32
NN = (((1,), (0,)), ((), ()))
NT = (((1,), (1,)), ((), ()))
TN = (((0,), (0,)), ((), ()))
ANY = pl.BlockSpec(memory_space=pl.ANY)
VMEM_BYTES = 40 * 1024 * 1024


def dot(a, b, dims=NN):
    return lax.dot_general(a, b, dims, preferred_element_type=F32)


def shift(value, axis, steps):
    count = lax.axis_size(axis)
    return lax.ppermute(value, axis, [(i, (i + steps) % count) for i in range(count)])


def sibling(value):
    count = lax.axis_size("node")
    return lax.ppermute(value, "node", [(i, i ^ 1) for i in range(count)])


def exchange(value):
    return lax.all_to_all(value, "node", split_axis=0, concat_axis=0, tiled=True)


def whole(shape):
    return pl.BlockSpec(shape, lambda i, ids, cols: (0,) * len(shape))


def of_span(shape):
    return pl.BlockSpec((None, *shape), lambda i, ids, cols: (ids[0], *((0,) * len(shape))))


def at_offset(shape, layer):
    return pl.BlockSpec(
        (None, *shape),
        lambda i, ids, cols: (lax.rem(layer - ids[0] + 4, 4), *((0,) * len(shape))),
    )


def sds(shape, dtype):
    return jax.ShapeDtypeStruct(shape, dtype)


def run(kernel, name, scalars, ins, outs, scratch=(), aliases=None, flops=0, moved=0):
    arrays = [a for a, _ in ins]
    return pl.pallas_call(
        kernel,
        name=name,
        grid_spec=pltpu.PrefetchScalarGridSpec(
            num_scalar_prefetch=2,
            grid=(1,),
            in_specs=[s for _, s in ins],
            out_specs=[s for _, s in outs],
            scratch_shapes=list(scratch),
        ),
        out_shape=[o for o, _ in outs],
        input_output_aliases={} if aliases is None else {k + 2: v for k, v in aliases.items()},
        compiler_params=pltpu.CompilerParams(vmem_limit_bytes=VMEM_BYTES),
        cost_estimate=pl.CostEstimate(flops=flops, bytes_accessed=moved, transcendentals=0),
    )(*scalars, *arrays)


def weight_copies(which, core, w_refs, w_scr, sems):
    own_s, own_n, left, left_x, right, right_x, far_a, far_b, far_ax, far_bx = w_refs
    half = w_scr.shape[1] // 2
    top, low = pl.ds(0, half), pl.ds(half, half)
    plans = {
        0: [(own_s, w_scr.at[0]), (own_n, w_scr.at[1])],
        1: [(right, w_scr.at[core]), (right_x, w_scr.at[1 - core])],
        2: [
            (far_a, w_scr.at[core, top]),
            (far_b, w_scr.at[core, low]),
            (far_ax, w_scr.at[1 - core, top]),
            (far_bx, w_scr.at[1 - core, low]),
        ],
        3: [(left, w_scr.at[core]), (left_x, w_scr.at[1 - core])],
    }
    return [pltpu.make_async_copy(s, d, sems.at[n]) for n, (s, d) in enumerate(plans[which])]


def each_weight(layer, ids, w_refs, w_scr, sems, act):
    which = lax.rem(layer - ids[0] + 4, 4)
    for option in range(4):

        @pl.when(which == option)
        def _():
            for copy in weight_copies(option, ids[1], w_refs, w_scr, sems):
                act(copy)


def start_weights(layer, ids, w_refs, w_scr, sems):
    each_weight(layer, ids, w_refs, w_scr, sems, lambda copy: copy.start())


def wait_weights(layer, ids, w_refs, w_scr, sems):
    each_weight(layer, ids, w_refs, w_scr, sems, lambda copy: copy.wait())


def side_by_side(vals_ref, r, degree):
    return jnp.concatenate([vals_ref[r, j] for j in range(degree)], axis=1)


def aggregate_rows(ids, cols, vals_ref, ext):
    tiles, degree, size = vals_ref.shape[0], vals_ref.shape[1], vals_ref.shape[2]
    parts = []
    for r in range(tiles):
        base = ids[0] * (tiles * degree) + r * degree
        picked = jnp.concatenate(
            [ext[pl.ds(pl.multiple_of(cols[base + j] * size, size), size), :] for j in range(degree)],
            axis=0,
        )
        parts.append(dot(side_by_side(vals_ref, r, degree), picked))
    return jnp.concatenate(parts, axis=0).astype(BF)


def spread_rows(ids, cols, vals_ref, d_agg, d_ext):
    tiles, degree, size = vals_ref.shape[0], vals_ref.shape[1], vals_ref.shape[2]
    d_ext[...] = jnp.zeros_like(d_ext)
    for r in range(tiles):
        base = ids[0] * (tiles * degree) + r * degree
        pieces = dot(side_by_side(vals_ref, r, degree), d_agg[r * size : (r + 1) * size], TN)
        for j in range(degree):
            rows = pl.ds(pl.multiple_of(cols[base + j] * size, size), size)
            d_ext[rows, :] += pieces[j * size : (j + 1) * size]


def sigmoid(v):
    return 1.0 / (1.0 + jnp.exp(-v))


def pre_kernel(ids, cols, h_ref, rows_ref, counts_ref, pick_ref, out_ref):
    peers, slots = rows_ref.shape
    total, node_rows = pick_ref.shape
    bits = slots.bit_length() - 1
    slot = lax.broadcasted_iota(jnp.int32, (total, peers), 0)
    owner = lax.broadcasted_iota(jnp.int32, (total, peers), 1)
    mine = lax.shift_right_logical(slot, bits) == owner
    wide = dot(mine.astype(F32).astype(BF), rows_ref[...].astype(F32).astype(BF))
    slot_k = lax.broadcasted_iota(jnp.int32, (total, slots), 0) & (slots - 1)
    in_slot = slot_k == lax.broadcasted_iota(jnp.int32, (total, slots), 1)
    row = jnp.sum(jnp.where(in_slot, wide, 0.0), axis=1, keepdims=True)
    counts = jnp.broadcast_to(counts_ref[...].astype(F32), (total, peers))
    count = jnp.sum(jnp.where(mine, counts, 0.0), axis=1, keepdims=True)
    k = (lax.broadcasted_iota(jnp.int32, (total, 1), 0) & (slots - 1)).astype(F32)
    row = jnp.where(k < count, row, -1.0)
    place = lax.broadcasted_iota(jnp.int32, (total, node_rows), 1).astype(F32)
    pick = (place == row).astype(F32).astype(BF)
    pick_ref[...] = pick
    out_ref[...] = dot(pick, h_ref[...]).astype(BF)


def forward_math(layer, ids, cols, h_ref, arr_ref, vals_ref, w_refs, ext, w_scr, sems):
    start_weights(layer, ids, w_refs, w_scr, sems)
    rows = h_ref.shape[0]
    ext[0:rows, :] = h_ref[...]
    ext[rows : 2 * rows, :] = arr_ref[...]
    agg = aggregate_rows(ids, cols, vals_ref, ext)
    wait_weights(layer, ids, w_refs, w_scr, sems)
    pre = dot(h_ref[...], w_scr[0]) + dot(agg, w_scr[1])
    sig = sigmoid(pre)
    return agg, pre, sig, (pre * sig).astype(BF)


def forward_kernel(layer, first, ids, cols, h_ref, arr_ref, vals_ref, pick_ref, *rest):
    w_refs, rest = rest[:10], rest[10:]
    if not first:
        rest = rest[1:]
    agg_ref, pre_ref, hid_ref, out_ref, buf_ref, ext, w_scr, sems = rest
    agg, pre, _, hid = forward_math(
        layer, ids, cols, h_ref, arr_ref, vals_ref, w_refs, ext, w_scr, sems
    )
    agg_ref[...] = agg
    pre_ref[...] = pre
    hid_ref[...] = hid
    buf_ref[...] = hid
    out_ref[...] = dot(pick_ref[...], hid).astype(BF)


def backward_math(ids, cols, d_pre, vals_ref, w_scr, d_ext):
    d_agg = dot(d_pre, w_scr[1], NT).astype(BF)
    spread_rows(ids, cols, vals_ref, d_agg, d_ext)
    return dot(d_pre, w_scr[0], NT)


def top_kernel(layer, ids, cols, h_ref, arr_ref, vals_ref, wout_ref, lab_ref, mask_ref, *rest):
    w_refs, rest = rest[:10], rest[11:]
    agg_ref, dpre_ref, remote_ref, part_ref, buf_ref, ext, w_scr, sems, d_ext = rest
    rows = h_ref.shape[0]
    agg, pre, sig, hid = forward_math(
        layer, ids, cols, h_ref, arr_ref, vals_ref, w_refs, ext, w_scr, sems
    )
    agg_ref[...] = agg
    buf_ref[...] = hid
    logits = dot(hid, wout_ref[...])
    expo = jnp.exp(logits)
    probs = expo / jnp.sum(expo, axis=1, keepdims=True)
    onehot = (lab_ref[...] == lax.broadcasted_iota(jnp.int32, logits.shape, 1)).astype(F32)
    g_logits = (mask_ref[...].astype(F32) * (probs - onehot)).astype(BF)
    d_out = dot(g_logits, wout_ref[...], NT).astype(BF)
    d_pre = (d_out.astype(F32) * (sig * (1.0 + pre * (1.0 - sig)))).astype(BF)
    dpre_ref[...] = d_pre
    back = backward_math(ids, cols, d_pre, vals_ref, w_scr, d_ext)
    part_ref[...] = back + d_ext[0:rows, :]
    remote_ref[...] = d_ext[rows : 2 * rows, :].astype(BF).reshape(remote_ref.shape)


def chunk_sum(block):
    total = block[0:2].astype(F32)
    for n in range(2, block.shape[0], 2):
        total = total + block[n : n + 2].astype(F32)
    return total


def backward_kernel(layer, carry, has_buf, ids, cols, ret_ref, part_in, pre_ref, vals_ref, pick_ref, *rest):
    w_refs, rest = rest[:10], rest[10:]
    if carry:
        keep_ref, recv_ref, rest = rest[0], rest[1], rest[2:]
    if has_buf:
        rest = rest[1:]
    got_chunk = ret_ref.shape[1] > 8
    dpre_ref, remote_ref, part_ref, buf_ref, rest = *rest[:4], rest[4:]
    if got_chunk:
        chunk_ref, rest = rest[0], rest[1:]
    w_scr, sems, d_ext = rest
    start_weights(layer, ids, w_refs, w_scr, sems)
    rows, feat = part_in.shape
    returned = ret_ref[:, 0:8, :].reshape(rows, feat)
    d_out = (part_in[...] + dot(pick_ref[...], returned, TN)).astype(BF)
    buf_ref[...] = d_out
    pre = pre_ref[...]
    sig = sigmoid(pre)
    d_pre = (d_out.astype(F32) * (sig * (1.0 + pre * (1.0 - sig)))).astype(BF)
    dpre_ref[...] = d_pre
    wait_weights(layer, ids, w_refs, w_scr, sems)
    back = backward_math(ids, cols, d_pre, vals_ref, w_scr, d_ext)
    part_ref[...] = back + d_ext[0:rows, :]
    remote = d_ext[rows : 2 * rows, :].astype(BF).reshape(ret_ref.shape[0], 8, feat)
    remote_ref[:, 0:8, :] = remote
    if carry:
        both = (keep_ref[...].astype(F32) + recv_ref[...].astype(F32)).astype(BF)
        remote_ref[:, 8:24, :] = both.reshape(ret_ref.shape[0], 16, feat)
    if got_chunk:
        chunk_ref[...] = chunk_sum(ret_ref[:, 8:24, :]).astype(BF)


def grad_kernel(ids, cols, h_ref, agg_ref, dpre_ref, keep_ref, send_ref):
    d_pre = dpre_ref[...]
    on_rows = dot(h_ref[...], d_pre, TN).astype(BF)
    on_agg = dot(agg_ref[...], d_pre, TN).astype(BF)

    @pl.when(ids[1] == 0)
    def _():
        keep_ref[...] = on_rows
        send_ref[...] = on_agg

    @pl.when(ids[1] != 0)
    def _():
        keep_ref[...] = on_agg
        send_ref[...] = on_rows


def join_kernel(ids, cols, remote_ref, keep_a, recv_a, keep_b, recv_b, out_ref):
    peers, feat = out_ref.shape[0], out_ref.shape[2]
    out_ref[:, 0:8, :] = remote_ref[:, 0:8, :]
    first = (keep_a[...].astype(F32) + recv_a[...].astype(F32)).astype(BF)
    out_ref[:, 8:24, :] = first.reshape(peers, 16, feat)
    second = (keep_b[...].astype(F32) + recv_b[...].astype(F32)).astype(BF)
    out_ref[:, 24:40, :] = second.reshape(peers, 16, feat)


def end_kernel(ids, cols, ret_ref, part_in, pick_ref, buf_in, c_3, c_2, buf_ref, chunks_ref):
    rows, feat = part_in.shape
    returned = ret_ref[:, 0:8, :].reshape(rows, feat)
    buf_ref[...] = (part_in[...] + dot(pick_ref[...], returned, TN)).astype(BF)
    home = ids[0]
    chunks_ref[lax.rem(7 - home, 4)] = c_3[...]
    chunks_ref[lax.rem(6 - home, 4)] = c_2[...]
    chunks_ref[lax.rem(5 - home, 4)] = chunk_sum(ret_ref[:, 8:24, :]).astype(BF)
    chunks_ref[lax.rem(4 - home, 4)] = chunk_sum(ret_ref[:, 24:40, :]).astype(BF)


def layer_sum_kernel(ids, cols, own_ref, a_ref, b_ref, c_ref, out_ref):
    total = own_ref[0].astype(F32) + a_ref[...].astype(F32)
    total = (total + b_ref[...].astype(F32) + c_ref[...].astype(F32)).astype(BF)
    for n in range(0, out_ref.shape[0], 2):
        out_ref[n : n + 2] = total


def scale_kernel(scale, ids, cols, mine_ref, other_ref, self_ref, neigh_ref):
    mine = mine_ref[...].astype(F32) * scale
    other = other_ref[...].astype(F32) * scale

    @pl.when(ids[1] == 0)
    def _():
        self_ref[0] = mine
        neigh_ref[0] = other

    @pl.when(ids[1] != 0)
    def _():
        self_ref[0] = other
        neigh_ref[0] = mine


def home_kernel(ids, cols, own_ref, a_ref, b_ref, c_ref, out_ref, sems):
    home = ids[0]
    copies = [
        pltpu.make_async_copy(own_ref.at[0], out_ref.at[0, home], sems.at[0]),
        pltpu.make_async_copy(a_ref, out_ref.at[0, lax.rem(home + 3, 4)], sems.at[1]),
        pltpu.make_async_copy(b_ref, out_ref.at[0, lax.rem(home + 2, 4)], sems.at[2]),
        pltpu.make_async_copy(c_ref, out_ref.at[0, lax.rem(home + 1, 4)], sems.at[3]),
    ]
    for copy in copies:
        copy.start()
    for copy in copies:
        copy.wait()


def body(
    features,
    w_self,
    w_neigh,
    w_out,
    labels,
    train_mask,
    tile_cols,
    tile_vals,
    send_rows,
    send_counts,
):
    home = lax.axis_index("layer")
    node = lax.axis_index("node")
    core = lax.rem(node, 2)
    spans, rows, feat = features.shape
    peers, slots = send_rows.shape[2], send_rows.shape[3]
    tiles, degree, size = tile_vals.shape[2], tile_vals.shape[3], tile_vals.shape[4]
    classes = w_out.shape[1]
    scale = 1.0 / (spans * rows * peers)
    scalars = (jnp.stack([home, core]).astype(jnp.int32), tile_cols.reshape(-1))
    act = sds((rows, feat), BF)
    square = sds((feat, feat), BF)
    stack = sds((spans, rows, feat), BF)
    wide = sds((rows, feat), F32)
    act_spec, square_spec = whole((rows, feat)), whole((feat, feat))

    mine = jnp.where(core == 0, w_self[0], w_neigh[0])
    left = shift(mine, "layer", 1)
    right = shift(mine, "layer", -1)
    half = feat // 2
    far_a = shift(left[:half], "layer", 1)
    far_b = shift(right[half:], "layer", -1)
    weights = [
        (w, ANY)
        for w in (
            w_self[0],
            w_neigh[0],
            left,
            sibling(left),
            right,
            sibling(right),
            far_a,
            far_b,
            sibling(far_a),
            sibling(far_b),
        )
    ]
    features_in = (features, of_span((rows, feat)))
    vals_in = (
        tile_vals.reshape(spans, tiles, degree, size, size),
        of_span((tiles, degree, size, size)),
    )
    w_scratch = [pltpu.VMEM((2, feat, feat), BF), pltpu.SemaphoreType.DMA((4,))]
    ext_scratch = pltpu.VMEM((2 * rows, feat), BF)
    d_ext_scratch = pltpu.VMEM((2 * rows, feat), F32)

    pick, outgoing = run(
        pre_kernel,
        "gather_rows",
        scalars,
        [
            features_in,
            (send_rows.reshape(spans, peers, slots), of_span((peers, slots))),
            (send_counts.reshape(spans, 1, peers), of_span((1, peers))),
        ],
        [
            (sds((peers * slots, rows), BF), whole((peers * slots, rows))),
            (sds((peers * slots, feat), BF), whole((peers * slots, feat))),
        ],
        flops=10**8,
        moved=10**6,
    )
    pick_in = (pick, whole(pick.shape))
    back_rows = lambda value: exchange(value.reshape(peers, slots, feat))

    hidden, aggs, pres = [features_in], [], []
    acts_buf = None
    for layer in range(spans - 1):
        arrived = back_rows(outgoing).reshape(rows, feat)
        ins = [hidden[layer], (arrived, act_spec), vals_in, pick_in, *weights]
        aliases = None
        if layer:
            ins.append((acts_buf, ANY))
            aliases = {len(ins) - 1: 4}
        agg, pre, hid, outgoing, acts_buf = run(
            functools.partial(forward_kernel, layer, layer == 0),
            f"layer_forward_{layer}",
            scalars,
            ins,
            [
                (act, act_spec),
                (wide, act_spec),
                (act, act_spec),
                (act, act_spec),
                (stack, at_offset((rows, feat), layer)),
            ],
            [ext_scratch, *w_scratch],
            aliases,
            flops=6 * 10**8,
            moved=4 * 10**6,
        )
        hidden.append((hid, act_spec))
        aggs.append(agg)
        pres.append(pre)

    top = spans - 1
    arrived = back_rows(outgoing).reshape(rows, feat)
    column = (rows, 1)
    ins = [
        hidden[top],
        (arrived, act_spec),
        vals_in,
        (w_out, whole((feat, classes))),
        (labels.reshape(spans, *column), of_span(column)),
        (train_mask.reshape(spans, *column), of_span(column)),
        *weights,
        (acts_buf, ANY),
    ]
    agg, d_pre, remote, part, acts_buf = run(
        functools.partial(top_kernel, top),
        "top_layer",
        scalars,
        ins,
        [
            (act, act_spec),
            (act, act_spec),
            (sds((peers, slots, feat), BF), whole((peers, slots, feat))),
            (wide, act_spec),
            (stack, at_offset((rows, feat), top)),
        ],
        [ext_scratch, *w_scratch, d_ext_scratch],
        {len(ins) - 1: 4},
        flops=10**9,
        moved=5 * 10**6,
    )
    aggs.append(agg)

    def send_home(buf):
        return run(
            home_kernel,
            "put_home",
            scalars,
            [(buf, ANY), *[(shift(buf[s], "layer", s), ANY) for s in range(1, spans)]],
            [(sds((1, spans, rows, feat), BF), ANY)],
            [pltpu.SemaphoreType.DMA((4,))],
            moved=2 * 10**6,
        )[0]

    def weight_partials(layer, d_pre):
        keep, send = run(
            grad_kernel,
            f"weight_partials_{layer}",
            scalars,
            [hidden[layer], (aggs[layer], act_spec), (d_pre, act_spec)],
            [(square, square_spec), (square, square_spec)],
            flops=3 * 10**8,
            moved=2 * 10**6,
        )
        return keep, sibling(send)

    layer_acts = send_home(acts_buf)
    chunk_rows = feat // peers
    chunk_shape = (2, chunk_rows, feat)
    grads_buf = None
    chunks = {}
    for layer in range(top - 1, -1, -1):
        returned = exchange(remote)
        got_chunk = returned.shape[1] > slots
        partials = weight_partials(layer + 1, d_pre)
        carry = layer > 0
        out_rows = slots + chunk_rows if carry else slots
        ins = [
            (returned, whole(returned.shape)),
            (part, act_spec),
            (pres[layer], act_spec),
            vals_in,
            pick_in,
            *weights,
        ]
        if carry:
            ins += [(partials[0], square_spec), (partials[1], square_spec)]
        aliases = None
        if grads_buf is not None:
            ins.append((grads_buf, ANY))
            aliases = {len(ins) - 1: 3}
        outs = [
            (act, act_spec),
            (sds((peers, out_rows, feat), BF), whole((peers, out_rows, feat))),
            (wide, act_spec),
            (stack, at_offset((rows, feat), layer + 1)),
        ]
        if got_chunk:
            outs.append((sds(chunk_shape, BF), whole(chunk_shape)))
        result = run(
            functools.partial(backward_kernel, layer, carry, grads_buf is not None),
            f"layer_backward_{layer}",
            scalars,
            ins,
            outs,
            [*w_scratch, d_ext_scratch],
            aliases,
            flops=7 * 10**8,
            moved=5 * 10**6,
        )
        d_pre, remote, part, grads_buf = result[:4]
        if got_chunk:
            chunks[layer + 2] = result[4]

    last = weight_partials(0, d_pre)
    joined = run(
        join_kernel,
        "join_rows",
        scalars,
        [
            (remote, whole(remote.shape)),
            (partials[0], square_spec),
            (partials[1], square_spec),
            (last[0], square_spec),
            (last[1], square_spec),
        ],
        [
            (
                sds((peers, slots + 2 * chunk_rows, feat), BF),
                whole((peers, slots + 2 * chunk_rows, feat)),
            )
        ],
        moved=3 * 10**6,
    )[0]
    returned = exchange(joined)
    c_2 = chunks[2]
    grads_buf, sums = run(
        end_kernel,
        "input_grads",
        scalars,
        [
            (returned, whole(returned.shape)),
            (part, act_spec),
            pick_in,
            (grads_buf, ANY),
            (chunks[3], whole(chunk_shape)),
            (c_2, whole(chunk_shape)),
        ],
        [
            (stack, at_offset((rows, feat), 0)),
            (sds((spans, *chunk_shape), BF), whole((spans, *chunk_shape))),
        ],
        aliases={3: 0},
        flops=10**8,
        moved=3 * 10**6,
    )
    spread = run(
        layer_sum_kernel,
        "sum_over_layer",
        scalars,
        [
            (sums, whole((spans, *chunk_shape))),
            *[(shift(sums[s], "layer", s), whole(chunk_shape)) for s in range(1, spans)],
        ],
        [(sds((peers, chunk_rows, feat), BF), whole((peers, chunk_rows, feat)))],
        moved=10**6,
    )[0]
    act_grads = send_home(grads_buf)
    gathered = exchange(spread).reshape(feat, feat)
    grad_self, grad_neigh = run(
        functools.partial(scale_kernel, scale),
        "scale_grads",
        scalars,
        [(gathered, square_spec), (sibling(gathered), square_spec)],
        [(sds((1, feat, feat), F32), whole((1, feat, feat)))] * 2,
        moved=3 * 10**6,
    )
    return (layer_acts, act_grads, grad_self, grad_neigh)


def solution(mesh):
    in_specs = (
        P(None, "node", None),
        P("layer", None, None),
        P("layer", None, None),
        P(),
        P(None, "node"),
        P(None, "node"),
        P(None, "node", None, None),
        P(None, "node", None, None, None, None),
        P(None, "node", None, None),
        P(None, "node", None),
    )
    out_specs = (
        P("layer", None, "node", None),
        P("layer", None, "node", None),
        P("layer", None, None),
        P("layer", None, None),
    )
    return jax.shard_map(body, mesh=mesh, in_specs=in_specs, out_specs=out_specs, check_vma=False)
```

time: 619 us -> 279 us (0.45)
  waiting for transfers between devices: 261 us -> 60.6 us
  matrix products: 99.3 us -> 0 us
  other arithmetic: 80.9 us -> 1.35 us
  blocking collectives: 0 us -> 78.2 us
  starting transfers between devices: 103 us -> 39.8 us
  Pallas kernels: 0 us -> 44.2 us
  between operations: 14.1 us -> 1.23 us
    psum x1 -> x0, waiting for transfers between devices: 103 us -> none  [finish_grads(): lax.psum(grad_pair[0].astype(jnp.bfloat16), 'node').astype(jnp.float32)]
    dot_general x65 -> x0, matrix products: 99.3 us -> none  [the longest x7 18.1 us: layer_backward(): lax.dot_general(hidden_in, d_pre, over_rows, preferred_element_type=jnp.f...]
    all_to_all x0 -> x5, blocking collectives: none -> 78.2 us  [exchange(): lax.all_to_all(value, 'node', split_axis=0, concat_axis=0, tiled=True)]
    all_to_all x14 -> x4, waiting for transfers between devices: 77.7 us -> 26.6 us  [exchange(): lax.all_to_all(value, 'node', split_axis=0, concat_axis=0, tiled=True)]
    unnamed x12 -> x150, local copies, waits for them, and re-layouts: 0.03 us -> 46.8 us
    all_to_all x14 -> x4, starting transfers between devices: 63.8 us -> 18 us  [exchange(): lax.all_to_all(value, 'node', split_axis=0, concat_axis=0, tiled=True)]
    ppermute x14 -> x22, waiting for transfers between devices: 79.7 us -> 34 us  [the longest x13 30.7 us: shift(): lax.ppermute(value, axis, [(i, (i + steps) % count) for i in range(count)])]
    pallas_call x0 -> x18, Pallas kernels: none -> 44.2 us  [run(): pl.pallas_call(kernel, name=name, grid_spec=pltpu.PrefetchScalarGridSpec(...]
  transfers between devices with their start and end apart: 29 -> 26, of which waited for: 29 -> 13; matrix products, arithmetic and copies ran while one was open for 12% -> 3% of each run, Pallas kernels for 0% -> 7%
where the time goes in v1:
time: 279 us; the launch traced here: 277 us
  blocking collectives  78.2 us (28%)
  waiting for transfers between devices  60.6 us (22%)
  local copies, waits for them, and re-layouts  51.4 us (18%)
  Pallas kernels  44.2 us (16%)
  starting transfers between devices  39.8 us (14%)
    all_to_all x5, blocking collectives, exchange(): lax.all_to_all(value, 'node', split_axis=0, concat_axis=0, tiled=True)  78.2 us
    unnamed x150, local copies, waits for them, and re-layouts  46.8 us
    pallas_call x18, Pallas kernels, run(): pl.pallas_call(kernel, name=name, grid_spec=pltpu.PrefetchScalarGridSpec(...  44.2 us
    ppermute x13, waiting for transfers between devices, shift(): lax.ppermute(value, axis, [(i, (i + steps) % count) for i in range(count)])  30.7 us
    all_to_all x4, waiting for transfers between devices, exchange(): lax.all_to_all(value, 'node', split_axis=0, concat_axis=0, tiled=True)  26.6 us
    ppermute x13, starting transfers between devices, shift(): lax.ppermute(value, axis, [(i, (i + steps) % count) for i in range(count)])  18.9 us
    all_to_all x4, starting transfers between devices, exchange(): lax.all_to_all(value, 'node', split_axis=0, concat_axis=0, tiled=True)  18 us
  transfers between devices with their start and end apart: 26, of which 13 were waited for; matrix products, arithmetic and copies ran while one was open for 3% of the time, Pallas kernels for 7%

profile of v1, /device:TPU:0, one launch (start us, length us, event | category | flops | bytes accessed | tf_op | source)
XLA Modules:
  0.0 276.7 jit_solution(10454596936326268870)
XLA Ops:
  0.7 1.3 broadcast_select_fusion
  2.0 2.9 %collective-permute-start.2 = (bf16[512,512]{1,0:T(8,128)(2,1)S(1)}, bf16[512,512]{1,0:T(8,128)(2,1)S(1)}, u32[]{:S(2)}, u32[]{:S(2)}) collective-permute-start(bf16[512,512]{1,0:T(8,128)(2,1)S(1)} %broadcast_select_fusion), channel_id=1, source_target_pairs={{0,96},{32,0},{64,32},{96,64},{1,97},{33,1},{65,33},{97,65},{2,98}... | collective-permute-start | bytes 1572872 | tf_op jit(solution)/shard_map/ppermute | solution.py:25
  4.9 11.2 %collective-permute-done.2.rest_4_ = bf16[512,512]{1,0:T(8,128)(2,1)S(1)} collective-permute-done((bf16[512,512]{1,0:T(8,128)(2,1)S(1)}, bf16[512,512]{1,0:T(8,128)(2,1)S(1)}, u32[]{:S(2)}, u32[]{:S(2)}) %collective-permute-start.2) | collective-permute-done | bytes 524320 | tf_op jit(solution)/shard_map/ppermute | solution.py:25
  16.8 3.7 %collective-permute-start.5 = (bf16[256,512]{1,0:T(8,128)(2,1)}, bf16[256,512]{1,0:T(8,128)(2,1)S(1)}, u32[]{:S(2)}, u32[]{:S(2)}) collective-permute-start(bf16[256,512]{1,0:T(8,128)(2,1)} %slice.45), channel_id=1, source_target_pairs={{0,96},{32,0},{64,32},{96,64},{1,97},{33,1},{65,33},{97,65},{2,98}... | collective-permute-start | bytes 786440 | tf_op jit(solution)/shard_map/ppermute | solution.py:25
  22.6 2.9 %collective-permute-done.5.rest_7_ = bf16[256,512]{1,0:T(8,128)(2,1)S(1)} collective-permute-done((bf16[256,512]{1,0:T(8,128)(2,1)}, bf16[256,512]{1,0:T(8,128)(2,1)S(1)}, u32[]{:S(2)}, u32[]{:S(2)}) %collective-permute-start.5) | collective-permute-done | bytes 262176 | tf_op jit(solution)/shard_map/ppermute | solution.py:25
  25.5 4.1 %collective-permute-done.4.rest_6_ = bf16[256,512]{1,0:T(8,128)(2,1)} collective-permute-done((bf16[256,512]{1,0:T(8,128)(2,1)}, bf16[256,512]{1,0:T(8,128)(2,1)}, u32[]{:S(2)}, u32[]{:S(2)}) %collective-permute-start.4) | collective-permute-done | bytes 262176 | tf_op jit(solution)/shard_map/ppermute | solution.py:25
  29.6 1.2 copy-done.23
  32.7 17.2 %all_to_all.45 = bf16[32,8,512]{2,1,0:T(8,128)(2,1)S(1)} all-to-all(bf16[32,8,512]{2,1,0:T(8,128)(2,1)S(1)} %bitcast.67), channel_id=1, replica_groups=mesh['layer'=4,'node'=32] {'node'}, dimensions={0} | all-to-all | bytes 524288 | tf_op jit(solution)/shard_map/all_to_all | solution.py:34
  49.9 1.8 layer_forward_0.1
  51.7 12.5 %all_to_all.46 = bf16[32,8,512]{2,1,0:T(8,128)(2,1)S(1)} all-to-all(bf16[32,8,512]{2,1,0:T(8,128)(2,1)S(1)} %bitcast.66), channel_id=1, replica_groups=mesh['layer'=4,'node'=32] {'node'}, dimensions={0} | all-to-all | bytes 524288 | tf_op jit(solution)/shard_map/all_to_all | solution.py:34
  64.2 2.4 layer_forward_1.1
  67.3 12.4 %all_to_all.47 = bf16[32,8,512]{2,1,0:T(8,128)(2,1)S(1)} all-to-all(bf16[32,8,512]{2,1,0:T(8,128)(2,1)S(1)} %bitcast.65), channel_id=1, replica_groups=mesh['layer'=4,'node'=32] {'node'}, dimensions={0} | all-to-all | bytes 524288 | tf_op jit(solution)/shard_map/all_to_all | solution.py:34
  79.8 2.3 layer_forward_2.1
  86.0 4.7 %all-to-all-start.3 = ((bf16[32,8,512]{2,1,0:T(8,128)(2,1)}), bf16[32,8,512]{2,1,0:T(8,128)(2,1)}, u32[]{:S(2)}, u32[]{:S(2)}) async-start(bf16[32,8,512]{2,1,0:T(8,128)(2,1)} %bitcast.64), calls=%async_computation.3 | async-start | bytes 524288 | tf_op jit(solution)/shard_map/all_to_all | solution.py:34
  90.7 1.8 copy.23.wout_ref
  94.5 5.1 %all-to-all-done.3 = bf16[32,8,512]{2,1,0:T(8,128)(2,1)} async-done(((bf16[32,8,512]{2,1,0:T(8,128)(2,1)}), bf16[32,8,512]{2,1,0:T(8,128)(2,1)}, u32[]{:S(2)}, u32[]{:S(2)}) %all-to-all-start.3) | async-done | bytes 262176 | tf_op jit(solution)/shard_map/all_to_all | solution.py:34
  99.6 1.2 copy-done.10
  106.7 4.3 %top_layer.1 = (bf16[256,512]{1,0:T(8,128)(2,1)S(1)}, bf16[256,512]{1,0:T(8,128)(2,1)S(1)}, bf16[32,8,512]{2,1,0:T(8,128)(2,1)S(1)}, f32[256,512]{1,0:T(8,128)S(1)}, bf16[4,256,512]{2,1,0:T(8,128)(2,1)S(1)}) custom-call(s32[2]{0:T(128)S(1)} %pad_add_fusion.ids, s32[32]{0:T(128)S(1)} %reshape.50.cols, ...), custom_call_target="tpu_custom_call", output_to_operand_aliasing={{4}: (18, {})} | custom-call | flops 1000000000 | bytes 5000000 | tf_op jit(solution)/shard_map/top_layer/pallas_call | solution.py:58
  111.2 1.1 weight_partials_3.1
  112.7 12.2 %all_to_all.48.ret_ref = bf16[32,8,512]{2,1,0:T(8,128)(2,1)S(1)} all-to-all(bf16[32,8,512]{2,1,0:T(8,128)(2,1)S(1)} %get-tuple-element.64), channel_id=1, replica_groups=mesh['layer'=4,'node'=32] {'node'}, dimensions={0} | all-to-all | bytes 524288 | tf_op jit(solution)/shard_map/all_to_all | solution.py:34
  124.9 2.6 layer_backward_2.1
  130.9 4.6 %all-to-all-start.5 = ((bf16[32,24,512]{2,1,0:T(8,128)(2,1)}), bf16[32,24,512]{2,1,0:T(8,128)(2,1)}, u32[]{:S(2)}, u32[]{:S(2)}) async-start(bf16[32,24,512]{2,1,0:T(8,128)(2,1)} %copy-done.28), calls=%async_computation.5 | async-start | bytes 1572864 | tf_op jit(solution)/shard_map/all_to_all | solution.py:34
  138.4 1.1 weight_partials_2.1
  140.5 1.8 collective-permute-done.12.rest_11_
  143.1 6.3 %all-to-all-done.5.ret_ref = bf16[32,24,512]{2,1,0:T(8,128)(2,1)} async-done(((bf16[32,24,512]{2,1,0:T(8,128)(2,1)}), bf16[32,24,512]{2,1,0:T(8,128)(2,1)}, u32[]{:S(2)}, u32[]{:S(2)}) %all-to-all-start.5) | async-done | bytes 786464 | tf_op jit(solution)/shard_map/all_to_all | solution.py:34
  149.4 1.2 copy-done.4
  156.7 3.9 %layer_backward_1.1 = (bf16[256,512]{1,0:T(8,128)(2,1)S(1)}, bf16[32,24,512]{2,1,0:T(8,128)(2,1)S(1)}, f32[256,512]{1,0:T(8,128)S(1)}, bf16[4,256,512]{2,1,0:T(8,128)(2,1)S(1)}, bf16[2,16,512]{2,1,0:T(8,128)(2,1)S(1)}) custom-call(s32[2]{0:T(128)S(1)} %pad_add_fusion.ids, s32[32]{0:T(128)S(1)} %reshape.50.cols, ...), custom_call_target="tpu_custom_call", output_to_operand_aliasing={{3}: (19, {})} | custom-call | flops 700000000 | bytes 5000000 | tf_op jit(solution)/shard_map/layer_backward_1/pallas_call | solution.py:58
  164.6 4.6 %all-to-all-start.6 = ((bf16[32,24,512]{2,1,0:T(8,128)(2,1)}), bf16[32,24,512]{2,1,0:T(8,128)(2,1)}, u32[]{:S(2)}, u32[]{:S(2)}) async-start(bf16[32,24,512]{2,1,0:T(8,128)(2,1)} %copy-done.29), calls=%async_computation.6 | async-start | bytes 1572864 | tf_op jit(solution)/shard_map/all_to_all | solution.py:34
  172.1 1.9 weight_partials_1.1
  175.2 7.8 %all-to-all-done.6.ret_ref = bf16[32,24,512]{2,1,0:T(8,128)(2,1)} async-done(((bf16[32,24,512]{2,1,0:T(8,128)(2,1)}), bf16[32,24,512]{2,1,0:T(8,128)(2,1)}, u32[]{:S(2)}, u32[]{:S(2)}) %all-to-all-start.6) | async-done | bytes 786464 | tf_op jit(solution)/shard_map/all_to_all | solution.py:34
  183.0 1.2 copy-done.6
  188.3 3.1 %layer_backward_0.1 = (bf16[256,512]{1,0:T(8,128)(2,1)S(1)}, bf16[32,8,512]{2,1,0:T(8,128)(2,1)S(1)}, f32[256,512]{1,0:T(8,128)S(1)}, bf16[4,256,512]{2,1,0:T(8,128)(2,1)S(1)}, bf16[2,16,512]{2,1,0:T(8,128)(2,1)S(1)}) custom-call(s32[2]{0:T(128)S(1)} %pad_add_fusion.ids, s32[32]{0:T(128)S(1)} %reshape.50.cols, ...), custom_call_target="tpu_custom_call", output_to_operand_aliasing={{3}: (17, {})} | custom-call | flops 700000000 | bytes 5000000 | tf_op jit(solution)/shard_map/layer_backward_0/pallas_call | solution.py:58
  191.4 1.1 weight_partials_0.1
  193.3 1.5 collective-permute-done.14.recv_b
  194.8 1.9 join_rows.1
  196.7 23.9 %all_to_all.49.ret_ref = bf16[32,40,512]{2,1,0:T(8,128)(2,1)S(1)} all-to-all(bf16[32,40,512]{2,1,0:T(8,128)(2,1)S(1)} %join_rows.1), channel_id=1, replica_groups=mesh['layer'=4,'node'=32] {'node'}, dimensions={0} | all-to-all | bytes 2621440 | tf_op jit(solution)/shard_map/all_to_all | solution.py:34
  224.5 1.9 collective-permute-done.20.c_ref
  226.5 2.0 collective-permute-done.19.b_ref
  229.1 1.4 sum_over_layer.1
  230.5 4.0 %all-to-all-start.8 = ((bf16[32,16,512]{2,1,0:T(8,128)(2,1)}), bf16[32,16,512]{2,1,0:T(8,128)(2,1)S(1)}, u32[]{:S(2)}, u32[]{:S(2)}) async-start(bf16[32,16,512]{2,1,0:T(8,128)(2,1)} %sum_over_layer.1), calls=%async_computation.8 | async-start | bytes 1048576 | tf_op jit(solution)/shard_map/all_to_all | solution.py:34
  235.4 2.0 collective-permute-start.10
  238.4 7.3 %all-to-all-done.8 = bf16[32,16,512]{2,1,0:T(8,128)(2,1)S(1)} async-done(((bf16[32,16,512]{2,1,0:T(8,128)(2,1)}), bf16[32,16,512]{2,1,0:T(8,128)(2,1)S(1)}, u32[]{:S(2)}, u32[]{:S(2)}) %all-to-all-start.8) | async-done | bytes 524320 | tf_op jit(solution)/shard_map/all_to_all | solution.py:34
  247.3 2.4 collective-permute-start.17
  250.8 3.7 %collective-permute-start.15 = (bf16[256,512]{1,0:T(8,128)(2,1)S(1)}, bf16[256,512]{1,0:T(8,128)(2,1)S(1)}, u32[]{:S(2)}, u32[]{:S(2)}) collective-permute-start(bf16[256,512]{1,0:T(8,128)(2,1)S(1)} %get-tuple-element.102), channel_id=1, source_target_pairs={{0,32},{32,64},{64,96},{96,0},{1,33},{33,65},{65,97},{97,1},{2,34}... | collective-permute-start | bytes 786440 | tf_op jit(solution)/shard_map/ppermute | solution.py:25
  254.4 7.9 %collective-permute-done.8.a_ref = bf16[256,512]{1,0:T(8,128)(2,1)S(1)} collective-permute-done((bf16[256,512]{1,0:T(8,128)(2,1)}, bf16[256,512]{1,0:T(8,128)(2,1)S(1)}, u32[]{:S(2)}, u32[]{:S(2)}) %collective-permute-start.8) | collective-permute-done | bytes 262176 | tf_op jit(solution)/shard_map/ppermute | solution.py:25
  263.3 9.6 %put_home.2 = bf16[1,4,256,512]{3,2,1,0:T(8,128)(2,1)} custom-call(s32[2]{0:T(128)S(1)} %pad_add_fusion.ids, s32[32]{0:T(128)S(1)} %reshape.50.cols, bf16[4,256,512]{2,1,0:T(8,128)(2,1)S(1)} %copy-done.12, bf16[256,512]{1,0:T(8,128)(2,1)S(1)} %collective-permute-done.8.a_ref, bf16[256,512]{1,0:T(8,128)(2,1)} %collective-permute-done.9.b_ref, ...), custom_call_target="tpu_custom_call" | custom-call | bytes 2000000 | tf_op jit(solution)/shard_map/put_home/pallas_call | solution.py:58
  272.9 1.5 put_home.3
  274.5 2.2 scale_grads.1
  (187 shorter events, 54.2 us)
Async XLA Ops:
  0.6 21.1 %copy-start.73 = (s32[4,1,2,4]{3,2,1,0:T(2,128)S(1)}, s32[4,1,2,4]{3,2,1,0:T(2,128)}, u32[]{:S(2)}) copy-start(s32[4,1,2,4]{3,2,1,0:T(2,128)} %param.16) | copy-start | bytes 388
  0.6 21.2 %copy-start.70 = (s32[4,1,32,8]{2,3,1,0:T(8,128)S(1)}, s32[4,1,32,8]{2,3,1,0:T(8,128)}, u32[]{:S(2)}) copy-start(s32[4,1,32,8]{2,3,1,0:T(8,128)} %param.18) | copy-start | bytes 12292
  0.7 29.0 %copy-start.61 = (s32[4,1,32]{2,1,0:T(1,128)S(1)}, s32[4,1,32]{2,1,0:T(1,128)}, u32[]{:S(2)}) copy-start(s32[4,1,32]{2,1,0:T(1,128)} %counts_ref.1) | copy-start | bytes 1540
  1.9 47.9 %copy-start = (bf16[4,1,2,4,128,128]{5,4,3,2,1,0:T(8,128)(2,1)S(1)}, bf16[4,1,2,4,128,128]{5,4,3,2,1,0:T(8,128)(2,1)}, u32[]{:S(2)}) copy-start(bf16[4,1,2,4,128,128]{5,4,3,2,1,0:T(8,128)(2,1)} %param.17) | copy-start | bytes 3145732
  2.0 47.9 %copy-start.1 = (bf16[1,512,512]{2,1,0:T(8,128)(2,1)S(1)}, bf16[1,512,512]{2,1,0:T(8,128)(2,1)}, u32[]{:S(2)}) copy-start(bf16[1,512,512]{2,1,0:T(8,128)(2,1)} %param.11) | copy-start | bytes 1572868
  2.0 47.9 %copy-start.2 = (bf16[1,512,512]{2,1,0:T(8,128)(2,1)S(1)}, bf16[1,512,512]{2,1,0:T(8,128)(2,1)}, u32[]{:S(2)}) copy-start(bf16[1,512,512]{2,1,0:T(8,128)(2,1)} %param.12) | copy-start | bytes 1572868
  2.0 14.1 %collective-permute-start.2 = (bf16[512,512]{1,0:T(8,128)(2,1)S(1)}, bf16[512,512]{1,0:T(8,128)(2,1)S(1)}, u32[]{:S(2)}, u32[]{:S(2)}) collective-permute-start(bf16[512,512]{1,0:T(8,128)(2,1)S(1)} %broadcast_select_fusion), channel_id=1, source_target_pairs={{0,96},{32,0},{64,32},{96,64},{1,97},{33,1},{65,33},{97,65},{2,98}... | collective-permute-start | bytes 1572872 | tf_op jit(solution)/shard_map/ppermute | solution.py:25
  4.9 15.6 %collective-permute-start = (bf16[512,512]{1,0:T(8,128)(2,1)S(1)}, bf16[512,512]{1,0:T(8,128)(2,1)S(1)}, u32[]{:S(2)}, u32[]{:S(2)}) collective-permute-start(bf16[512,512]{1,0:T(8,128)(2,1)S(1)} %broadcast_select_fusion), channel_id=1, source_target_pairs={{0,32},{32,64},{64,96},{96,0},{1,33},{33,65},{65,97},{97,1},{2,34}... | collective-permute-start | bytes 1572872 | tf_op jit(solution)/shard_map/ppermute | solution.py:25
  16.8 8.7 %collective-permute-start.5 = (bf16[256,512]{1,0:T(8,128)(2,1)}, bf16[256,512]{1,0:T(8,128)(2,1)S(1)}, u32[]{:S(2)}, u32[]{:S(2)}) collective-permute-start(bf16[256,512]{1,0:T(8,128)(2,1)} %slice.45), channel_id=1, source_target_pairs={{0,96},{32,0},{64,32},{96,64},{1,97},{33,1},{65,33},{97,65},{2,98}... | collective-permute-start | bytes 786440 | tf_op jit(solution)/shard_map/ppermute | solution.py:25
  21.2 8.4 %collective-permute-start.4 = (bf16[256,512]{1,0:T(8,128)(2,1)}, bf16[256,512]{1,0:T(8,128)(2,1)}, u32[]{:S(2)}, u32[]{:S(2)}) collective-permute-start(bf16[256,512]{1,0:T(8,128)(2,1)} %slice.44), channel_id=1, source_target_pairs={{0,32},{32,64},{64,96},{96,0},{1,33},{33,65},{65,97},{97,1},{2,34}... | collective-permute-start | bytes 786440 | tf_op jit(solution)/shard_map/ppermute | solution.py:25
  21.2 28.6 %collective-permute-start.3 = (bf16[512,512]{1,0:T(8,128)(2,1)S(1)}, bf16[512,512]{1,0:T(8,128)(2,1)}, u32[]{:S(2)}, u32[]{:S(2)}) collective-permute-start(bf16[512,512]{1,0:T(8,128)(2,1)S(1)} %collective-permute-done.2.rest_4_), channel_id=1, source_target_pairs={{0,1},{1,0},{2,3},{3,2},{4,5},{5,4},{6,7},{7,6},{8,9},{9,8},{10,11... | collective-permute-start | bytes 1572872 | tf_op jit(solution)/shard_map/ppermute | solution.py:30
  21.2 28.7 %collective-permute-start.1 = (bf16[512,512]{1,0:T(8,128)(2,1)S(1)}, bf16[512,512]{1,0:T(8,128)(2,1)}, u32[]{:S(2)}, u32[]{:S(2)}) collective-permute-start(bf16[512,512]{1,0:T(8,128)(2,1)S(1)} %collective-permute-done.rest_2_), channel_id=1, source_target_pairs={{0,1},{1,0},{2,3},{3,2},{4,5},{5,4},{6,7},{7,6},{8,9},{9,8},{10,11... | collective-permute-start | bytes 1572872 | tf_op jit(solution)/shard_map/ppermute | solution.py:30
  25.5 24.3 %collective-permute-start.7 = (bf16[256,512]{1,0:T(8,128)(2,1)S(1)}, bf16[256,512]{1,0:T(8,128)(2,1)S(1)}, u32[]{:S(2)}, u32[]{:S(2)}) collective-permute-start(bf16[256,512]{1,0:T(8,128)(2,1)S(1)} %collective-permute-done.5.rest_7_), channel_id=1, source_target_pairs={{0,1},{1,0},{2,3},{3,2},{4,5},{5,4},{6,7},{7,6},{8,9},{9,8},{10,11... | collective-permute-start | bytes 786440 | tf_op jit(solution)/shard_map/ppermute | solution.py:30
  29.6 20.2 %collective-permute-start.6 = (bf16[256,512]{1,0:T(8,128)(2,1)}, bf16[256,512]{1,0:T(8,128)(2,1)S(1)}, u32[]{:S(2)}, u32[]{:S(2)}) collective-permute-start(bf16[256,512]{1,0:T(8,128)(2,1)} %collective-permute-done.4.rest_6_), channel_id=1, source_target_pairs={{0,1},{1,0},{2,3},{3,2},{4,5},{5,4},{6,7},{7,6},{8,9},{9,8},{10,11... | collective-permute-start | bytes 786440 | tf_op jit(solution)/shard_map/ppermute | solution.py:30
  49.8 30.0 %copy-start.13 = (bf16[256,512]{1,0:T(8,128)(2,1)}, bf16[256,512]{1,0:T(8,128)(2,1)S(1)}, u32[]{:S(2)}) copy-start(bf16[256,512]{1,0:T(8,128)(2,1)S(1)} %collective-permute-done.7.rest_9_) | copy-start | bytes 786436
  49.9 29.9 %copy-start.18 = (bf16[256,512]{1,0:T(8,128)(2,1)}, bf16[256,512]{1,0:T(8,128)(2,1)S(1)}, u32[]{:S(2)}) copy-start(bf16[256,512]{1,0:T(8,128)(2,1)S(1)} %collective-permute-done.6.rest_8_) | copy-start | bytes 786436
  51.7 12.5 %copy-start.30 = (f32[256,512]{1,0:T(8,128)}, f32[256,512]{1,0:T(8,128)S(1)}, u32[]{:S(2)}) copy-start(f32[256,512]{1,0:T(8,128)S(1)} %get-tuple-element.81.pre_ref) | copy-start | bytes 1572868
  51.7 14.9 %copy-start.46 = (bf16[256,512]{1,0:T(8,128)(2,1)}, bf16[256,512]{1,0:T(8,128)(2,1)S(1)}, u32[]{:S(2)}) copy-start(bf16[256,512]{1,0:T(8,128)(2,1)S(1)} %get-tuple-element.54.h_ref) | copy-start | bytes 786436
  51.7 14.9 %copy-start.55 = (bf16[256,512]{1,0:T(8,128)(2,1)}, bf16[256,512]{1,0:T(8,128)(2,1)S(1)}, u32[]{:S(2)}) copy-start(bf16[256,512]{1,0:T(8,128)(2,1)S(1)} %get-tuple-element.88.agg_ref) | copy-start | bytes 786436
  67.3 12.5 %copy-start.32 = (f32[256,512]{1,0:T(8,128)}, f32[256,512]{1,0:T(8,128)S(1)}, u32[]{:S(2)}) copy-start(f32[256,512]{1,0:T(8,128)S(1)} %get-tuple-element.73.pre_ref) | copy-start | bytes 1572868
  67.3 14.8 %copy-start.48 = (bf16[256,512]{1,0:T(8,128)(2,1)}, bf16[256,512]{1,0:T(8,128)(2,1)S(1)}, u32[]{:S(2)}) copy-start(bf16[256,512]{1,0:T(8,128)(2,1)S(1)} %get-tuple-element.57.h_ref) | copy-start | bytes 786436
  79.8 12.7 %copy-start.71 = (s32[4,256]{1,0:T(4,128)S(1)}, s32[4,256]{1,0:T(4,128)}, u32[]{:S(2)}) copy-start(s32[4,256]{1,0:T(4,128)} %param.14) | copy-start | bytes 12292
  86.0 7.5 %copy-start.72 = (s32[4,256]{1,0:T(4,128)S(1)}, s32[4,256]{1,0:T(4,128)}, u32[]{:S(2)}) copy-start(s32[4,256]{1,0:T(4,128)} %param.15) | copy-start | bytes 12292
  86.0 13.6 %all-to-all-start.3 = ((bf16[32,8,512]{2,1,0:T(8,128)(2,1)}), bf16[32,8,512]{2,1,0:T(8,128)(2,1)}, u32[]{:S(2)}, u32[]{:S(2)}) async-start(bf16[32,8,512]{2,1,0:T(8,128)(2,1)} %bitcast.64), calls=%async_computation.3 | async-start | bytes 524288 | tf_op jit(solution)/shard_map/all_to_all | solution.py:34
  111.1 13.8 %copy-start.11 = (bf16[4,256,512]{2,1,0:T(8,128)(2,1)}, bf16[4,256,512]{2,1,0:T(8,128)(2,1)S(1)}, u32[]{:S(2)}) copy-start(bf16[4,256,512]{2,1,0:T(8,128)(2,1)S(1)} %get-tuple-element.63.own_ref) | copy-start | bytes 3145732
  111.1 13.8 %copy-start.15 = (bf16[256,512]{1,0:T(8,128)(2,1)S(1)}, bf16[256,512]{1,0:T(8,128)(2,1)}, u32[]{:S(2)}) copy-start(bf16[256,512]{1,0:T(8,128)(2,1)} %copy-done.13) | copy-start | bytes 786436
  111.1 13.8 %copy-start.20 = (bf16[256,512]{1,0:T(8,128)(2,1)S(1)}, bf16[256,512]{1,0:T(8,128)(2,1)}, u32[]{:S(2)}) copy-start(bf16[256,512]{1,0:T(8,128)(2,1)} %copy-done.18) | copy-start | bytes 786436
  111.1 13.8 %copy-start.35 = (f32[256,512]{1,0:T(8,128)S(1)}, f32[256,512]{1,0:T(8,128)}, u32[]{:S(2)}) copy-start(f32[256,512]{1,0:T(8,128)} %copy-done.34) | copy-start | bytes 1572868
  112.3 12.6 %collective-permute-start.11 = (bf16[512,512]{1,0:T(8,128)(2,1)S(1)}, bf16[512,512]{1,0:T(8,128)(2,1)S(1)}, u32[]{:S(2)}, u32[]{:S(2)}) collective-permute-start(bf16[512,512]{1,0:T(8,128)(2,1)S(1)} %get-tuple-element.70), channel_id=1, source_target_pairs={{0,1},{1,0},{2,3},{3,2},{4,5},{5,4},{6,7},{7,6},{8,9},{9,8},{10,11... | collective-permute-start | bytes 1572872 | tf_op jit(solution)/shard_map/ppermute | solution.py:30
  130.9 18.5 %all-to-all-start.5 = ((bf16[32,24,512]{2,1,0:T(8,128)(2,1)}), bf16[32,24,512]{2,1,0:T(8,128)(2,1)}, u32[]{:S(2)}, u32[]{:S(2)}) async-start(bf16[32,24,512]{2,1,0:T(8,128)(2,1)} %copy-done.28), calls=%async_computation.5 | async-start | bytes 1572864 | tf_op jit(solution)/shard_map/all_to_all | solution.py:34
  140.4 1.9 collective-permute-start.12
  164.6 18.5 %all-to-all-start.6 = ((bf16[32,24,512]{2,1,0:T(8,128)(2,1)}), bf16[32,24,512]{2,1,0:T(8,128)(2,1)}, u32[]{:S(2)}, u32[]{:S(2)}) async-start(bf16[32,24,512]{2,1,0:T(8,128)(2,1)} %copy-done.29), calls=%async_computation.6 | async-start | bytes 1572864 | tf_op jit(solution)/shard_map/all_to_all | solution.py:34
  174.8 18.5 %collective-permute-start.13 = (bf16[512,512]{1,0:T(8,128)(2,1)}, bf16[512,512]{1,0:T(8,128)(2,1)}, u32[]{:S(2)}, u32[]{:S(2)}) collective-permute-start(bf16[512,512]{1,0:T(8,128)(2,1)} %get-tuple-element.87), channel_id=1, source_target_pairs={{0,1},{1,0},{2,3},{3,2},{4,5},{5,4},{6,7},{7,6},{8,9},{9,8},{10,11... | collective-permute-start | bytes 1572872 | tf_op jit(solution)/shard_map/ppermute | solution.py:30
  192.5 2.3 collective-permute-start.14
  196.7 23.9 %copy-start.60 = (bf16[2,16,512]{2,1,0:T(8,128)(2,1)S(1)}, bf16[2,16,512]{2,1,0:T(8,128)(2,1)}, u32[]{:S(2)}) copy-start(bf16[2,16,512]{2,1,0:T(8,128)(2,1)} %copy-done.59) | copy-start | bytes 98308
  222.4 12.1 %copy-start.12 = (bf16[4,256,512]{2,1,0:T(8,128)(2,1)S(1)}, bf16[4,256,512]{2,1,0:T(8,128)(2,1)}, u32[]{:S(2)}) copy-start(bf16[4,256,512]{2,1,0:T(8,128)(2,1)} %copy-done.11) | copy-start | bytes 3145732
  222.4 4.0 %collective-permute-start.20 = (bf16[2,16,512]{2,1,0:T(8,128)(2,1)S(1)}, bf16[2,16,512]{2,1,0:T(8,128)(2,1)S(1)}, u32[]{:S(2)}, u32[]{:S(2)}) collective-permute-start(bf16[2,16,512]{2,1,0:T(8,128)(2,1)S(1)} %get-tuple-element.106), channel_id=1, source_target_pairs={{0,96},{32,0},{64,32},{96,64},{1,97},{33,1},{65,33},{97,65},{2,98}... | collective-permute-start | bytes 98312 | tf_op jit(solution)/shard_map/ppermute | solution.py:25
  223.0 5.5 %collective-permute-start.19 = (bf16[2,16,512]{2,1,0:T(8,128)(2,1)S(1)}, bf16[2,16,512]{2,1,0:T(8,128)(2,1)S(1)}, u32[]{:S(2)}, u32[]{:S(2)}) collective-permute-start(bf16[2,16,512]{2,1,0:T(8,128)(2,1)S(1)} %get-tuple-element.107), channel_id=1, source_target_pairs={{0,64},{32,96},{64,0},{96,32},{1,65},{33,97},{65,1},{97,33},{2,66}... | collective-permute-start | bytes 98312 | tf_op jit(solution)/shard_map/ppermute | solution.py:25
  223.8 5.3 %collective-permute-start.18 = (bf16[2,16,512]{2,1,0:T(8,128)(2,1)S(1)}, bf16[2,16,512]{2,1,0:T(8,128)(2,1)S(1)}, u32[]{:S(2)}, u32[]{:S(2)}) collective-permute-start(bf16[2,16,512]{2,1,0:T(8,128)(2,1)S(1)} %get-tuple-element.108), channel_id=1, source_target_pairs={{0,32},{32,64},{64,96},{96,0},{1,33},{33,65},{65,97},{97,1},{2,34}... | collective-permute-start | bytes 98312 | tf_op jit(solution)/shard_map/ppermute | solution.py:25
  230.5 16.8 %copy-start.8 = (bf16[4,256,512]{2,1,0:T(8,128)(2,1)S(1)}, bf16[4,256,512]{2,1,0:T(8,128)(2,1)}, u32[]{:S(2)}) copy-start(bf16[4,256,512]{2,1,0:T(8,128)(2,1)} %copy-done.7) | copy-start | bytes 3145732
  230.5 15.2 %all-to-all-start.8 = ((bf16[32,16,512]{2,1,0:T(8,128)(2,1)}), bf16[32,16,512]{2,1,0:T(8,128)(2,1)S(1)}, u32[]{:S(2)}, u32[]{:S(2)}) async-start(bf16[32,16,512]{2,1,0:T(8,128)(2,1)} %sum_over_layer.1), calls=%async_computation.8 | async-start | bytes 1048576 | tf_op jit(solution)/shard_map/all_to_all | solution.py:34
  235.4 14.3 %collective-permute-start.10 = (bf16[256,512]{1,0:T(8,128)(2,1)}, bf16[256,512]{1,0:T(8,128)(2,1)S(1)}, u32[]{:S(2)}, u32[]{:S(2)}) collective-permute-start(bf16[256,512]{1,0:T(8,128)(2,1)} %get-tuple-element.103), channel_id=1, source_target_pairs={{0,96},{32,0},{64,32},{96,64},{1,97},{33,1},{65,33},{97,65},{2,98}... | collective-permute-start | bytes 786440 | tf_op jit(solution)/shard_map/ppermute | solution.py:25
  237.5 13.3 %collective-permute-start.9 = (bf16[256,512]{1,0:T(8,128)(2,1)}, bf16[256,512]{1,0:T(8,128)(2,1)}, u32[]{:S(2)}, u32[]{:S(2)}) collective-permute-start(bf16[256,512]{1,0:T(8,128)(2,1)} %get-tuple-element.104), channel_id=1, source_target_pairs={{0,64},{32,96},{64,0},{96,32},{1,65},{33,97},{65,1},{97,33},{2,66}... | collective-permute-start | bytes 786440 | tf_op jit(solution)/shard_map/ppermute | solution.py:25
  245.7 28.8 %collective-permute-start.21 = (bf16[512,512]{1,0:T(8,128)(2,1)S(1)}, bf16[512,512]{1,0:T(8,128)(2,1)S(1)}, u32[]{:S(2)}, u32[]{:S(2)}) collective-permute-start(bf16[512,512]{1,0:T(8,128)(2,1)S(1)} %bitcast.58), channel_id=1, source_target_pairs={{0,1},{1,0},{2,3},{3,2},{4,5},{5,4},{6,7},{7,6},{8,9},{9,8},{10,11... | collective-permute-start | bytes 1572872 | tf_op jit(solution)/shard_map/ppermute | solution.py:30
  246.4 15.9 %collective-permute-start.8 = (bf16[256,512]{1,0:T(8,128)(2,1)}, bf16[256,512]{1,0:T(8,128)(2,1)S(1)}, u32[]{:S(2)}, u32[]{:S(2)}) collective-permute-start(bf16[256,512]{1,0:T(8,128)(2,1)} %get-tuple-element.105), channel_id=1, source_target_pairs={{0,32},{32,64},{64,96},{96,0},{1,33},{33,65},{65,97},{97,1},{2,34}... | collective-permute-start | bytes 786440 | tf_op jit(solution)/shard_map/ppermute | solution.py:25
  247.3 25.6 %collective-permute-start.17 = (bf16[256,512]{1,0:T(8,128)(2,1)S(1)}, bf16[256,512]{1,0:T(8,128)(2,1)S(1)}, u32[]{:S(2)}, u32[]{:S(2)}) collective-permute-start(bf16[256,512]{1,0:T(8,128)(2,1)S(1)} %get-tuple-element.100), channel_id=1, source_target_pairs={{0,96},{32,0},{64,32},{96,64},{1,97},{33,1},{65,33},{97,65},{2,98}... | collective-permute-start | bytes 786440 | tf_op jit(solution)/shard_map/ppermute | solution.py:25
  250.5 22.4 %collective-permute-start.16 = (bf16[256,512]{1,0:T(8,128)(2,1)S(1)}, bf16[256,512]{1,0:T(8,128)(2,1)S(1)}, u32[]{:S(2)}, u32[]{:S(2)}) collective-permute-start(bf16[256,512]{1,0:T(8,128)(2,1)S(1)} %get-tuple-element.101), channel_id=1, source_target_pairs={{0,64},{32,96},{64,0},{96,32},{1,65},{33,97},{65,1},{97,33},{2,66}... | collective-permute-start | bytes 786440 | tf_op jit(solution)/shard_map/ppermute | solution.py:25
  250.8 22.2 %collective-permute-start.15 = (bf16[256,512]{1,0:T(8,128)(2,1)S(1)}, bf16[256,512]{1,0:T(8,128)(2,1)S(1)}, u32[]{:S(2)}, u32[]{:S(2)}) collective-permute-start(bf16[256,512]{1,0:T(8,128)(2,1)S(1)} %get-tuple-element.102), channel_id=1, source_target_pairs={{0,32},{32,64},{64,96},{96,0},{1,33},{33,65},{65,97},{97,1},{2,34}... | collective-permute-start | bytes 786440 | tf_op jit(solution)/shard_map/ppermute | solution.py:25
  (52 other events, 58.4 us)

commit v2 on v1

--- a/solution.py
+++ b/solution.py
@@ -12,7 +12,8 @@
 NN = (((1,), (0,)), ((), ()))
 NT = (((1,), (1,)), ((), ()))
 TN = (((0,), (0,)), ((), ()))
-ANY = pl.BlockSpec(memory_space=pl.ANY)
+ANY = pl.BlockSpec(memory_space=pltpu.HBM)
+LOCAL = pl.BlockSpec(memory_space=pltpu.VMEM)
 VMEM_BYTES = 40 * 1024 * 1024
 
 
@@ -54,7 +55,9 @@
 
 
 def run(kernel, name, scalars, ins, outs, scratch=(), aliases=None, flops=0, moved=0):
-    arrays = [a for a, _ in ins]
+    arrays = [
+        a if s is LOCAL else pltpu.with_memory_space_constraint(a, pltpu.HBM) for a, s in ins
+    ]
     return pl.pallas_call(
         kernel,
         name=name,
@@ -65,7 +68,7 @@
             out_specs=[s for _, s in outs],
             scratch_shapes=list(scratch),
         ),
-        out_shape=[o for o, _ in outs],
+        out_shape=[pltpu.HBM(o.shape, o.dtype) for o, _ in outs],
         input_output_aliases={} if aliases is None else {k + 2: v for k, v in aliases.items()},
         compiler_params=pltpu.CompilerParams(vmem_limit_bytes=VMEM_BYTES),
         cost_estimate=pl.CostEstimate(flops=flops, bytes_accessed=moved, transcendentals=0),
@@ -73,18 +76,11 @@
 
 
 def weight_copies(which, core, w_refs, w_scr, sems):
-    own_s, own_n, left, left_x, right, right_x, far_a, far_b, far_ax, far_bx = w_refs
-    half = w_scr.shape[1] // 2
-    top, low = pl.ds(0, half), pl.ds(half, half)
+    own_s, own_n, left, left_x, right, right_x, far, far_x = w_refs
     plans = {
         0: [(own_s, w_scr.at[0]), (own_n, w_scr.at[1])],
         1: [(right, w_scr.at[core]), (right_x, w_scr.at[1 - core])],
-        2: [
-            (far_a, w_scr.at[core, top]),
-            (far_b, w_scr.at[core, low]),
-            (far_ax, w_scr.at[1 - core, top]),
-            (far_bx, w_scr.at[1 - core, low]),
-        ],
+        2: [(far, w_scr.at[core]), (far_x, w_scr.at[1 - core])],
         3: [(left, w_scr.at[core]), (left_x, w_scr.at[1 - core])],
     }
     return [pltpu.make_async_copy(s, d, sems.at[n]) for n, (s, d) in enumerate(plans[which])]
@@ -174,7 +170,7 @@
 
 
 def forward_kernel(layer, first, ids, cols, h_ref, arr_ref, vals_ref, pick_ref, *rest):
-    w_refs, rest = rest[:10], rest[10:]
+    w_refs, rest = rest[:8], rest[8:]
     if not first:
         rest = rest[1:]
     agg_ref, pre_ref, hid_ref, out_ref, buf_ref, ext, w_scr, sems = rest
@@ -195,7 +191,7 @@
 
 
 def top_kernel(layer, ids, cols, h_ref, arr_ref, vals_ref, wout_ref, lab_ref, mask_ref, *rest):
-    w_refs, rest = rest[:10], rest[11:]
+    w_refs, rest = rest[:8], rest[9:]
     agg_ref, dpre_ref, remote_ref, part_ref, buf_ref, ext, w_scr, sems, d_ext = rest
     rows = h_ref.shape[0]
     agg, pre, sig, hid = forward_math(
@@ -223,20 +219,13 @@
     return total
 
 
-def backward_kernel(layer, carry, has_buf, ids, cols, ret_ref, part_in, pre_ref, vals_ref, pick_ref, *rest):
-    w_refs, rest = rest[:10], rest[10:]
-    if carry:
-        keep_ref, recv_ref, rest = rest[0], rest[1], rest[2:]
-    if has_buf:
-        rest = rest[1:]
-    got_chunk = ret_ref.shape[1] > 8
-    dpre_ref, remote_ref, part_ref, buf_ref, rest = *rest[:4], rest[4:]
-    if got_chunk:
-        chunk_ref, rest = rest[0], rest[1:]
-    w_scr, sems, d_ext = rest
+def backward_kernel(layer, has_buf, ids, cols, ret_ref, part_in, pre_ref, vals_ref, pick_ref, *rest):
+    w_refs, rest = rest[:8], rest[9 + has_buf :]
+    dpre_ref, out_ref, part_ref, buf_ref, w_scr, sems, d_ext, remote, out_sem = rest
     start_weights(layer, ids, w_refs, w_scr, sems)
     rows, feat = part_in.shape
-    returned = ret_ref[:, 0:8, :].reshape(rows, feat)
+    peers, slots = remote.shape[0], remote.shape[1]
+    returned = ret_ref[:, 0:slots, :].reshape(rows, feat)
     d_out = (part_in[...] + dot(pick_ref[...], returned, TN)).astype(BF)
     buf_ref[...] = d_out
     pre = pre_ref[...]
@@ -245,14 +234,11 @@
     dpre_ref[...] = d_pre
     wait_weights(layer, ids, w_refs, w_scr, sems)
     back = backward_math(ids, cols, d_pre, vals_ref, w_scr, d_ext)
+    remote[...] = d_ext[rows : 2 * rows, :].astype(BF).reshape(peers, slots, feat)
+    copy = pltpu.make_async_copy(remote, out_ref.at[:, pl.ds(0, slots), :], out_sem)
+    copy.start()
     part_ref[...] = back + d_ext[0:rows, :]
-    remote = d_ext[rows : 2 * rows, :].astype(BF).reshape(ret_ref.shape[0], 8, feat)
-    remote_ref[:, 0:8, :] = remote
-    if carry:
-        both = (keep_ref[...].astype(F32) + recv_ref[...].astype(F32)).astype(BF)
-        remote_ref[:, 8:24, :] = both.reshape(ret_ref.shape[0], 16, feat)
-    if got_chunk:
-        chunk_ref[...] = chunk_sum(ret_ref[:, 8:24, :]).astype(BF)
+    copy.wait()
 
 
 def grad_kernel(ids, cols, h_ref, agg_ref, dpre_ref, keep_ref, send_ref):
@@ -271,13 +257,17 @@
         send_ref[...] = on_rows
 
 
-def join_kernel(ids, cols, remote_ref, keep_a, recv_a, keep_b, recv_b, out_ref):
-    peers, feat = out_ref.shape[0], out_ref.shape[2]
-    out_ref[:, 0:8, :] = remote_ref[:, 0:8, :]
-    first = (keep_a[...].astype(F32) + recv_a[...].astype(F32)).astype(BF)
-    out_ref[:, 8:24, :] = first.reshape(peers, 16, feat)
-    second = (keep_b[...].astype(F32) + recv_b[...].astype(F32)).astype(BF)
-    out_ref[:, 24:40, :] = second.reshape(peers, 16, feat)
+def carry_kernel(first, ids, cols, keep_ref, recv_ref, *rest):
+    out_ref, both, sem = rest[-3:]
+    total = (keep_ref[...].astype(F32) + recv_ref[...].astype(F32)).astype(BF)
+    both[...] = total.reshape(both.shape)
+    copy = pltpu.make_async_copy(both, out_ref.at[:, pl.ds(first, both.shape[1]), :], sem)
+    copy.start()
+    copy.wait()
+
+
+def chunk_kernel(ids, cols, ret_ref, out_ref):
+    out_ref[...] = chunk_sum(ret_ref[:, 8:24, :]).astype(BF)
 
 
 def end_kernel(ids, cols, ret_ref, part_in, pick_ref, buf_in, c_3, c_2, buf_ref, chunks_ref):
@@ -313,18 +303,12 @@
         neigh_ref[0] = mine
 
 
-def home_kernel(ids, cols, own_ref, a_ref, b_ref, c_ref, out_ref, sems):
+def home_kernel(ids, cols, own_ref, a_ref, b_ref, c_ref, out_ref):
     home = ids[0]
-    copies = [
-        pltpu.make_async_copy(own_ref.at[0], out_ref.at[0, home], sems.at[0]),
-        pltpu.make_async_copy(a_ref, out_ref.at[0, lax.rem(home + 3, 4)], sems.at[1]),
-        pltpu.make_async_copy(b_ref, out_ref.at[0, lax.rem(home + 2, 4)], sems.at[2]),
-        pltpu.make_async_copy(c_ref, out_ref.at[0, lax.rem(home + 1, 4)], sems.at[3]),
-    ]
-    for copy in copies:
-        copy.start()
-    for copy in copies:
-        copy.wait()
+    out_ref[0, home] = own_ref[...]
+    out_ref[0, lax.rem(home + 3, 4)] = a_ref[...]
+    out_ref[0, lax.rem(home + 2, 4)] = b_ref[...]
+    out_ref[0, lax.rem(home + 1, 4)] = c_ref[...]
 
 
 def body(
@@ -354,36 +338,19 @@
     wide = sds((rows, feat), F32)
     act_spec, square_spec = whole((rows, feat)), whole((feat, feat))
 
-    mine = jnp.where(core == 0, w_self[0], w_neigh[0])
-    left = shift(mine, "layer", 1)
-    right = shift(mine, "layer", -1)
-    half = feat // 2
-    far_a = shift(left[:half], "layer", 1)
-    far_b = shift(right[half:], "layer", -1)
-    weights = [
-        (w, ANY)
-        for w in (
-            w_self[0],
-            w_neigh[0],
-            left,
-            sibling(left),
-            right,
-            sibling(right),
-            far_a,
-            far_b,
-            sibling(far_a),
-            sibling(far_b),
-        )
-    ]
     features_in = (features, of_span((rows, feat)))
     vals_in = (
         tile_vals.reshape(spans, tiles, degree, size, size),
         of_span((tiles, degree, size, size)),
     )
-    w_scratch = [pltpu.VMEM((2, feat, feat), BF), pltpu.SemaphoreType.DMA((4,))]
+    w_scratch = [pltpu.VMEM((2, feat, feat), BF), pltpu.SemaphoreType.DMA((2,))]
     ext_scratch = pltpu.VMEM((2 * rows, feat), BF)
     d_ext_scratch = pltpu.VMEM((2 * rows, feat), F32)
 
+    mine = jnp.where(core == 0, w_self[0], w_neigh[0])
+    left = shift(mine, "layer", 1)
+    right = shift(mine, "layer", -1)
+    far = shift(mine, "layer", 2)
     pick, outgoing = run(
         pre_kernel,
         "gather_rows",
@@ -401,13 +368,17 @@
         moved=10**6,
     )
     pick_in = (pick, whole(pick.shape))
-    back_rows = lambda value: exchange(value.reshape(peers, slots, feat))
+    arrived = exchange(outgoing.reshape(peers, slots, feat))
+    arrived, left, right, far = lax.optimization_barrier((arrived, left, right, far))
+    sources = (w_self[0], w_neigh[0], left, sibling(left), right, sibling(right), far, sibling(far))
+    weights = [(w, ANY) for w in sources]
 
     hidden, aggs, pres = [features_in], [], []
     acts_buf = None
     for layer in range(spans - 1):
-        arrived = back_rows(outgoing).reshape(rows, feat)
-        ins = [hidden[layer], (arrived, act_spec), vals_in, pick_in, *weights]
+        if layer:
+            arrived = exchange(outgoing.reshape(peers, slots, feat))
+        ins = [hidden[layer], (arrived.reshape(rows, feat), LOCAL), vals_in, pick_in, *weights]
         aliases = None
         if layer:
             ins.append((acts_buf, ANY))
@@ -434,11 +405,11 @@
         pres.append(pre)
 
     top = spans - 1
-    arrived = back_rows(outgoing).reshape(rows, feat)
+    arrived = exchange(outgoing.reshape(peers, slots, feat)).reshape(rows, feat)
     column = (rows, 1)
     ins = [
         hidden[top],
-        (arrived, act_spec),
+        (arrived, LOCAL),
         vals_in,
         (w_out, whole((feat, classes))),
         (labels.reshape(spans, *column), of_span(column)),
@@ -465,14 +436,18 @@
     )
     aggs.append(agg)
 
-    def send_home(buf):
+    def travel(buf):
+        return [shift(buf[s], "layer", s) for s in range(1, spans)]
+
+    def send_home(buf, pieces):
+        block = pl.BlockSpec((None, rows, feat), lambda i, ids, cols: (0, 0, 0))
+        shape = (1, spans, rows, feat)
         return run(
             home_kernel,
             "put_home",
             scalars,
-            [(buf, ANY), *[(shift(buf[s], "layer", s), ANY) for s in range(1, spans)]],
-            [(sds((1, spans, rows, feat), BF), ANY)],
-            [pltpu.SemaphoreType.DMA((4,))],
+            [(buf, block), *[(piece, LOCAL) for piece in pieces]],
+            [(sds(shape, BF), whole(shape))],
             moved=2 * 10**6,
         )[0]
 
@@ -488,87 +463,91 @@
         )
         return keep, sibling(send)
 
-    layer_acts = send_home(acts_buf)
+    layer_acts = send_home(acts_buf, travel(acts_buf))
     chunk_rows = feat // peers
     chunk_shape = (2, chunk_rows, feat)
+    chunk_scratch = [pltpu.VMEM((peers, chunk_rows, feat), BF), pltpu.SemaphoreType.DMA]
+
+    def carry(partials, first, width, buf=None):
+        ins = [(partials[0], square_spec), (partials[1], LOCAL)]
+        if buf is not None:
+            ins.append((buf, ANY))
+        return run(
+            functools.partial(carry_kernel, first),
+            "carry_partials",
+            scalars,
+            ins,
+            [(sds((peers, width, feat), BF), ANY)],
+            chunk_scratch,
+            None if buf is None else {2: 0},
+            moved=2 * 10**6,
+        )[0]
+
     grads_buf = None
     chunks = {}
     for layer in range(top - 1, -1, -1):
         returned = exchange(remote)
-        got_chunk = returned.shape[1] > slots
-        partials = weight_partials(layer + 1, d_pre)
-        carry = layer > 0
-        out_rows = slots + chunk_rows if carry else slots
+        if layer < top - 1:
+            chunks[layer + 2] = run(
+                chunk_kernel,
+                "sum_chunks",
+                scalars,
+                [(returned, LOCAL)],
+                [(sds(chunk_shape, BF), whole(chunk_shape))],
+                moved=10**6,
+            )[0]
+        width = slots + chunk_rows * (1 if layer else 2)
+        carried = carry(weight_partials(layer + 1, d_pre), slots, width)
         ins = [
-            (returned, whole(returned.shape)),
+            (returned, LOCAL),
             (part, act_spec),
             (pres[layer], act_spec),
             vals_in,
             pick_in,
             *weights,
+            (carried, ANY),
         ]
-        if carry:
-            ins += [(partials[0], square_spec), (partials[1], square_spec)]
-        aliases = None
+        aliases = {len(ins) - 1: 1}
         if grads_buf is not None:
             ins.append((grads_buf, ANY))
-            aliases = {len(ins) - 1: 3}
-        outs = [
-            (act, act_spec),
-            (sds((peers, out_rows, feat), BF), whole((peers, out_rows, feat))),
-            (wide, act_spec),
-            (stack, at_offset((rows, feat), layer + 1)),
-        ]
-        if got_chunk:
-            outs.append((sds(chunk_shape, BF), whole(chunk_shape)))
-        result = run(
-            functools.partial(backward_kernel, layer, carry, grads_buf is not None),
+            aliases[len(ins) - 1] = 3
+        d_pre, remote, part, grads_buf = run(
+            functools.partial(backward_kernel, layer, grads_buf is not None),
             f"layer_backward_{layer}",
             scalars,
             ins,
-            outs,
-            [*w_scratch, d_ext_scratch],
+            [
+                (act, act_spec),
+                (sds((peers, width, feat), BF), ANY),
+                (wide, act_spec),
+                (stack, at_offset((rows, feat), layer + 1)),
+            ],
+            [
+                *w_scratch,
+                d_ext_scratch,
+                pltpu.VMEM((peers, slots, feat), BF),
+                pltpu.SemaphoreType.DMA,
+            ],
             aliases,
             flops=7 * 10**8,
             moved=5 * 10**6,
         )
-        d_pre, remote, part, grads_buf = result[:4]
-        if got_chunk:
-            chunks[layer + 2] = result[4]
-
-    last = weight_partials(0, d_pre)
-    joined = run(
-        join_kernel,
-        "join_rows",
-        scalars,
-        [
-            (remote, whole(remote.shape)),
-            (partials[0], square_spec),
-            (partials[1], square_spec),
-            (last[0], square_spec),
-            (last[1], square_spec),
-        ],
-        [
-            (
-                sds((peers, slots + 2 * chunk_rows, feat), BF),
-                whole((peers, slots + 2 * chunk_rows, feat)),
-            )
-        ],
-        moved=3 * 10**6,
-    )[0]
+        if layer == 1:
+            remote, layer_acts = lax.optimization_barrier((remote, layer_acts))
+
+    joined = carry(weight_partials(0, d_pre), slots + chunk_rows, remote.shape[1], remote)
     returned = exchange(joined)
-    c_2 = chunks[2]
     grads_buf, sums = run(
         end_kernel,
         "input_grads",
         scalars,
         [
-            (returned, whole(returned.shape)),
+            (returned, LOCAL),
             (part, act_spec),
             pick_in,
             (grads_buf, ANY),
             (chunks[3], whole(chunk_shape)),
-            (c_2, whole(chunk_shape)),
+            (chunks[2], whole(chunk_shape)),
         ],
         [
             (stack, at_offset((rows, feat), 0)),
@@ -584,18 +563,21 @@
         scalars,
         [
             (sums, whole((spans, *chunk_shape))),
-            *[(shift(sums[s], "layer", s), whole(chunk_shape)) for s in range(1, spans)],
+            *[(shift(sums[s], "layer", s), LOCAL) for s in range(1, spans)],
         ],
         [(sds((peers, chunk_rows, feat), BF), whole((peers, chunk_rows, feat)))],
         moved=10**6,
     )[0]
-    act_grads = send_home(grads_buf)
-    gathered = exchange(spread).reshape(feat, feat)
+    spread, grads_buf = lax.optimization_barrier((spread, grads_buf))
+    pieces = travel(grads_buf)
+    gathered, *pieces = lax.optimization_barrier((exchange(spread), *pieces))
+    act_grads = send_home(grads_buf, pieces)
+    gathered = gathered.reshape(feat, feat)
     grad_self, grad_neigh = run(
         functools.partial(scale_kernel, scale),
         "scale_grads",
         scalars,
-        [(gathered, square_spec), (sibling(gathered), square_spec)],
+        [(gathered, LOCAL), (sibling(gathered), LOCAL)],
         [(sds((1, feat, feat), F32), whole((1, feat, feat)))] * 2,
         moved=3 * 10**6,
     )

time: 279 us -> 254 us (0.910)
  local copies, waits for them, and re-layouts: 51.4 us -> 5.5 us
  Pallas kernels: 44.2 us -> 76.6 us
  blocking collectives: 78.2 us -> 47.4 us
  waiting for transfers between devices: 60.6 us -> 75.5 us
  starting transfers between devices: 39.8 us -> 43.9 us
    unnamed x150 -> x28, local copies, waits for them, and re-layouts: 46.8 us -> 2.38 us
    pallas_call x18 -> x23, Pallas kernels: 44.2 us -> 76.6 us  [run(): pl.pallas_call(kernel, name=name, grid_spec=pltpu.PrefetchScalarGridSpec(...]
    all_to_all x5 -> x3, blocking collectives: 78.2 us -> 47.4 us  [exchange(): lax.all_to_all(value, 'node', split_axis=0, concat_axis=0, tiled=True)]
    all_to_all x4 -> x6, waiting for transfers between devices: 26.6 us -> 35.8 us  [exchange(): lax.all_to_all(value, 'node', split_axis=0, concat_axis=0, tiled=True)]
    all_to_all x4 -> x6, starting transfers between devices: 18 us -> 27.1 us  [exchange(): lax.all_to_all(value, 'node', split_axis=0, concat_axis=0, tiled=True)]
    ppermute x13 -> x12, starting transfers between devices: 18.9 us -> 14.7 us  [shift(): lax.ppermute(value, axis, [(i, (i + steps) % count) for i in range(count)])]
    ppermute x9 -> x8, waiting for transfers between devices: 3.37 us -> 6.41 us  [sibling(): return lax.ppermute(value, 'node', [(i, i ^ 1) for i in range(count)])]
    ppermute x13 -> x12, waiting for transfers between devices: 30.7 us -> 33.2 us  [shift(): lax.ppermute(value, axis, [(i, (i + steps) % count) for i in range(count)])]
  transfers between devices with their start and end apart: 26 -> 26, of which waited for: 13 -> 17; matrix products, arithmetic and copies ran while one was open for 3% -> 2% of each run, Pallas kernels for 7% -> 10%
where the time goes in v2:
time: 254 us; the launch traced here: 251 us
  Pallas kernels  76.6 us (30%)
  waiting for transfers between devices  75.5 us (30%)
  blocking collectives  47.4 us (19%)
  starting transfers between devices  43.9 us (17%)
  local copies, waits for them, and re-layouts  5.5 us (2%)
    pallas_call x23, Pallas kernels, run(): pl.pallas_call(kernel, name=name, grid_spec=pltpu.PrefetchScalarGridSpec(...  76.6 us
    all_to_all x3, blocking collectives, exchange(): lax.all_to_all(value, 'node', split_axis=0, concat_axis=0, tiled=True)  47.4 us
    all_to_all x6, waiting for transfers between devices, exchange(): lax.all_to_all(value, 'node', split_axis=0, concat_axis=0, tiled=True)  35.8 us
    ppermute x12, waiting for transfers between devices, shift(): lax.ppermute(value, axis, [(i, (i + steps) % count) for i in range(count)])  33.2 us
    all_to_all x6, starting transfers between devices, exchange(): lax.all_to_all(value, 'node', split_axis=0, concat_axis=0, tiled=True)  27.1 us
    ppermute x12, starting transfers between devices, shift(): lax.ppermute(value, axis, [(i, (i + steps) % count) for i in range(count)])  14.7 us
    ppermute x8, waiting for transfers between devices, sibling(): return lax.ppermute(value, 'node', [(i, i ^ 1) for i in range(count)])  6.41 us
  transfers between devices with their start and end apart: 26, of which 17 were waited for; matrix products, arithmetic and copies ran while one was open for 2% of the time, Pallas kernels for 10%

profile of v2, /device:TPU:0, one launch (start us, length us, event | category | flops | bytes accessed | tf_op | source)
XLA Modules:
  0.0 251.1 jit_solution(7862000058493679100)
XLA Ops:
  0.7 1.3 broadcast_select_fusion
  1.9 3.2 %collective-permute-start.2 = (bf16[512,512]{1,0:T(8,128)(2,1)S(1)}, bf16[512,512]{1,0:T(8,128)(2,1)S(1)}, u32[]{:S(2)}, u32[]{:S(2)}) collective-permute-start(bf16[512,512]{1,0:T(8,128)(2,1)S(1)} %broadcast_select_fusion), channel_id=1, source_target_pairs={{0,64},{32,96},{64,0},{96,32},{1,65},{33,97},{65,1},{97,33},{2,66}... | collective-permute-start | bytes 1572872 | tf_op jit(solution)/shard_map/ppermute | solution.py:26
  8.0 2.6 %gather_rows.1 = (bf16[256,256]{1,0:T(8,128)(2,1)}, bf16[256,512]{1,0:T(8,128)(2,1)}) custom-call(s32[2]{0:T(128)S(1)} %pad_add_fusion.ids, s32[32]{0:T(128)S(1)} %reshape.50.cols, bf16[4,256,512]{2,1,0:T(8,128)(2,1)} %h_ref.5, s32[4,32,8]{2,1,0:T(8,128)} %bitcast.64, s32[4,1,32]{2,1,0:T(1,128)} %counts_ref.1), custom_call_target="tpu_custom_call" | custom-call | flops 100000000 | bytes 1000000 | tf_op jit(solution)/shard_map/gather_rows/pallas_call | solution.py:61
  10.6 17.3 %all_to_all.45 = bf16[32,8,512]{2,1,0:T(8,128)(2,1)S(1)} all-to-all(bf16[32,8,512]{2,1,0:T(8,128)(2,1)} %bitcast.68), channel_id=1, replica_groups=mesh['layer'=4,'node'=32] {'node'}, dimensions={0} | all-to-all | bytes 524288 | tf_op jit(solution)/shard_map/all_to_all | solution.py:35
  29.3 1.3 collective-permute-done.3.rest_3_
  32.9 4.5 %layer_forward_0.1 = (bf16[256,512]{1,0:T(8,128)(2,1)}, f32[256,512]{1,0:T(8,128)}, bf16[256,512]{1,0:T(8,128)(2,1)}, bf16[256,512]{1,0:T(8,128)(2,1)}, bf16[4,256,512]{2,1,0:T(8,128)(2,1)}) custom-call(s32[2]{0:T(128)S(1)} %pad_add_fusion.ids, s32[32]{0:T(128)S(1)} %reshape.50.cols, bf16[4,256,512]{2,1,0:T(8,128)(2,1)} %h_ref.5, ...), custom_call_target="tpu_custom_call" | custom-call | flops 600000000 | bytes 4000000 | tf_op jit(solution)/shard_map/layer_forward_0/pallas_call | solution.py:61
  37.4 17.3 %all_to_all.46 = bf16[32,8,512]{2,1,0:T(8,128)(2,1)S(1)} all-to-all(bf16[32,8,512]{2,1,0:T(8,128)(2,1)} %bitcast.67), channel_id=1, replica_groups=mesh['layer'=4,'node'=32] {'node'}, dimensions={0} | all-to-all | bytes 524288 | tf_op jit(solution)/shard_map/all_to_all | solution.py:35
  54.7 4.6 %layer_forward_1.1 = (bf16[256,512]{1,0:T(8,128)(2,1)}, f32[256,512]{1,0:T(8,128)}, bf16[256,512]{1,0:T(8,128)(2,1)}, bf16[256,512]{1,0:T(8,128)(2,1)}, bf16[4,256,512]{2,1,0:T(8,128)(2,1)}) custom-call(s32[2]{0:T(128)S(1)} %pad_add_fusion.ids, s32[32]{0:T(128)S(1)} %reshape.50.cols, ...), custom_call_target="tpu_custom_call", output_to_operand_aliasing={{4}: (14, {})} | custom-call | flops 600000000 | bytes 4000000 | tf_op jit(solution)/shard_map/layer_forward_1/pallas_call | solution.py:61
  59.3 12.8 %all_to_all.47 = bf16[32,8,512]{2,1,0:T(8,128)(2,1)S(1)} all-to-all(bf16[32,8,512]{2,1,0:T(8,128)(2,1)} %bitcast.66), channel_id=1, replica_groups=mesh['layer'=4,'node'=32] {'node'}, dimensions={0} | all-to-all | bytes 524288 | tf_op jit(solution)/shard_map/all_to_all | solution.py:35
  72.1 4.6 %layer_forward_2.1 = (bf16[256,512]{1,0:T(8,128)(2,1)}, f32[256,512]{1,0:T(8,128)}, bf16[256,512]{1,0:T(8,128)(2,1)}, bf16[256,512]{1,0:T(8,128)(2,1)}, bf16[4,256,512]{2,1,0:T(8,128)(2,1)}) custom-call(s32[2]{0:T(128)S(1)} %pad_add_fusion.ids, s32[32]{0:T(128)S(1)} %reshape.50.cols, ...), custom_call_target="tpu_custom_call", output_to_operand_aliasing={{4}: (14, {})} | custom-call | flops 600000000 | bytes 4000000 | tf_op jit(solution)/shard_map/layer_forward_2/pallas_call | solution.py:61
  76.8 3.9 %all-to-all-start.3 = ((bf16[32,8,512]{2,1,0:T(8,128)(2,1)}), bf16[32,8,512]{2,1,0:T(8,128)(2,1)S(1)}, u32[]{:S(2)}, u32[]{:S(2)}) async-start(bf16[32,8,512]{2,1,0:T(8,128)(2,1)} %bitcast.65), calls=%async_computation.3 | async-start | bytes 524288 | tf_op jit(solution)/shard_map/all_to_all | solution.py:35
  83.6 6.0 %all-to-all-done.3 = bf16[32,8,512]{2,1,0:T(8,128)(2,1)S(1)} async-done(((bf16[32,8,512]{2,1,0:T(8,128)(2,1)}), bf16[32,8,512]{2,1,0:T(8,128)(2,1)S(1)}, u32[]{:S(2)}, u32[]{:S(2)}) %all-to-all-start.3) | async-done | bytes 262176 | tf_op jit(solution)/shard_map/all_to_all | solution.py:35
  89.6 5.9 %top_layer.1 = (bf16[256,512]{1,0:T(8,128)(2,1)}, bf16[256,512]{1,0:T(8,128)(2,1)}, bf16[32,8,512]{2,1,0:T(8,128)(2,1)}, f32[256,512]{1,0:T(8,128)}, bf16[4,256,512]{2,1,0:T(8,128)(2,1)}) custom-call(s32[2]{0:T(128)S(1)} %pad_add_fusion.ids, s32[32]{0:T(128)S(1)} %reshape.50.cols, ...), custom_call_target="tpu_custom_call", output_to_operand_aliasing={{4}: (16, {})} | custom-call | flops 1000000000 | bytes 5000000 | tf_op jit(solution)/shard_map/top_layer/pallas_call | solution.py:61
  95.4 3.2 %weight_partials_3.1 = (bf16[512,512]{1,0:T(8,128)(2,1)}, bf16[512,512]{1,0:T(8,128)(2,1)}) custom-call(s32[2]{0:T(128)S(1)} %pad_add_fusion.ids, s32[32]{0:T(128)S(1)} %reshape.50.cols, bf16[256,512]{1,0:T(8,128)(2,1)} %get-tuple-element.74.h_ref, bf16[256,512]{1,0:T(8,128)(2,1)} %get-tuple-element.80.agg_ref, bf16[256,512]{1,0:T(8,128)(2,1)} %get-tuple-element.81.dpre_ref), custom_call_target="tpu_custom_call" | custom-call | flops 300000000 | bytes 2000000 | tf_op jit(solution)/shard_map/weight_partials_3/pallas_call | solution.py:61
  99.0 3.9 %all-to-all-start.4 = ((bf16[32,8,512]{2,1,0:T(8,128)(2,1)}), bf16[32,8,512]{2,1,0:T(8,128)(2,1)S(1)}, u32[]{:S(2)}, u32[]{:S(2)}) async-start(bf16[32,8,512]{2,1,0:T(8,128)(2,1)} %get-tuple-element.77), calls=%async_computation.4 | async-start | bytes 524288 | tf_op jit(solution)/shard_map/all_to_all | solution.py:35
  102.8 2.6 %carry_partials.4.rest_8_ = bf16[32,24,512]{2,1,0:T(8,128)(2,1)} custom-call(s32[2]{0:T(128)S(1)} %pad_add_fusion.ids, s32[32]{0:T(128)S(1)} %reshape.50.cols, bf16[512,512]{1,0:T(8,128)(2,1)} %get-tuple-element.82.keep_ref, bf16[512,512]{1,0:T(8,128)(2,1)S(1)} %collective-permute-done.6.recv_ref), custom_call_target="tpu_custom_call" | custom-call | bytes 2000000 | tf_op jit(solution)/shard_map/carry_partials/pallas_call | solution.py:61
  105.4 6.4 %all-to-all-done.4.ret_ref = bf16[32,8,512]{2,1,0:T(8,128)(2,1)S(1)} async-done(((bf16[32,8,512]{2,1,0:T(8,128)(2,1)}), bf16[32,8,512]{2,1,0:T(8,128)(2,1)S(1)}, u32[]{:S(2)}, u32[]{:S(2)}) %all-to-all-start.4) | async-done | bytes 262176 | tf_op jit(solution)/shard_map/all_to_all | solution.py:35
  111.8 5.5 %layer_backward_2.1 = (bf16[256,512]{1,0:T(8,128)(2,1)}, bf16[32,24,512]{2,1,0:T(8,128)(2,1)}, f32[256,512]{1,0:T(8,128)}, bf16[4,256,512]{2,1,0:T(8,128)(2,1)}) custom-call(s32[2]{0:T(128)S(1)} %pad_add_fusion.ids, s32[32]{0:T(128)S(1)} %reshape.50.cols, bf16[32,8,512]{2,1,0:T(8,128)(2,1)S(1)} %all-to-all-done.4.ret_ref, ...), custom_call_target="tpu_custom_call", output_to_operand_aliasing={{1}: (15, {})} | custom-call | flops 700000000 | bytes 5000000 | tf_op jit(solution)/shard_map/layer_backward_2/pallas_call | solution.py:61
  117.3 4.1 %all-to-all-start.5 = ((bf16[32,24,512]{2,1,0:T(8,128)(2,1)}), bf16[32,24,512]{2,1,0:T(8,128)(2,1)S(1)}, u32[]{:S(2)}, u32[]{:S(2)}) async-start(bf16[32,24,512]{2,1,0:T(8,128)(2,1)} %get-tuple-element.84), calls=%async_computation.5 | async-start | bytes 1572864 | tf_op jit(solution)/shard_map/all_to_all | solution.py:35
  121.4 3.2 %weight_partials_2.1 = (bf16[512,512]{1,0:T(8,128)(2,1)}, bf16[512,512]{1,0:T(8,128)(2,1)}) custom-call(s32[2]{0:T(128)S(1)} %pad_add_fusion.ids, s32[32]{0:T(128)S(1)} %reshape.50.cols, bf16[256,512]{1,0:T(8,128)(2,1)} %get-tuple-element.71.h_ref, bf16[256,512]{1,0:T(8,128)(2,1)} %get-tuple-element.87.agg_ref, bf16[256,512]{1,0:T(8,128)(2,1)} %get-tuple-element.88.dpre_ref), custom_call_target="tpu_custom_call" | custom-call | flops 300000000 | bytes 2000000 | tf_op jit(solution)/shard_map/weight_partials_2/pallas_call | solution.py:61
  124.8 2.7 %collective-permute-start.10 = (bf16[256,512]{1,0:T(8,128)(2,1)S(1)}, bf16[256,512]{1,0:T(8,128)(2,1)S(1)}, u32[]{:S(2)}, u32[]{:S(2)}) collective-permute-start(bf16[256,512]{1,0:T(8,128)(2,1)S(1)} %get-tuple-element.123), channel_id=1, source_target_pairs={{0,96},{32,0},{64,32},{96,64},{1,97},{33,1},{65,33},{97,65},{2,98}... | collective-permute-start | bytes 786440 | tf_op jit(solution)/shard_map/ppermute | solution.py:26
  129.1 10.2 %collective-permute-done.10.c_ref = bf16[256,512]{1,0:T(8,128)(2,1)S(1)} collective-permute-done((bf16[256,512]{1,0:T(8,128)(2,1)S(1)}, bf16[256,512]{1,0:T(8,128)(2,1)S(1)}, u32[]{:S(2)}, u32[]{:S(2)}) %collective-permute-start.10) | collective-permute-done | bytes 262176 | tf_op jit(solution)/shard_map/ppermute | solution.py:26
  139.3 3.7 %collective-permute-done.8.a_ref = bf16[256,512]{1,0:T(8,128)(2,1)S(1)} collective-permute-done((bf16[256,512]{1,0:T(8,128)(2,1)S(1)}, bf16[256,512]{1,0:T(8,128)(2,1)S(1)}, u32[]{:S(2)}, u32[]{:S(2)}) %collective-permute-start.8) | collective-permute-done | bytes 262176 | tf_op jit(solution)/shard_map/ppermute | solution.py:26
  142.9 2.5 %put_home.2 = bf16[1,4,256,512]{3,2,1,0:T(8,128)(2,1)} custom-call(s32[2]{0:T(128)S(1)} %pad_add_fusion.ids, s32[32]{0:T(128)S(1)} %reshape.50.cols, bf16[4,256,512]{2,1,0:T(8,128)(2,1)} %get-tuple-element.93.own_ref, bf16[256,512]{1,0:T(8,128)(2,1)S(1)} %collective-permute-done.8.a_ref, bf16[256,512]{1,0:T(8,128)(2,1)S(1)} %collective-permute-done.9.b_ref, ...), custom_call_target="tpu_custom_call" | custom-call | bytes 2000000 | tf_op jit(solution)/shard_map/put_home/pallas_call | solution.py:61
  145.5 2.6 %carry_partials.5.rest_8_ = bf16[32,24,512]{2,1,0:T(8,128)(2,1)} custom-call(s32[2]{0:T(128)S(1)} %pad_add_fusion.ids, s32[32]{0:T(128)S(1)} %reshape.50.cols, bf16[512,512]{1,0:T(8,128)(2,1)} %get-tuple-element.89.keep_ref, bf16[512,512]{1,0:T(8,128)(2,1)S(1)} %collective-permute-done.7.recv_ref), custom_call_target="tpu_custom_call" | custom-call | bytes 2000000 | tf_op jit(solution)/shard_map/carry_partials/pallas_call | solution.py:61
  148.0 5.6 %layer_backward_1.1 = (bf16[256,512]{1,0:T(8,128)(2,1)}, bf16[32,24,512]{2,1,0:T(8,128)(2,1)}, f32[256,512]{1,0:T(8,128)}, bf16[4,256,512]{2,1,0:T(8,128)(2,1)}) custom-call(s32[2]{0:T(128)S(1)} %pad_add_fusion.ids, s32[32]{0:T(128)S(1)} %reshape.50.cols, ...), custom_call_target="tpu_custom_call", output_to_operand_aliasing={{1}: (15, {}), {3}: (16, {})} | custom-call | flops 700000000 | bytes 5000000 | tf_op jit(solution)/shard_map/layer_backward_1/pallas_call | solution.py:61
  153.6 7.4 %all-to-all-start.6 = ((bf16[32,24,512]{2,1,0:T(8,128)(2,1)}), bf16[32,24,512]{2,1,0:T(8,128)(2,1)S(1)}, u32[]{:S(2)}, u32[]{:S(2)}) async-start(bf16[32,24,512]{2,1,0:T(8,128)(2,1)} %get-tuple-element.96), calls=%async_computation.6 | async-start | bytes 1572864 | tf_op jit(solution)/shard_map/all_to_all | solution.py:35
  161.0 3.2 %weight_partials_1.1 = (bf16[512,512]{1,0:T(8,128)(2,1)}, bf16[512,512]{1,0:T(8,128)(2,1)}) custom-call(s32[2]{0:T(128)S(1)} %pad_add_fusion.ids, s32[32]{0:T(128)S(1)} %reshape.50.cols, bf16[256,512]{1,0:T(8,128)(2,1)} %get-tuple-element.68.h_ref, bf16[256,512]{1,0:T(8,128)(2,1)} %get-tuple-element.99.agg_ref, bf16[256,512]{1,0:T(8,128)(2,1)} %get-tuple-element.100.dpre_ref), custom_call_target="tpu_custom_call" | custom-call | flops 300000000 | bytes 2000000 | tf_op jit(solution)/shard_map/weight_partials_1/pallas_call | solution.py:61
  164.5 1.9 collective-permute-done.11.recv_ref
  166.3 2.6 %carry_partials.6.rest_8_ = bf16[32,40,512]{2,1,0:T(8,128)(2,1)} custom-call(s32[2]{0:T(128)S(1)} %pad_add_fusion.ids, s32[32]{0:T(128)S(1)} %reshape.50.cols, bf16[512,512]{1,0:T(8,128)(2,1)} %get-tuple-element.101.keep_ref, bf16[512,512]{1,0:T(8,128)(2,1)S(1)} %collective-permute-done.11.recv_ref), custom_call_target="tpu_custom_call" | custom-call | bytes 2000000 | tf_op jit(solution)/shard_map/carry_partials/pallas_call | solution.py:61
  168.9 5.9 %all-to-all-done.6.ret_ref = bf16[32,24,512]{2,1,0:T(8,128)(2,1)S(1)} async-done(((bf16[32,24,512]{2,1,0:T(8,128)(2,1)}), bf16[32,24,512]{2,1,0:T(8,128)(2,1)S(1)}, u32[]{:S(2)}, u32[]{:S(2)}) %all-to-all-start.6) | async-done | bytes 786464 | tf_op jit(solution)/shard_map/all_to_all | solution.py:35
  174.8 5.6 %layer_backward_0.1 = (bf16[256,512]{1,0:T(8,128)(2,1)}, bf16[32,40,512]{2,1,0:T(8,128)(2,1)}, f32[256,512]{1,0:T(8,128)}, bf16[4,256,512]{2,1,0:T(8,128)(2,1)}) custom-call(s32[2]{0:T(128)S(1)} %pad_add_fusion.ids, s32[32]{0:T(128)S(1)} %reshape.50.cols, ...), custom_call_target="tpu_custom_call", output_to_operand_aliasing={{1}: (15, {}), {3}: (16, {})} | custom-call | flops 700000000 | bytes 5000000 | tf_op jit(solution)/shard_map/layer_backward_0/pallas_call | solution.py:61
  180.4 3.2 %weight_partials_0.1 = (bf16[512,512]{1,0:T(8,128)(2,1)}, bf16[512,512]{1,0:T(8,128)(2,1)}) custom-call(s32[2]{0:T(128)S(1)} %pad_add_fusion.ids, s32[32]{0:T(128)S(1)} %reshape.50.cols, bf16[4,256,512]{2,1,0:T(8,128)(2,1)} %h_ref.5, bf16[256,512]{1,0:T(8,128)(2,1)} %get-tuple-element.95.agg_ref, bf16[256,512]{1,0:T(8,128)(2,1)} %get-tuple-element.104.dpre_ref), custom_call_target="tpu_custom_call" | custom-call | flops 300000000 | bytes 2000000 | tf_op jit(solution)/shard_map/weight_partials_0/pallas_call | solution.py:61
  184.3 1.7 collective-permute-done.12.recv_ref
  186.0 2.6 %carry_partials.7 = bf16[32,40,512]{2,1,0:T(8,128)(2,1)} custom-call(s32[2]{0:T(128)S(1)} %pad_add_fusion.ids, s32[32]{0:T(128)S(1)} %reshape.50.cols, bf16[512,512]{1,0:T(8,128)(2,1)} %get-tuple-element.105.keep_ref, bf16[512,512]{1,0:T(8,128)(2,1)S(1)} %collective-permute-done.12.recv_ref, ...), custom_call_target="tpu_custom_call", output_to_operand_aliasing={{}: (4, {})} | custom-call | bytes 2000000 | tf_op jit(solution)/shard_map/carry_partials/pallas_call | solution.py:61
  188.6 4.0 %all-to-all-start.7 = ((bf16[32,40,512]{2,1,0:T(8,128)(2,1)}), bf16[32,40,512]{2,1,0:T(8,128)(2,1)S(1)}, u32[]{:S(2)}, u32[]{:S(2)}) async-start(bf16[32,40,512]{2,1,0:T(8,128)(2,1)} %carry_partials.7), calls=%async_computation.7 | async-start | bytes 2621440 | tf_op jit(solution)/shard_map/all_to_all | solution.py:35
  192.6 1.2 sum_chunks.2.c_3
  195.0 17.5 %all-to-all-done.7.ret_ref = bf16[32,40,512]{2,1,0:T(8,128)(2,1)S(1)} async-done(((bf16[32,40,512]{2,1,0:T(8,128)(2,1)}), bf16[32,40,512]{2,1,0:T(8,128)(2,1)S(1)}, u32[]{:S(2)}, u32[]{:S(2)}) %all-to-all-start.7) | async-done | bytes 1310752 | tf_op jit(solution)/shard_map/all_to_all | solution.py:35
  212.5 2.7 %input_grads.1 = (bf16[4,256,512]{2,1,0:T(8,128)(2,1)}, bf16[4,2,16,512]{3,2,1,0:T(8,128)(2,1)}) custom-call(s32[2]{0:T(128)S(1)} %pad_add_fusion.ids, s32[32]{0:T(128)S(1)} %reshape.50.cols, bf16[32,40,512]{2,1,0:T(8,128)(2,1)S(1)} %all-to-all-done.7.ret_ref, f32[256,512]{1,0:T(8,128)} %get-tuple-element.108.part_in, ...), custom_call_target="tpu_custom_call", output_to_operand_aliasing={{0}: (5, {})} | custom-call | flops 100000000 | bytes 3000000 | tf_op jit(solution)/shard_map/input_grads/pallas_call | solution.py:61
  218.3 1.8 collective-permute-done.15.c_ref
  220.1 2.1 collective-permute-done.14.b_ref
  222.7 2.3 sum_over_layer.1
  225.0 3.9 %all-to-all-start.8 = ((bf16[32,16,512]{2,1,0:T(8,128)(2,1)}), bf16[32,16,512]{2,1,0:T(8,128)(2,1)S(1)}, u32[]{:S(2)}, u32[]{:S(2)}) async-start(bf16[32,16,512]{2,1,0:T(8,128)(2,1)} %sum_over_layer.1), calls=%async_computation.8 | async-start | bytes 1048576 | tf_op jit(solution)/shard_map/all_to_all | solution.py:35
  229.0 2.1 collective-permute-start.18
  232.0 10.6 %collective-permute-done.18.c_ref = bf16[256,512]{1,0:T(8,128)(2,1)S(1)} collective-permute-done((bf16[256,512]{1,0:T(8,128)(2,1)S(1)}, bf16[256,512]{1,0:T(8,128)(2,1)S(1)}, u32[]{:S(2)}, u32[]{:S(2)}) %collective-permute-start.18) | collective-permute-done | bytes 262176 | tf_op jit(solution)/shard_map/ppermute | solution.py:26
  242.6 3.7 %collective-permute-done.16.a_ref = bf16[256,512]{1,0:T(8,128)(2,1)S(1)} collective-permute-done((bf16[256,512]{1,0:T(8,128)(2,1)S(1)}, bf16[256,512]{1,0:T(8,128)(2,1)S(1)}, u32[]{:S(2)}, u32[]{:S(2)}) %collective-permute-start.16) | collective-permute-done | bytes 262176 | tf_op jit(solution)/shard_map/ppermute | solution.py:26
  246.3 2.5 %put_home.3 = bf16[1,4,256,512]{3,2,1,0:T(8,128)(2,1)} custom-call(s32[2]{0:T(128)S(1)} %pad_add_fusion.ids, s32[32]{0:T(128)S(1)} %reshape.50.cols, bf16[4,256,512]{2,1,0:T(8,128)(2,1)} %get-tuple-element.112.own_ref, bf16[256,512]{1,0:T(8,128)(2,1)S(1)} %collective-permute-done.16.a_ref, bf16[256,512]{1,0:T(8,128)(2,1)S(1)} %collective-permute-done.17.b_ref, ...), custom_call_target="tpu_custom_call" | custom-call | bytes 2000000 | tf_op jit(solution)/shard_map/put_home/pallas_call | solution.py:61
  248.9 2.2 scale_grads.1
  (66 shorter events, 18.4 us)
Async XLA Ops:
  0.6 6.5 %copy-start.12 = (s32[4,1,2,4]{3,2,1,0:T(2,128)S(1)}, s32[4,1,2,4]{3,2,1,0:T(2,128)}, u32[]{:S(2)}) copy-start(s32[4,1,2,4]{3,2,1,0:T(2,128)} %param.16) | copy-start | bytes 388
  0.6 6.6 %copy-start.9 = (s32[4,1,32,8]{2,3,1,0:T(8,128)S(1)}, s32[4,1,32,8]{2,3,1,0:T(8,128)}, u32[]{:S(2)}) copy-start(s32[4,1,32,8]{2,3,1,0:T(8,128)} %param.18) | copy-start | bytes 12292
  1.9 26.0 %collective-permute-start.2 = (bf16[512,512]{1,0:T(8,128)(2,1)S(1)}, bf16[512,512]{1,0:T(8,128)(2,1)S(1)}, u32[]{:S(2)}, u32[]{:S(2)}) collective-permute-start(bf16[512,512]{1,0:T(8,128)(2,1)S(1)} %broadcast_select_fusion), channel_id=1, source_target_pairs={{0,64},{32,96},{64,0},{96,32},{1,65},{33,97},{65,1},{97,33},{2,66}... | collective-permute-start | bytes 1572872 | tf_op jit(solution)/shard_map/ppermute | solution.py:26
  5.1 23.5 %collective-permute-start.1 = (bf16[512,512]{1,0:T(8,128)(2,1)S(1)}, bf16[512,512]{1,0:T(8,128)(2,1)S(1)}, u32[]{:S(2)}, u32[]{:S(2)}) collective-permute-start(bf16[512,512]{1,0:T(8,128)(2,1)S(1)} %broadcast_select_fusion), channel_id=1, source_target_pairs={{0,96},{32,0},{64,32},{96,64},{1,97},{33,1},{65,33},{97,65},{2,98}... | collective-permute-start | bytes 1572872 | tf_op jit(solution)/shard_map/ppermute | solution.py:26
  6.2 22.4 %collective-permute-start = (bf16[512,512]{1,0:T(8,128)(2,1)S(1)}, bf16[512,512]{1,0:T(8,128)(2,1)S(1)}, u32[]{:S(2)}, u32[]{:S(2)}) collective-permute-start(bf16[512,512]{1,0:T(8,128)(2,1)S(1)} %broadcast_select_fusion), channel_id=1, source_target_pairs={{0,32},{32,64},{64,96},{96,0},{1,33},{33,65},{65,97},{97,1},{2,34}... | collective-permute-start | bytes 1572872 | tf_op jit(solution)/shard_map/ppermute | solution.py:26
  27.9 4.2 %copy-start = (bf16[512,512]{1,0:T(8,128)(2,1)}, bf16[512,512]{1,0:T(8,128)(2,1)S(1)}, u32[]{:S(2)}) copy-start(bf16[512,512]{1,0:T(8,128)(2,1)S(1)} %collective-permute-done.2.rest_6_) | copy-start | bytes 1572868
  28.6 3.5 %copy-start.1 = (bf16[512,512]{1,0:T(8,128)(2,1)}, bf16[512,512]{1,0:T(8,128)(2,1)S(1)}, u32[]{:S(2)}) copy-start(bf16[512,512]{1,0:T(8,128)(2,1)S(1)} %collective-permute-done.1.rest_4_) | copy-start | bytes 1572868
  28.6 3.5 %copy-start.2 = (bf16[512,512]{1,0:T(8,128)(2,1)}, bf16[512,512]{1,0:T(8,128)(2,1)S(1)}, u32[]{:S(2)}) copy-start(bf16[512,512]{1,0:T(8,128)(2,1)S(1)} %collective-permute-done.rest_2_) | copy-start | bytes 1572868
  28.6 2.0 collective-permute-start.3
  28.7 2.6 %collective-permute-start.4 = (bf16[512,512]{1,0:T(8,128)(2,1)S(1)}, bf16[512,512]{1,0:T(8,128)(2,1)S(1)}, u32[]{:S(2)}, u32[]{:S(2)}) collective-permute-start(bf16[512,512]{1,0:T(8,128)(2,1)S(1)} %collective-permute-done.1.rest_4_), channel_id=1, source_target_pairs={{0,1},{1,0},{2,3},{3,2},{4,5},{5,4},{6,7},{7,6},{8,9},{9,8},{10,11... | collective-permute-start | bytes 1572872 | tf_op jit(solution)/shard_map/ppermute | solution.py:31
  29.2 2.9 %collective-permute-start.5 = (bf16[512,512]{1,0:T(8,128)(2,1)S(1)}, bf16[512,512]{1,0:T(8,128)(2,1)S(1)}, u32[]{:S(2)}, u32[]{:S(2)}) collective-permute-start(bf16[512,512]{1,0:T(8,128)(2,1)S(1)} %collective-permute-done.2.rest_6_), channel_id=1, source_target_pairs={{0,1},{1,0},{2,3},{3,2},{4,5},{5,4},{6,7},{7,6},{8,9},{9,8},{10,11... | collective-permute-start | bytes 1572872 | tf_op jit(solution)/shard_map/ppermute | solution.py:31
  30.6 1.5 copy-start.3
  31.4 0.8 copy-start.4
  32.1 0.8 copy-start.5
  72.1 8.5 %copy-start.8 = (bf16[512,172]{0,1:T(8,128)(2,1)S(1)}, bf16[512,172]{0,1:T(8,128)(2,1)}, u32[]{:S(2)}) copy-start(bf16[512,172]{0,1:T(8,128)(2,1)} %param.13) | copy-start | bytes 528388
  72.1 9.4 %copy-start.10 = (s32[4,256]{1,0:T(4,128)S(1)}, s32[4,256]{1,0:T(4,128)}, u32[]{:S(2)}) copy-start(s32[4,256]{1,0:T(4,128)} %param.14) | copy-start | bytes 12292
  76.7 5.8 %copy-start.11 = (s32[4,256]{1,0:T(4,128)S(1)}, s32[4,256]{1,0:T(4,128)}, u32[]{:S(2)}) copy-start(s32[4,256]{1,0:T(4,128)} %param.15) | copy-start | bytes 12292
  76.8 12.8 %all-to-all-start.3 = ((bf16[32,8,512]{2,1,0:T(8,128)(2,1)}), bf16[32,8,512]{2,1,0:T(8,128)(2,1)S(1)}, u32[]{:S(2)}, u32[]{:S(2)}) async-start(bf16[32,8,512]{2,1,0:T(8,128)(2,1)} %bitcast.65), calls=%async_computation.3 | async-start | bytes 524288 | tf_op jit(solution)/shard_map/all_to_all | solution.py:35
  98.6 4.2 %collective-permute-start.6 = (bf16[512,512]{1,0:T(8,128)(2,1)}, bf16[512,512]{1,0:T(8,128)(2,1)S(1)}, u32[]{:S(2)}, u32[]{:S(2)}) collective-permute-start(bf16[512,512]{1,0:T(8,128)(2,1)} %get-tuple-element.83), channel_id=1, source_target_pairs={{0,1},{1,0},{2,3},{3,2},{4,5},{5,4},{6,7},{7,6},{8,9},{9,8},{10,11... | collective-permute-start | bytes 1572872 | tf_op jit(solution)/shard_map/ppermute | solution.py:31
  99.0 12.8 %all-to-all-start.4 = ((bf16[32,8,512]{2,1,0:T(8,128)(2,1)}), bf16[32,8,512]{2,1,0:T(8,128)(2,1)S(1)}, u32[]{:S(2)}, u32[]{:S(2)}) async-start(bf16[32,8,512]{2,1,0:T(8,128)(2,1)} %get-tuple-element.77), calls=%async_computation.4 | async-start | bytes 524288 | tf_op jit(solution)/shard_map/all_to_all | solution.py:35
  117.3 7.4 %copy-start.7 = (bf16[4,256,512]{2,1,0:T(8,128)(2,1)S(1)}, bf16[4,256,512]{2,1,0:T(8,128)(2,1)}, u32[]{:S(2)}) copy-start(bf16[4,256,512]{2,1,0:T(8,128)(2,1)} %get-tuple-element.93.own_ref) | copy-start | bytes 3145732
  117.3 30.7 %all-to-all-start.5 = ((bf16[32,24,512]{2,1,0:T(8,128)(2,1)}), bf16[32,24,512]{2,1,0:T(8,128)(2,1)S(1)}, u32[]{:S(2)}, u32[]{:S(2)}) async-start(bf16[32,24,512]{2,1,0:T(8,128)(2,1)} %get-tuple-element.84), calls=%async_computation.5 | async-start | bytes 1572864 | tf_op jit(solution)/shard_map/all_to_all | solution.py:35
  124.6 20.9 %collective-permute-start.7 = (bf16[512,512]{1,0:T(8,128)(2,1)}, bf16[512,512]{1,0:T(8,128)(2,1)S(1)}, u32[]{:S(2)}, u32[]{:S(2)}) collective-permute-start(bf16[512,512]{1,0:T(8,128)(2,1)} %get-tuple-element.90), channel_id=1, source_target_pairs={{0,1},{1,0},{2,3},{3,2},{4,5},{5,4},{6,7},{7,6},{8,9},{9,8},{10,11... | collective-permute-start | bytes 1572872 | tf_op jit(solution)/shard_map/ppermute | solution.py:31
  124.8 14.4 %collective-permute-start.10 = (bf16[256,512]{1,0:T(8,128)(2,1)S(1)}, bf16[256,512]{1,0:T(8,128)(2,1)S(1)}, u32[]{:S(2)}, u32[]{:S(2)}) collective-permute-start(bf16[256,512]{1,0:T(8,128)(2,1)S(1)} %get-tuple-element.123), channel_id=1, source_target_pairs={{0,96},{32,0},{64,32},{96,64},{1,97},{33,1},{65,33},{97,65},{2,98}... | collective-permute-start | bytes 786440 | tf_op jit(solution)/shard_map/ppermute | solution.py:26
  127.5 11.7 %collective-permute-start.9 = (bf16[256,512]{1,0:T(8,128)(2,1)S(1)}, bf16[256,512]{1,0:T(8,128)(2,1)S(1)}, u32[]{:S(2)}, u32[]{:S(2)}) collective-permute-start(bf16[256,512]{1,0:T(8,128)(2,1)S(1)} %get-tuple-element.124), channel_id=1, source_target_pairs={{0,64},{32,96},{64,0},{96,32},{1,65},{33,97},{65,1},{97,33},{2,66}... | collective-permute-start | bytes 786440 | tf_op jit(solution)/shard_map/ppermute | solution.py:26
  128.3 14.7 %collective-permute-start.8 = (bf16[256,512]{1,0:T(8,128)(2,1)S(1)}, bf16[256,512]{1,0:T(8,128)(2,1)S(1)}, u32[]{:S(2)}, u32[]{:S(2)}) collective-permute-start(bf16[256,512]{1,0:T(8,128)(2,1)S(1)} %get-tuple-element.125), channel_id=1, source_target_pairs={{0,32},{32,64},{64,96},{96,0},{1,33},{33,65},{65,97},{97,1},{2,34}... | collective-permute-start | bytes 786440 | tf_op jit(solution)/shard_map/ppermute | solution.py:26
  153.6 21.2 %all-to-all-start.6 = ((bf16[32,24,512]{2,1,0:T(8,128)(2,1)}), bf16[32,24,512]{2,1,0:T(8,128)(2,1)S(1)}, u32[]{:S(2)}, u32[]{:S(2)}) async-start(bf16[32,24,512]{2,1,0:T(8,128)(2,1)} %get-tuple-element.96), calls=%async_computation.6 | async-start | bytes 1572864 | tf_op jit(solution)/shard_map/all_to_all | solution.py:35
  164.2 2.1 collective-permute-start.11
  183.6 2.4 collective-permute-start.12
  188.6 23.9 %all-to-all-start.7 = ((bf16[32,40,512]{2,1,0:T(8,128)(2,1)}), bf16[32,40,512]{2,1,0:T(8,128)(2,1)S(1)}, u32[]{:S(2)}, u32[]{:S(2)}) async-start(bf16[32,40,512]{2,1,0:T(8,128)(2,1)} %carry_partials.7), calls=%async_computation.7 | async-start | bytes 2621440 | tf_op jit(solution)/shard_map/all_to_all | solution.py:35
  215.2 13.7 %copy-start.6 = (bf16[4,256,512]{2,1,0:T(8,128)(2,1)S(1)}, bf16[4,256,512]{2,1,0:T(8,128)(2,1)}, u32[]{:S(2)}) copy-start(bf16[4,256,512]{2,1,0:T(8,128)(2,1)} %get-tuple-element.112.own_ref) | copy-start | bytes 3145732
  216.1 4.0 %collective-permute-start.15 = (bf16[2,16,512]{2,1,0:T(8,128)(2,1)S(1)}, bf16[2,16,512]{2,1,0:T(8,128)(2,1)S(1)}, u32[]{:S(2)}, u32[]{:S(2)}) collective-permute-start(bf16[2,16,512]{2,1,0:T(8,128)(2,1)S(1)} %get-tuple-element.126), channel_id=1, source_target_pairs={{0,96},{32,0},{64,32},{96,64},{1,97},{33,1},{65,33},{97,65},{2,98}... | collective-permute-start | bytes 98312 | tf_op jit(solution)/shard_map/ppermute | solution.py:26
  216.8 5.4 %collective-permute-start.14 = (bf16[2,16,512]{2,1,0:T(8,128)(2,1)S(1)}, bf16[2,16,512]{2,1,0:T(8,128)(2,1)S(1)}, u32[]{:S(2)}, u32[]{:S(2)}) collective-permute-start(bf16[2,16,512]{2,1,0:T(8,128)(2,1)S(1)} %get-tuple-element.127), channel_id=1, source_target_pairs={{0,64},{32,96},{64,0},{96,32},{1,65},{33,97},{65,1},{97,33},{2,66}... | collective-permute-start | bytes 98312 | tf_op jit(solution)/shard_map/ppermute | solution.py:26
  217.5 5.2 %collective-permute-start.13 = (bf16[2,16,512]{2,1,0:T(8,128)(2,1)S(1)}, bf16[2,16,512]{2,1,0:T(8,128)(2,1)S(1)}, u32[]{:S(2)}, u32[]{:S(2)}) collective-permute-start(bf16[2,16,512]{2,1,0:T(8,128)(2,1)S(1)} %get-tuple-element.128), channel_id=1, source_target_pairs={{0,32},{32,64},{64,96},{96,0},{1,33},{33,65},{65,97},{97,1},{2,34}... | collective-permute-start | bytes 98312 | tf_op jit(solution)/shard_map/ppermute | solution.py:26
  225.0 21.3 %all-to-all-start.8 = ((bf16[32,16,512]{2,1,0:T(8,128)(2,1)}), bf16[32,16,512]{2,1,0:T(8,128)(2,1)S(1)}, u32[]{:S(2)}, u32[]{:S(2)}) async-start(bf16[32,16,512]{2,1,0:T(8,128)(2,1)} %sum_over_layer.1), calls=%async_computation.8 | async-start | bytes 1048576 | tf_op jit(solution)/shard_map/all_to_all | solution.py:35
  229.0 13.6 %collective-permute-start.18 = (bf16[256,512]{1,0:T(8,128)(2,1)S(1)}, bf16[256,512]{1,0:T(8,128)(2,1)S(1)}, u32[]{:S(2)}, u32[]{:S(2)}) collective-permute-start(bf16[256,512]{1,0:T(8,128)(2,1)S(1)} %get-tuple-element.120), channel_id=1, source_target_pairs={{0,96},{32,0},{64,32},{96,64},{1,97},{33,1},{65,33},{97,65},{2,98}... | collective-permute-start | bytes 786440 | tf_op jit(solution)/shard_map/ppermute | solution.py:26
  231.1 11.5 %collective-permute-start.17 = (bf16[256,512]{1,0:T(8,128)(2,1)S(1)}, bf16[256,512]{1,0:T(8,128)(2,1)S(1)}, u32[]{:S(2)}, u32[]{:S(2)}) collective-permute-start(bf16[256,512]{1,0:T(8,128)(2,1)S(1)} %get-tuple-element.121), channel_id=1, source_target_pairs={{0,64},{32,96},{64,0},{96,32},{1,65},{33,97},{65,1},{97,33},{2,66}... | collective-permute-start | bytes 786440 | tf_op jit(solution)/shard_map/ppermute | solution.py:26
  232.0 14.3 %collective-permute-start.16 = (bf16[256,512]{1,0:T(8,128)(2,1)S(1)}, bf16[256,512]{1,0:T(8,128)(2,1)S(1)}, u32[]{:S(2)}, u32[]{:S(2)}) collective-permute-start(bf16[256,512]{1,0:T(8,128)(2,1)S(1)} %get-tuple-element.122), channel_id=1, source_target_pairs={{0,32},{32,64},{64,96},{96,0},{1,33},{33,65},{65,97},{97,1},{2,34}... | collective-permute-start | bytes 786440 | tf_op jit(solution)/shard_map/ppermute | solution.py:26
  246.3 2.6 %collective-permute-start.19 = (bf16[512,512]{1,0:T(8,128)(2,1)S(1)}, bf16[512,512]{1,0:T(8,128)(2,1)S(1)}, u32[]{:S(2)}, u32[]{:S(2)}) collective-permute-start(bf16[512,512]{1,0:T(8,128)(2,1)S(1)} %bitcast.37), channel_id=1, source_target_pairs={{0,1},{1,0},{2,3},{3,2},{4,5},{5,4},{6,7},{7,6},{8,9},{9,8},{10,11... | collective-permute-start | bytes 1572872 | tf_op jit(solution)/shard_map/ppermute | solution.py:31

commit v3 on v2

v3 whole, which is shorter than its diff:
```python
import functools

import jax
import jax.numpy as jnp
from jax import lax
from jax.experimental import pallas as pl
from jax.experimental.pallas import tpu as pltpu
from jax.sharding import PartitionSpec as P

BF = jnp.bfloat16
F32 = jnp.float32
NN = (((1,), (0,)), ((), ()))
NT = (((1,), (1,)), ((), ()))
TN = (((0,), (0,)), ((), ()))
FAR = pl.BlockSpec(memory_space=pltpu.HBM)
LOCAL = pl.BlockSpec(memory_space=pltpu.VMEM)
VMEM_BYTES = 16 * 1024 * 1024


def dot(a, b, dims=NN):
    return lax.dot_general(a, b, dims, preferred_element_type=F32)


def shift(value, axis, steps):
    count = lax.axis_size(axis)
    return lax.ppermute(value, axis, [(i, (i + steps) % count) for i in range(count)])


def sibling(value):
    count = lax.axis_size("node")
    return lax.ppermute(value, "node", [(i, i ^ 1) for i in range(count)])


def exchange(value):
    return lax.all_to_all(value, "node", split_axis=0, concat_axis=0, tiled=True)


def of_span(shape):
    return pl.BlockSpec((None, *shape), lambda i, ids, cols: (ids[0], *((0,) * len(shape))))


def whole(shape):
    return pl.BlockSpec(shape, lambda i, ids, cols: (0,) * len(shape))


def near(shape, dtype=BF):
    return pltpu.VMEM(shape, dtype), LOCAL


def far_block(shape, dtype=BF):
    return pltpu.HBM(shape, dtype), whole(shape)


def run(kernel, name, scalars, ins, outs, scratch=(), aliases=None, flops=0, moved=0):
    ins = [v if isinstance(v, tuple) else (v, LOCAL) for v in ins]
    arrays = [
        pltpu.with_memory_space_constraint(a, pltpu.VMEM if s is LOCAL else pltpu.HBM)
        for a, s in ins
    ]
    return pl.pallas_call(
        kernel,
        name=name,
        grid_spec=pltpu.PrefetchScalarGridSpec(
            num_scalar_prefetch=2,
            grid=(1,),
            in_specs=[s for _, s in ins],
            out_specs=[s for _, s in outs],
            scratch_shapes=list(scratch),
        ),
        out_shape=[o for o, _ in outs],
        input_output_aliases={} if aliases is None else {k + 2: v for k, v in aliases.items()},
        compiler_params=pltpu.CompilerParams(vmem_limit_bytes=VMEM_BYTES),
        cost_estimate=pl.CostEstimate(flops=flops, bytes_accessed=moved, transcendentals=0),
    )(*scalars, *arrays)


def tie(*values):
    return lax.optimization_barrier(values)


def weight_copies(layer, ids, w_refs, w_scr, sems, act):
    own_s, own_n, left, left_x, right, right_x, far, far_x = w_refs
    core = ids[1]
    pairs = [
        [(own_s, 0), (own_n, 1)],
        [(right, core), (right_x, 1 - core)],
        [(far, core), (far_x, 1 - core)],
        [(left, core), (left_x, 1 - core)],
    ]
    which = lax.rem(layer - ids[0] + 4, 4)
    for option, pair in enumerate(pairs):

        @pl.when(which == option)
        def _():
            for n, (ref, place) in enumerate(pair):
                act(pltpu.make_async_copy(ref, w_scr.at[place], sems.at[n]))


def start_weights(*args):
    weight_copies(*args, lambda copy: copy.start())


def wait_weights(*args):
    weight_copies(*args, lambda copy: copy.wait())


def side_by_side(vals_ref, r, degree):
    return jnp.concatenate([vals_ref[r, j] for j in range(degree)], axis=1)


def aggregate_rows(ids, cols, vals_ref, ext):
    tiles, degree, size = vals_ref.shape[0], vals_ref.shape[1], vals_ref.shape[2]
    parts = []
    for r in range(tiles):
        picked = jnp.concatenate(
            [ext[pl.ds(pl.multiple_of(cols[ids[0], r, j] * size, size), size), :] for j in range(degree)],
            axis=0,
        )
        parts.append(dot(side_by_side(vals_ref, r, degree), picked))
    return jnp.concatenate(parts, axis=0).astype(BF)


def spread_rows(ids, cols, vals_ref, d_agg, d_ext):
    tiles, degree, size = vals_ref.shape[0], vals_ref.shape[1], vals_ref.shape[2]
    d_ext[...] = jnp.zeros_like(d_ext)
    for r in range(tiles):
        pieces = dot(side_by_side(vals_ref, r, degree), d_agg[r * size : (r + 1) * size], TN)
        for j in range(degree):
            rows = pl.ds(pl.multiple_of(cols[ids[0], r, j] * size, size), size)
            d_ext[rows, :] += pieces[j * size : (j + 1) * size]


def to_slot(value_ref, layer, ids, buf_ref, sem):
    return pltpu.make_async_copy(value_ref, buf_ref.at[lax.rem(layer - ids[0] + 4, 4)], sem)


def sigmoid(v):
    return 1.0 / (1.0 + jnp.exp(-v))


def pre_kernel(ids, cols, h_ref, rows_ref, counts_ref, vals_ref, pick_ref, out_ref, h_out, vals_out, pick_far):
    slots, peers = rows_ref.shape
    total, node_rows = pick_ref.shape
    bits = slots.bit_length() - 1
    slot = lax.broadcasted_iota(jnp.int32, (total, peers), 0)
    owner = lax.broadcasted_iota(jnp.int32, (total, peers), 1)
    mine = lax.shift_right_logical(slot, bits) == owner
    wide = dot(mine.astype(F32).astype(BF), rows_ref[...].astype(F32).astype(BF), NT)
    slot_k = lax.broadcasted_iota(jnp.int32, (total, slots), 0) & (slots - 1)
    in_slot = slot_k == lax.broadcasted_iota(jnp.int32, (total, slots), 1)
    row = jnp.sum(jnp.where(in_slot, wide, 0.0), axis=1, keepdims=True)
    counts = jnp.broadcast_to(counts_ref[...].astype(F32), (total, peers))
    count = jnp.sum(jnp.where(mine, counts, 0.0), axis=1, keepdims=True)
    k = (lax.broadcasted_iota(jnp.int32, (total, 1), 0) & (slots - 1)).astype(F32)
    row = jnp.where(k < count, row, -1.0)
    place = lax.broadcasted_iota(jnp.int32, (total, node_rows), 1).astype(F32)
    pick = (place == row).astype(F32).astype(BF)
    pick_ref[...] = pick
    pick_far[...] = pick
    out_ref[...] = dot(pick, h_ref[...]).astype(BF)
    h_out[...] = h_ref[...]
    vals_out[...] = vals_ref[...]


def forward_math(layer, ids, cols, h_ref, arr_ref, vals_ref, w_refs, w_ref, sems, ext):
    start_weights(layer, ids, w_refs, w_ref, sems)
    rows = h_ref.shape[0]
    ext[0:rows, :] = h_ref[...]
    ext[rows : 2 * rows, :] = arr_ref[...]
    agg = aggregate_rows(ids, cols, vals_ref, ext)
    wait_weights(layer, ids, w_refs, w_ref, sems)
    pre = dot(h_ref[...], w_ref[0]) + dot(agg, w_ref[1])
    sig = sigmoid(pre)
    return agg, pre, sig, (pre * sig).astype(BF)


def forward_kernel(layer, ids, cols, h_ref, arr_ref, vals_ref, pick_ref, *rest):
    w_refs, rest = rest[:8], rest[-9:]
    agg_ref, pre_ref, hid_ref, out_ref, w_ref, buf_ref, ext, sems, buf_sem = rest
    agg, pre, _, hid = forward_math(
        layer, ids, cols, h_ref, arr_ref, vals_ref, w_refs, w_ref, sems, ext
    )
    hid_ref[...] = hid
    copy = to_slot(hid_ref, layer, ids, buf_ref, buf_sem)
    copy.start()
    out_ref[...] = dot(pick_ref[...], hid).astype(BF)
    agg_ref[...] = agg
    pre_ref[...] = pre
    copy.wait()


def backward_math(ids, cols, d_pre, vals_ref, w_ref, d_ext):
    d_agg = dot(d_pre, w_ref[1], NT).astype(BF)
    spread_rows(ids, cols, vals_ref, d_agg, d_ext)
    return dot(d_pre, w_ref[0], NT)


def weight_partials(ids, h_ref, agg, d_pre, keep_ref, send_ref):
    on_rows = dot(h_ref[...], d_pre, TN).astype(BF)
    on_agg = dot(agg, d_pre, TN).astype(BF)

    @pl.when(ids[1] == 0)
    def _():
        keep_ref[...] = on_rows
        send_ref[...] = on_agg

    @pl.when(ids[1] != 0)
    def _():
        keep_ref[...] = on_agg
        send_ref[...] = on_rows


def top_kernel(layer, ids, cols, h_ref, arr_ref, vals_ref, wout_ref, lab_ref, mask_ref, *rest):
    w_refs, rest = rest[:8], rest[9:]
    remote_ref, part_ref, keep_ref, send_ref, buf_ref, hid_ref, w_ref, ext, d_ext, sems, buf_sem = rest
    rows = h_ref.shape[0]
    agg, pre, sig, hid = forward_math(
        layer, ids, cols, h_ref, arr_ref, vals_ref, w_refs, w_ref, sems, ext
    )
    hid_ref[...] = hid
    copy = to_slot(hid_ref, layer, ids, buf_ref, buf_sem)
    copy.start()
    logits = dot(wout_ref[...], hid, NT)
    expo = jnp.exp(logits)
    probs = expo / jnp.sum(expo, axis=0, keepdims=True)
    label = lab_ref[pl.ds(ids[0], 1), :]
    onehot = (label == lax.broadcasted_iota(jnp.int32, logits.shape, 0)).astype(F32)
    live = mask_ref[pl.ds(ids[0], 1), :].astype(F32)
    g_logits = (live * (probs - onehot)).astype(BF)
    d_out = dot(g_logits, wout_ref[...], TN).astype(BF)
    d_pre = (d_out.astype(F32) * (sig * (1.0 + pre * (1.0 - sig)))).astype(BF)
    back = backward_math(ids, cols, d_pre, vals_ref, w_ref, d_ext)
    remote_ref[...] = d_ext[rows : 2 * rows, :].astype(BF).reshape(remote_ref.shape)
    part_ref[...] = back + d_ext[0:rows, :]
    weight_partials(ids, h_ref, agg, d_pre, keep_ref, send_ref)
    copy.wait()


def chunk_sum(block):
    total = block[0:2].astype(F32)
    for n in range(2, block.shape[0], 2):
        total = total + block[n : n + 2].astype(F32)
    return total


def backward_kernel(layer, carry, ids, cols, ret_ref, part_in, pre_ref, h_ref, agg_ref, *rest):
    (vals_ref, pick_ref, w_ref), rest = rest[:3], rest[3:]
    if carry:
        keep_in, recv_in, rest = rest[0], rest[1], rest[2:]
    if layer < 2:
        rest = rest[1:]
    out_ref, part_ref, buf_ref, keep_ref, send_ref, *rest = rest
    *chunk, dout_ref, d_ext, buf_sem = rest
    rows, feat = part_in.shape
    peers = out_ref.shape[0]
    slots = rows // peers
    returned = ret_ref[:, 0:slots, :].reshape(rows, feat)
    d_out = (part_in[...] + dot(pick_ref[...], returned, TN)).astype(BF)
    dout_ref[...] = d_out
    copy = to_slot(dout_ref, layer + 1, ids, buf_ref, buf_sem)
    copy.start()
    pre = pre_ref[...]
    sig = sigmoid(pre)
    d_pre = (d_out.astype(F32) * (sig * (1.0 + pre * (1.0 - sig)))).astype(BF)
    back = backward_math(ids, cols, d_pre, vals_ref, w_ref, d_ext)
    out_ref[:, 0:slots, :] = d_ext[rows : 2 * rows, :].astype(BF).reshape(peers, slots, feat)
    part_ref[...] = back + d_ext[0:rows, :]
    weight_partials(ids, h_ref, agg_ref[...], d_pre, keep_ref, send_ref)
    if carry:
        put_carry(keep_in, recv_in, out_ref, slots)
    if chunk:
        chunk[0][...] = chunk_sum(ret_ref[:, slots:, :]).astype(BF)
    copy.wait()


def put_carry(keep_ref, recv_ref, out_ref, first):
    peers, feat = out_ref.shape[0], out_ref.shape[2]
    size = keep_ref.shape[0] // peers
    total = (keep_ref[...].astype(F32) + recv_ref[...].astype(F32)).astype(BF)
    out_ref[:, first : first + size, :] = total.reshape(peers, size, feat)


def join_kernel(ids, cols, keep_a, recv_a, keep_b, recv_b, buf_in, out_ref):
    size = keep_a.shape[0] // out_ref.shape[0]
    first = out_ref.shape[1] - 2 * size
    put_carry(keep_a, recv_a, out_ref, first)
    put_carry(keep_b, recv_b, out_ref, first + size)


def end_kernel(ids, cols, ret_ref, part_in, pick_ref, c_3, dout_ref, o_0, o_1, o_2, o_3, all_sums):
    rows, feat = part_in.shape
    slots = rows // ret_ref.shape[0]
    size = c_3.shape[1]
    all_sums[3] = c_3[...]
    for n, layer in enumerate((2, 1, 0)):
        first = slots + n * size
        all_sums[layer] = chunk_sum(ret_ref[:, first : first + size, :]).astype(BF)
    for s, out_ref in enumerate((o_0, o_1, o_2, o_3)):
        out_ref[...] = all_sums[lax.rem(ids[0] + s, 4)]
    returned = ret_ref[:, 0:slots, :].reshape(rows, feat)
    dout_ref[...] = (part_in[...] + dot(pick_ref[...], returned, TN)).astype(BF)


def layer_sum_kernel(ids, cols, own_ref, a_ref, b_ref, c_ref, out_ref):
    total = own_ref[...].astype(F32) + a_ref[...].astype(F32)
    total = (total + b_ref[...].astype(F32) + c_ref[...].astype(F32)).astype(BF)
    for n in range(0, out_ref.shape[0], 2):
        out_ref[n : n + 2] = total


def scale_kernel(scale, ids, cols, mine_ref, other_ref, self_ref, neigh_ref):
    mine = mine_ref[...].astype(F32) * scale
    other = other_ref[...].astype(F32) * scale

    @pl.when(ids[1] == 0)
    def _():
        self_ref[0] = mine
        neigh_ref[0] = other

    @pl.when(ids[1] != 0)
    def _():
        self_ref[0] = other
        neigh_ref[0] = mine


def home_kernel(ids, cols, *refs):
    pieces, out_ref = refs[:-1], refs[-1]
    home = ids[0]
    for s, piece in enumerate(pieces[:4]):
        out_ref[0, lax.rem(home + 4 - s, 4)] = piece[...]
    if len(pieces) > 4:

        @pl.when(home == 0)
        def _():
            for s, piece in enumerate(pieces[4:]):
                out_ref[0, lax.rem(4 - s, 4)] = piece[...]


def body(
    features,
    w_self,
    w_neigh,
    w_out,
    labels,
    train_mask,
    tile_cols,
    tile_vals,
    send_rows,
    send_counts,
):
    home = lax.axis_index("layer")
    node = lax.axis_index("node")
    core = lax.rem(node, 2)
    spans, rows, feat = features.shape
    peers, slots = send_rows.shape[2], send_rows.shape[3]
    tiles, degree, size = tile_vals.shape[2], tile_vals.shape[3], tile_vals.shape[4]
    scale = 1.0 / (spans * rows * peers)
    scalars = (jnp.stack([home, core]).astype(jnp.int32), tile_cols.reshape(spans, tiles, degree))
    act, wide, square = near((rows, feat)), near((rows, feat), F32), near((feat, feat))
    ext_scratch = pltpu.VMEM((2 * rows, feat), BF)
    d_ext_scratch = pltpu.VMEM((2 * rows, feat), F32)
    all_shifts = range(1, spans)

    mine = jnp.where(core == 0, w_self[0], w_neigh[0])
    left, right, far = (shift(mine, "layer", s) for s in (1, -1, 2))
    pick, outgoing, features_0, vals, pick_far = run(
        pre_kernel,
        "gather_rows",
        scalars,
        [
            (features, of_span((rows, feat))),
            (send_rows.reshape(spans, peers, slots).swapaxes(1, 2), of_span((slots, peers))),
            (send_counts.reshape(spans, 1, peers), of_span((1, peers))),
            (
                tile_vals.reshape(spans, tiles, degree, size, size),
                of_span((tiles, degree, size, size)),
            ),
        ],
        [
            near((peers * slots, rows)),
            act,
            act,
            near((tiles, degree, size, size)),
            far_block((peers * slots, rows)),
        ],
        flops=10**8,
        moved=10**6,
    )
    arrived = exchange(outgoing.reshape(peers, slots, feat))
    arrived, left, right, far = tie(arrived, left, right, far)
    sources = [(w_self[0], FAR), (w_neigh[0], FAR), left, sibling(left), right, sibling(right)]
    sources += [far, sibling(far)]
    w_scratch = [pltpu.SemaphoreType.DMA((2,))]
    weight = near((2, feat, feat))

    hidden, aggs, pres, weights = [features_0], [], [], []
    top = spans - 1
    stack = (pltpu.HBM((spans, rows, feat), BF), FAR)
    buf_sem = pltpu.SemaphoreType.DMA
    acts_buf = None
    for layer in range(top):
        ins = [hidden[layer], arrived.reshape(rows, feat), vals, pick, *sources]
        if layer:
            ins.append((acts_buf, FAR))
        agg, pre, hid, outgoing, arranged, acts_buf = run(
            functools.partial(forward_kernel, layer),
            f"layer_forward_{layer}",
            scalars,
            ins,
            [act, wide, act, act, weight, stack],
            [ext_scratch, *w_scratch, buf_sem],
            {len(ins) - 1: 5} if layer else None,
            flops=6 * 10**8,
            moved=4 * 10**6,
        )
        hidden.append(hid)
        aggs.append(agg)
        pres.append(pre)
        weights.append(arranged)
        arrived = exchange(outgoing.reshape(peers, slots, feat))

    ins = [
        hidden[top],
        arrived.reshape(rows, feat),
        vals,
        w_out.T,
        labels,
        train_mask,
        *sources,
        (acts_buf, FAR),
    ]
    remote, part, keep, send, acts_buf = run(
        functools.partial(top_kernel, top),
        "top_layer",
        scalars,
        ins,
        [near((peers, slots, feat)), wide, square, square, stack],
        [
            pltpu.VMEM((rows, feat), BF),
            pltpu.VMEM((2, feat, feat), BF),
            ext_scratch,
            d_ext_scratch,
            *w_scratch,
            buf_sem,
        ],
        {len(ins) - 1: 4},
        flops=10**9,
        moved=5 * 10**6,
    )

    def travel(buf, home_too=True):
        pieces = []
        for s in all_shifts:
            pairs = [(i, (i + s) % spans) for i in range(spans) if home_too or (i + s) % spans]
            pieces.append(lax.ppermute(buf[s], "layer", pairs))
        return pieces

    def put_home(buf, *pieces):
        block = pl.BlockSpec((None, rows, feat), lambda i, ids, cols: (0, 0, 0))
        shape = (1, spans, rows, feat)
        return run(
            home_kernel,
            "put_home",
            scalars,
            [(buf, block), *pieces],
            [far_block(shape)],
            moved=2 * 10**6,
        )[0]

    chunk_rows = feat // peers
    chunk = near((2, chunk_rows, feat))
    pairs, grads_buf = [], None
    for layer in range(top - 1, -1, -1):
        returned, send = tie(exchange(remote), send)
        pairs.append((keep, sibling(send)))
        carry = layer < top - 1
        width = slots + chunk_rows * (carry + 2 * (layer == 0))
        ins = [
            returned,
            part,
            pres[layer],
            hidden[layer],
            aggs[layer],
            vals,
            pick,
            weights[layer],
        ]
        if carry:
            ins += pairs[-2]
        aliases = None
        if grads_buf is not None:
            ins.append((grads_buf, FAR))
            aliases = {len(ins) - 1: 2}
        last = far_block if layer == 0 else near
        outs = [near((peers, width, feat)), last((rows, feat), F32), stack, square, square]
        if layer == 0:
            outs.append(far_block((2, chunk_rows, feat)))
        remote, part, grads_buf, keep, send, *c_3 = run(
            functools.partial(backward_kernel, layer, carry),
            f"layer_backward_{layer}",
            scalars,
            ins,
            outs,
            [pltpu.VMEM((rows, feat), BF), d_ext_scratch, buf_sem],
            aliases,
            flops=10**9,
            moved=5 * 10**6,
        )
        if layer:
            remote, recv = tie(remote, pairs[-1][1])
            pairs[-1] = (pairs[-1][0], recv)

    joined = run(
        join_kernel,
        "join_rows",
        scalars,
        [*pairs[-1], keep, sibling(send), remote],
        [near((peers, slots + 3 * chunk_rows, feat))],
        aliases={4: 0},
        moved=3 * 10**6,
    )[0]
    joined, acts_buf, grads_buf = tie(joined, acts_buf, grads_buf)
    acts = travel(acts_buf)
    early = travel(grads_buf, False)
    returned, *pieces = tie(exchange(joined), *acts, *early)
    acts, early = pieces[:3], pieces[3:]
    layer_acts = put_home(acts_buf, *acts)
    d_out, own_sum, *sums = run(
        end_kernel,
        "input_grads",
        scalars,
        [
            returned,
            (part, whole((rows, feat))),
            (pick_far, whole(pick_far.shape)),
            (c_3[0], whole(c_3[0].shape)),
        ],
        [far_block((rows, feat)), chunk, chunk, chunk, chunk],
        [pltpu.VMEM((spans, 2, chunk_rows, feat), BF)],
        flops=10**8,
        moved=3 * 10**6,
    )
    spread = run(
        layer_sum_kernel,
        "sum_over_layer",
        scalars,
        [own_sum, *[shift(v, "layer", s) for s, v in zip(all_shifts, sums)]],
        [near((peers, chunk_rows, feat))],
        moved=10**6,
    )[0]
    late = [lax.ppermute(d_out, "layer", [(spans - s, 0)]) for s in all_shifts]
    gathered, layer_acts, *late = tie(exchange(spread), layer_acts, *late)
    gathered = gathered.reshape(feat, feat)
    other = sibling(gathered)
    act_grads = put_home(grads_buf, *early, (d_out, whole((rows, feat))), *late)
    out_square = (1, feat, feat)
    grad_self, grad_neigh = run(
        functools.partial(scale_kernel, scale),
        "scale_grads",
        scalars,
        [gathered, other],
        [(pltpu.HBM(out_square, F32), whole(out_square))] * 2,
        moved=3 * 10**6,
    )
    return (layer_acts, act_grads, grad_self, grad_neigh)


def solution(mesh):
    in_specs = (
        P(None, "node", None),
        P("layer", None, None),
        P("layer", None, None),
        P(),
        P(None, "node"),
        P(None, "node"),
        P(None, "node", None, None),
        P(None, "node", None, None, None, None),
        P(None, "node", None, None),
        P(None, "node", None),
    )
    out_specs = (
        P("layer", None, "node", None),
        P("layer", None, "node", None),
        P("layer", None, None),
        P("layer", None, None),
    )
    return jax.shard_map(body, mesh=mesh, in_specs=in_specs, out_specs=out_specs, check_vma=False)
```

time: 254 us -> 221 us (0.87)
  blocking collectives: 47.4 us -> 101 us
  Pallas kernels: 76.6 us -> 34.5 us
  waiting for transfers between devices: 75.5 us -> 35.1 us
  local copies, waits for them, and re-layouts: 5.5 us -> 2.09 us
    all_to_all x3 -> x7, blocking collectives: 47.4 us -> 101 us  [exchange(): lax.all_to_all(value, 'node', split_axis=0, concat_axis=0, tiled=True)]
    pallas_call x23 -> x14, Pallas kernels: 76.6 us -> 34.5 us  [run(): pl.pallas_call(kernel, name=name, grid_spec=pltpu.PrefetchScalarGridSpec(...]
    all_to_all x6 -> x2, waiting for transfers between devices: 35.8 us -> 0.01 us  [exchange(): lax.all_to_all(value, 'node', split_axis=0, concat_axis=0, tiled=True)]
    ppermute x12 -> x6, waiting for transfers between devices: 33.2 us -> 4.78 us  [shift(): lax.ppermute(value, axis, [(i, (i + steps) % count) for i in range(count)])]
    ppermute x0 -> x9, waiting for transfers between devices: none -> 25.2 us  [the longest x6 12.7 us: travel(): pieces.append(lax.ppermute(buf[s], 'layer', pairs))]
    ppermute x0 -> x9, starting transfers between devices: none -> 17.2 us  [the longest x6 13.4 us: travel(): pieces.append(lax.ppermute(buf[s], 'layer', pairs))]
    all_to_all x6 -> x2, starting transfers between devices: 27.1 us -> 11.4 us  [exchange(): lax.all_to_all(value, 'node', split_axis=0, concat_axis=0, tiled=True)]
    ppermute x12 -> x6, starting transfers between devices: 14.7 us -> 13.7 us  [shift(): lax.ppermute(value, axis, [(i, (i + steps) % count) for i in range(count)])]
  transfers between devices with their start and end apart: 26 -> 25, of which waited for: 17 -> 15; matrix products, arithmetic and copies ran while one was open for 2% -> 0% of each run, Pallas kernels for 10% -> 6%
where the time goes in v3:
time: 221 us; the launch traced here: 219 us
  blocking collectives  101 us (46%)
  starting transfers between devices  44.3 us (20%)
  waiting for transfers between devices  35.1 us (16%)
  Pallas kernels  34.5 us (16%)
    all_to_all x7, blocking collectives, exchange(): lax.all_to_all(value, 'node', split_axis=0, concat_axis=0, tiled=True)  101 us
    pallas_call x14, Pallas kernels, run(): pl.pallas_call(kernel, name=name, grid_spec=pltpu.PrefetchScalarGridSpec(...  34.5 us
    ppermute x6, starting transfers between devices, shift(): lax.ppermute(value, axis, [(i, (i + steps) % count) for i in range(count)])  13.7 us
    ppermute x6, starting transfers between devices, travel(): pieces.append(lax.ppermute(buf[s], 'layer', pairs))  13.4 us
    ppermute x6, waiting for transfers between devices, travel(): pieces.append(lax.ppermute(buf[s], 'layer', pairs))  12.7 us
    ppermute x3, waiting for transfers between devices, body(): late = [lax.ppermute(d_out, 'layer', [(spans - s, 0)]) for s in all_shifts]  12.5 us
    all_to_all x2, starting transfers between devices, exchange(): lax.all_to_all(value, 'node', split_axis=0, concat_axis=0, tiled=True)  11.4 us
    ppermute x8, waiting for transfers between devices, sibling(): return lax.ppermute(value, 'node', [(i, i ^ 1) for i in range(count)])  5.1 us
  transfers between devices with their start and end apart: 25, of which 15 were waited for; matrix products, arithmetic and copies ran while one was open for 0% of the time, Pallas kernels for 6%

profile of v3, /device:TPU:0, one launch (start us, length us, event | category | flops | bytes accessed | tf_op | source)
XLA Modules:
  0.0 219.2 jit_solution(17605458677824947804)
XLA Ops:
  0.6 1.3 broadcast_select_fusion
  1.9 3.2 %collective-permute-start.2 = (bf16[512,512]{1,0:T(8,128)(2,1)S(1)}, bf16[512,512]{1,0:T(8,128)(2,1)S(1)}, u32[]{:S(2)}, u32[]{:S(2)}) collective-permute-start(bf16[512,512]{1,0:T(8,128)(2,1)S(1)} %broadcast_select_fusion), channel_id=1, source_target_pairs={{0,64},{32,96},{64,0},{96,32},{1,65},{33,97},{65,1},{97,33},{2,66}... | collective-permute-start | bytes 1572872 | tf_op jit(solution)/shard_map/ppermute | solution.py:26
  5.1 1.1 collective-permute-start.1
  6.2 0.9 collective-permute-start
  7.9 2.6 %gather_rows.1 = (bf16[256,256]{1,0:T(8,128)(2,1)S(1)}, bf16[256,512]{1,0:T(8,128)(2,1)S(1)}, bf16[256,512]{1,0:T(8,128)(2,1)S(1)}, bf16[2,4,128,128]{3,2,1,0:T(8,128)(2,1)S(1)}, bf16[256,256]{1,0:T(8,128)(2,1)}) custom-call(s32[2]{0:T(128)S(1)} %pad_add_fusion.ids, s32[4,2,4]{2,1,0:T(2,128)S(1)} %bitcast.39, bf16[4,256,512]{2,1,0:T(8,128)(2,1)} %h_ref.1, ...), custom_call_target="tpu_custom_call" | custom-call | flops 100000000 | bytes 1000000 | tf_op jit(solution)/shard_map/gather_rows/pallas_call | solution.py:60
  10.5 17.1 %all_to_all.45 = bf16[32,8,512]{2,1,0:T(8,128)(2,1)S(1)} all-to-all(bf16[32,8,512]{2,1,0:T(8,128)(2,1)S(1)} %bitcast.56), channel_id=1, replica_groups=mesh['layer'=4,'node'=32] {'node'}, dimensions={0} | all-to-all | bytes 524288 | tf_op jit(solution)/shard_map/all_to_all | solution.py:35
  27.6 1.0 collective-permute-done.1.rest_4_
  29.1 1.4 collective-permute-done.3.rest_3_
  32.0 3.1 %layer_forward_0.1 = (bf16[256,512]{1,0:T(8,128)(2,1)S(1)}, f32[256,512]{1,0:T(8,128)S(1)}, bf16[256,512]{1,0:T(8,128)(2,1)S(1)}, bf16[256,512]{1,0:T(8,128)(2,1...) custom-call(s32[2]{0:T(128)S(1)} %pad_add_fusion.ids, s32[4,2,4]{2,1,0:T(2,128)S(1)} %bitcast.40, ...), custom_call_target="tpu_custom_call" | custom-call | flops 600000000 | bytes 4000000 | tf_op jit(solution)/shard_map/layer_forward_0/pallas_call | solution.py:60
  35.1 17.1 %all_to_all.46 = bf16[32,8,512]{2,1,0:T(8,128)(2,1)S(1)} all-to-all(bf16[32,8,512]{2,1,0:T(8,128)(2,1)S(1)} %bitcast.55), channel_id=1, replica_groups=mesh['layer'=4,'node'=32] {'node'}, dimensions={0} | all-to-all | bytes 524288 | tf_op jit(solution)/shard_map/all_to_all | solution.py:35
  52.2 2.3 %layer_forward_1.1 = (bf16[256,512]{1,0:T(8,128)(2,1)S(1)}, f32[256,512]{1,0:T(8,128)S(1)}, bf16[256,512]{1,0:T(8,128)(2,1)S(1)}, bf16[256,512]{1,0:T(8,128)(2,1...) custom-call(s32[2]{0:T(128)S(1)} %pad_add_fusion.ids, ...), custom_call_target="tpu_custom_call", output_to_operand_aliasing={{5}: (14, {})} | custom-call | flops 600000000 | bytes 4000000 | tf_op jit(solution)/shard_map/layer_forward_1/pallas_call | solution.py:60
  54.5 12.5 %all_to_all.47 = bf16[32,8,512]{2,1,0:T(8,128)(2,1)S(1)} all-to-all(bf16[32,8,512]{2,1,0:T(8,128)(2,1)S(1)} %bitcast.53), channel_id=1, replica_groups=mesh['layer'=4,'node'=32] {'node'}, dimensions={0} | all-to-all | bytes 524288 | tf_op jit(solution)/shard_map/all_to_all | solution.py:35
  67.0 2.3 %layer_forward_2.1 = (bf16[256,512]{1,0:T(8,128)(2,1)S(1)}, f32[256,512]{1,0:T(8,128)S(1)}, bf16[256,512]{1,0:T(8,128)(2,1)S(1)}, bf16[256,512]{1,0:T(8,128)(2,1...) custom-call(s32[2]{0:T(128)S(1)} %pad_add_fusion.ids, ...), custom_call_target="tpu_custom_call", output_to_operand_aliasing={{5}: (14, {})} | custom-call | flops 600000000 | bytes 4000000 | tf_op jit(solution)/shard_map/layer_forward_2/pallas_call | solution.py:60
  69.3 12.5 %all_to_all.48 = bf16[32,8,512]{2,1,0:T(8,128)(2,1)S(1)} all-to-all(bf16[32,8,512]{2,1,0:T(8,128)(2,1)S(1)} %bitcast.54), channel_id=1, replica_groups=mesh['layer'=4,'node'=32] {'node'}, dimensions={0} | all-to-all | bytes 524288 | tf_op jit(solution)/shard_map/all_to_all | solution.py:35
  81.8 3.6 %top_layer.1 = (bf16[32,8,512]{2,1,0:T(8,128)(2,1)S(1)}, f32[256,512]{1,0:T(8,128)S(1)}, bf16[512,512]{1,0:T(8,128)(2,1)S(1)}, bf16[512,512]{1,0:T(8,128)(2,1)S(1)}, bf16[4,256,512]{2,1,0:T(8,128)(2,1)}) custom-call(s32[2]{0:T(128)S(1)} %pad_add_fusion.ids, s32[4,2,4]{2,1,0:T(2,128)S(1)} %bitcast.43, ...), custom_call_target="tpu_custom_call", output_to_operand_aliasing={{4}: (16, {})} | custom-call | flops 1000000000 | bytes 5000000 | tf_op jit(solution)/shard_map/top_layer/pallas_call | solution.py:60
  85.4 12.5 %all_to_all.49.ret_ref = bf16[32,8,512]{2,1,0:T(8,128)(2,1)S(1)} all-to-all(bf16[32,8,512]{2,1,0:T(8,128)(2,1)S(1)} %get-tuple-element.101), channel_id=1, replica_groups=mesh['layer'=4,'node'=32] {'node'}, dimensions={0} | all-to-all | bytes 524288 | tf_op jit(solution)/shard_map/all_to_all | solution.py:35
  98.2 2.4 %layer_backward_2.1 = (bf16[32,8,512]{2,1,0:T(8,128)(2,1)S(1)}, f32[256,512]{1,0:T(8,128)S(1)}, bf16[4,256,512]{2,1,0:T(8,128)(2,1)}, bf16[512,512]{1,0:T(8,128)(2,1)S(1)}, bf16[512,512]{1,0:T(8,128)(2,1)S(1)}) custom-call(s32[2]{0:T(128)S(1)} %pad_add_fusion.ids, s32[4,2,4]{2,1,0:T(2,128)S(1)} %bitcast.44, bf16[32,8,512]{2,1,0:T(8,128)(2,1)S(1)} %all_to_all.49.ret_ref, ...), custom_call_target="tpu_custom_call" | custom-call | flops 1000000000 | bytes 5000000 | tf_op jit(solution)/shard_map/layer_backward_2/pallas_call | solution.py:60
  100.6 12.3 %all_to_all.50.ret_ref = bf16[32,8,512]{2,1,0:T(8,128)(2,1)S(1)} all-to-all(bf16[32,8,512]{2,1,0:T(8,128)(2,1)S(1)} %get-tuple-element.110), channel_id=1, replica_groups=mesh['layer'=4,'node'=32] {'node'}, dimensions={0} | all-to-all | bytes 524288 | tf_op jit(solution)/shard_map/all_to_all | solution.py:35
  113.1 2.4 %layer_backward_1.1 = (bf16[32,24,512]{2,1,0:T(8,128)(2,1)S(1)}, f32[256,512]{1,0:T(8,128)S(1)}, bf16[4,256,512]{2,1,0:T(8,128)(2,1)}, bf16[512,512]{1,0:T(8,128)(2,1)S(1)}, bf16[512,512]{1,0:T(8,128)(2,1)S(1)}) custom-call(s32[2]{0:T(128)S(1)} %pad_add_fusion.ids, s32[4,2,4]{2,1,0:T(2,128)S(1)} %bitcast.45, ...), custom_call_target="tpu_custom_call", output_to_operand_aliasing={{2}: (12, {})} | custom-call | flops 1000000000 | bytes 5000000 | tf_op jit(solution)/shard_map/layer_backward_1/pallas_call | solution.py:60
  115.6 17.1 %all_to_all.51.ret_ref = bf16[32,24,512]{2,1,0:T(8,128)(2,1)S(1)} all-to-all(bf16[32,24,512]{2,1,0:T(8,128)(2,1)S(1)} %get-tuple-element.123), channel_id=1, replica_groups=mesh['layer'=4,'node'=32] {'node'}, dimensions={0} | all-to-all | bytes 1572864 | tf_op jit(solution)/shard_map/all_to_all | solution.py:35
  132.7 3.2 %layer_backward_0.1 = (bf16[32,56,512]{2,1,0:T(8,128)(2,1)S(1)}, f32[256,512]{1,0:T(8,128)}, bf16[4,256,512]{2,1,0:T(8,128)(2,1)}, bf16[512,512]{1,0:T(8,128)(2,...) custom-call(s32[2]{0:T(128)S(1)} %pad_add_fusion.ids, ...), custom_call_target="tpu_custom_call", output_to_operand_aliasing={{2}: (12, {})} | custom-call | flops 1000000000 | bytes 5000000 | tf_op jit(solution)/shard_map/layer_backward_0/pallas_call | solution.py:60
  136.7 1.4 collective-permute-done.9.recv_b
  138.9 0.8 join_rows.1
  139.8 1.3 copy-done
  141.0 4.1 %all-to-all-start.7 = ((bf16[32,56,512]{2,1,0:T(8,128)(2,1)}), bf16[32,56,512]{2,1,0:T(8,128)(2,1)S(1)}, u32[]{:S(2)}, u32[]{:S(2)}) async-start(bf16[32,56,512]{2,1,0:T(8,128)(2,1)} %copy-done), calls=%async_computation.7 | async-start | bytes 3670016 | tf_op jit(solution)/shard_map/all_to_all | solution.py:35
  145.2 2.7 %collective-permute-start.12 = (bf16[256,512]{1,0:T(8,128)(2,1)S(1)}, bf16[256,512]{1,0:T(8,128)(2,1)S(1)}, u32[]{:S(2)}, u32[]{:S(2)}) collective-permute-start(bf16[256,512]{1,0:T(8,128)(2,1)S(1)} %get-tuple-element.167), channel_id=1, source_target_pairs={{0,96},{32,0},{64,32},{96,64},{1,97},{33,1},{65,33},{97,65},{2,98}... | collective-permute-start | bytes 786440 | tf_op jit(solution)/shard_map/ppermute | solution.py:455
  147.9 0.9 collective-permute-start.11
  149.7 4.3 %collective-permute-start.15 = (bf16[256,512]{1,0:T(8,128)(2,1)S(1)}, bf16[256,512]{1,0:T(8,128)(2,1)S(1)}, u32[]{:S(2)}, u32[]{:S(2)}) collective-permute-start(bf16[256,512]{1,0:T(8,128)(2,1)S(1)} %get-tuple-element.164), channel_id=1, source_target_pairs={{0,96},{64,32},{96,64},{1,97},{65,33},{97,65},{2,98},{66,34},{98,6... | collective-permute-start | bytes 786440 | tf_op jit(solution)/shard_map/ppermute | solution.py:455
  154.0 3.4 %collective-permute-start.14 = (bf16[256,512]{1,0:T(8,128)(2,1)S(1)}, bf16[256,512]{1,0:T(8,128)(2,1)S(1)}, u32[]{:S(2)}, u32[]{:S(2)}) collective-permute-start(bf16[256,512]{1,0:T(8,128)(2,1)S(1)} %get-tuple-element.165), channel_id=1, source_target_pairs={{0,64},{32,96},{96,32},{1,65},{33,97},{97,33},{2,66},{34,98},{98,3... | collective-permute-start | bytes 786440 | tf_op jit(solution)/shard_map/ppermute | solution.py:455
  157.4 8.4 %collective-permute-done.12.refs_3_ = bf16[256,512]{1,0:T(8,128)(2,1)S(1)} collective-permute-done((bf16[256,512]{1,0:T(8,128)(2,1)S(1)}, bf16[256,512]{1,0:T(8,128)(2,1)S(1)}, u32[]{:S(2)}, u32[]{:S(2)}) %collective-permute-start.12) | collective-permute-done | bytes 262176 | tf_op jit(solution)/shard_map/ppermute | solution.py:455
  165.8 1.3 collective-permute-start.13
  167.1 3.6 %collective-permute-done.15.refs_3_ = bf16[256,512]{1,0:T(8,128)(2,1)S(1)} collective-permute-done((bf16[256,512]{1,0:T(8,128)(2,1)S(1)}, bf16[256,512]{1,0:T(8,128)(2,1)S(1)}, u32[]{:S(2)}, u32[]{:S(2)}) %collective-permute-start.15) | collective-permute-done | bytes 262176 | tf_op jit(solution)/shard_map/ppermute | solution.py:455
  171.4 2.8 %input_grads.1 = (bf16[256,512]{1,0:T(8,128)(2,1)}, bf16[2,16,512]{2,1,0:T(8,128)(2,1)S(1)}, bf16[2,16,512]{2,1,0:T(8,128)(2,1)S(1)}, bf16[2,16,512]{2,1,0:T(8,128)(2,1)S(1)}, bf16[2,16,512]{2,1,0:T(8,128)(2,1)S(1)}) custom-call(s32[2]{0:T(128)S(1)} %pad_add_fusion.ids, s32[4,2,4]{2,1,0:T(2,128)S(1)} %bitcast.48, ...), custom_call_target="tpu_custom_call" | custom-call | flops 100000000 | bytes 3000000 | tf_op jit(solution)/shard_map/input_grads/pallas_call | solution.py:60
  174.1 2.5 %collective-permute-start.16 = (bf16[2,16,512]{2,1,0:T(8,128)(2,1)S(1)}, bf16[2,16,512]{2,1,0:T(8,128)(2,1)S(1)}, u32[]{:S(2)}, u32[]{:S(2)}) collective-permute-start(bf16[2,16,512]{2,1,0:T(8,128)(2,1)S(1)} %get-tuple-element.147), channel_id=1, source_target_pairs={{0,32},{32,64},{64,96},{96,0},{1,33},{33,65},{65,97},{97,1},{2,34}... | collective-permute-start | bytes 98312 | tf_op jit(solution)/shard_map/ppermute | solution.py:26
  176.6 5.9 %collective-permute-start.17 = (bf16[2,16,512]{2,1,0:T(8,128)(2,1)S(1)}, bf16[2,16,512]{2,1,0:T(8,128)(2,1)S(1)}, u32[]{:S(2)}, u32[]{:S(2)}) collective-permute-start(bf16[2,16,512]{2,1,0:T(8,128)(2,1)S(1)} %get-tuple-element.148), channel_id=1, source_target_pairs={{0,64},{32,96},{64,0},{96,32},{1,65},{33,97},{65,1},{97,33},{2,66}... | collective-permute-start | bytes 98312 | tf_op jit(solution)/shard_map/ppermute | solution.py:26
  182.9 1.8 collective-permute-done.17.b_ref
  184.7 1.7 collective-permute-done.18.c_ref
  186.4 1.4 sum_over_layer.1
  187.9 7.2 %all-to-all-start.8 = ((bf16[32,16,512]{2,1,0:T(8,128)(2,1)}), bf16[32,16,512]{2,1,0:T(8,128)(2,1)S(1)}, u32[]{:S(2)}, u32[]{:S(2)}) async-start(bf16[32,16,512]{2,1,0:T(8,128)(2,1)} %sum_over_layer.1), calls=%async_computation.8 | async-start | bytes 1048576 | tf_op jit(solution)/shard_map/all_to_all | solution.py:35
  195.1 1.3 collective-permute-start.21
  196.4 1.3 collective-permute-start.20
  197.7 1.3 collective-permute-start.19
  199.0 2.6 %put_home.2 = bf16[1,4,256,512]{3,2,1,0:T(8,128)(2,1)} custom-call(s32[2]{0:T(128)S(1)} %pad_add_fusion.ids, s32[4,2,4]{2,1,0:T(2,128)S(1)} %bitcast.50, bf16[4,256,512]{2,1,0:T(8,128)(2,1)} %get-tuple-element.140.refs_0_, bf16[256,512]{1,0:T(8,128)(2,1)S(1)} %collective-permute-done.10.refs_1_, bf16[256,512]{1,0:T(8,128)(2,1)S(1)} %collective-permute-done.11.refs_2_, ...), custom_call_target="tpu_custom_call" | custom-call | bytes 2000000 | tf_op jit(solution)/shard_map/put_home/pallas_call | solution.py:60
  201.6 4.1 %collective-permute-done.21.refs_7_ = bf16[256,512]{1,0:T(8,128)(2,1)S(1)} collective-permute-done((bf16[256,512]{1,0:T(8,128)(2,1)}, bf16[256,512]{1,0:T(8,128)(2,1)S(1)}, u32[]{:S(2)}, u32[]{:S(2)}) %collective-permute-start.21) | collective-permute-done | bytes 262176 | tf_op jit(solution)/shard_map/ppermute | solution.py:551
  205.7 2.9 %collective-permute-done.20.refs_6_ = bf16[256,512]{1,0:T(8,128)(2,1)S(1)} collective-permute-done((bf16[256,512]{1,0:T(8,128)(2,1)}, bf16[256,512]{1,0:T(8,128)(2,1)S(1)}, u32[]{:S(2)}, u32[]{:S(2)}) %collective-permute-start.20) | collective-permute-done | bytes 262176 | tf_op jit(solution)/shard_map/ppermute | solution.py:551
  208.6 5.5 %collective-permute-done.19.refs_5_ = bf16[256,512]{1,0:T(8,128)(2,1)S(1)} collective-permute-done((bf16[256,512]{1,0:T(8,128)(2,1)}, bf16[256,512]{1,0:T(8,128)(2,1)S(1)}, u32[]{:S(2)}, u32[]{:S(2)}) %collective-permute-start.19) | collective-permute-done | bytes 262176 | tf_op jit(solution)/shard_map/ppermute | solution.py:551
  214.2 2.7 %put_home.3 = bf16[1,4,256,512]{3,2,1,0:T(8,128)(2,1)} custom-call(s32[2]{0:T(128)S(1)} %pad_add_fusion.ids, s32[4,2,4]{2,1,0:T(2,128)S(1)} %bitcast.51, bf16[4,256,512]{2,1,0:T(8,128)(2,1)} %get-tuple-element.141.refs_0_, bf16[256,512]{1,0:T(8,128)(2,1)S(1)} %collective-permute-done.13.refs_1_, bf16[256,512]{1,0:T(8,128)(2,1)S(1)} %collective-permute-done.14.refs_2_, ...), custom_call_target="tpu_custom_call" | custom-call | bytes 2000000 | tf_op jit(solution)/shard_map/put_home/pallas_call | solution.py:60
  216.9 2.3 %scale_grads.1 = (f32[1,512,512]{2,1,0:T(8,128)}, f32[1,512,512]{2,1,0:T(8,128)}) custom-call(s32[2]{0:T(128)S(1)} %pad_add_fusion.ids, s32[4,2,4]{2,1,0:T(2,128)S(1)} %bitcast.52, bf16[512,512]{1,0:T(8,128)(2,1)S(1)} %bitcast.34, bf16[512,512]{1,0:T(8,128)(2,1)S(1)} %collective-permute-done.22.other_ref), custom_call_target="tpu_custom_call" | custom-call | bytes 3000000 | tf_op jit(solution)/shard_map/scale_grads/pallas_call | solution.py:60
  (43 shorter events, 7.1 us)
Async XLA Ops:
  0.6 31.4 %copy-start.2 = (s32[4,1,2,4]{3,2,1,0:T(2,128)S(1)}, s32[4,1,2,4]{3,2,1,0:T(2,128)}, u32[]{:S(2)}) copy-start(s32[4,1,2,4]{3,2,1,0:T(2,128)} %param.16) | copy-start | bytes 388
  1.9 25.7 %collective-permute-start.2 = (bf16[512,512]{1,0:T(8,128)(2,1)S(1)}, bf16[512,512]{1,0:T(8,128)(2,1)S(1)}, u32[]{:S(2)}, u32[]{:S(2)}) collective-permute-start(bf16[512,512]{1,0:T(8,128)(2,1)S(1)} %broadcast_select_fusion), channel_id=1, source_target_pairs={{0,64},{32,96},{64,0},{96,32},{1,65},{33,97},{65,1},{97,33},{2,66}... | collective-permute-start | bytes 1572872 | tf_op jit(solution)/shard_map/ppermute | solution.py:26
  5.1 23.5 %collective-permute-start.1 = (bf16[512,512]{1,0:T(8,128)(2,1)S(1)}, bf16[512,512]{1,0:T(8,128)(2,1)S(1)}, u32[]{:S(2)}, u32[]{:S(2)}) collective-permute-start(bf16[512,512]{1,0:T(8,128)(2,1)S(1)} %broadcast_select_fusion), channel_id=1, source_target_pairs={{0,96},{32,0},{64,32},{96,64},{1,97},{33,1},{65,33},{97,65},{2,98}... | collective-permute-start | bytes 1572872 | tf_op jit(solution)/shard_map/ppermute | solution.py:26
  6.2 22.4 %collective-permute-start = (bf16[512,512]{1,0:T(8,128)(2,1)S(1)}, bf16[512,512]{1,0:T(8,128)(2,1)S(1)}, u32[]{:S(2)}, u32[]{:S(2)}) collective-permute-start(bf16[512,512]{1,0:T(8,128)(2,1)S(1)} %broadcast_select_fusion), channel_id=1, source_target_pairs={{0,32},{32,64},{64,96},{96,0},{1,33},{33,65},{65,97},{97,1},{2,34}... | collective-permute-start | bytes 1572872 | tf_op jit(solution)/shard_map/ppermute | solution.py:26
  7.2 0.7 copy-start.1
  28.6 1.9 collective-permute-start.3
  28.6 2.7 %collective-permute-start.4 = (bf16[512,512]{1,0:T(8,128)(2,1)S(1)}, bf16[512,512]{1,0:T(8,128)(2,1)S(1)}, u32[]{:S(2)}, u32[]{:S(2)}) collective-permute-start(bf16[512,512]{1,0:T(8,128)(2,1)S(1)} %collective-permute-done.1.rest_4_), channel_id=1, source_target_pairs={{0,1},{1,0},{2,3},{3,2},{4,5},{5,4},{6,7},{7,6},{8,9},{9,8},{10,11... | collective-permute-start | bytes 1572872 | tf_op jit(solution)/shard_map/ppermute | solution.py:31
  29.1 2.9 %collective-permute-start.5 = (bf16[512,512]{1,0:T(8,128)(2,1)S(1)}, bf16[512,512]{1,0:T(8,128)(2,1)S(1)}, u32[]{:S(2)}, u32[]{:S(2)}) collective-permute-start(bf16[512,512]{1,0:T(8,128)(2,1)S(1)} %collective-permute-done.2.rest_6_), channel_id=1, source_target_pairs={{0,1},{1,0},{2,3},{3,2},{4,5},{5,4},{6,7},{7,6},{8,9},{9,8},{10,11... | collective-permute-start | bytes 1572872 | tf_op jit(solution)/shard_map/ppermute | solution.py:31
  67.0 14.8 %copy-start.3 = (bf16[512,172]{0,1:T(8,128)(2,1)S(1)}, bf16[512,172]{0,1:T(8,128)(2,1)}, u32[]{:S(2)}) copy-start(bf16[512,172]{0,1:T(8,128)(2,1)} %param.13) | copy-start | bytes 528388
  67.0 14.8 %copy-start.4 = (s32[4,256]{1,0:T(4,128)S(1)}, s32[4,256]{1,0:T(4,128)}, u32[]{:S(2)}) copy-start(s32[4,256]{1,0:T(4,128)} %lab_ref.1) | copy-start | bytes 12292
  67.0 14.8 %copy-start.5 = (s32[4,256]{1,0:T(4,128)S(1)}, s32[4,256]{1,0:T(4,128)}, u32[]{:S(2)}) copy-start(s32[4,256]{1,0:T(4,128)} %mask_ref.1) | copy-start | bytes 12292
  97.9 2.7 %collective-permute-start.6 = (bf16[512,512]{1,0:T(8,128)(2,1)S(1)}, bf16[512,512]{1,0:T(8,128)(2,1)S(1)}, u32[]{:S(2)}, u32[]{:S(2)}) collective-permute-start(bf16[512,512]{1,0:T(8,128)(2,1)S(1)} %get-tuple-element.109), channel_id=1, source_target_pairs={{0,1},{1,0},{2,3},{3,2},{4,5},{5,4},{6,7},{7,6},{8,9},{9,8},{10,11... | collective-permute-start | bytes 1572872 | tf_op jit(solution)/shard_map/ppermute | solution.py:31
  112.8 2.7 %collective-permute-start.7 = (bf16[512,512]{1,0:T(8,128)(2,1)S(1)}, bf16[512,512]{1,0:T(8,128)(2,1)S(1)}, u32[]{:S(2)}, u32[]{:S(2)}) collective-permute-start(bf16[512,512]{1,0:T(8,128)(2,1)S(1)} %get-tuple-element.122), channel_id=1, source_target_pairs={{0,1},{1,0},{2,3},{3,2},{4,5},{5,4},{6,7},{7,6},{8,9},{9,8},{10,11... | collective-permute-start | bytes 1572872 | tf_op jit(solution)/shard_map/ppermute | solution.py:31
  135.9 2.3 %collective-permute-start.9 = (bf16[512,512]{1,0:T(8,128)(2,1)S(1)}, bf16[512,512]{1,0:T(8,128)(2,1)S(1)}, u32[]{:S(2)}, u32[]{:S(2)}) collective-permute-start(bf16[512,512]{1,0:T(8,128)(2,1)S(1)} %get-tuple-element.135), channel_id=1, source_target_pairs={{0,1},{1,0},{2,3},{3,2},{4,5},{5,4},{6,7},{7,6},{8,9},{9,8},{10,11... | collective-permute-start | bytes 1572872 | tf_op jit(solution)/shard_map/ppermute | solution.py:31
  136.6 2.3 %collective-permute-start.8 = (bf16[512,512]{1,0:T(8,128)(2,1)S(1)}, bf16[512,512]{1,0:T(8,128)(2,1)S(1)}, u32[]{:S(2)}, u32[]{:S(2)}) collective-permute-start(bf16[512,512]{1,0:T(8,128)(2,1)S(1)} %get-tuple-element.125), channel_id=1, source_target_pairs={{0,1},{1,0},{2,3},{3,2},{4,5},{5,4},{6,7},{7,6},{8,9},{9,8},{10,11... | collective-permute-start | bytes 1572872 | tf_op jit(solution)/shard_map/ppermute | solution.py:31
  139.7 1.3 copy-start
  141.0 4.1 %copy-start.6 = (bf16[4,256,512]{2,1,0:T(8,128)(2,1)S(1)}, bf16[4,256,512]{2,1,0:T(8,128)(2,1)}, u32[]{:S(2)}) copy-start(bf16[4,256,512]{2,1,0:T(8,128)(2,1)} %get-tuple-element.140.refs_0_) | copy-start | bytes 3145732
  141.0 30.4 %all-to-all-start.7 = ((bf16[32,56,512]{2,1,0:T(8,128)(2,1)}), bf16[32,56,512]{2,1,0:T(8,128)(2,1)S(1)}, u32[]{:S(2)}, u32[]{:S(2)}) async-start(bf16[32,56,512]{2,1,0:T(8,128)(2,1)} %copy-done), calls=%async_computation.7 | async-start | bytes 3670016 | tf_op jit(solution)/shard_map/all_to_all | solution.py:35
  145.2 4.4 %copy-start.7 = (bf16[4,256,512]{2,1,0:T(8,128)(2,1)S(1)}, bf16[4,256,512]{2,1,0:T(8,128)(2,1)}, u32[]{:S(2)}) copy-start(bf16[4,256,512]{2,1,0:T(8,128)(2,1)} %get-tuple-element.141.refs_0_) | copy-start | bytes 3145732
  145.2 20.6 %collective-permute-start.12 = (bf16[256,512]{1,0:T(8,128)(2,1)S(1)}, bf16[256,512]{1,0:T(8,128)(2,1)S(1)}, u32[]{:S(2)}, u32[]{:S(2)}) collective-permute-start(bf16[256,512]{1,0:T(8,128)(2,1)S(1)} %get-tuple-element.167), channel_id=1, source_target_pairs={{0,96},{32,0},{64,32},{96,64},{1,97},{33,1},{65,33},{97,65},{2,98}... | collective-permute-start | bytes 786440 | tf_op jit(solution)/shard_map/ppermute | solution.py:455
  147.9 19.2 %collective-permute-start.11 = (bf16[256,512]{1,0:T(8,128)(2,1)S(1)}, bf16[256,512]{1,0:T(8,128)(2,1)S(1)}, u32[]{:S(2)}, u32[]{:S(2)}) collective-permute-start(bf16[256,512]{1,0:T(8,128)(2,1)S(1)} %get-tuple-element.168), channel_id=1, source_target_pairs={{0,64},{32,96},{64,0},{96,32},{1,65},{33,97},{65,1},{97,33},{2,66}... | collective-permute-start | bytes 786440 | tf_op jit(solution)/shard_map/ppermute | solution.py:455
  148.8 18.3 %collective-permute-start.10 = (bf16[256,512]{1,0:T(8,128)(2,1)S(1)}, bf16[256,512]{1,0:T(8,128)(2,1)S(1)}, u32[]{:S(2)}, u32[]{:S(2)}) collective-permute-start(bf16[256,512]{1,0:T(8,128)(2,1)S(1)} %get-tuple-element.169), channel_id=1, source_target_pairs={{0,32},{32,64},{64,96},{96,0},{1,33},{33,65},{65,97},{97,1},{2,34}... | collective-permute-start | bytes 786440 | tf_op jit(solution)/shard_map/ppermute | solution.py:455
  149.7 21.1 %collective-permute-start.15 = (bf16[256,512]{1,0:T(8,128)(2,1)S(1)}, bf16[256,512]{1,0:T(8,128)(2,1)S(1)}, u32[]{:S(2)}, u32[]{:S(2)}) collective-permute-start(bf16[256,512]{1,0:T(8,128)(2,1)S(1)} %get-tuple-element.164), channel_id=1, source_target_pairs={{0,96},{64,32},{96,64},{1,97},{65,33},{97,65},{2,98},{66,34},{98,6... | collective-permute-start | bytes 786440 | tf_op jit(solution)/shard_map/ppermute | solution.py:455
  154.0 16.7 %collective-permute-start.14 = (bf16[256,512]{1,0:T(8,128)(2,1)S(1)}, bf16[256,512]{1,0:T(8,128)(2,1)S(1)}, u32[]{:S(2)}, u32[]{:S(2)}) collective-permute-start(bf16[256,512]{1,0:T(8,128)(2,1)S(1)} %get-tuple-element.165), channel_id=1, source_target_pairs={{0,64},{32,96},{96,32},{1,65},{33,97},{97,33},{2,66},{34,98},{98,3... | collective-permute-start | bytes 786440 | tf_op jit(solution)/shard_map/ppermute | solution.py:455
  165.8 5.6 %collective-permute-start.13 = (bf16[256,512]{1,0:T(8,128)(2,1)S(1)}, bf16[256,512]{1,0:T(8,128)(2,1)S(1)}, u32[]{:S(2)}, u32[]{:S(2)}) collective-permute-start(bf16[256,512]{1,0:T(8,128)(2,1)S(1)} %get-tuple-element.166), channel_id=1, source_target_pairs={{0,32},{32,64},{64,96},{1,33},{33,65},{65,97},{2,34},{34,66},{66,9... | collective-permute-start | bytes 786440 | tf_op jit(solution)/shard_map/ppermute | solution.py:455
  174.1 8.8 %collective-permute-start.16 = (bf16[2,16,512]{2,1,0:T(8,128)(2,1)S(1)}, bf16[2,16,512]{2,1,0:T(8,128)(2,1)S(1)}, u32[]{:S(2)}, u32[]{:S(2)}) collective-permute-start(bf16[2,16,512]{2,1,0:T(8,128)(2,1)S(1)} %get-tuple-element.147), channel_id=1, source_target_pairs={{0,32},{32,64},{64,96},{96,0},{1,33},{33,65},{65,97},{97,1},{2,34}... | collective-permute-start | bytes 98312 | tf_op jit(solution)/shard_map/ppermute | solution.py:26
  176.6 8.1 %collective-permute-start.17 = (bf16[2,16,512]{2,1,0:T(8,128)(2,1)S(1)}, bf16[2,16,512]{2,1,0:T(8,128)(2,1)S(1)}, u32[]{:S(2)}, u32[]{:S(2)}) collective-permute-start(bf16[2,16,512]{2,1,0:T(8,128)(2,1)S(1)} %get-tuple-element.148), channel_id=1, source_target_pairs={{0,64},{32,96},{64,0},{96,32},{1,65},{33,97},{65,1},{97,33},{2,66}... | collective-permute-start | bytes 98312 | tf_op jit(solution)/shard_map/ppermute | solution.py:26
  182.5 3.9 %collective-permute-start.18 = (bf16[2,16,512]{2,1,0:T(8,128)(2,1)S(1)}, bf16[2,16,512]{2,1,0:T(8,128)(2,1)S(1)}, u32[]{:S(2)}, u32[]{:S(2)}) collective-permute-start(bf16[2,16,512]{2,1,0:T(8,128)(2,1)S(1)} %get-tuple-element.149), channel_id=1, source_target_pairs={{0,96},{32,0},{64,32},{96,64},{1,97},{33,1},{65,33},{97,65},{2,98}... | collective-permute-start | bytes 98312 | tf_op jit(solution)/shard_map/ppermute | solution.py:26
  187.9 26.3 %all-to-all-start.8 = ((bf16[32,16,512]{2,1,0:T(8,128)(2,1)}), bf16[32,16,512]{2,1,0:T(8,128)(2,1)S(1)}, u32[]{:S(2)}, u32[]{:S(2)}) async-start(bf16[32,16,512]{2,1,0:T(8,128)(2,1)} %sum_over_layer.1), calls=%async_computation.8 | async-start | bytes 1048576 | tf_op jit(solution)/shard_map/all_to_all | solution.py:35
  195.1 10.6 %collective-permute-start.21 = (bf16[256,512]{1,0:T(8,128)(2,1)}, bf16[256,512]{1,0:T(8,128)(2,1)S(1)}, u32[]{:S(2)}, u32[]{:S(2)}) collective-permute-start(bf16[256,512]{1,0:T(8,128)(2,1)} %get-tuple-element.153.refs_4_), channel_id=1, source_target_pairs={{32,0},{33,1},{34,2},{35,3},{36,4},{37,5},{38,6},{39,7},{40,8},{41... | collective-permute-start | bytes 786440 | tf_op jit(solution)/shard_map/ppermute | solution.py:551
  196.4 12.2 %collective-permute-start.20 = (bf16[256,512]{1,0:T(8,128)(2,1)}, bf16[256,512]{1,0:T(8,128)(2,1)S(1)}, u32[]{:S(2)}, u32[]{:S(2)}) collective-permute-start(bf16[256,512]{1,0:T(8,128)(2,1)} %get-tuple-element.153.refs_4_), channel_id=1, source_target_pairs={{64,0},{65,1},{66,2},{67,3},{68,4},{69,5},{70,6},{71,7},{72,8},{73... | collective-permute-start | bytes 786440 | tf_op jit(solution)/shard_map/ppermute | solution.py:551
  197.7 16.4 %collective-permute-start.19 = (bf16[256,512]{1,0:T(8,128)(2,1)}, bf16[256,512]{1,0:T(8,128)(2,1)S(1)}, u32[]{:S(2)}, u32[]{:S(2)}) collective-permute-start(bf16[256,512]{1,0:T(8,128)(2,1)} %get-tuple-element.153.refs_4_), channel_id=1, source_target_pairs={{96,0},{97,1},{98,2},{99,3},{100,4},{101,5},{102,6},{103,7},{104,8... | collective-permute-start | bytes 786440 | tf_op jit(solution)/shard_map/ppermute | solution.py:551
  214.1 2.8 %collective-permute-start.22 = (bf16[512,512]{1,0:T(8,128)(2,1)S(1)}, bf16[512,512]{1,0:T(8,128)(2,1)S(1)}, u32[]{:S(2)}, u32[]{:S(2)}) collective-permute-start(bf16[512,512]{1,0:T(8,128)(2,1)S(1)} %bitcast.33), channel_id=1, source_target_pairs={{0,1},{1,0},{2,3},{3,2},{4,5},{5,4},{6,7},{7,6},{8,9},{9,8},{10,11... | collective-permute-start | bytes 1572872 | tf_op jit(solution)/shard_map/ppermute | solution.py:31

commit v4 on v3

--- a/solution.py
+++ b/solution.py
@@ -162,24 +162,32 @@
     vals_out[...] = vals_ref[...]
 
 
-def forward_math(layer, ids, cols, h_ref, arr_ref, vals_ref, w_refs, w_ref, sems, ext):
-    start_weights(layer, ids, w_refs, w_ref, sems)
+def forward_math(ids, cols, h_ref, arr_ref, vals_ref, w_ref, ext, ready=None):
     rows = h_ref.shape[0]
     ext[0:rows, :] = h_ref[...]
     ext[rows : 2 * rows, :] = arr_ref[...]
     agg = aggregate_rows(ids, cols, vals_ref, ext)
-    wait_weights(layer, ids, w_refs, w_ref, sems)
+    if ready is not None:
+        ready()
     pre = dot(h_ref[...], w_ref[0]) + dot(agg, w_ref[1])
     sig = sigmoid(pre)
     return agg, pre, sig, (pre * sig).astype(BF)
 
 
 def forward_kernel(layer, ids, cols, h_ref, arr_ref, vals_ref, pick_ref, *rest):
-    w_refs, rest = rest[:8], rest[-9:]
-    agg_ref, pre_ref, hid_ref, out_ref, w_ref, buf_ref, ext, sems, buf_sem = rest
-    agg, pre, _, hid = forward_math(
-        layer, ids, cols, h_ref, arr_ref, vals_ref, w_refs, w_ref, sems, ext
-    )
+    w_refs, rest = rest[:8], rest[8:]
+    first = layer == 0
+    w_ref, rest = (rest[6], rest) if first else (rest[0], rest[2:])
+    agg_ref, pre_ref, hid_ref, out_ref, buf_ref, next_ref = rest[:6]
+    ext, buf_sem, sems = rest[-3:]
+    ready = None
+    if first:
+        here = (layer, ids, w_refs, w_ref, sems.at[0])
+        start_weights(*here)
+        ready = lambda: wait_weights(*here)
+    ahead = (layer + 1, ids, w_refs, next_ref, sems.at[1])
+    start_weights(*ahead)
+    agg, pre, _, hid = forward_math(ids, cols, h_ref, arr_ref, vals_ref, w_ref, ext, ready)
     hid_ref[...] = hid
     copy = to_slot(hid_ref, layer, ids, buf_ref, buf_sem)
     copy.start()
@@ -187,6 +195,7 @@
     agg_ref[...] = agg
     pre_ref[...] = pre
     copy.wait()
+    wait_weights(*ahead)
 
 
 def backward_math(ids, cols, d_pre, vals_ref, w_ref, d_ext):
@@ -210,13 +219,10 @@
         send_ref[...] = on_rows
 
 
-def top_kernel(layer, ids, cols, h_ref, arr_ref, vals_ref, wout_ref, lab_ref, mask_ref, *rest):
-    w_refs, rest = rest[:8], rest[9:]
-    remote_ref, part_ref, keep_ref, send_ref, buf_ref, hid_ref, w_ref, ext, d_ext, sems, buf_sem = rest
+def top_kernel(layer, ids, cols, h_ref, arr_ref, vals_ref, wout_ref, lab_ref, mask_ref, w_ref, *rest):
+    remote_ref, part_ref, keep_ref, send_ref, buf_ref, hid_ref, ext, d_ext, buf_sem = rest[1:]
     rows = h_ref.shape[0]
-    agg, pre, sig, hid = forward_math(
-        layer, ids, cols, h_ref, arr_ref, vals_ref, w_refs, w_ref, sems, ext
-    )
+    agg, pre, sig, hid = forward_math(ids, cols, h_ref, arr_ref, vals_ref, w_ref, ext)
     hid_ref[...] = hid
     copy = to_slot(hid_ref, layer, ids, buf_ref, buf_sem)
     copy.start()
@@ -250,6 +256,8 @@
     if layer < 2:
         rest = rest[1:]
     out_ref, part_ref, buf_ref, keep_ref, send_ref, *rest = rest
+    if not layer:
+        *rest, local, local_sem = rest
     *chunk, dout_ref, d_ext, buf_sem = rest
     rows, feat = part_in.shape
     peers = out_ref.shape[0]
@@ -263,14 +271,20 @@
     sig = sigmoid(pre)
     d_pre = (d_out.astype(F32) * (sig * (1.0 + pre * (1.0 - sig)))).astype(BF)
     back = backward_math(ids, cols, d_pre, vals_ref, w_ref, d_ext)
-    out_ref[:, 0:slots, :] = d_ext[rows : 2 * rows, :].astype(BF).reshape(peers, slots, feat)
+    target = out_ref if layer else local
+    target[:, 0:slots, :] = d_ext[rows : 2 * rows, :].astype(BF).reshape(peers, slots, feat)
+    if carry:
+        put_carry(keep_in, recv_in, target, slots)
+    if not layer:
+        away = pltpu.make_async_copy(local, out_ref.at[:, pl.ds(0, local.shape[1]), :], local_sem)
+        away.start()
     part_ref[...] = back + d_ext[0:rows, :]
     weight_partials(ids, h_ref, agg_ref[...], d_pre, keep_ref, send_ref)
-    if carry:
-        put_carry(keep_in, recv_in, out_ref, slots)
     if chunk:
         chunk[0][...] = chunk_sum(ret_ref[:, slots:, :]).astype(BF)
     copy.wait()
+    if not layer:
+        away.wait()
 
 
 def put_carry(keep_ref, recv_ref, out_ref, first):
@@ -280,30 +294,39 @@
     out_ref[:, first : first + size, :] = total.reshape(peers, size, feat)
 
 
-def join_kernel(ids, cols, keep_a, recv_a, keep_b, recv_b, buf_in, out_ref):
-    size = keep_a.shape[0] // out_ref.shape[0]
+def join_kernel(ids, cols, keep_a, recv_a, keep_b, recv_b, buf_in, out_ref, local, sem):
+    size = local.shape[1] // 2
     first = out_ref.shape[1] - 2 * size
-    put_carry(keep_a, recv_a, out_ref, first)
-    put_carry(keep_b, recv_b, out_ref, first + size)
-
-
-def end_kernel(ids, cols, ret_ref, part_in, pick_ref, c_3, dout_ref, o_0, o_1, o_2, o_3, all_sums):
-    rows, feat = part_in.shape
-    slots = rows // ret_ref.shape[0]
+    put_carry(keep_a, recv_a, local, 0)
+    put_carry(keep_b, recv_b, local, size)
+    copy = pltpu.make_async_copy(local, out_ref.at[:, pl.ds(first, 2 * size), :], sem)
+    copy.start()
+    copy.wait()
+
+
+def chunk_kernel(ids, cols, ret_ref, c_3, out_ref):
     size = c_3.shape[1]
-    all_sums[3] = c_3[...]
+    slots = ret_ref.shape[1] - 3 * size
+    out_ref[3] = c_3[...]
     for n, layer in enumerate((2, 1, 0)):
         first = slots + n * size
-        all_sums[layer] = chunk_sum(ret_ref[:, first : first + size, :]).astype(BF)
-    for s, out_ref in enumerate((o_0, o_1, o_2, o_3)):
-        out_ref[...] = all_sums[lax.rem(ids[0] + s, 4)]
-    returned = ret_ref[:, 0:slots, :].reshape(rows, feat)
+        out_ref[layer] = chunk_sum(ret_ref[:, first : first + size, :]).astype(BF)
+
+
+def end_kernel(ids, cols, ret_ref, part_in, pick_ref, buf_in, buf_ref, dout_ref, buf_sem):
+    rows, feat = part_in.shape
+    returned = ret_ref[:, 0 : rows // ret_ref.shape[0], :].reshape(rows, feat)
     dout_ref[...] = (part_in[...] + dot(pick_ref[...], returned, TN)).astype(BF)
-
-
-def layer_sum_kernel(ids, cols, own_ref, a_ref, b_ref, c_ref, out_ref):
-    total = own_ref[...].astype(F32) + a_ref[...].astype(F32)
-    total = (total + b_ref[...].astype(F32) + c_ref[...].astype(F32)).astype(BF)
+    copy = to_slot(dout_ref, 0, ids, buf_ref, buf_sem)
+    copy.start()
+    copy.wait()
+
+
+def layer_sum_kernel(ids, cols, sums_ref, out_ref):
+    total = sums_ref[0].astype(F32)
+    for span in range(1, sums_ref.shape[0]):
+        total = total + sums_ref[span].astype(F32)
+    total = total.astype(BF)
     for n in range(0, out_ref.shape[0], 2):
         out_ref[n : n + 2] = total
 
@@ -325,15 +348,8 @@
 
 def home_kernel(ids, cols, *refs):
     pieces, out_ref = refs[:-1], refs[-1]
-    home = ids[0]
-    for s, piece in enumerate(pieces[:4]):
-        out_ref[0, lax.rem(home + 4 - s, 4)] = piece[...]
-    if len(pieces) > 4:
-
-        @pl.when(home == 0)
-        def _():
-            for s, piece in enumerate(pieces[4:]):
-                out_ref[0, lax.rem(4 - s, 4)] = piece[...]
+    for s, piece in enumerate(pieces):
+        out_ref[0, lax.rem(ids[0] + 4 - s, 4)] = piece[...]
 
 
 def body(
@@ -390,7 +406,6 @@
     arrived, left, right, far = tie(arrived, left, right, far)
     sources = [(w_self[0], FAR), (w_neigh[0], FAR), left, sibling(left), right, sibling(right)]
     sources += [far, sibling(far)]
-    w_scratch = [pltpu.SemaphoreType.DMA((2,))]
     weight = near((2, feat, feat))
 
     hidden, aggs, pres, weights = [features_0], [], [], []
@@ -401,22 +416,22 @@
     for layer in range(top):
         ins = [hidden[layer], arrived.reshape(rows, feat), vals, pick, *sources]
         if layer:
-            ins.append((acts_buf, FAR))
-        agg, pre, hid, outgoing, arranged, acts_buf = run(
+            ins += [weights[layer], (acts_buf, FAR)]
+        agg, pre, hid, outgoing, acts_buf, *arranged = run(
             functools.partial(forward_kernel, layer),
             f"layer_forward_{layer}",
             scalars,
             ins,
-            [act, wide, act, act, weight, stack],
-            [ext_scratch, *w_scratch, buf_sem],
-            {len(ins) - 1: 5} if layer else None,
+            [act, wide, act, act, stack] + [weight] * (2 if layer == 0 else 1),
+            [ext_scratch, buf_sem, pltpu.SemaphoreType.DMA((2, 2))],
+            {len(ins) - 1: 4} if layer else None,
             flops=6 * 10**8,
             moved=4 * 10**6,
         )
         hidden.append(hid)
         aggs.append(agg)
         pres.append(pre)
-        weights.append(arranged)
+        weights += arranged[::-1]
         arrived = exchange(outgoing.reshape(peers, slots, feat))
 
     ins = [
@@ -426,7 +441,7 @@
         w_out.T,
         labels,
         train_mask,
-        *sources,
+        weights[top],
         (acts_buf, FAR),
     ]
     remote, part, keep, send, acts_buf = run(
@@ -437,10 +452,8 @@
         [near((peers, slots, feat)), wide, square, square, stack],
         [
             pltpu.VMEM((rows, feat), BF),
-            pltpu.VMEM((2, feat, feat), BF),
             ext_scratch,
             d_ext_scratch,
-            *w_scratch,
             buf_sem,
         ],
         {len(ins) - 1: 4},
@@ -448,12 +461,8 @@
         moved=5 * 10**6,
     )
 
-    def travel(buf, home_too=True):
-        pieces = []
-        for s in all_shifts:
-            pairs = [(i, (i + s) % spans) for i in range(spans) if home_too or (i + s) % spans]
-            pieces.append(lax.ppermute(buf[s], "layer", pairs))
-        return pieces
+    def travel(buf):
+        return [shift(buf[s], "layer", s) for s in all_shifts]
 
     def put_home(buf, *pieces):
         block = pl.BlockSpec((None, rows, feat), lambda i, ids, cols: (0, 0, 0))
@@ -468,7 +477,6 @@
         )[0]
 
     chunk_rows = feat // peers
-    chunk = near((2, chunk_rows, feat))
     pairs, grads_buf = [], None
     for layer in range(top - 1, -1, -1):
         returned, send = tie(exchange(remote), send)
@@ -492,7 +500,12 @@
             ins.append((grads_buf, FAR))
             aliases = {len(ins) - 1: 2}
         last = far_block if layer == 0 else near
-        outs = [near((peers, width, feat)), last((rows, feat), F32), stack, square, square]
+        operand = near((peers, width, feat))
+        scratch = [pltpu.VMEM((rows, feat), BF), d_ext_scratch, buf_sem]
+        if layer == 0:
+            operand = (pltpu.HBM((peers, width, feat), BF), FAR)
+            scratch += [pltpu.VMEM((peers, slots + chunk_rows, feat), BF), buf_sem]
+        outs = [operand, last((rows, feat), F32), stack, square, square]
         if layer == 0:
             outs.append(far_block((2, chunk_rows, feat)))
         remote, part, grads_buf, keep, send, *c_3 = run(
@@ -501,7 +514,7 @@
             scalars,
             ins,
             outs,
-            [pltpu.VMEM((rows, feat), BF), d_ext_scratch, buf_sem],
+            scratch,
             aliases,
             flops=10**9,
             moved=5 * 10**6,
@@ -514,18 +527,25 @@
         join_kernel,
         "join_rows",
         scalars,
-        [*pairs[-1], keep, sibling(send), remote],
-        [near((peers, slots + 3 * chunk_rows, feat))],
+        [*pairs[-1], keep, sibling(send), (remote, FAR)],
+        [(pltpu.HBM((peers, slots + 3 * chunk_rows, feat), BF), FAR)],
+        [pltpu.VMEM((peers, 2 * chunk_rows, feat), BF), buf_sem],
         aliases={4: 0},
         moved=3 * 10**6,
     )[0]
-    joined, acts_buf, grads_buf = tie(joined, acts_buf, grads_buf)
+    joined, acts_buf = tie(joined, acts_buf)
     acts = travel(acts_buf)
-    early = travel(grads_buf, False)
-    returned, *pieces = tie(exchange(joined), *acts, *early)
-    acts, early = pieces[:3], pieces[3:]
-    layer_acts = put_home(acts_buf, *acts)
-    d_out, own_sum, *sums = run(
+    returned, *acts = tie(exchange(joined), *acts)
+    sums = run(
+        chunk_kernel,
+        "sum_chunks",
+        scalars,
+        [returned, (c_3[0], whole(c_3[0].shape))],
+        [far_block((spans, 2, chunk_rows, feat))],
+        moved=10**6,
+    )[0]
+    sums = lax.all_to_all(sums, "layer", split_axis=0, concat_axis=0, tiled=True)
+    grads_buf = run(
         end_kernel,
         "input_grads",
         scalars,
@@ -533,26 +553,28 @@
             returned,
             (part, whole((rows, feat))),
             (pick_far, whole(pick_far.shape)),
-            (c_3[0], whole(c_3[0].shape)),
+            (grads_buf, FAR),
         ],
-        [far_block((rows, feat)), chunk, chunk, chunk, chunk],
-        [pltpu.VMEM((spans, 2, chunk_rows, feat), BF)],
+        [stack],
+        [pltpu.VMEM((rows, feat), BF), buf_sem],
+        {3: 0},
         flops=10**8,
-        moved=3 * 10**6,
-    )
+        moved=10**6,
+    )[0]
     spread = run(
         layer_sum_kernel,
         "sum_over_layer",
         scalars,
-        [own_sum, *[shift(v, "layer", s) for s, v in zip(all_shifts, sums)]],
-        [near((peers, chunk_rows, feat))],
+        [sums],
+        [far_block((peers, chunk_rows, feat))],
         moved=10**6,
     )[0]
-    late = [lax.ppermute(d_out, "layer", [(spans - s, 0)]) for s in all_shifts]
-    gathered, layer_acts, *late = tie(exchange(spread), layer_acts, *late)
+    layer_acts = put_home(acts_buf, *acts)
+    grads = travel(grads_buf)
+    gathered, layer_acts, *grads = tie(exchange(spread), layer_acts, *grads)
     gathered = gathered.reshape(feat, feat)
     other = sibling(gathered)
-    act_grads = put_home(grads_buf, *early, (d_out, whole((rows, feat))), *late)
+    act_grads = put_home(grads_buf, *grads)
     out_square = (1, feat, feat)
     grad_self, grad_neigh = run(
         functools.partial(scale_kernel, scale),

time: 221 us -> 212 us (0.959)
  starting transfers between devices: 44.3 us -> 24.9 us
  waiting for transfers between devices: 35.1 us -> 41.8 us
  Pallas kernels: 34.5 us -> 38 us
    ppermute x9 -> x0, waiting for transfers between devices: 25.2 us -> none  [the longest x6 12.7 us: travel(): pieces.append(lax.ppermute(buf[s], 'layer', pairs))]
    ppermute x6 -> x9, waiting for transfers between devices: 4.78 us -> 25.8 us  [shift(): lax.ppermute(value, axis, [(i, (i + steps) % count) for i in range(count)])]
    ppermute x9 -> x0, starting transfers between devices: 17.2 us -> none  [the longest x6 13.4 us: travel(): pieces.append(lax.ppermute(buf[s], 'layer', pairs))]
    all_to_all x2, waiting for transfers between devices: 0.01 us -> 7.6 us  [exchange(): lax.all_to_all(value, 'node', split_axis=0, concat_axis=0, tiled=True)]
    pallas_call x14 -> x15, Pallas kernels: 34.5 us -> 38 us  [run(): pl.pallas_call(kernel, name=name, grid_spec=pltpu.PrefetchScalarGridSpec(...]
    all_to_all x2, starting transfers between devices: 11.4 us -> 7.89 us  [exchange(): lax.all_to_all(value, 'node', split_axis=0, concat_axis=0, tiled=True)]
    all_to_all x0 -> x1, starting transfers between devices: none -> 3.43 us  [body(): lax.all_to_all(sums, 'layer', split_axis=0, concat_axis=0, tiled=True)]
    all_to_all x0 -> x1, waiting for transfers between devices: none -> 3.34 us  [body(): lax.all_to_all(sums, 'layer', split_axis=0, concat_axis=0, tiled=True)]
  transfers between devices with their start and end apart: 25 -> 20, of which waited for: 15 -> 13; matrix products, arithmetic and copies ran while one was open for 0% -> 1% of each run, Pallas kernels for 6% -> 7%
where the time goes in v4:
time: 212 us; the launch traced here: 210 us
  blocking collectives  101 us (48%)
  waiting for transfers between devices  41.8 us (20%)
  Pallas kernels  38 us (18%)
  starting transfers between devices  24.9 us (12%)
    all_to_all x7, blocking collectives, exchange(): lax.all_to_all(value, 'node', split_axis=0, concat_axis=0, tiled=True)  101 us
    pallas_call x15, Pallas kernels, run(): pl.pallas_call(kernel, name=name, grid_spec=pltpu.PrefetchScalarGridSpec(...  38 us
    ppermute x9, waiting for transfers between devices, shift(): lax.ppermute(value, axis, [(i, (i + steps) % count) for i in range(count)])  25.8 us
    ppermute x9, starting transfers between devices, shift(): lax.ppermute(value, axis, [(i, (i + steps) % count) for i in range(count)])  11.6 us
    all_to_all x2, starting transfers between devices, exchange(): lax.all_to_all(value, 'node', split_axis=0, concat_axis=0, tiled=True)  7.89 us
    all_to_all x2, waiting for transfers between devices, exchange(): lax.all_to_all(value, 'node', split_axis=0, concat_axis=0, tiled=True)  7.6 us
    ppermute x8, waiting for transfers between devices, sibling(): return lax.ppermute(value, 'node', [(i, i ^ 1) for i in range(count)])  5.1 us
  transfers between devices with their start and end apart: 20, of which 13 were waited for; matrix products, arithmetic and copies ran while one was open for 1% of the time, Pallas kernels for 7%

profile of v4, /device:TPU:0, one launch (start us, length us, event | category | flops | bytes accessed | tf_op | source)
XLA Modules:
  0.0 209.7 jit_solution(8724404605411655675)
XLA Ops:
  0.6 1.3 broadcast_select_fusion
  1.9 3.2 %collective-permute-start.2 = (bf16[512,512]{1,0:T(8,128)(2,1)S(1)}, bf16[512,512]{1,0:T(8,128)(2,1)S(1)}, u32[]{:S(2)}, u32[]{:S(2)}) collective-permute-start(bf16[512,512]{1,0:T(8,128)(2,1)S(1)} %broadcast_select_fusion), channel_id=1, source_target_pairs={{0,64},{32,96},{64,0},{96,32},{1,65},{33,97},{65,1},{97,33},{2,66}... | collective-permute-start | bytes 1572872 | tf_op jit(solution)/shard_map/ppermute | solution.py:26
  5.1 1.1 collective-permute-start.1
  6.2 0.9 collective-permute-start
  7.9 2.6 %gather_rows.1 = (bf16[256,256]{1,0:T(8,128)(2,1)S(1)}, bf16[256,512]{1,0:T(8,128)(2,1)S(1)}, bf16[256,512]{1,0:T(8,128)(2,1)S(1)}, bf16[2,4,128,128]{3,2,1,0:T(8,128)(2,1)S(1)}, bf16[256,256]{1,0:T(8,128)(2,1)}) custom-call(s32[2]{0:T(128)S(1)} %pad_add_fusion.ids, s32[4,2,4]{2,1,0:T(2,128)S(1)} %bitcast.38, bf16[4,256,512]{2,1,0:T(8,128)(2,1)} %h_ref.1, ...), custom_call_target="tpu_custom_call" | custom-call | flops 100000000 | bytes 1000000 | tf_op jit(solution)/shard_map/gather_rows/pallas_call | solution.py:60
  10.5 17.1 %all_to_all.50 = bf16[32,8,512]{2,1,0:T(8,128)(2,1)S(1)} all-to-all(bf16[32,8,512]{2,1,0:T(8,128)(2,1)S(1)} %bitcast.57), channel_id=1, replica_groups=mesh['layer'=4,'node'=32] {'node'}, dimensions={0} | all-to-all | bytes 524288 | tf_op jit(solution)/shard_map/all_to_all | solution.py:35
  27.6 1.0 collective-permute-done.1.rest_4_
  29.1 1.4 collective-permute-done.3.rest_3_
  30.5 0.7 collective-permute-done.4.rest_5_
  31.3 0.7 collective-permute-done.5.rest_7_
  32.0 3.1 %layer_forward_0.1 = (bf16[256,512]{1,0:T(8,128)(2,1)S(1)}, f32[256,512]{1,0:T(8,128)S(1)}, bf16[256,512]{1,0:T(8,128)(2,1)S(1)}, bf16[256,512]{1,0:T(8,128)(2,1...) custom-call(s32[2]{0:T(128)S(1)} %pad_add_fusion.ids, ...), custom_call_target="tpu_custom_call" | custom-call | flops 600000000 | bytes 4000000 | tf_op jit(solution)/shard_map/layer_forward_0/pallas_call | solution.py:60
  35.1 17.1 %all_to_all.51 = bf16[32,8,512]{2,1,0:T(8,128)(2,1)S(1)} all-to-all(bf16[32,8,512]{2,1,0:T(8,128)(2,1)S(1)} %bitcast.55), channel_id=1, replica_groups=mesh['layer'=4,'node'=32] {'node'}, dimensions={0} | all-to-all | bytes 524288 | tf_op jit(solution)/shard_map/all_to_all | solution.py:35
  52.2 2.2 %layer_forward_1.1 = (bf16[256,512]{1,0:T(8,128)(2,1)S(1)}, f32[256,512]{1,0:T(8,128)S(1)}, bf16[256,512]{1,0:T(8,128)(2,1)S(1)}, bf16[256,512]{1,0:T(8,128)(2,1...) custom-call(s32[2]{0:T(128)S(1)} %pad_add_fusion.ids, ...), custom_call_target="tpu_custom_call", output_to_operand_aliasing={{4}: (15, {})} | custom-call | flops 600000000 | bytes 4000000 | tf_op jit(solution)/shard_map/layer_forward_1/pallas_call | solution.py:60
  54.4 12.5 %all_to_all.52 = bf16[32,8,512]{2,1,0:T(8,128)(2,1)S(1)} all-to-all(bf16[32,8,512]{2,1,0:T(8,128)(2,1)S(1)} %bitcast.56), channel_id=1, replica_groups=mesh['layer'=4,'node'=32] {'node'}, dimensions={0} | all-to-all | bytes 524288 | tf_op jit(solution)/shard_map/all_to_all | solution.py:35
  66.9 2.2 %layer_forward_2.1 = (bf16[256,512]{1,0:T(8,128)(2,1)S(1)}, f32[256,512]{1,0:T(8,128)S(1)}, bf16[256,512]{1,0:T(8,128)(2,1)S(1)}, bf16[256,512]{1,0:T(8,128)(2,1...) custom-call(s32[2]{0:T(128)S(1)} %pad_add_fusion.ids, ...), custom_call_target="tpu_custom_call", output_to_operand_aliasing={{4}: (15, {})} | custom-call | flops 600000000 | bytes 4000000 | tf_op jit(solution)/shard_map/layer_forward_2/pallas_call | solution.py:60
  69.1 12.5 %all_to_all.53 = bf16[32,8,512]{2,1,0:T(8,128)(2,1)S(1)} all-to-all(bf16[32,8,512]{2,1,0:T(8,128)(2,1)S(1)} %bitcast.53), channel_id=1, replica_groups=mesh['layer'=4,'node'=32] {'node'}, dimensions={0} | all-to-all | bytes 524288 | tf_op jit(solution)/shard_map/all_to_all | solution.py:35
  81.6 3.4 %top_layer.1 = (bf16[32,8,512]{2,1,0:T(8,128)(2,1)S(1)}, f32[256,512]{1,0:T(8,128)S(1)}, bf16[512,512]{1,0:T(8,128)(2,1)S(1)}, bf16[512,512]{1,0:T(8,128)(2,1)S(1)}, bf16[4,256,512]{2,1,0:T(8,128)(2,1)}) custom-call(s32[2]{0:T(128)S(1)} %pad_add_fusion.ids, s32[4,2,4]{2,1,0:T(2,128)S(1)} %bitcast.42, ...), custom_call_target="tpu_custom_call", output_to_operand_aliasing={{4}: (9, {})} | custom-call | flops 1000000000 | bytes 5000000 | tf_op jit(solution)/shard_map/top_layer/pallas_call | solution.py:60
  85.0 12.5 %all_to_all.54.ret_ref = bf16[32,8,512]{2,1,0:T(8,128)(2,1)S(1)} all-to-all(bf16[32,8,512]{2,1,0:T(8,128)(2,1)S(1)} %get-tuple-element.96), channel_id=1, replica_groups=mesh['layer'=4,'node'=32] {'node'}, dimensions={0} | all-to-all | bytes 524288 | tf_op jit(solution)/shard_map/all_to_all | solution.py:35
  97.7 2.4 %layer_backward_2.1 = (bf16[32,8,512]{2,1,0:T(8,128)(2,1)S(1)}, f32[256,512]{1,0:T(8,128)S(1)}, bf16[4,256,512]{2,1,0:T(8,128)(2,1)}, bf16[512,512]{1,0:T(8,128)(2,1)S(1)}, bf16[512,512]{1,0:T(8,128)(2,1)S(1)}) custom-call(s32[2]{0:T(128)S(1)} %pad_add_fusion.ids, s32[4,2,4]{2,1,0:T(2,128)S(1)} %bitcast.43, bf16[32,8,512]{2,1,0:T(8,128)(2,1)S(1)} %all_to_all.54.ret_ref, ...), custom_call_target="tpu_custom_call" | custom-call | flops 1000000000 | bytes 5000000 | tf_op jit(solution)/shard_map/layer_backward_2/pallas_call | solution.py:60
  100.2 12.3 %all_to_all.55.ret_ref = bf16[32,8,512]{2,1,0:T(8,128)(2,1)S(1)} all-to-all(bf16[32,8,512]{2,1,0:T(8,128)(2,1)S(1)} %get-tuple-element.104), channel_id=1, replica_groups=mesh['layer'=4,'node'=32] {'node'}, dimensions={0} | all-to-all | bytes 524288 | tf_op jit(solution)/shard_map/all_to_all | solution.py:35
  112.7 2.7 %layer_backward_1.1 = (bf16[32,24,512]{2,1,0:T(8,128)(2,1)S(1)}, f32[256,512]{1,0:T(8,128)S(1)}, bf16[4,256,512]{2,1,0:T(8,128)(2,1)}, bf16[512,512]{1,0:T(8,128)(2,1)S(1)}, bf16[512,512]{1,0:T(8,128)(2,1)S(1)}) custom-call(s32[2]{0:T(128)S(1)} %pad_add_fusion.ids, s32[4,2,4]{2,1,0:T(2,128)S(1)} %bitcast.44, ...), custom_call_target="tpu_custom_call", output_to_operand_aliasing={{2}: (12, {})} | custom-call | flops 1000000000 | bytes 5000000 | tf_op jit(solution)/shard_map/layer_backward_1/pallas_call | solution.py:60
  115.4 17.2 %all_to_all.56.ret_ref = bf16[32,24,512]{2,1,0:T(8,128)(2,1)S(1)} all-to-all(bf16[32,24,512]{2,1,0:T(8,128)(2,1)S(1)} %get-tuple-element.116), channel_id=1, replica_groups=mesh['layer'=4,'node'=32] {'node'}, dimensions={0} | all-to-all | bytes 1572864 | tf_op jit(solution)/shard_map/all_to_all | solution.py:35
  132.6 3.9 %layer_backward_0.1 = (bf16[32,56,512]{2,1,0:T(8,128)(2,1)}, f32[256,512]{1,0:T(8,128)}, bf16[4,256,512]{2,1,0:T(8,128)(2,1)}, bf16[512,512]{1,0:T(8,128)(2,1)S(...) custom-call(s32[2]{0:T(128)S(1)} %pad_add_fusion.ids, ...), custom_call_target="tpu_custom_call", output_to_operand_aliasing={{2}: (12, {})} | custom-call | flops 1000000000 | bytes 5000000 | tf_op jit(solution)/shard_map/layer_backward_0/pallas_call | solution.py:60
  137.3 1.4 collective-permute-done.9.recv_b
  138.7 0.7 collective-permute-done.8.recv_a
  139.5 1.8 join_rows.1
  141.3 4.0 %all-to-all-start.7 = ((bf16[32,56,512]{2,1,0:T(8,128)(2,1)}), bf16[32,56,512]{2,1,0:T(8,128)(2,1)S(1)}, u32[]{:S(2)}, u32[]{:S(2)}) async-start(bf16[32,56,512]{2,1,0:T(8,128)(2,1)} %join_rows.1), calls=%async_computation.7 | async-start | bytes 3670016 | tf_op jit(solution)/shard_map/all_to_all | solution.py:35
  145.3 1.2 slice_bitcast_fusion.3
  146.5 2.0 collective-permute-start.12
  148.5 0.9 collective-permute-start.11
  149.3 0.8 collective-permute-start.10
  150.2 9.9 %collective-permute-done.12.refs_3_ = bf16[256,512]{1,0:T(8,128)(2,1)S(1)} collective-permute-done((bf16[256,512]{1,0:T(8,128)(2,1)S(1)}, bf16[256,512]{1,0:T(8,128)(2,1)S(1)}, u32[]{:S(2)}, u32[]{:S(2)}) %collective-permute-start.12) | collective-permute-done | bytes 262176 | tf_op jit(solution)/shard_map/ppermute | solution.py:26
  160.1 3.7 %collective-permute-done.10.refs_1_ = bf16[256,512]{1,0:T(8,128)(2,1)S(1)} collective-permute-done((bf16[256,512]{1,0:T(8,128)(2,1)S(1)}, bf16[256,512]{1,0:T(8,128)(2,1)S(1)}, u32[]{:S(2)}, u32[]{:S(2)}) %collective-permute-start.10) | collective-permute-done | bytes 262176 | tf_op jit(solution)/shard_map/ppermute | solution.py:26
  163.8 7.6 %all-to-all-done.7.ret_ref = bf16[32,56,512]{2,1,0:T(8,128)(2,1)S(1)} async-done(((bf16[32,56,512]{2,1,0:T(8,128)(2,1)}), bf16[32,56,512]{2,1,0:T(8,128)(2,1)S(1)}, u32[]{:S(2)}, u32[]{:S(2)}) %all-to-all-start.7) | async-done | bytes 1835040 | tf_op jit(solution)/shard_map/all_to_all | solution.py:35
  171.4 2.2 %sum_chunks.1 = bf16[4,2,16,512]{3,2,1,0:T(8,128)(2,1)} custom-call(s32[2]{0:T(128)S(1)} %pad_add_fusion.ids, s32[4,2,4]{2,1,0:T(2,128)S(1)} %bitcast.47, bf16[32,56,512]{2,1,0:T(8,128)(2,1)S(1)} %all-to-all-done.7.ret_ref, bf16[2,16,512]{2,1,0:T(8,128)(2,1)} %get-tuple-element.134.c_3), custom_call_target="tpu_custom_call" | custom-call | bytes 1000000 | tf_op jit(solution)/shard_map/sum_chunks/pallas_call | solution.py:60
  173.6 3.4 %all-to-all-start.8 = ((bf16[4,2,16,512]{3,2,1,0:T(8,128)(2,1)}), bf16[4,2,16,512]{3,2,1,0:T(8,128)(2,1)S(1)}, u32[]{:S(2)}, u32[]{:S(2)}) async-start(bf16[4,2,16,512]{3,2,1,0:T(8,128)(2,1)} %sum_chunks.1), calls=%async_computation.8 | async-start | bytes 262144 | tf_op jit(solution)/shard_map/all_to_all | solution.py:547
  177.0 2.6 %input_grads.1.refs_0_ = bf16[4,256,512]{2,1,0:T(8,128)(2,1)} custom-call(s32[2]{0:T(128)S(1)} %pad_add_fusion.ids, s32[4,2,4]{2,1,0:T(2,128)S(1)} %bitcast.48, bf16[32,56,512]{2,1,0:T(8,128)(2,1)S(1)} %all-to-all-done.7.ret_ref, f32[256,512]{1,0:T(8,128)} %get-tuple-element.138.part_in, ...), custom_call_target="tpu_custom_call", output_to_operand_aliasing={{}: (5, {})} | custom-call | flops 100000000 | bytes 1000000 | tf_op jit(solution)/shard_map/input_grads/pallas_call | solution.py:60
  179.6 3.3 %all-to-all-done.8.sums_ref = bf16[4,2,16,512]{3,2,1,0:T(8,128)(2,1)S(1)} async-done(((bf16[4,2,16,512]{3,2,1,0:T(8,128)(2,1)}), bf16[4,2,16,512]{3,2,1,0:T(8,128)(2,1)S(1)}, u32[]{:S(2)}, u32[]{:S(2)}) %all-to-all-start.8) | async-done | bytes 131104 | tf_op jit(solution)/shard_map/all_to_all | solution.py:547
  183.0 1.4 sum_over_layer.1
  184.4 3.9 %all-to-all-start.9 = ((bf16[32,16,512]{2,1,0:T(8,128)(2,1)}), bf16[32,16,512]{2,1,0:T(8,128)(2,1)S(1)}, u32[]{:S(2)}, u32[]{:S(2)}) async-start(bf16[32,16,512]{2,1,0:T(8,128)(2,1)} %sum_over_layer.1), calls=%async_computation.9 | async-start | bytes 1048576 | tf_op jit(solution)/shard_map/all_to_all | solution.py:35
  188.4 1.2 collective-permute-start.15
  189.6 1.5 collective-permute-start.14
  191.1 2.6 %put_home.2 = bf16[1,4,256,512]{3,2,1,0:T(8,128)(2,1)} custom-call(s32[2]{0:T(128)S(1)} %pad_add_fusion.ids, s32[4,2,4]{2,1,0:T(2,128)S(1)} %bitcast.50, bf16[4,256,512]{2,1,0:T(8,128)(2,1)} %get-tuple-element.132.refs_0_, bf16[256,512]{1,0:T(8,128)(2,1)S(1)} %collective-permute-done.10.refs_1_, bf16[256,512]{1,0:T(8,128)(2,1)S(1)} %collective-permute-done.11.refs_2_, ...), custom_call_target="tpu_custom_call" | custom-call | bytes 2000000 | tf_op jit(solution)/shard_map/put_home/pallas_call | solution.py:60
  193.7 3.9 %collective-permute-done.15.refs_3_ = bf16[256,512]{1,0:T(8,128)(2,1)S(1)} collective-permute-done((bf16[256,512]{1,0:T(8,128)(2,1)S(1)}, bf16[256,512]{1,0:T(8,128)(2,1)S(1)}, u32[]{:S(2)}, u32[]{:S(2)}) %collective-permute-start.15) | collective-permute-done | bytes 262176 | tf_op jit(solution)/shard_map/ppermute | solution.py:26
  197.6 2.8 %collective-permute-done.14.refs_2_ = bf16[256,512]{1,0:T(8,128)(2,1)S(1)} collective-permute-done((bf16[256,512]{1,0:T(8,128)(2,1)S(1)}, bf16[256,512]{1,0:T(8,128)(2,1)S(1)}, u32[]{:S(2)}, u32[]{:S(2)}) %collective-permute-start.14) | collective-permute-done | bytes 262176 | tf_op jit(solution)/shard_map/ppermute | solution.py:26
  200.4 4.5 %collective-permute-done.13.refs_1_ = bf16[256,512]{1,0:T(8,128)(2,1)S(1)} collective-permute-done((bf16[256,512]{1,0:T(8,128)(2,1)S(1)}, bf16[256,512]{1,0:T(8,128)(2,1)S(1)}, u32[]{:S(2)}, u32[]{:S(2)}) %collective-permute-start.13) | collective-permute-done | bytes 262176 | tf_op jit(solution)/shard_map/ppermute | solution.py:26
  204.9 2.6 %put_home.3 = bf16[1,4,256,512]{3,2,1,0:T(8,128)(2,1)} custom-call(s32[2]{0:T(128)S(1)} %pad_add_fusion.ids, s32[4,2,4]{2,1,0:T(2,128)S(1)} %bitcast.51, bf16[4,256,512]{2,1,0:T(8,128)(2,1)} %input_grads.1.refs_0_, bf16[256,512]{1,0:T(8,128)(2,1)S(1)} %collective-permute-done.13.refs_1_, bf16[256,512]{1,0:T(8,128)(2,1)S(1)} %collective-permute-done.14.refs_2_, ...), custom_call_target="tpu_custom_call" | custom-call | bytes 2000000 | tf_op jit(solution)/shard_map/put_home/pallas_call | solution.py:60
  207.5 2.3 %scale_grads.1 = (f32[1,512,512]{2,1,0:T(8,128)}, f32[1,512,512]{2,1,0:T(8,128)}) custom-call(s32[2]{0:T(128)S(1)} %pad_add_fusion.ids, s32[4,2,4]{2,1,0:T(2,128)S(1)} %bitcast.52, bf16[512,512]{1,0:T(8,128)(2,1)S(1)} %bitcast.34, bf16[512,512]{1,0:T(8,128)(2,1)S(1)} %collective-permute-done.16.other_ref), custom_call_target="tpu_custom_call" | custom-call | bytes 3000000 | tf_op jit(solution)/shard_map/scale_grads/pallas_call | solution.py:60
  (30 shorter events, 2.9 us)
Async XLA Ops:
  1.9 25.7 %collective-permute-start.2 = (bf16[512,512]{1,0:T(8,128)(2,1)S(1)}, bf16[512,512]{1,0:T(8,128)(2,1)S(1)}, u32[]{:S(2)}, u32[]{:S(2)}) collective-permute-start(bf16[512,512]{1,0:T(8,128)(2,1)S(1)} %broadcast_select_fusion), channel_id=1, source_target_pairs={{0,64},{32,96},{64,0},{96,32},{1,65},{33,97},{65,1},{97,33},{2,66}... | collective-permute-start | bytes 1572872 | tf_op jit(solution)/shard_map/ppermute | solution.py:26
  5.1 23.5 %collective-permute-start.1 = (bf16[512,512]{1,0:T(8,128)(2,1)S(1)}, bf16[512,512]{1,0:T(8,128)(2,1)S(1)}, u32[]{:S(2)}, u32[]{:S(2)}) collective-permute-start(bf16[512,512]{1,0:T(8,128)(2,1)S(1)} %broadcast_select_fusion), channel_id=1, source_target_pairs={{0,96},{32,0},{64,32},{96,64},{1,97},{33,1},{65,33},{97,65},{2,98}... | collective-permute-start | bytes 1572872 | tf_op jit(solution)/shard_map/ppermute | solution.py:26
  6.2 22.4 %collective-permute-start = (bf16[512,512]{1,0:T(8,128)(2,1)S(1)}, bf16[512,512]{1,0:T(8,128)(2,1)S(1)}, u32[]{:S(2)}, u32[]{:S(2)}) collective-permute-start(bf16[512,512]{1,0:T(8,128)(2,1)S(1)} %broadcast_select_fusion), channel_id=1, source_target_pairs={{0,32},{32,64},{64,96},{96,0},{1,33},{33,65},{65,97},{97,1},{2,34}... | collective-permute-start | bytes 1572872 | tf_op jit(solution)/shard_map/ppermute | solution.py:26
  7.2 0.7 copy-start
  28.6 1.9 collective-permute-start.3
  28.6 2.7 %collective-permute-start.4 = (bf16[512,512]{1,0:T(8,128)(2,1)S(1)}, bf16[512,512]{1,0:T(8,128)(2,1)S(1)}, u32[]{:S(2)}, u32[]{:S(2)}) collective-permute-start(bf16[512,512]{1,0:T(8,128)(2,1)S(1)} %collective-permute-done.1.rest_4_), channel_id=1, source_target_pairs={{0,1},{1,0},{2,3},{3,2},{4,5},{5,4},{6,7},{7,6},{8,9},{9,8},{10,11... | collective-permute-start | bytes 1572872 | tf_op jit(solution)/shard_map/ppermute | solution.py:31
  29.1 2.9 %collective-permute-start.5 = (bf16[512,512]{1,0:T(8,128)(2,1)S(1)}, bf16[512,512]{1,0:T(8,128)(2,1)S(1)}, u32[]{:S(2)}, u32[]{:S(2)}) collective-permute-start(bf16[512,512]{1,0:T(8,128)(2,1)S(1)} %collective-permute-done.2.rest_6_), channel_id=1, source_target_pairs={{0,1},{1,0},{2,3},{3,2},{4,5},{5,4},{6,7},{7,6},{8,9},{9,8},{10,11... | collective-permute-start | bytes 1572872 | tf_op jit(solution)/shard_map/ppermute | solution.py:31
  66.9 14.7 %copy-start.2 = (bf16[512,172]{0,1:T(8,128)(2,1)S(1)}, bf16[512,172]{0,1:T(8,128)(2,1)}, u32[]{:S(2)}) copy-start(bf16[512,172]{0,1:T(8,128)(2,1)} %param.13) | copy-start | bytes 528388
  66.9 14.7 %copy-start.3 = (s32[4,256]{1,0:T(4,128)S(1)}, s32[4,256]{1,0:T(4,128)}, u32[]{:S(2)}) copy-start(s32[4,256]{1,0:T(4,128)} %lab_ref.1) | copy-start | bytes 12292
  66.9 14.7 %copy-start.4 = (s32[4,256]{1,0:T(4,128)S(1)}, s32[4,256]{1,0:T(4,128)}, u32[]{:S(2)}) copy-start(s32[4,256]{1,0:T(4,128)} %mask_ref.1) | copy-start | bytes 12292
  97.4 2.7 %collective-permute-start.6 = (bf16[512,512]{1,0:T(8,128)(2,1)S(1)}, bf16[512,512]{1,0:T(8,128)(2,1)S(1)}, u32[]{:S(2)}, u32[]{:S(2)}) collective-permute-start(bf16[512,512]{1,0:T(8,128)(2,1)S(1)} %get-tuple-element.103), channel_id=1, source_target_pairs={{0,1},{1,0},{2,3},{3,2},{4,5},{5,4},{6,7},{7,6},{8,9},{9,8},{10,11... | collective-permute-start | bytes 1572872 | tf_op jit(solution)/shard_map/ppermute | solution.py:31
  112.4 3.0 %collective-permute-start.7 = (bf16[512,512]{1,0:T(8,128)(2,1)S(1)}, bf16[512,512]{1,0:T(8,128)(2,1)S(1)}, u32[]{:S(2)}, u32[]{:S(2)}) collective-permute-start(bf16[512,512]{1,0:T(8,128)(2,1)S(1)} %get-tuple-element.115), channel_id=1, source_target_pairs={{0,1},{1,0},{2,3},{3,2},{4,5},{5,4},{6,7},{7,6},{8,9},{9,8},{10,11... | collective-permute-start | bytes 1572872 | tf_op jit(solution)/shard_map/ppermute | solution.py:31
  136.5 2.3 %collective-permute-start.9 = (bf16[512,512]{1,0:T(8,128)(2,1)S(1)}, bf16[512,512]{1,0:T(8,128)(2,1)S(1)}, u32[]{:S(2)}, u32[]{:S(2)}) collective-permute-start(bf16[512,512]{1,0:T(8,128)(2,1)S(1)} %get-tuple-element.128), channel_id=1, source_target_pairs={{0,1},{1,0},{2,3},{3,2},{4,5},{5,4},{6,7},{7,6},{8,9},{9,8},{10,11... | collective-permute-start | bytes 1572872 | tf_op jit(solution)/shard_map/ppermute | solution.py:31
  137.2 2.3 %collective-permute-start.8 = (bf16[512,512]{1,0:T(8,128)(2,1)S(1)}, bf16[512,512]{1,0:T(8,128)(2,1)S(1)}, u32[]{:S(2)}, u32[]{:S(2)}) collective-permute-start(bf16[512,512]{1,0:T(8,128)(2,1)S(1)} %get-tuple-element.118), channel_id=1, source_target_pairs={{0,1},{1,0},{2,3},{3,2},{4,5},{5,4},{6,7},{7,6},{8,9},{9,8},{10,11... | collective-permute-start | bytes 1572872 | tf_op jit(solution)/shard_map/ppermute | solution.py:31
  141.3 30.0 %copy-start.1 = (s32[4,1,2,4]{3,2,1,0:T(2,128)S(1)}, s32[4,1,2,4]{3,2,1,0:T(2,128)}, u32[]{:S(2)}) copy-start(s32[4,1,2,4]{3,2,1,0:T(2,128)} %param.16) | copy-start | bytes 388
  141.3 30.0 %all-to-all-start.7 = ((bf16[32,56,512]{2,1,0:T(8,128)(2,1)}), bf16[32,56,512]{2,1,0:T(8,128)(2,1)S(1)}, u32[]{:S(2)}, u32[]{:S(2)}) async-start(bf16[32,56,512]{2,1,0:T(8,128)(2,1)} %join_rows.1), calls=%async_computation.7 | async-start | bytes 3670016 | tf_op jit(solution)/shard_map/all_to_all | solution.py:35
  146.5 13.6 %collective-permute-start.12 = (bf16[256,512]{1,0:T(8,128)(2,1)S(1)}, bf16[256,512]{1,0:T(8,128)(2,1)S(1)}, u32[]{:S(2)}, u32[]{:S(2)}) collective-permute-start(bf16[256,512]{1,0:T(8,128)(2,1)S(1)} %get-tuple-element.151), channel_id=1, source_target_pairs={{0,96},{32,0},{64,32},{96,64},{1,97},{33,1},{65,33},{97,65},{2,98}... | collective-permute-start | bytes 786440 | tf_op jit(solution)/shard_map/ppermute | solution.py:26
  148.5 11.6 %collective-permute-start.11 = (bf16[256,512]{1,0:T(8,128)(2,1)S(1)}, bf16[256,512]{1,0:T(8,128)(2,1)S(1)}, u32[]{:S(2)}, u32[]{:S(2)}) collective-permute-start(bf16[256,512]{1,0:T(8,128)(2,1)S(1)} %get-tuple-element.152), channel_id=1, source_target_pairs={{0,64},{32,96},{64,0},{96,32},{1,65},{33,97},{65,1},{97,33},{2,66}... | collective-permute-start | bytes 786440 | tf_op jit(solution)/shard_map/ppermute | solution.py:26
  149.3 14.4 %collective-permute-start.10 = (bf16[256,512]{1,0:T(8,128)(2,1)S(1)}, bf16[256,512]{1,0:T(8,128)(2,1)S(1)}, u32[]{:S(2)}, u32[]{:S(2)}) collective-permute-start(bf16[256,512]{1,0:T(8,128)(2,1)S(1)} %get-tuple-element.153), channel_id=1, source_target_pairs={{0,32},{32,64},{64,96},{96,0},{1,33},{33,65},{65,97},{97,1},{2,34}... | collective-permute-start | bytes 786440 | tf_op jit(solution)/shard_map/ppermute | solution.py:26
  173.6 9.4 %all-to-all-start.8 = ((bf16[4,2,16,512]{3,2,1,0:T(8,128)(2,1)}), bf16[4,2,16,512]{3,2,1,0:T(8,128)(2,1)S(1)}, u32[]{:S(2)}, u32[]{:S(2)}) async-start(bf16[4,2,16,512]{3,2,1,0:T(8,128)(2,1)} %sum_chunks.1), calls=%async_computation.8 | async-start | bytes 262144 | tf_op jit(solution)/shard_map/all_to_all | solution.py:547
  179.6 8.7 %copy-start.5 = (bf16[4,256,512]{2,1,0:T(8,128)(2,1)S(1)}, bf16[4,256,512]{2,1,0:T(8,128)(2,1)}, u32[]{:S(2)}) copy-start(bf16[4,256,512]{2,1,0:T(8,128)(2,1)} %input_grads.1.refs_0_) | copy-start | bytes 3145732
  184.4 20.4 %all-to-all-start.9 = ((bf16[32,16,512]{2,1,0:T(8,128)(2,1)}), bf16[32,16,512]{2,1,0:T(8,128)(2,1)S(1)}, u32[]{:S(2)}, u32[]{:S(2)}) async-start(bf16[32,16,512]{2,1,0:T(8,128)(2,1)} %sum_over_layer.1), calls=%async_computation.9 | async-start | bytes 1048576 | tf_op jit(solution)/shard_map/all_to_all | solution.py:35
  188.4 9.2 %collective-permute-start.15 = (bf16[256,512]{1,0:T(8,128)(2,1)S(1)}, bf16[256,512]{1,0:T(8,128)(2,1)S(1)}, u32[]{:S(2)}, u32[]{:S(2)}) collective-permute-start(bf16[256,512]{1,0:T(8,128)(2,1)S(1)} %get-tuple-element.148), channel_id=1, source_target_pairs={{0,96},{32,0},{64,32},{96,64},{1,97},{33,1},{65,33},{97,65},{2,98}... | collective-permute-start | bytes 786440 | tf_op jit(solution)/shard_map/ppermute | solution.py:26
  189.6 10.7 %collective-permute-start.14 = (bf16[256,512]{1,0:T(8,128)(2,1)S(1)}, bf16[256,512]{1,0:T(8,128)(2,1)S(1)}, u32[]{:S(2)}, u32[]{:S(2)}) collective-permute-start(bf16[256,512]{1,0:T(8,128)(2,1)S(1)} %get-tuple-element.149), channel_id=1, source_target_pairs={{0,64},{32,96},{64,0},{96,32},{1,65},{33,97},{65,1},{97,33},{2,66}... | collective-permute-start | bytes 786440 | tf_op jit(solution)/shard_map/ppermute | solution.py:26
  191.1 13.8 %collective-permute-start.13 = (bf16[256,512]{1,0:T(8,128)(2,1)S(1)}, bf16[256,512]{1,0:T(8,128)(2,1)S(1)}, u32[]{:S(2)}, u32[]{:S(2)}) collective-permute-start(bf16[256,512]{1,0:T(8,128)(2,1)S(1)} %get-tuple-element.150), channel_id=1, source_target_pairs={{0,32},{32,64},{64,96},{96,0},{1,33},{33,65},{65,97},{97,1},{2,34}... | collective-permute-start | bytes 786440 | tf_op jit(solution)/shard_map/ppermute | solution.py:26
  204.8 2.6 %collective-permute-start.16 = (bf16[512,512]{1,0:T(8,128)(2,1)S(1)}, bf16[512,512]{1,0:T(8,128)(2,1)S(1)}, u32[]{:S(2)}, u32[]{:S(2)}) collective-permute-start(bf16[512,512]{1,0:T(8,128)(2,1)S(1)} %bitcast.33), channel_id=1, source_target_pairs={{0,1},{1,0},{2,3},{3,2},{4,5},{5,4},{6,7},{7,6},{8,9},{9,8},{10,11... | collective-permute-start | bytes 1572872 | tf_op jit(solution)/shard_map/ppermute | solution.py:31

commit v5 on v4

--- a/solution.py
+++ b/solution.py
@@ -249,42 +249,66 @@
     return total
 
 
-def backward_kernel(layer, carry, ids, cols, ret_ref, part_in, pre_ref, h_ref, agg_ref, *rest):
-    (vals_ref, pick_ref, w_ref), rest = rest[:3], rest[3:]
-    if carry:
-        keep_in, recv_in, rest = rest[0], rest[1], rest[2:]
-    if layer < 2:
-        rest = rest[1:]
-    out_ref, part_ref, buf_ref, keep_ref, send_ref, *rest = rest
-    if not layer:
-        *rest, local, local_sem = rest
-    *chunk, dout_ref, d_ext, buf_sem = rest
+def slope_math(ids, layer, ret_ref, part_in, pre_ref, pick_ref, dout_ref, buf_ref, buf_sem):
     rows, feat = part_in.shape
-    peers = out_ref.shape[0]
-    slots = rows // peers
-    returned = ret_ref[:, 0:slots, :].reshape(rows, feat)
+    returned = ret_ref[:, 0 : rows // ret_ref.shape[0], :].reshape(rows, feat)
     d_out = (part_in[...] + dot(pick_ref[...], returned, TN)).astype(BF)
     dout_ref[...] = d_out
     copy = to_slot(dout_ref, layer + 1, ids, buf_ref, buf_sem)
     copy.start()
     pre = pre_ref[...]
     sig = sigmoid(pre)
-    d_pre = (d_out.astype(F32) * (sig * (1.0 + pre * (1.0 - sig)))).astype(BF)
+    return (d_out.astype(F32) * (sig * (1.0 + pre * (1.0 - sig)))).astype(BF), copy
+
+
+def backward_kernel(layer, carry, ids, cols, ret_ref, part_in, pre_ref, h_ref, agg_ref, *rest):
+    (vals_ref, pick_ref, w_ref), rest = rest[:3], rest[3:]
+    if carry:
+        keep_in, recv_in, rest = rest[0], rest[1], rest[3:]
+    out_ref, part_ref, buf_ref, keep_ref, send_ref, dout_ref, d_ext, buf_sem = rest
+    rows, feat = part_in.shape
+    d_pre, copy = slope_math(
+        ids, layer, ret_ref, part_in, pre_ref, pick_ref, dout_ref, buf_ref, buf_sem
+    )
     back = backward_math(ids, cols, d_pre, vals_ref, w_ref, d_ext)
-    target = out_ref if layer else local
-    target[:, 0:slots, :] = d_ext[rows : 2 * rows, :].astype(BF).reshape(peers, slots, feat)
+    peers, slots = out_ref.shape[0], rows // out_ref.shape[0]
+    out_ref[:, 0:slots, :] = d_ext[rows : 2 * rows, :].astype(BF).reshape(peers, slots, feat)
     if carry:
-        put_carry(keep_in, recv_in, target, slots)
-    if not layer:
-        away = pltpu.make_async_copy(local, out_ref.at[:, pl.ds(0, local.shape[1]), :], local_sem)
-        away.start()
+        put_carry(keep_in, recv_in, out_ref, slots)
     part_ref[...] = back + d_ext[0:rows, :]
     weight_partials(ids, h_ref, agg_ref[...], d_pre, keep_ref, send_ref)
-    if chunk:
-        chunk[0][...] = chunk_sum(ret_ref[:, slots:, :]).astype(BF)
     copy.wait()
-    if not layer:
-        away.wait()
+
+
+def last_slope_kernel(
+    ids, cols, ret_ref, part_in, pre_ref, h_ref, agg_ref, pick_ref, buf_in,
+    dpre_ref, buf_ref, keep_ref, send_ref, chunk_ref, dout_ref, buf_sem,
+):
+    d_pre, copy = slope_math(
+        ids, 0, ret_ref, part_in, pre_ref, pick_ref, dout_ref, buf_ref, buf_sem
+    )
+    dpre_ref[...] = d_pre
+    weight_partials(ids, h_ref, agg_ref[...], d_pre, keep_ref, send_ref)
+    slots = part_in.shape[0] // ret_ref.shape[0]
+    chunk_ref[...] = chunk_sum(ret_ref[:, slots:, :]).astype(BF)
+    copy.wait()
+
+
+def last_spread_kernel(
+    ids, cols, dpre_ref, vals_ref, w_ref, keep_a, recv_a, keep_b, recv_b,
+    out_ref, part_ref, d_ext, local, sem,
+):
+    rows, feat = dpre_ref.shape
+    peers, used = local.shape[0], local.shape[1]
+    slots, size = rows // peers, keep_a.shape[0] // peers
+    put_carry(keep_a, recv_a, local, slots)
+    put_carry(keep_b, recv_b, local, slots + size)
+    back = backward_math(ids, cols, dpre_ref[...], vals_ref, w_ref, d_ext)
+    local[:, 0:slots, :] = d_ext[rows : 2 * rows, :].astype(BF).reshape(peers, slots, feat)
+    away = pltpu.make_async_copy(local, out_ref.at[:, pl.ds(0, used), :], sem)
+    away.start()
+    part_ref[...] = back + d_ext[0:rows, :]
+    away.wait()
 
 
 def put_carry(keep_ref, recv_ref, out_ref, first):
@@ -294,12 +318,11 @@
     out_ref[:, first : first + size, :] = total.reshape(peers, size, feat)
 
 
-def join_kernel(ids, cols, keep_a, recv_a, keep_b, recv_b, buf_in, out_ref, local, sem):
-    size = local.shape[1] // 2
-    first = out_ref.shape[1] - 2 * size
-    put_carry(keep_a, recv_a, local, 0)
-    put_carry(keep_b, recv_b, local, size)
-    copy = pltpu.make_async_copy(local, out_ref.at[:, pl.ds(first, 2 * size), :], sem)
+def join_kernel(ids, cols, keep_ref, recv_ref, buf_in, out_ref, local, sem):
+    size = local.shape[1]
+    put_carry(keep_ref, recv_ref, local, 0)
+    first = out_ref.shape[1] - size
+    copy = pltpu.make_async_copy(local, out_ref.at[:, pl.ds(first, size), :], sem)
     copy.start()
     copy.wait()
 
@@ -331,7 +354,13 @@
         out_ref[n : n + 2] = total
 
 
-def scale_kernel(scale, ids, cols, mine_ref, other_ref, self_ref, neigh_ref):
+def final_kernel(scale, ids, cols, mine_ref, other_ref, own, one, two, three, late, home_ref, self_ref, neigh_ref):
+    home_kernel(ids, cols, own, one, two, three, home_ref)
+
+    @pl.when(ids[0] == 0)
+    def _():
+        home_ref[0, 2] = late[...]
+
     mine = mine_ref[...].astype(F32) * scale
     other = other_ref[...].astype(F32) * scale
 
@@ -478,11 +507,11 @@
 
     chunk_rows = feat // peers
     pairs, grads_buf = [], None
-    for layer in range(top - 1, -1, -1):
+    for layer in range(top - 1, 0, -1):
         returned, send = tie(exchange(remote), send)
         pairs.append((keep, sibling(send)))
         carry = layer < top - 1
-        width = slots + chunk_rows * (carry + 2 * (layer == 0))
+        width = slots + chunk_rows * carry
         ins = [
             returned,
             part,
@@ -493,59 +522,76 @@
             pick,
             weights[layer],
         ]
+        aliases = None
         if carry:
-            ins += pairs[-2]
-        aliases = None
-        if grads_buf is not None:
-            ins.append((grads_buf, FAR))
+            ins += [*pairs[-2], (grads_buf, FAR)]
             aliases = {len(ins) - 1: 2}
-        last = far_block if layer == 0 else near
-        operand = near((peers, width, feat))
-        scratch = [pltpu.VMEM((rows, feat), BF), d_ext_scratch, buf_sem]
-        if layer == 0:
-            operand = (pltpu.HBM((peers, width, feat), BF), FAR)
-            scratch += [pltpu.VMEM((peers, slots + chunk_rows, feat), BF), buf_sem]
-        outs = [operand, last((rows, feat), F32), stack, square, square]
-        if layer == 0:
-            outs.append(far_block((2, chunk_rows, feat)))
-        remote, part, grads_buf, keep, send, *c_3 = run(
+        remote, part, grads_buf, keep, send = run(
             functools.partial(backward_kernel, layer, carry),
             f"layer_backward_{layer}",
             scalars,
             ins,
-            outs,
-            scratch,
+            [near((peers, width, feat)), wide, stack, square, square],
+            [pltpu.VMEM((rows, feat), BF), d_ext_scratch, buf_sem],
             aliases,
             flops=10**9,
             moved=5 * 10**6,
         )
-        if layer:
-            remote, recv = tie(remote, pairs[-1][1])
-            pairs[-1] = (pairs[-1][0], recv)
-
+        remote, recv = tie(remote, pairs[-1][1])
+        pairs[-1] = (pairs[-1][0], recv)
+
+    returned, send = tie(exchange(remote), send)
+    recv_1, keep_1 = sibling(send), keep
+    d_pre, grads_buf, keep, send, c_3 = run(
+        last_slope_kernel,
+        "last_slope",
+        scalars,
+        [returned, part, pres[0], hidden[0], aggs[0], pick, (grads_buf, FAR)],
+        [act, stack, square, square, far_block((2, chunk_rows, feat))],
+        [pltpu.VMEM((rows, feat), BF), buf_sem],
+        {6: 1},
+        flops=4 * 10**8,
+        moved=3 * 10**6,
+    )
+    d_pre, recv_1, send = tie(d_pre, recv_1, send)
+    recv = sibling(send)
+    width = slots + 3 * chunk_rows
+    operand = (pltpu.HBM((peers, width, feat), BF), FAR)
+    remote, part = run(
+        last_spread_kernel,
+        "last_spread",
+        scalars,
+        [d_pre, vals, weights[0], *pairs[-1], keep_1, recv_1],
+        [operand, far_block((rows, feat), F32)],
+        [d_ext_scratch, pltpu.VMEM((peers, width - chunk_rows, feat), BF), buf_sem],
+        flops=5 * 10**8,
+        moved=4 * 10**6,
+    )
+    remote, recv = tie(remote, recv)
     joined = run(
         join_kernel,
         "join_rows",
         scalars,
-        [*pairs[-1], keep, sibling(send), (remote, FAR)],
-        [(pltpu.HBM((peers, slots + 3 * chunk_rows, feat), BF), FAR)],
-        [pltpu.VMEM((peers, 2 * chunk_rows, feat), BF), buf_sem],
-        aliases={4: 0},
-        moved=3 * 10**6,
+        [keep, recv, (remote, FAR)],
+        [operand],
+        [pltpu.VMEM((peers, chunk_rows, feat), BF), buf_sem],
+        aliases={2: 0},
+        moved=2 * 10**6,
     )[0]
-    joined, acts_buf = tie(joined, acts_buf)
+    joined, acts_buf, grads_buf = tie(joined, acts_buf, grads_buf)
     acts = travel(acts_buf)
-    returned, *acts = tie(exchange(joined), *acts)
+    early = lax.ppermute(grads_buf[2], "layer", [(0, 2), (1, 3), (3, 1)])
+    returned, early, *acts = tie(exchange(joined), early, *acts)
     sums = run(
         chunk_kernel,
         "sum_chunks",
         scalars,
-        [returned, (c_3[0], whole(c_3[0].shape))],
+        [returned, (c_3, whole(c_3.shape))],
         [far_block((spans, 2, chunk_rows, feat))],
         moved=10**6,
     )[0]
     sums = lax.all_to_all(sums, "layer", split_axis=0, concat_axis=0, tiled=True)
-    grads_buf = run(
+    grads_buf, d_out = run(
         end_kernel,
         "input_grads",
         scalars,
@@ -555,12 +601,13 @@
             (pick_far, whole(pick_far.shape)),
             (grads_buf, FAR),
         ],
-        [stack],
-        [pltpu.VMEM((rows, feat), BF), buf_sem],
+        [stack, far_block((rows, feat))],
+        [buf_sem],
         {3: 0},
         flops=10**8,
         moved=10**6,
-    )[0]
+    )
+    sums, grads_buf, d_out = tie(sums, grads_buf, d_out)
     spread = run(
         layer_sum_kernel,
         "sum_over_layer",
@@ -570,19 +617,26 @@
         moved=10**6,
     )[0]
     layer_acts = put_home(acts_buf, *acts)
-    grads = travel(grads_buf)
-    gathered, layer_acts, *grads = tie(exchange(spread), layer_acts, *grads)
+    grads = [shift(grads_buf[s], "layer", s) for s in (1, 3)]
+    late = lax.ppermute(d_out, "layer", [(2, 0)])
+    gathered, layer_acts, late, *grads = tie(exchange(spread), layer_acts, late, *grads)
     gathered = gathered.reshape(feat, feat)
-    other = sibling(gathered)
-    act_grads = put_home(grads_buf, *grads)
-    out_square = (1, feat, feat)
-    grad_self, grad_neigh = run(
-        functools.partial(scale_kernel, scale),
-        "scale_grads",
-        scalars,
-        [gathered, other],
-        [(pltpu.HBM(out_square, F32), whole(out_square))] * 2,
-        moved=3 * 10**6,
+    out_square, shape = (1, feat, feat), (1, spans, rows, feat)
+    act_grads, grad_self, grad_neigh = run(
+        functools.partial(final_kernel, scale),
+        "final_outputs",
+        scalars,
+        [
+            gathered,
+            sibling(gathered),
+            (grads_buf, pl.BlockSpec((None, rows, feat), lambda i, ids, cols: (0, 0, 0))),
+            grads[0],
+            early,
+            grads[1],
+            late,
+        ],
+        [far_block(shape), far_block(out_square, F32), far_block(out_square, F32)],
+        moved=6 * 10**6,
     )
     return (layer_acts, act_grads, grad_self, grad_neigh)
 

time: 212 us -> 215 us (1.014)
  starting transfers between devices: 24.9 us -> 30.2 us
  waiting for transfers between devices: 41.8 us -> 37.2 us
    ppermute x0 -> x2, waiting for transfers between devices: none -> 9.5 us  [the longest x1 6.74 us: body(): late = lax.ppermute(d_out, 'layer', [(2, 0)])]
    ppermute x9 -> x8, waiting for transfers between devices: 25.8 us -> 16.8 us  [shift(): lax.ppermute(value, axis, [(i, (i + steps) % count) for i in range(count)])]
    ppermute x0 -> x2, starting transfers between devices: none -> 5.38 us  [the longest x1 4.08 us: body(): early = lax.ppermute(grads_buf[2], 'layer', [(0, 2), (1, 3), (3, 1)])]
    all_to_all x2, waiting for transfers between devices: 7.6 us -> 3.47 us  [exchange(): lax.all_to_all(value, 'node', split_axis=0, concat_axis=0, tiled=True)]
    ppermute x9 -> x8, starting transfers between devices: 11.6 us -> 10 us  [shift(): lax.ppermute(value, axis, [(i, (i + steps) % count) for i in range(count)])]
  transfers between devices with their start and end apart: 20 -> 21, of which waited for: 13 -> 12; matrix products, arithmetic and copies ran while one was open for 1% -> 1% of each run, Pallas kernels for 7% -> 9%
where the time goes in v5:
time: 215 us; the launch traced here: 213 us
  blocking collectives  101 us (47%)
  Pallas kernels  39.7 us (18%)
  waiting for transfers between devices  37.2 us (17%)
  starting transfers between devices  30.2 us (14%)
  local copies, waits for them, and re-layouts  2.88 us (1%)
    all_to_all x7, blocking collectives, exchange(): lax.all_to_all(value, 'node', split_axis=0, concat_axis=0, tiled=True)  101 us
    pallas_call x15, Pallas kernels, run(): pl.pallas_call(kernel, name=name, grid_spec=pltpu.PrefetchScalarGridSpec(...  39.7 us
    ppermute x8, waiting for transfers between devices, shift(): lax.ppermute(value, axis, [(i, (i + steps) % count) for i in range(count)])  16.8 us
    ppermute x8, starting transfers between devices, shift(): lax.ppermute(value, axis, [(i, (i + steps) % count) for i in range(count)])  10 us
    all_to_all x2, starting transfers between devices, exchange(): lax.all_to_all(value, 'node', split_axis=0, concat_axis=0, tiled=True)  9.41 us
    ppermute x1, waiting for transfers between devices, body(): late = lax.ppermute(d_out, 'layer', [(2, 0)])  6.74 us
    ppermute x8, waiting for transfers between devices, sibling(): return lax.ppermute(value, 'node', [(i, i ^ 1) for i in range(count)])  4.79 us
  transfers between devices with their start and end apart: 21, of which 12 were waited for; matrix products, arithmetic and copies ran while one was open for 1% of the time, Pallas kernels for 9%

profile of v5, /device:TPU:0, one launch (start us, length us, event | category | flops | bytes accessed | tf_op | source)
XLA Modules:
  0.0 213.0 jit_solution(16456996421213446504)
XLA Ops:
  0.6 1.3 broadcast_select_fusion
  1.9 3.2 %collective-permute-start.2 = (bf16[512,512]{1,0:T(8,128)(2,1)S(1)}, bf16[512,512]{1,0:T(8,128)(2,1)S(1)}, u32[]{:S(2)}, u32[]{:S(2)}) collective-permute-start(bf16[512,512]{1,0:T(8,128)(2,1)S(1)} %broadcast_select_fusion), channel_id=1, source_target_pairs={{0,64},{32,96},{64,0},{96,32},{1,65},{33,97},{65,1},{97,33},{2,66}... | collective-permute-start | bytes 1572872 | tf_op jit(solution)/shard_map/ppermute | solution.py:26
  5.1 1.1 collective-permute-start.1
  6.2 0.9 collective-permute-start
  7.9 2.6 %gather_rows.1 = (bf16[256,256]{1,0:T(8,128)(2,1)S(1)}, bf16[256,512]{1,0:T(8,128)(2,1)S(1)}, bf16[256,512]{1,0:T(8,128)(2,1)S(1)}, bf16[2,4,128,128]{3,2,1,0:T(8,128)(2,1)S(1)}, bf16[256,256]{1,0:T(8,128)(2,1)}) custom-call(s32[2]{0:T(128)S(1)} %pad_add_fusion.ids, s32[4,2,4]{2,1,0:T(2,128)S(1)} %bitcast.38, bf16[4,256,512]{2,1,0:T(8,128)(2,1)} %h_ref.1, ...), custom_call_target="tpu_custom_call" | custom-call | flops 100000000 | bytes 1000000 | tf_op jit(solution)/shard_map/gather_rows/pallas_call | solution.py:60
  10.5 17.1 %all_to_all.50 = bf16[32,8,512]{2,1,0:T(8,128)(2,1)S(1)} all-to-all(bf16[32,8,512]{2,1,0:T(8,128)(2,1)S(1)} %bitcast.57), channel_id=1, replica_groups=mesh['layer'=4,'node'=32] {'node'}, dimensions={0} | all-to-all | bytes 524288 | tf_op jit(solution)/shard_map/all_to_all | solution.py:35
  27.6 1.0 collective-permute-done.1.rest_4_
  29.1 1.4 collective-permute-done.3.rest_3_
  30.5 0.7 collective-permute-done.4.rest_5_
  31.3 0.7 collective-permute-done.5.rest_7_
  32.0 3.1 %layer_forward_0.1 = (bf16[256,512]{1,0:T(8,128)(2,1)S(1)}, f32[256,512]{1,0:T(8,128)S(1)}, bf16[256,512]{1,0:T(8,128)(2,1)S(1)}, bf16[256,512]{1,0:T(8,128)(2,1...) custom-call(s32[2]{0:T(128)S(1)} %pad_add_fusion.ids, ...), custom_call_target="tpu_custom_call" | custom-call | flops 600000000 | bytes 4000000 | tf_op jit(solution)/shard_map/layer_forward_0/pallas_call | solution.py:60
  35.1 17.1 %all_to_all.51 = bf16[32,8,512]{2,1,0:T(8,128)(2,1)S(1)} all-to-all(bf16[32,8,512]{2,1,0:T(8,128)(2,1)S(1)} %bitcast.55), channel_id=1, replica_groups=mesh['layer'=4,'node'=32] {'node'}, dimensions={0} | all-to-all | bytes 524288 | tf_op jit(solution)/shard_map/all_to_all | solution.py:35
  52.2 2.2 %layer_forward_1.1 = (bf16[256,512]{1,0:T(8,128)(2,1)S(1)}, f32[256,512]{1,0:T(8,128)S(1)}, bf16[256,512]{1,0:T(8,128)(2,1)S(1)}, bf16[256,512]{1,0:T(8,128)(2,1...) custom-call(s32[2]{0:T(128)S(1)} %pad_add_fusion.ids, ...), custom_call_target="tpu_custom_call", output_to_operand_aliasing={{4}: (15, {})} | custom-call | flops 600000000 | bytes 4000000 | tf_op jit(solution)/shard_map/layer_forward_1/pallas_call | solution.py:60
  54.4 12.5 %all_to_all.52 = bf16[32,8,512]{2,1,0:T(8,128)(2,1)S(1)} all-to-all(bf16[32,8,512]{2,1,0:T(8,128)(2,1)S(1)} %bitcast.56), channel_id=1, replica_groups=mesh['layer'=4,'node'=32] {'node'}, dimensions={0} | all-to-all | bytes 524288 | tf_op jit(solution)/shard_map/all_to_all | solution.py:35
  66.9 2.2 %layer_forward_2.1 = (bf16[256,512]{1,0:T(8,128)(2,1)S(1)}, f32[256,512]{1,0:T(8,128)S(1)}, bf16[256,512]{1,0:T(8,128)(2,1)S(1)}, bf16[256,512]{1,0:T(8,128)(2,1...) custom-call(s32[2]{0:T(128)S(1)} %pad_add_fusion.ids, ...), custom_call_target="tpu_custom_call", output_to_operand_aliasing={{4}: (15, {})} | custom-call | flops 600000000 | bytes 4000000 | tf_op jit(solution)/shard_map/layer_forward_2/pallas_call | solution.py:60
  69.1 12.5 %all_to_all.53 = bf16[32,8,512]{2,1,0:T(8,128)(2,1)S(1)} all-to-all(bf16[32,8,512]{2,1,0:T(8,128)(2,1)S(1)} %bitcast.53), channel_id=1, replica_groups=mesh['layer'=4,'node'=32] {'node'}, dimensions={0} | all-to-all | bytes 524288 | tf_op jit(solution)/shard_map/all_to_all | solution.py:35
  81.6 3.4 %top_layer.1 = (bf16[32,8,512]{2,1,0:T(8,128)(2,1)S(1)}, f32[256,512]{1,0:T(8,128)S(1)}, bf16[512,512]{1,0:T(8,128)(2,1)S(1)}, bf16[512,512]{1,0:T(8,128)(2,1)S(1)}, bf16[4,256,512]{2,1,0:T(8,128)(2,1)}) custom-call(s32[2]{0:T(128)S(1)} %pad_add_fusion.ids, s32[4,2,4]{2,1,0:T(2,128)S(1)} %bitcast.42, ...), custom_call_target="tpu_custom_call", output_to_operand_aliasing={{4}: (9, {})} | custom-call | flops 1000000000 | bytes 5000000 | tf_op jit(solution)/shard_map/top_layer/pallas_call | solution.py:60
  85.0 12.5 %all_to_all.54.ret_ref = bf16[32,8,512]{2,1,0:T(8,128)(2,1)S(1)} all-to-all(bf16[32,8,512]{2,1,0:T(8,128)(2,1)S(1)} %get-tuple-element.110), channel_id=1, replica_groups=mesh['layer'=4,'node'=32] {'node'}, dimensions={0} | all-to-all | bytes 524288 | tf_op jit(solution)/shard_map/all_to_all | solution.py:35
  97.7 2.4 %layer_backward_2.1 = (bf16[32,8,512]{2,1,0:T(8,128)(2,1)S(1)}, f32[256,512]{1,0:T(8,128)S(1)}, bf16[4,256,512]{2,1,0:T(8,128)(2,1)}, bf16[512,512]{1,0:T(8,128)(2,1)S(1)}, bf16[512,512]{1,0:T(8,128)(2,1)S(1)}) custom-call(s32[2]{0:T(128)S(1)} %pad_add_fusion.ids, s32[4,2,4]{2,1,0:T(2,128)S(1)} %bitcast.43, bf16[32,8,512]{2,1,0:T(8,128)(2,1)S(1)} %all_to_all.54.ret_ref, ...), custom_call_target="tpu_custom_call" | custom-call | flops 1000000000 | bytes 5000000 | tf_op jit(solution)/shard_map/layer_backward_2/pallas_call | solution.py:60
  100.2 12.3 %all_to_all.55.ret_ref = bf16[32,8,512]{2,1,0:T(8,128)(2,1)S(1)} all-to-all(bf16[32,8,512]{2,1,0:T(8,128)(2,1)S(1)} %get-tuple-element.118), channel_id=1, replica_groups=mesh['layer'=4,'node'=32] {'node'}, dimensions={0} | all-to-all | bytes 524288 | tf_op jit(solution)/shard_map/all_to_all | solution.py:35
  112.7 2.6 %layer_backward_1.1 = (bf16[32,24,512]{2,1,0:T(8,128)(2,1)S(1)}, f32[256,512]{1,0:T(8,128)S(1)}, bf16[4,256,512]{2,1,0:T(8,128)(2,1)}, bf16[512,512]{1,0:T(8,128)(2,1)S(1)}, bf16[512,512]{1,0:T(8,128)(2,1)S(1)}) custom-call(s32[2]{0:T(128)S(1)} %pad_add_fusion.ids, s32[4,2,4]{2,1,0:T(2,128)S(1)} %bitcast.44, ...), custom_call_target="tpu_custom_call", output_to_operand_aliasing={{2}: (12, {})} | custom-call | flops 1000000000 | bytes 5000000 | tf_op jit(solution)/shard_map/layer_backward_1/pallas_call | solution.py:60
  115.4 17.2 %all_to_all.56.ret_ref = bf16[32,24,512]{2,1,0:T(8,128)(2,1)S(1)} all-to-all(bf16[32,24,512]{2,1,0:T(8,128)(2,1)S(1)} %get-tuple-element.129), channel_id=1, replica_groups=mesh['layer'=4,'node'=32] {'node'}, dimensions={0} | all-to-all | bytes 1572864 | tf_op jit(solution)/shard_map/all_to_all | solution.py:35
  133.2 2.4 %last_slope.1 = (bf16[256,512]{1,0:T(8,128)(2,1)S(1)}, bf16[4,256,512]{2,1,0:T(8,128)(2,1)}, bf16[512,512]{1,0:T(8,128)(2,1)S(1)}, bf16[512,512]{1,0:T(8,128)(2,1)S(1)}, bf16[2,16,512]{2,1,0:T(8,128)(2,1)}) custom-call(s32[2]{0:T(128)S(1)} %pad_add_fusion.ids, s32[4,2,4]{2,1,0:T(2,128)S(1)} %bitcast.45, ...), custom_call_target="tpu_custom_call", output_to_operand_aliasing={{1}: (8, {})} | custom-call | flops 400000000 | bytes 3000000 | tf_op jit(solution)/shard_map/last_slope/pallas_call | solution.py:60
  135.8 3.9 %last_spread.1 = (bf16[32,56,512]{2,1,0:T(8,128)(2,1)}, f32[256,512]{1,0:T(8,128)}) custom-call(s32[2]{0:T(128)S(1)} %pad_add_fusion.ids, s32[4,2,4]{2,1,0:T(2,128)S(1)} %bitcast.46, bf16[256,512]{1,0:T(8,128)(2,1)S(1)} %get-tuple-element.140.dpre_ref, bf16[2,4,128,128]{3,2,1,0:T(8,128)(2,1)S(1)} %get-tuple-element.93.vals_ref.rest_0_, ...), custom_call_target="tpu_custom_call" | custom-call | flops 500000000 | bytes 4000000 | tf_op jit(solution)/shard_map/last_spread/pallas_call | solution.py:60
  139.7 1.6 join_rows.1
  141.2 4.1 %all-to-all-start.7 = ((bf16[32,56,512]{2,1,0:T(8,128)(2,1)}), bf16[32,56,512]{2,1,0:T(8,128)(2,1)S(1)}, u32[]{:S(2)}, u32[]{:S(2)}) async-start(bf16[32,56,512]{2,1,0:T(8,128)(2,1)} %join_rows.1), calls=%async_computation.7 | async-start | bytes 3670016 | tf_op jit(solution)/shard_map/all_to_all | solution.py:35
  145.3 1.0 slice_bitcast_fusion.5
  146.3 4.1 %collective-permute-start.10 = (bf16[256,512]{1,0:T(8,128)(2,1)S(1)}, bf16[256,512]{1,0:T(8,128)(2,1)S(1)}, u32[]{:S(2)}, u32[]{:S(2)}) collective-permute-start(bf16[256,512]{1,0:T(8,128)(2,1)S(1)} %slice_bitcast_fusion.5), channel_id=1, source_target_pairs={{0,64},{32,96},{96,32},{1,65},{33,97},{97,33},{2,66},{34,98},{98,3... | collective-permute-start | bytes 786440 | tf_op jit(solution)/shard_map/ppermute | solution.py:583
  150.4 1.2 slice_bitcast_fusion.2
  151.5 1.3 collective-permute-start.13
  152.8 1.5 collective-permute-start.12
  154.3 2.8 %collective-permute-done.10.two = bf16[256,512]{1,0:T(8,128)(2,1)S(1)} collective-permute-done((bf16[256,512]{1,0:T(8,128)(2,1)S(1)}, bf16[256,512]{1,0:T(8,128)(2,1)S(1)}, u32[]{:S(2)}, u32[]{:S(2)}) %collective-permute-start.10) | collective-permute-done | bytes 262176 | tf_op jit(solution)/shard_map/ppermute | solution.py:583
  157.0 6.7 %collective-permute-done.13.refs_3_ = bf16[256,512]{1,0:T(8,128)(2,1)S(1)} collective-permute-done((bf16[256,512]{1,0:T(8,128)(2,1)S(1)}, bf16[256,512]{1,0:T(8,128)(2,1)S(1)}, u32[]{:S(2)}, u32[]{:S(2)}) %collective-permute-start.13) | collective-permute-done | bytes 262176 | tf_op jit(solution)/shard_map/ppermute | solution.py:26
  163.7 4.1 %collective-permute-done.11.refs_1_ = bf16[256,512]{1,0:T(8,128)(2,1)S(1)} collective-permute-done((bf16[256,512]{1,0:T(8,128)(2,1)S(1)}, bf16[256,512]{1,0:T(8,128)(2,1)S(1)}, u32[]{:S(2)}, u32[]{:S(2)}) %collective-permute-start.11) | collective-permute-done | bytes 262176 | tf_op jit(solution)/shard_map/ppermute | solution.py:26
  167.9 3.5 %all-to-all-done.7.ret_ref = bf16[32,56,512]{2,1,0:T(8,128)(2,1)S(1)} async-done(((bf16[32,56,512]{2,1,0:T(8,128)(2,1)}), bf16[32,56,512]{2,1,0:T(8,128)(2,1)S(1)}, u32[]{:S(2)}, u32[]{:S(2)}) %all-to-all-start.7) | async-done | bytes 1835040 | tf_op jit(solution)/shard_map/all_to_all | solution.py:35
  171.3 2.2 %sum_chunks.1 = bf16[4,2,16,512]{3,2,1,0:T(8,128)(2,1)} custom-call(s32[2]{0:T(128)S(1)} %pad_add_fusion.ids, s32[4,2,4]{2,1,0:T(2,128)S(1)} %bitcast.48, bf16[32,56,512]{2,1,0:T(8,128)(2,1)S(1)} %all-to-all-done.7.ret_ref, bf16[2,16,512]{2,1,0:T(8,128)(2,1)} %get-tuple-element.156.c_3), custom_call_target="tpu_custom_call" | custom-call | bytes 1000000 | tf_op jit(solution)/shard_map/sum_chunks/pallas_call | solution.py:60
  173.5 3.4 %all-to-all-start.8 = ((bf16[4,2,16,512]{3,2,1,0:T(8,128)(2,1)}), bf16[4,2,16,512]{3,2,1,0:T(8,128)(2,1)S(1)}, u32[]{:S(2)}, u32[]{:S(2)}) async-start(bf16[4,2,16,512]{3,2,1,0:T(8,128)(2,1)} %sum_chunks.1), calls=%async_computation.8 | async-start | bytes 262144 | tf_op jit(solution)/shard_map/all_to_all | solution.py:593
  177.0 3.3 %input_grads.1 = (bf16[4,256,512]{2,1,0:T(8,128)(2,1)}, bf16[256,512]{1,0:T(8,128)(2,1)}) custom-call(s32[2]{0:T(128)S(1)} %pad_add_fusion.ids, s32[4,2,4]{2,1,0:T(2,128)S(1)} %bitcast.49, bf16[32,56,512]{2,1,0:T(8,128)(2,1)S(1)} %all-to-all-done.7.ret_ref, f32[256,512]{1,0:T(8,128)} %get-tuple-element.157.part_in, ...), custom_call_target="tpu_custom_call", output_to_operand_aliasing={{0}: (5, {})} | custom-call | flops 100000000 | bytes 1000000 | tf_op jit(solution)/shard_map/input_grads/pallas_call | solution.py:60
  180.3 2.6 %all-to-all-done.8.sums_ref = bf16[4,2,16,512]{3,2,1,0:T(8,128)(2,1)S(1)} async-done(((bf16[4,2,16,512]{3,2,1,0:T(8,128)(2,1)}), bf16[4,2,16,512]{3,2,1,0:T(8,128)(2,1)S(1)}, u32[]{:S(2)}, u32[]{:S(2)}) %all-to-all-start.8) | async-done | bytes 131104 | tf_op jit(solution)/shard_map/all_to_all | solution.py:593
  182.9 1.4 sum_over_layer.1
  184.4 5.3 %all-to-all-start.9 = ((bf16[32,16,512]{2,1,0:T(8,128)(2,1)}), bf16[32,16,512]{2,1,0:T(8,128)(2,1)S(1)}, u32[]{:S(2)}, u32[]{:S(2)}) async-start(bf16[32,16,512]{2,1,0:T(8,128)(2,1)} %sum_over_layer.1), calls=%async_computation.9 | async-start | bytes 1048576 | tf_op jit(solution)/shard_map/all_to_all | solution.py:35
  189.7 1.3 collective-permute-start.14
  191.7 1.5 collective-permute-start.15
  193.2 2.6 %put_home.1 = bf16[1,4,256,512]{3,2,1,0:T(8,128)(2,1)} custom-call(s32[2]{0:T(128)S(1)} %pad_add_fusion.ids, s32[4,2,4]{2,1,0:T(2,128)S(1)} %bitcast.51, bf16[4,256,512]{2,1,0:T(8,128)(2,1)} %get-tuple-element.154.refs_0_, bf16[256,512]{1,0:T(8,128)(2,1)S(1)} %collective-permute-done.11.refs_1_, bf16[256,512]{1,0:T(8,128)(2,1)S(1)} %collective-permute-done.12.refs_2_, ...), custom_call_target="tpu_custom_call" | custom-call | bytes 2000000 | tf_op jit(solution)/shard_map/put_home/pallas_call | solution.py:60
  195.8 6.7 %collective-permute-done.14.late = bf16[256,512]{1,0:T(8,128)(2,1)S(1)} collective-permute-done((bf16[256,512]{1,0:T(8,128)(2,1)}, bf16[256,512]{1,0:T(8,128)(2,1)S(1)}, u32[]{:S(2)}, u32[]{:S(2)}) %collective-permute-start.14) | collective-permute-done | bytes 262176 | tf_op jit(solution)/shard_map/ppermute | solution.py:621
  202.5 4.9 %collective-permute-done.15.one = bf16[256,512]{1,0:T(8,128)(2,1)S(1)} collective-permute-done((bf16[256,512]{1,0:T(8,128)(2,1)S(1)}, bf16[256,512]{1,0:T(8,128)(2,1)S(1)}, u32[]{:S(2)}, u32[]{:S(2)}) %collective-permute-start.15) | collective-permute-done | bytes 262176 | tf_op jit(solution)/shard_map/ppermute | solution.py:26
  207.5 1.9 collective-permute-done.17.other_ref
  209.4 3.7 %final_outputs.1 = (bf16[1,4,256,512]{3,2,1,0:T(8,128)(2,1)}, f32[1,512,512]{2,1,0:T(8,128)}, f32[1,512,512]{2,1,0:T(8,128)}) custom-call(s32[2]{0:T(128)S(1)} %pad_add_fusion.ids, s32[4,2,4]{2,1,0:T(2,128)S(1)} %bitcast.52, bf16[512,512]{1,0:T(8,128)(2,1)S(1)} %bitcast.34, bf16[512,512]{1,0:T(8,128)(2,1)S(1)} %collective-permute-done.17.other_ref, ...), custom_call_target="tpu_custom_call" | custom-call | bytes 6000000 | tf_op jit(solution)/shard_map/final_outputs/pallas_call | solution.py:60
  (33 shorter events, 3.4 us)
Async XLA Ops:
  1.9 25.7 %collective-permute-start.2 = (bf16[512,512]{1,0:T(8,128)(2,1)S(1)}, bf16[512,512]{1,0:T(8,128)(2,1)S(1)}, u32[]{:S(2)}, u32[]{:S(2)}) collective-permute-start(bf16[512,512]{1,0:T(8,128)(2,1)S(1)} %broadcast_select_fusion), channel_id=1, source_target_pairs={{0,64},{32,96},{64,0},{96,32},{1,65},{33,97},{65,1},{97,33},{2,66}... | collective-permute-start | bytes 1572872 | tf_op jit(solution)/shard_map/ppermute | solution.py:26
  5.1 23.5 %collective-permute-start.1 = (bf16[512,512]{1,0:T(8,128)(2,1)S(1)}, bf16[512,512]{1,0:T(8,128)(2,1)S(1)}, u32[]{:S(2)}, u32[]{:S(2)}) collective-permute-start(bf16[512,512]{1,0:T(8,128)(2,1)S(1)} %broadcast_select_fusion), channel_id=1, source_target_pairs={{0,96},{32,0},{64,32},{96,64},{1,97},{33,1},{65,33},{97,65},{2,98}... | collective-permute-start | bytes 1572872 | tf_op jit(solution)/shard_map/ppermute | solution.py:26
  6.2 22.4 %collective-permute-start = (bf16[512,512]{1,0:T(8,128)(2,1)S(1)}, bf16[512,512]{1,0:T(8,128)(2,1)S(1)}, u32[]{:S(2)}, u32[]{:S(2)}) collective-permute-start(bf16[512,512]{1,0:T(8,128)(2,1)S(1)} %broadcast_select_fusion), channel_id=1, source_target_pairs={{0,32},{32,64},{64,96},{96,0},{1,33},{33,65},{65,97},{97,1},{2,34}... | collective-permute-start | bytes 1572872 | tf_op jit(solution)/shard_map/ppermute | solution.py:26
  7.2 0.7 copy-start
  28.6 1.9 collective-permute-start.3
  28.6 2.7 %collective-permute-start.4 = (bf16[512,512]{1,0:T(8,128)(2,1)S(1)}, bf16[512,512]{1,0:T(8,128)(2,1)S(1)}, u32[]{:S(2)}, u32[]{:S(2)}) collective-permute-start(bf16[512,512]{1,0:T(8,128)(2,1)S(1)} %collective-permute-done.1.rest_4_), channel_id=1, source_target_pairs={{0,1},{1,0},{2,3},{3,2},{4,5},{5,4},{6,7},{7,6},{8,9},{9,8},{10,11... | collective-permute-start | bytes 1572872 | tf_op jit(solution)/shard_map/ppermute | solution.py:31
  29.1 2.9 %collective-permute-start.5 = (bf16[512,512]{1,0:T(8,128)(2,1)S(1)}, bf16[512,512]{1,0:T(8,128)(2,1)S(1)}, u32[]{:S(2)}, u32[]{:S(2)}) collective-permute-start(bf16[512,512]{1,0:T(8,128)(2,1)S(1)} %collective-permute-done.2.rest_6_), channel_id=1, source_target_pairs={{0,1},{1,0},{2,3},{3,2},{4,5},{5,4},{6,7},{7,6},{8,9},{9,8},{10,11... | collective-permute-start | bytes 1572872 | tf_op jit(solution)/shard_map/ppermute | solution.py:31
  66.9 14.7 %copy-start.2 = (bf16[512,172]{0,1:T(8,128)(2,1)S(1)}, bf16[512,172]{0,1:T(8,128)(2,1)}, u32[]{:S(2)}) copy-start(bf16[512,172]{0,1:T(8,128)(2,1)} %param.13) | copy-start | bytes 528388
  66.9 14.7 %copy-start.3 = (s32[4,256]{1,0:T(4,128)S(1)}, s32[4,256]{1,0:T(4,128)}, u32[]{:S(2)}) copy-start(s32[4,256]{1,0:T(4,128)} %lab_ref.1) | copy-start | bytes 12292
  66.9 14.7 %copy-start.4 = (s32[4,256]{1,0:T(4,128)S(1)}, s32[4,256]{1,0:T(4,128)}, u32[]{:S(2)}) copy-start(s32[4,256]{1,0:T(4,128)} %mask_ref.1) | copy-start | bytes 12292
  97.4 2.7 %collective-permute-start.6 = (bf16[512,512]{1,0:T(8,128)(2,1)S(1)}, bf16[512,512]{1,0:T(8,128)(2,1)S(1)}, u32[]{:S(2)}, u32[]{:S(2)}) collective-permute-start(bf16[512,512]{1,0:T(8,128)(2,1)S(1)} %get-tuple-element.117), channel_id=1, source_target_pairs={{0,1},{1,0},{2,3},{3,2},{4,5},{5,4},{6,7},{7,6},{8,9},{9,8},{10,11... | collective-permute-start | bytes 1572872 | tf_op jit(solution)/shard_map/ppermute | solution.py:31
  112.4 3.0 %collective-permute-start.7 = (bf16[512,512]{1,0:T(8,128)(2,1)S(1)}, bf16[512,512]{1,0:T(8,128)(2,1)S(1)}, u32[]{:S(2)}, u32[]{:S(2)}) collective-permute-start(bf16[512,512]{1,0:T(8,128)(2,1)S(1)} %get-tuple-element.128), channel_id=1, source_target_pairs={{0,1},{1,0},{2,3},{3,2},{4,5},{5,4},{6,7},{7,6},{8,9},{9,8},{10,11... | collective-permute-start | bytes 1572872 | tf_op jit(solution)/shard_map/ppermute | solution.py:31
  132.6 3.1 %collective-permute-start.8 = (bf16[512,512]{1,0:T(8,128)(2,1)S(1)}, bf16[512,512]{1,0:T(8,128)(2,1)S(1)}, u32[]{:S(2)}, u32[]{:S(2)}) collective-permute-start(bf16[512,512]{1,0:T(8,128)(2,1)S(1)} %get-tuple-element.138), channel_id=1, source_target_pairs={{0,1},{1,0},{2,3},{3,2},{4,5},{5,4},{6,7},{7,6},{8,9},{9,8},{10,11... | collective-permute-start | bytes 1572872 | tf_op jit(solution)/shard_map/ppermute | solution.py:31
  135.7 4.0 %collective-permute-start.9 = (bf16[512,512]{1,0:T(8,128)(2,1)S(1)}, bf16[512,512]{1,0:T(8,128)(2,1)S(1)}, u32[]{:S(2)}, u32[]{:S(2)}) collective-permute-start(bf16[512,512]{1,0:T(8,128)(2,1)S(1)} %get-tuple-element.147), channel_id=1, source_target_pairs={{0,1},{1,0},{2,3},{3,2},{4,5},{5,4},{6,7},{7,6},{8,9},{9,8},{10,11... | collective-permute-start | bytes 1572872 | tf_op jit(solution)/shard_map/ppermute | solution.py:31
  141.2 30.1 %all-to-all-start.7 = ((bf16[32,56,512]{2,1,0:T(8,128)(2,1)}), bf16[32,56,512]{2,1,0:T(8,128)(2,1)S(1)}, u32[]{:S(2)}, u32[]{:S(2)}) async-start(bf16[32,56,512]{2,1,0:T(8,128)(2,1)} %join_rows.1), calls=%async_computation.7 | async-start | bytes 3670016 | tf_op jit(solution)/shard_map/all_to_all | solution.py:35
  145.3 26.0 %copy-start.1 = (s32[4,1,2,4]{3,2,1,0:T(2,128)S(1)}, s32[4,1,2,4]{3,2,1,0:T(2,128)}, u32[]{:S(2)}) copy-start(s32[4,1,2,4]{3,2,1,0:T(2,128)} %param.16) | copy-start | bytes 388
  146.3 10.8 %collective-permute-start.10 = (bf16[256,512]{1,0:T(8,128)(2,1)S(1)}, bf16[256,512]{1,0:T(8,128)(2,1)S(1)}, u32[]{:S(2)}, u32[]{:S(2)}) collective-permute-start(bf16[256,512]{1,0:T(8,128)(2,1)S(1)} %slice_bitcast_fusion.5), channel_id=1, source_target_pairs={{0,64},{32,96},{96,32},{1,65},{33,97},{97,33},{2,66},{34,98},{98,3... | collective-permute-start | bytes 786440 | tf_op jit(solution)/shard_map/ppermute | solution.py:583
  151.5 12.2 %collective-permute-start.13 = (bf16[256,512]{1,0:T(8,128)(2,1)S(1)}, bf16[256,512]{1,0:T(8,128)(2,1)S(1)}, u32[]{:S(2)}, u32[]{:S(2)}) collective-permute-start(bf16[256,512]{1,0:T(8,128)(2,1)S(1)} %get-tuple-element.178), channel_id=1, source_target_pairs={{0,96},{32,0},{64,32},{96,64},{1,97},{33,1},{65,33},{97,65},{2,98}... | collective-permute-start | bytes 786440 | tf_op jit(solution)/shard_map/ppermute | solution.py:26
  152.8 10.9 %collective-permute-start.12 = (bf16[256,512]{1,0:T(8,128)(2,1)S(1)}, bf16[256,512]{1,0:T(8,128)(2,1)S(1)}, u32[]{:S(2)}, u32[]{:S(2)}) collective-permute-start(bf16[256,512]{1,0:T(8,128)(2,1)S(1)} %get-tuple-element.179), channel_id=1, source_target_pairs={{0,64},{32,96},{64,0},{96,32},{1,65},{33,97},{65,1},{97,33},{2,66}... | collective-permute-start | bytes 786440 | tf_op jit(solution)/shard_map/ppermute | solution.py:26
  154.3 13.6 %collective-permute-start.11 = (bf16[256,512]{1,0:T(8,128)(2,1)S(1)}, bf16[256,512]{1,0:T(8,128)(2,1)S(1)}, u32[]{:S(2)}, u32[]{:S(2)}) collective-permute-start(bf16[256,512]{1,0:T(8,128)(2,1)S(1)} %get-tuple-element.180), channel_id=1, source_target_pairs={{0,32},{32,64},{64,96},{96,0},{1,33},{33,65},{65,97},{97,1},{2,34}... | collective-permute-start | bytes 786440 | tf_op jit(solution)/shard_map/ppermute | solution.py:26
  173.5 9.4 %all-to-all-start.8 = ((bf16[4,2,16,512]{3,2,1,0:T(8,128)(2,1)}), bf16[4,2,16,512]{3,2,1,0:T(8,128)(2,1)S(1)}, u32[]{:S(2)}, u32[]{:S(2)}) async-start(bf16[4,2,16,512]{3,2,1,0:T(8,128)(2,1)} %sum_chunks.1), calls=%async_computation.8 | async-start | bytes 262144 | tf_op jit(solution)/shard_map/all_to_all | solution.py:593
  180.3 10.7 %copy-start.5 = (bf16[4,256,512]{2,1,0:T(8,128)(2,1)S(1)}, bf16[4,256,512]{2,1,0:T(8,128)(2,1)}, u32[]{:S(2)}) copy-start(bf16[4,256,512]{2,1,0:T(8,128)(2,1)} %get-tuple-element.166.own) | copy-start | bytes 3145732
  184.4 23.1 %all-to-all-start.9 = ((bf16[32,16,512]{2,1,0:T(8,128)(2,1)}), bf16[32,16,512]{2,1,0:T(8,128)(2,1)S(1)}, u32[]{:S(2)}, u32[]{:S(2)}) async-start(bf16[32,16,512]{2,1,0:T(8,128)(2,1)} %sum_over_layer.1), calls=%async_computation.9 | async-start | bytes 1048576 | tf_op jit(solution)/shard_map/all_to_all | solution.py:35
  189.7 12.8 %collective-permute-start.14 = (bf16[256,512]{1,0:T(8,128)(2,1)}, bf16[256,512]{1,0:T(8,128)(2,1)S(1)}, u32[]{:S(2)}, u32[]{:S(2)}) collective-permute-start(bf16[256,512]{1,0:T(8,128)(2,1)} %get-tuple-element.165), channel_id=1, source_target_pairs={{64,0},{65,1},{66,2},{67,3},{68,4},{69,5},{70,6},{71,7},{72,8},{73... | collective-permute-start | bytes 786440 | tf_op jit(solution)/shard_map/ppermute | solution.py:621
  191.1 11.4 %collective-permute-start.16 = (bf16[256,512]{1,0:T(8,128)(2,1)S(1)}, bf16[256,512]{1,0:T(8,128)(2,1)S(1)}, u32[]{:S(2)}, u32[]{:S(2)}) collective-permute-start(bf16[256,512]{1,0:T(8,128)(2,1)S(1)} %get-tuple-element.176), channel_id=1, source_target_pairs={{0,96},{32,0},{64,32},{96,64},{1,97},{33,1},{65,33},{97,65},{2,98}... | collective-permute-start | bytes 786440 | tf_op jit(solution)/shard_map/ppermute | solution.py:26
  191.7 15.7 %collective-permute-start.15 = (bf16[256,512]{1,0:T(8,128)(2,1)S(1)}, bf16[256,512]{1,0:T(8,128)(2,1)S(1)}, u32[]{:S(2)}, u32[]{:S(2)}) collective-permute-start(bf16[256,512]{1,0:T(8,128)(2,1)S(1)} %get-tuple-element.177), channel_id=1, source_target_pairs={{0,32},{32,64},{64,96},{96,0},{1,33},{33,65},{65,97},{97,1},{2,34}... | collective-permute-start | bytes 786440 | tf_op jit(solution)/shard_map/ppermute | solution.py:26
  207.5 1.9 collective-permute-start.17

commit v6 on v4

--- a/solution.py
+++ b/solution.py
@@ -177,9 +177,15 @@
 def forward_kernel(layer, ids, cols, h_ref, arr_ref, vals_ref, pick_ref, *rest):
     w_refs, rest = rest[:8], rest[8:]
     first = layer == 0
-    w_ref, rest = (rest[6], rest) if first else (rest[0], rest[2:])
-    agg_ref, pre_ref, hid_ref, out_ref, buf_ref, next_ref = rest[:6]
+    if first:
+        agg_ref, pre_ref, hid_ref, out_ref, next_ref, w_ref = rest[:6]
+    else:
+        w_ref, *rest = rest[0:1] + rest[1 + (layer > 1) :]
+        agg_ref, pre_ref, hid_ref, out_ref, next_ref, buf_ref = rest[:6]
     ext, buf_sem, sems = rest[-3:]
+    if not first:
+        copy = to_slot(h_ref, layer - 1, ids, buf_ref, buf_sem)
+        copy.start()
     ready = None
     if first:
         here = (layer, ids, w_refs, w_ref, sems.at[0])
@@ -189,12 +195,11 @@
     start_weights(*ahead)
     agg, pre, _, hid = forward_math(ids, cols, h_ref, arr_ref, vals_ref, w_ref, ext, ready)
     hid_ref[...] = hid
-    copy = to_slot(hid_ref, layer, ids, buf_ref, buf_sem)
-    copy.start()
     out_ref[...] = dot(pick_ref[...], hid).astype(BF)
     agg_ref[...] = agg
     pre_ref[...] = pre
-    copy.wait()
+    if not first:
+        copy.wait()
     wait_weights(*ahead)
 
 
@@ -221,11 +226,14 @@
 
 def top_kernel(layer, ids, cols, h_ref, arr_ref, vals_ref, wout_ref, lab_ref, mask_ref, w_ref, *rest):
     remote_ref, part_ref, keep_ref, send_ref, buf_ref, hid_ref, ext, d_ext, buf_sem = rest[1:]
+    copy = to_slot(h_ref, layer - 1, ids, buf_ref, buf_sem)
+    copy.start()
     rows = h_ref.shape[0]
     agg, pre, sig, hid = forward_math(ids, cols, h_ref, arr_ref, vals_ref, w_ref, ext)
     hid_ref[...] = hid
-    copy = to_slot(hid_ref, layer, ids, buf_ref, buf_sem)
-    copy.start()
+    last = to_slot(hid_ref, layer, ids, buf_ref, buf_sem)
+    copy.wait()
+    last.start()
     logits = dot(wout_ref[...], hid, NT)
     expo = jnp.exp(logits)
     probs = expo / jnp.sum(expo, axis=0, keepdims=True)
@@ -239,7 +247,7 @@
     remote_ref[...] = d_ext[rows : 2 * rows, :].astype(BF).reshape(remote_ref.shape)
     part_ref[...] = back + d_ext[0:rows, :]
     weight_partials(ids, h_ref, agg, d_pre, keep_ref, send_ref)
-    copy.wait()
+    last.wait()
 
 
 def chunk_sum(block):
@@ -416,22 +424,28 @@
     for layer in range(top):
         ins = [hidden[layer], arrived.reshape(rows, feat), vals, pick, *sources]
         if layer:
-            ins += [weights[layer], (acts_buf, FAR)]
-        agg, pre, hid, outgoing, acts_buf, *arranged = run(
+            ins.append(weights[layer])
+        if layer > 1:
+            ins.append((acts_buf, FAR))
+        agg, pre, hid, outgoing, arranged, last = run(
             functools.partial(forward_kernel, layer),
             f"layer_forward_{layer}",
             scalars,
             ins,
-            [act, wide, act, act, stack] + [weight] * (2 if layer == 0 else 1),
+            [act, wide, act, act, weight, stack if layer else weight],
             [ext_scratch, buf_sem, pltpu.SemaphoreType.DMA((2, 2))],
-            {len(ins) - 1: 4} if layer else None,
+            {len(ins) - 1: 5} if layer > 1 else None,
             flops=6 * 10**8,
             moved=4 * 10**6,
         )
+        if layer:
+            acts_buf = last
+        else:
+            weights.append(last)
+        weights.append(arranged)
         hidden.append(hid)
         aggs.append(agg)
         pres.append(pre)
-        weights += arranged[::-1]
         arrived = exchange(outgoing.reshape(peers, slots, feat))
 
     ins = [
@@ -535,7 +549,8 @@
     )[0]
     joined, acts_buf = tie(joined, acts_buf)
     acts = travel(acts_buf)
-    returned, *acts = tie(exchange(joined), *acts)
+    layer_acts = put_home(acts_buf, *acts)
+    returned, layer_acts = tie(exchange(joined), layer_acts)
     sums = run(
         chunk_kernel,
         "sum_chunks",
@@ -561,6 +576,7 @@
         flops=10**8,
         moved=10**6,
     )[0]
+    sums, *to_send = tie(sums, *[grads_buf[s] for s in all_shifts])
     spread = run(
         layer_sum_kernel,
         "sum_over_layer",
@@ -569,9 +585,8 @@
         [far_block((peers, chunk_rows, feat))],
         moved=10**6,
     )[0]
-    layer_acts = put_home(acts_buf, *acts)
-    grads = travel(grads_buf)
-    gathered, layer_acts, *grads = tie(exchange(spread), layer_acts, *grads)
+    grads = [shift(v, "layer", s) for s, v in zip(all_shifts, to_send)]
+    gathered, *grads = tie(exchange(spread), *grads)
     gathered = gathered.reshape(feat, feat)
     other = sibling(gathered)
     act_grads = put_home(grads_buf, *grads)

time: 212 us -> 210 us (level)
  waiting for transfers between devices: 41.8 us -> 39.5 us
  transfers between devices with their start and end apart: 20 -> 20, of which waited for: 13 -> 12; matrix products, arithmetic and copies ran while one was open for 1% -> 1% of each run, Pallas kernels for 7% -> 7%
where the time goes in v6:
time: 210 us; the launch traced here: 208 us
  blocking collectives  101 us (48%)
  waiting for transfers between devices  39.5 us (19%)
  Pallas kernels  36.6 us (17%)
  starting transfers between devices  26.9 us (13%)
    all_to_all x7, blocking collectives, exchange(): lax.all_to_all(value, 'node', split_axis=0, concat_axis=0, tiled=True)  101 us
    pallas_call x15, Pallas kernels, run(): pl.pallas_call(kernel, name=name, grid_spec=pltpu.PrefetchScalarGridSpec(...  36.6 us
    ppermute x9, waiting for transfers between devices, shift(): lax.ppermute(value, axis, [(i, (i + steps) % count) for i in range(count)])  26.4 us
    ppermute x9, starting transfers between devices, shift(): lax.ppermute(value, axis, [(i, (i + steps) % count) for i in range(count)])  13.2 us
    all_to_all x2, starting transfers between devices, exchange(): lax.all_to_all(value, 'node', split_axis=0, concat_axis=0, tiled=True)  8.03 us
    all_to_all x2, waiting for transfers between devices, exchange(): lax.all_to_all(value, 'node', split_axis=0, concat_axis=0, tiled=True)  5.81 us
    ppermute x8, waiting for transfers between devices, sibling(): return lax.ppermute(value, 'node', [(i, i ^ 1) for i in range(count)])  5.1 us
  transfers between devices with their start and end apart: 20, of which 12 were waited for; matrix products, arithmetic and copies ran while one was open for 1% of the time, Pallas kernels for 7%

profile of v6, /device:TPU:0, one launch (start us, length us, event | category | flops | bytes accessed | tf_op | source)
XLA Modules:
  0.0 208.1 jit_solution(206100623887445312)
XLA Ops:
  0.6 1.3 broadcast_select_fusion
  1.9 3.2 %collective-permute-start.2 = (bf16[512,512]{1,0:T(8,128)(2,1)S(1)}, bf16[512,512]{1,0:T(8,128)(2,1)S(1)}, u32[]{:S(2)}, u32[]{:S(2)}) collective-permute-start(bf16[512,512]{1,0:T(8,128)(2,1)S(1)} %broadcast_select_fusion), channel_id=1, source_target_pairs={{0,64},{32,96},{64,0},{96,32},{1,65},{33,97},{65,1},{97,33},{2,66}... | collective-permute-start | bytes 1572872 | tf_op jit(solution)/shard_map/ppermute | solution.py:26
  5.1 1.1 collective-permute-start.1
  6.2 0.9 collective-permute-start
  7.2 0.7 copy-done
  7.9 2.6 %gather_rows.1 = (bf16[256,256]{1,0:T(8,128)(2,1)S(1)}, bf16[256,512]{1,0:T(8,128)(2,1)S(1)}, bf16[256,512]{1,0:T(8,128)(2,1)S(1)}, bf16[2,4,128,128]{3,2,1,0:T(8,128)(2,1)S(1)}, bf16[256,256]{1,0:T(8,128)(2,1)}) custom-call(s32[2]{0:T(128)S(1)} %pad_add_fusion.ids, s32[4,2,4]{2,1,0:T(2,128)S(1)} %bitcast.38, bf16[4,256,512]{2,1,0:T(8,128)(2,1)} %h_ref.1, ...), custom_call_target="tpu_custom_call" | custom-call | flops 100000000 | bytes 1000000 | tf_op jit(solution)/shard_map/gather_rows/pallas_call | solution.py:60
  10.5 17.1 %all_to_all.50 = bf16[32,8,512]{2,1,0:T(8,128)(2,1)S(1)} all-to-all(bf16[32,8,512]{2,1,0:T(8,128)(2,1)S(1)} %bitcast.57), channel_id=1, replica_groups=mesh['layer'=4,'node'=32] {'node'}, dimensions={0} | all-to-all | bytes 524288 | tf_op jit(solution)/shard_map/all_to_all | solution.py:35
  27.6 1.0 collective-permute-done.1.rest_4_
  29.1 1.4 collective-permute-done.3.rest_3_
  30.5 0.7 collective-permute-done.4.rest_5_
  31.3 0.7 collective-permute-done.5.rest_7_
  32.0 2.6 %layer_forward_0.1 = (bf16[256,512]{1,0:T(8,128)(2,1)S(1)}, f32[256,512]{1,0:T(8,128)S(1)}, bf16[256,512]{1,0:T(8,128)(2,1)S(1)}, bf16[256,512]{1,0:T(8,128)(2,1...) custom-call(s32[2]{0:T(128)S(1)} %pad_add_fusion.ids, s32[4,2,4]{2,1,0:T(2,128)S(1)} %bitcast.39, ...), custom_call_target="tpu_custom_call" | custom-call | flops 600000000 | bytes 4000000 | tf_op jit(solution)/shard_map/layer_forward_0/pallas_call | solution.py:60
  34.6 17.1 %all_to_all.51 = bf16[32,8,512]{2,1,0:T(8,128)(2,1)S(1)} all-to-all(bf16[32,8,512]{2,1,0:T(8,128)(2,1)S(1)} %bitcast.55), channel_id=1, replica_groups=mesh['layer'=4,'node'=32] {'node'}, dimensions={0} | all-to-all | bytes 524288 | tf_op jit(solution)/shard_map/all_to_all | solution.py:35
  51.7 1.7 layer_forward_1.1
  53.4 12.5 %all_to_all.52 = bf16[32,8,512]{2,1,0:T(8,128)(2,1)S(1)} all-to-all(bf16[32,8,512]{2,1,0:T(8,128)(2,1)S(1)} %bitcast.56), channel_id=1, replica_groups=mesh['layer'=4,'node'=32] {'node'}, dimensions={0} | all-to-all | bytes 524288 | tf_op jit(solution)/shard_map/all_to_all | solution.py:35
  65.9 1.7 layer_forward_2.1
  67.6 12.5 %all_to_all.53 = bf16[32,8,512]{2,1,0:T(8,128)(2,1)S(1)} all-to-all(bf16[32,8,512]{2,1,0:T(8,128)(2,1)S(1)} %bitcast.53), channel_id=1, replica_groups=mesh['layer'=4,'node'=32] {'node'}, dimensions={0} | all-to-all | bytes 524288 | tf_op jit(solution)/shard_map/all_to_all | solution.py:35
  80.1 3.5 %top_layer.1 = (bf16[32,8,512]{2,1,0:T(8,128)(2,1)S(1)}, f32[256,512]{1,0:T(8,128)S(1)}, bf16[512,512]{1,0:T(8,128)(2,1)S(1)}, bf16[512,512]{1,0:T(8,128)(2,1)S(1)}, bf16[4,256,512]{2,1,0:T(8,128)(2,1)}) custom-call(s32[2]{0:T(128)S(1)} %pad_add_fusion.ids, s32[4,2,4]{2,1,0:T(2,128)S(1)} %bitcast.42, ...), custom_call_target="tpu_custom_call", output_to_operand_aliasing={{4}: (9, {})} | custom-call | flops 1000000000 | bytes 5000000 | tf_op jit(solution)/shard_map/top_layer/pallas_call | solution.py:60
  83.6 12.5 %all_to_all.54.ret_ref = bf16[32,8,512]{2,1,0:T(8,128)(2,1)S(1)} all-to-all(bf16[32,8,512]{2,1,0:T(8,128)(2,1)S(1)} %get-tuple-element.95), channel_id=1, replica_groups=mesh['layer'=4,'node'=32] {'node'}, dimensions={0} | all-to-all | bytes 524288 | tf_op jit(solution)/shard_map/all_to_all | solution.py:35
  96.4 2.4 %layer_backward_2.1 = (bf16[32,8,512]{2,1,0:T(8,128)(2,1)S(1)}, f32[256,512]{1,0:T(8,128)S(1)}, bf16[4,256,512]{2,1,0:T(8,128)(2,1)}, bf16[512,512]{1,0:T(8,128)(2,1)S(1)}, bf16[512,512]{1,0:T(8,128)(2,1)S(1)}) custom-call(s32[2]{0:T(128)S(1)} %pad_add_fusion.ids, s32[4,2,4]{2,1,0:T(2,128)S(1)} %bitcast.43, bf16[32,8,512]{2,1,0:T(8,128)(2,1)S(1)} %all_to_all.54.ret_ref, ...), custom_call_target="tpu_custom_call" | custom-call | flops 1000000000 | bytes 5000000 | tf_op jit(solution)/shard_map/layer_backward_2/pallas_call | solution.py:60
  98.8 12.3 %all_to_all.55.ret_ref = bf16[32,8,512]{2,1,0:T(8,128)(2,1)S(1)} all-to-all(bf16[32,8,512]{2,1,0:T(8,128)(2,1)S(1)} %get-tuple-element.103), channel_id=1, replica_groups=mesh['layer'=4,'node'=32] {'node'}, dimensions={0} | all-to-all | bytes 524288 | tf_op jit(solution)/shard_map/all_to_all | solution.py:35
  111.4 2.6 %layer_backward_1.1 = (bf16[32,24,512]{2,1,0:T(8,128)(2,1)S(1)}, f32[256,512]{1,0:T(8,128)S(1)}, bf16[4,256,512]{2,1,0:T(8,128)(2,1)}, bf16[512,512]{1,0:T(8,128)(2,1)S(1)}, bf16[512,512]{1,0:T(8,128)(2,1)S(1)}) custom-call(s32[2]{0:T(128)S(1)} %pad_add_fusion.ids, s32[4,2,4]{2,1,0:T(2,128)S(1)} %bitcast.44, ...), custom_call_target="tpu_custom_call", output_to_operand_aliasing={{2}: (12, {})} | custom-call | flops 1000000000 | bytes 5000000 | tf_op jit(solution)/shard_map/layer_backward_1/pallas_call | solution.py:60
  114.0 17.2 %all_to_all.56.ret_ref = bf16[32,24,512]{2,1,0:T(8,128)(2,1)S(1)} all-to-all(bf16[32,24,512]{2,1,0:T(8,128)(2,1)S(1)} %get-tuple-element.115), channel_id=1, replica_groups=mesh['layer'=4,'node'=32] {'node'}, dimensions={0} | all-to-all | bytes 1572864 | tf_op jit(solution)/shard_map/all_to_all | solution.py:35
  131.2 3.8 %layer_backward_0.1 = (bf16[32,56,512]{2,1,0:T(8,128)(2,1)}, f32[256,512]{1,0:T(8,128)}, bf16[4,256,512]{2,1,0:T(8,128)(2,1)}, bf16[512,512]{1,0:T(8,128)(2,1)S(...) custom-call(s32[2]{0:T(128)S(1)} %pad_add_fusion.ids, ...), custom_call_target="tpu_custom_call", output_to_operand_aliasing={{2}: (12, {})} | custom-call | flops 1000000000 | bytes 5000000 | tf_op jit(solution)/shard_map/layer_backward_0/pallas_call | solution.py:60
  135.0 0.7 collective-permute-start.9
  135.9 1.4 collective-permute-done.9.recv_b
  137.3 0.7 collective-permute-done.8.recv_a
  138.1 1.8 join_rows.1
  139.9 4.1 %all-to-all-start.7 = ((bf16[32,56,512]{2,1,0:T(8,128)(2,1)}), bf16[32,56,512]{2,1,0:T(8,128)(2,1)S(1)}, u32[]{:S(2)}, u32[]{:S(2)}) async-start(bf16[32,56,512]{2,1,0:T(8,128)(2,1)} %join_rows.1), calls=%async_computation.7 | async-start | bytes 3670016 | tf_op jit(solution)/shard_map/all_to_all | solution.py:35
  144.1 2.2 %collective-permute-start.12 = (bf16[256,512]{1,0:T(8,128)(2,1)S(1)}, bf16[256,512]{1,0:T(8,128)(2,1)S(1)}, u32[]{:S(2)}, u32[]{:S(2)}) collective-permute-start(bf16[256,512]{1,0:T(8,128)(2,1)S(1)} %get-tuple-element.151), channel_id=1, source_target_pairs={{0,96},{32,0},{64,32},{96,64},{1,97},{33,1},{65,33},{97,65},{2,98}... | collective-permute-start | bytes 786440 | tf_op jit(solution)/shard_map/ppermute | solution.py:26
  146.4 0.7 collective-permute-start.11
  147.1 1.0 collective-permute-start.10
  148.1 9.9 %collective-permute-done.12.refs_3_ = bf16[256,512]{1,0:T(8,128)(2,1)S(1)} collective-permute-done((bf16[256,512]{1,0:T(8,128)(2,1)S(1)}, bf16[256,512]{1,0:T(8,128)(2,1)S(1)}, u32[]{:S(2)}, u32[]{:S(2)}) %collective-permute-start.12) | collective-permute-done | bytes 262176 | tf_op jit(solution)/shard_map/ppermute | solution.py:26
  158.0 3.7 %collective-permute-done.10.refs_1_ = bf16[256,512]{1,0:T(8,128)(2,1)S(1)} collective-permute-done((bf16[256,512]{1,0:T(8,128)(2,1)S(1)}, bf16[256,512]{1,0:T(8,128)(2,1)S(1)}, u32[]{:S(2)}, u32[]{:S(2)}) %collective-permute-start.10) | collective-permute-done | bytes 262176 | tf_op jit(solution)/shard_map/ppermute | solution.py:26
  161.7 2.6 %put_home.2 = bf16[1,4,256,512]{3,2,1,0:T(8,128)(2,1)} custom-call(s32[2]{0:T(128)S(1)} %pad_add_fusion.ids, s32[4,2,4]{2,1,0:T(2,128)S(1)} %bitcast.47, bf16[4,256,512]{2,1,0:T(8,128)(2,1)} %get-tuple-element.131.refs_0_, bf16[256,512]{1,0:T(8,128)(2,1)S(1)} %collective-permute-done.10.refs_1_, bf16[256,512]{1,0:T(8,128)(2,1)S(1)} %collective-permute-done.11.refs_2_, ...), custom_call_target="tpu_custom_call" | custom-call | bytes 2000000 | tf_op jit(solution)/shard_map/put_home/pallas_call | solution.py:60
  164.3 5.8 %all-to-all-done.7.ret_ref = bf16[32,56,512]{2,1,0:T(8,128)(2,1)S(1)} async-done(((bf16[32,56,512]{2,1,0:T(8,128)(2,1)}), bf16[32,56,512]{2,1,0:T(8,128)(2,1)S(1)}, u32[]{:S(2)}, u32[]{:S(2)}) %all-to-all-start.7) | async-done | bytes 1835040 | tf_op jit(solution)/shard_map/all_to_all | solution.py:35
  170.1 2.2 %sum_chunks.1 = bf16[4,2,16,512]{3,2,1,0:T(8,128)(2,1)} custom-call(s32[2]{0:T(128)S(1)} %pad_add_fusion.ids, s32[4,2,4]{2,1,0:T(2,128)S(1)} %bitcast.48, bf16[32,56,512]{2,1,0:T(8,128)(2,1)S(1)} %all-to-all-done.7.ret_ref, bf16[2,16,512]{2,1,0:T(8,128)(2,1)} %get-tuple-element.137.c_3), custom_call_target="tpu_custom_call" | custom-call | bytes 1000000 | tf_op jit(solution)/shard_map/sum_chunks/pallas_call | solution.py:60
  172.3 3.7 %all-to-all-start.8 = ((bf16[4,2,16,512]{3,2,1,0:T(8,128)(2,1)}), bf16[4,2,16,512]{3,2,1,0:T(8,128)(2,1)S(1)}, u32[]{:S(2)}, u32[]{:S(2)}) async-start(bf16[4,2,16,512]{3,2,1,0:T(8,128)(2,1)} %sum_chunks.1), calls=%async_computation.8 | async-start | bytes 262144 | tf_op jit(solution)/shard_map/all_to_all | solution.py:562
  176.0 2.6 %input_grads.1.refs_0_ = bf16[4,256,512]{2,1,0:T(8,128)(2,1)} custom-call(s32[2]{0:T(128)S(1)} %pad_add_fusion.ids, s32[4,2,4]{2,1,0:T(2,128)S(1)} %bitcast.49, bf16[32,56,512]{2,1,0:T(8,128)(2,1)S(1)} %all-to-all-done.7.ret_ref, f32[256,512]{1,0:T(8,128)} %get-tuple-element.134.part_in, ...), custom_call_target="tpu_custom_call", output_to_operand_aliasing={{}: (5, {})} | custom-call | flops 100000000 | bytes 1000000 | tf_op jit(solution)/shard_map/input_grads/pallas_call | solution.py:60
  178.6 1.2 slice_bitcast_fusion
  179.8 2.2 %all-to-all-done.8.sums_ref = bf16[4,2,16,512]{3,2,1,0:T(8,128)(2,1)S(1)} async-done(((bf16[4,2,16,512]{3,2,1,0:T(8,128)(2,1)}), bf16[4,2,16,512]{3,2,1,0:T(8,128)(2,1)S(1)}, u32[]{:S(2)}, u32[]{:S(2)}) %all-to-all-start.8) | async-done | bytes 131104 | tf_op jit(solution)/shard_map/all_to_all | solution.py:562
  182.0 1.4 sum_over_layer.1
  183.4 3.9 %all-to-all-start.9 = ((bf16[32,16,512]{2,1,0:T(8,128)(2,1)}), bf16[32,16,512]{2,1,0:T(8,128)(2,1)S(1)}, u32[]{:S(2)}, u32[]{:S(2)}) async-start(bf16[32,16,512]{2,1,0:T(8,128)(2,1)} %sum_over_layer.1), calls=%async_computation.9 | async-start | bytes 1048576 | tf_op jit(solution)/shard_map/all_to_all | solution.py:35
  188.0 2.1 collective-permute-start.14
  190.0 1.4 collective-permute-start.15
  191.4 11.2 %collective-permute-done.13.refs_1_ = bf16[256,512]{1,0:T(8,128)(2,1)S(1)} collective-permute-done((bf16[256,512]{1,0:T(8,128)(2,1)S(1)}, bf16[256,512]{1,0:T(8,128)(2,1)S(1)}, u32[]{:S(2)}, u32[]{:S(2)}) %collective-permute-start.13) | collective-permute-done | bytes 262176 | tf_op jit(solution)/shard_map/ppermute | solution.py:26
  203.2 2.6 %put_home.3 = bf16[1,4,256,512]{3,2,1,0:T(8,128)(2,1)} custom-call(s32[2]{0:T(128)S(1)} %pad_add_fusion.ids, s32[4,2,4]{2,1,0:T(2,128)S(1)} %bitcast.51, bf16[4,256,512]{2,1,0:T(8,128)(2,1)} %input_grads.1.refs_0_, bf16[256,512]{1,0:T(8,128)(2,1)S(1)} %collective-permute-done.13.refs_1_, bf16[256,512]{1,0:T(8,128)(2,1)S(1)} %collective-permute-done.14.refs_2_, ...), custom_call_target="tpu_custom_call" | custom-call | bytes 2000000 | tf_op jit(solution)/shard_map/put_home/pallas_call | solution.py:60
  205.8 2.3 %scale_grads.1 = (f32[1,512,512]{2,1,0:T(8,128)}, f32[1,512,512]{2,1,0:T(8,128)}) custom-call(s32[2]{0:T(128)S(1)} %pad_add_fusion.ids, s32[4,2,4]{2,1,0:T(2,128)S(1)} %bitcast.52, bf16[512,512]{1,0:T(8,128)(2,1)S(1)} %bitcast.34, bf16[512,512]{1,0:T(8,128)(2,1)S(1)} %collective-permute-done.16.other_ref), custom_call_target="tpu_custom_call" | custom-call | bytes 3000000 | tf_op jit(solution)/shard_map/scale_grads/pallas_call | solution.py:60
  (30 shorter events, 2.7 us)
Async XLA Ops:
  1.9 25.7 %collective-permute-start.2 = (bf16[512,512]{1,0:T(8,128)(2,1)S(1)}, bf16[512,512]{1,0:T(8,128)(2,1)S(1)}, u32[]{:S(2)}, u32[]{:S(2)}) collective-permute-start(bf16[512,512]{1,0:T(8,128)(2,1)S(1)} %broadcast_select_fusion), channel_id=1, source_target_pairs={{0,64},{32,96},{64,0},{96,32},{1,65},{33,97},{65,1},{97,33},{2,66}... | collective-permute-start | bytes 1572872 | tf_op jit(solution)/shard_map/ppermute | solution.py:26
  5.1 23.5 %collective-permute-start.1 = (bf16[512,512]{1,0:T(8,128)(2,1)S(1)}, bf16[512,512]{1,0:T(8,128)(2,1)S(1)}, u32[]{:S(2)}, u32[]{:S(2)}) collective-permute-start(bf16[512,512]{1,0:T(8,128)(2,1)S(1)} %broadcast_select_fusion), channel_id=1, source_target_pairs={{0,96},{32,0},{64,32},{96,64},{1,97},{33,1},{65,33},{97,65},{2,98}... | collective-permute-start | bytes 1572872 | tf_op jit(solution)/shard_map/ppermute | solution.py:26
  6.2 22.4 %collective-permute-start = (bf16[512,512]{1,0:T(8,128)(2,1)S(1)}, bf16[512,512]{1,0:T(8,128)(2,1)S(1)}, u32[]{:S(2)}, u32[]{:S(2)}) collective-permute-start(bf16[512,512]{1,0:T(8,128)(2,1)S(1)} %broadcast_select_fusion), channel_id=1, source_target_pairs={{0,32},{32,64},{64,96},{96,0},{1,33},{33,65},{65,97},{97,1},{2,34}... | collective-permute-start | bytes 1572872 | tf_op jit(solution)/shard_map/ppermute | solution.py:26
  7.2 0.7 copy-start
  28.6 1.9 collective-permute-start.3
  28.6 2.7 %collective-permute-start.4 = (bf16[512,512]{1,0:T(8,128)(2,1)S(1)}, bf16[512,512]{1,0:T(8,128)(2,1)S(1)}, u32[]{:S(2)}, u32[]{:S(2)}) collective-permute-start(bf16[512,512]{1,0:T(8,128)(2,1)S(1)} %collective-permute-done.1.rest_4_), channel_id=1, source_target_pairs={{0,1},{1,0},{2,3},{3,2},{4,5},{5,4},{6,7},{7,6},{8,9},{9,8},{10,11... | collective-permute-start | bytes 1572872 | tf_op jit(solution)/shard_map/ppermute | solution.py:31
  29.1 2.9 %collective-permute-start.5 = (bf16[512,512]{1,0:T(8,128)(2,1)S(1)}, bf16[512,512]{1,0:T(8,128)(2,1)S(1)}, u32[]{:S(2)}, u32[]{:S(2)}) collective-permute-start(bf16[512,512]{1,0:T(8,128)(2,1)S(1)} %collective-permute-done.2.rest_6_), channel_id=1, source_target_pairs={{0,1},{1,0},{2,3},{3,2},{4,5},{5,4},{6,7},{7,6},{8,9},{9,8},{10,11... | collective-permute-start | bytes 1572872 | tf_op jit(solution)/shard_map/ppermute | solution.py:31
  65.9 14.2 %copy-start.2 = (bf16[512,172]{0,1:T(8,128)(2,1)S(1)}, bf16[512,172]{0,1:T(8,128)(2,1)}, u32[]{:S(2)}) copy-start(bf16[512,172]{0,1:T(8,128)(2,1)} %param.13) | copy-start | bytes 528388
  65.9 14.2 %copy-start.3 = (s32[4,256]{1,0:T(4,128)S(1)}, s32[4,256]{1,0:T(4,128)}, u32[]{:S(2)}) copy-start(s32[4,256]{1,0:T(4,128)} %lab_ref.1) | copy-start | bytes 12292
  65.9 14.2 %copy-start.4 = (s32[4,256]{1,0:T(4,128)S(1)}, s32[4,256]{1,0:T(4,128)}, u32[]{:S(2)}) copy-start(s32[4,256]{1,0:T(4,128)} %mask_ref.1) | copy-start | bytes 12292
  96.1 2.7 %collective-permute-start.6 = (bf16[512,512]{1,0:T(8,128)(2,1)S(1)}, bf16[512,512]{1,0:T(8,128)(2,1)S(1)}, u32[]{:S(2)}, u32[]{:S(2)}) collective-permute-start(bf16[512,512]{1,0:T(8,128)(2,1)S(1)} %get-tuple-element.102), channel_id=1, source_target_pairs={{0,1},{1,0},{2,3},{3,2},{4,5},{5,4},{6,7},{7,6},{8,9},{9,8},{10,11... | collective-permute-start | bytes 1572872 | tf_op jit(solution)/shard_map/ppermute | solution.py:31
  111.1 3.0 %collective-permute-start.7 = (bf16[512,512]{1,0:T(8,128)(2,1)S(1)}, bf16[512,512]{1,0:T(8,128)(2,1)S(1)}, u32[]{:S(2)}, u32[]{:S(2)}) collective-permute-start(bf16[512,512]{1,0:T(8,128)(2,1)S(1)} %get-tuple-element.114), channel_id=1, source_target_pairs={{0,1},{1,0},{2,3},{3,2},{4,5},{5,4},{6,7},{7,6},{8,9},{9,8},{10,11... | collective-permute-start | bytes 1572872 | tf_op jit(solution)/shard_map/ppermute | solution.py:31
  135.0 2.3 %collective-permute-start.9 = (bf16[512,512]{1,0:T(8,128)(2,1)S(1)}, bf16[512,512]{1,0:T(8,128)(2,1)S(1)}, u32[]{:S(2)}, u32[]{:S(2)}) collective-permute-start(bf16[512,512]{1,0:T(8,128)(2,1)S(1)} %get-tuple-element.127), channel_id=1, source_target_pairs={{0,1},{1,0},{2,3},{3,2},{4,5},{5,4},{6,7},{7,6},{8,9},{9,8},{10,11... | collective-permute-start | bytes 1572872 | tf_op jit(solution)/shard_map/ppermute | solution.py:31
  135.8 2.3 %collective-permute-start.8 = (bf16[512,512]{1,0:T(8,128)(2,1)S(1)}, bf16[512,512]{1,0:T(8,128)(2,1)S(1)}, u32[]{:S(2)}, u32[]{:S(2)}) collective-permute-start(bf16[512,512]{1,0:T(8,128)(2,1)S(1)} %get-tuple-element.117), channel_id=1, source_target_pairs={{0,1},{1,0},{2,3},{3,2},{4,5},{5,4},{6,7},{7,6},{8,9},{9,8},{10,11... | collective-permute-start | bytes 1572872 | tf_op jit(solution)/shard_map/ppermute | solution.py:31
  139.9 4.2 %copy-start.5 = (bf16[4,256,512]{2,1,0:T(8,128)(2,1)S(1)}, bf16[4,256,512]{2,1,0:T(8,128)(2,1)}, u32[]{:S(2)}) copy-start(bf16[4,256,512]{2,1,0:T(8,128)(2,1)} %get-tuple-element.131.refs_0_) | copy-start | bytes 3145732
  139.9 21.7 %copy-start.1 = (s32[4,1,2,4]{3,2,1,0:T(2,128)S(1)}, s32[4,1,2,4]{3,2,1,0:T(2,128)}, u32[]{:S(2)}) copy-start(s32[4,1,2,4]{3,2,1,0:T(2,128)} %param.16) | copy-start | bytes 388
  139.9 30.1 %all-to-all-start.7 = ((bf16[32,56,512]{2,1,0:T(8,128)(2,1)}), bf16[32,56,512]{2,1,0:T(8,128)(2,1)S(1)}, u32[]{:S(2)}, u32[]{:S(2)}) async-start(bf16[32,56,512]{2,1,0:T(8,128)(2,1)} %join_rows.1), calls=%async_computation.7 | async-start | bytes 3670016 | tf_op jit(solution)/shard_map/all_to_all | solution.py:35
  144.1 13.8 %collective-permute-start.12 = (bf16[256,512]{1,0:T(8,128)(2,1)S(1)}, bf16[256,512]{1,0:T(8,128)(2,1)S(1)}, u32[]{:S(2)}, u32[]{:S(2)}) collective-permute-start(bf16[256,512]{1,0:T(8,128)(2,1)S(1)} %get-tuple-element.151), channel_id=1, source_target_pairs={{0,96},{32,0},{64,32},{96,64},{1,97},{33,1},{65,33},{97,65},{2,98}... | collective-permute-start | bytes 786440 | tf_op jit(solution)/shard_map/ppermute | solution.py:26
  146.4 11.6 %collective-permute-start.11 = (bf16[256,512]{1,0:T(8,128)(2,1)S(1)}, bf16[256,512]{1,0:T(8,128)(2,1)S(1)}, u32[]{:S(2)}, u32[]{:S(2)}) collective-permute-start(bf16[256,512]{1,0:T(8,128)(2,1)S(1)} %get-tuple-element.152), channel_id=1, source_target_pairs={{0,64},{32,96},{64,0},{96,32},{1,65},{33,97},{65,1},{97,33},{2,66}... | collective-permute-start | bytes 786440 | tf_op jit(solution)/shard_map/ppermute | solution.py:26
  147.1 14.6 %collective-permute-start.10 = (bf16[256,512]{1,0:T(8,128)(2,1)S(1)}, bf16[256,512]{1,0:T(8,128)(2,1)S(1)}, u32[]{:S(2)}, u32[]{:S(2)}) collective-permute-start(bf16[256,512]{1,0:T(8,128)(2,1)S(1)} %get-tuple-element.153), channel_id=1, source_target_pairs={{0,32},{32,64},{64,96},{96,0},{1,33},{33,65},{65,97},{97,1},{2,34}... | collective-permute-start | bytes 786440 | tf_op jit(solution)/shard_map/ppermute | solution.py:26
  172.3 9.7 %all-to-all-start.8 = ((bf16[4,2,16,512]{3,2,1,0:T(8,128)(2,1)}), bf16[4,2,16,512]{3,2,1,0:T(8,128)(2,1)S(1)}, u32[]{:S(2)}, u32[]{:S(2)}) async-start(bf16[4,2,16,512]{3,2,1,0:T(8,128)(2,1)} %sum_chunks.1), calls=%async_computation.8 | async-start | bytes 262144 | tf_op jit(solution)/shard_map/all_to_all | solution.py:562
  183.4 19.8 %all-to-all-start.9 = ((bf16[32,16,512]{2,1,0:T(8,128)(2,1)}), bf16[32,16,512]{2,1,0:T(8,128)(2,1)S(1)}, u32[]{:S(2)}, u32[]{:S(2)}) async-start(bf16[32,16,512]{2,1,0:T(8,128)(2,1)} %sum_over_layer.1), calls=%async_computation.9 | async-start | bytes 1048576 | tf_op jit(solution)/shard_map/all_to_all | solution.py:35
  187.3 15.3 %collective-permute-start.13 = (bf16[256,512]{1,0:T(8,128)(2,1)S(1)}, bf16[256,512]{1,0:T(8,128)(2,1)S(1)}, u32[]{:S(2)}, u32[]{:S(2)}) collective-permute-start(bf16[256,512]{1,0:T(8,128)(2,1)S(1)} %get-tuple-element.139), channel_id=1, source_target_pairs={{0,32},{32,64},{64,96},{96,0},{1,33},{33,65},{65,97},{97,1},{2,34}... | collective-permute-start | bytes 786440 | tf_op jit(solution)/shard_map/ppermute | solution.py:26
  188.0 14.6 %collective-permute-start.14 = (bf16[256,512]{1,0:T(8,128)(2,1)S(1)}, bf16[256,512]{1,0:T(8,128)(2,1)S(1)}, u32[]{:S(2)}, u32[]{:S(2)}) collective-permute-start(bf16[256,512]{1,0:T(8,128)(2,1)S(1)} %get-tuple-element.140), channel_id=1, source_target_pairs={{0,64},{32,96},{64,0},{96,32},{1,65},{33,97},{65,1},{97,33},{2,66}... | collective-permute-start | bytes 786440 | tf_op jit(solution)/shard_map/ppermute | solution.py:26
  190.0 13.2 %collective-permute-start.15 = (bf16[256,512]{1,0:T(8,128)(2,1)S(1)}, bf16[256,512]{1,0:T(8,128)(2,1)S(1)}, u32[]{:S(2)}, u32[]{:S(2)}) collective-permute-start(bf16[256,512]{1,0:T(8,128)(2,1)S(1)} %get-tuple-element.141), channel_id=1, source_target_pairs={{0,96},{32,0},{64,32},{96,64},{1,97},{33,1},{65,33},{97,65},{2,98}... | collective-permute-start | bytes 786440 | tf_op jit(solution)/shard_map/ppermute | solution.py:26
  203.2 2.6 %collective-permute-start.16 = (bf16[512,512]{1,0:T(8,128)(2,1)S(1)}, bf16[512,512]{1,0:T(8,128)(2,1)S(1)}, u32[]{:S(2)}, u32[]{:S(2)}) collective-permute-start(bf16[512,512]{1,0:T(8,128)(2,1)S(1)} %bitcast.33), channel_id=1, source_target_pairs={{0,1},{1,0},{2,3},{3,2},{4,5},{5,4},{6,7},{7,6},{8,9},{9,8},{10,11... | collective-permute-start | bytes 1572872 | tf_op jit(solution)/shard_map/ppermute | solution.py:31

commit v7 on v5

--- a/solution.py
+++ b/solution.py
@@ -177,9 +177,15 @@
 def forward_kernel(layer, ids, cols, h_ref, arr_ref, vals_ref, pick_ref, *rest):
     w_refs, rest = rest[:8], rest[8:]
     first = layer == 0
-    w_ref, rest = (rest[6], rest) if first else (rest[0], rest[2:])
-    agg_ref, pre_ref, hid_ref, out_ref, buf_ref, next_ref = rest[:6]
+    if first:
+        agg_ref, pre_ref, hid_ref, out_ref, next_ref, w_ref = rest[:6]
+    else:
+        w_ref, *rest = rest[0:1] + rest[1 + (layer > 1) :]
+        agg_ref, pre_ref, hid_ref, out_ref, next_ref, buf_ref = rest[:6]
     ext, buf_sem, sems = rest[-3:]
+    if not first:
+        copy = to_slot(h_ref, layer - 1, ids, buf_ref, buf_sem)
+        copy.start()
     ready = None
     if first:
         here = (layer, ids, w_refs, w_ref, sems.at[0])
@@ -189,12 +195,11 @@
     start_weights(*ahead)
     agg, pre, _, hid = forward_math(ids, cols, h_ref, arr_ref, vals_ref, w_ref, ext, ready)
     hid_ref[...] = hid
-    copy = to_slot(hid_ref, layer, ids, buf_ref, buf_sem)
-    copy.start()
     out_ref[...] = dot(pick_ref[...], hid).astype(BF)
     agg_ref[...] = agg
     pre_ref[...] = pre
-    copy.wait()
+    if not first:
+        copy.wait()
     wait_weights(*ahead)
 
 
@@ -221,11 +226,14 @@
 
 def top_kernel(layer, ids, cols, h_ref, arr_ref, vals_ref, wout_ref, lab_ref, mask_ref, w_ref, *rest):
     remote_ref, part_ref, keep_ref, send_ref, buf_ref, hid_ref, ext, d_ext, buf_sem = rest[1:]
+    copy = to_slot(h_ref, layer - 1, ids, buf_ref, buf_sem)
+    copy.start()
     rows = h_ref.shape[0]
     agg, pre, sig, hid = forward_math(ids, cols, h_ref, arr_ref, vals_ref, w_ref, ext)
     hid_ref[...] = hid
-    copy = to_slot(hid_ref, layer, ids, buf_ref, buf_sem)
-    copy.start()
+    last = to_slot(hid_ref, layer, ids, buf_ref, buf_sem)
+    copy.wait()
+    last.start()
     logits = dot(wout_ref[...], hid, NT)
     expo = jnp.exp(logits)
     probs = expo / jnp.sum(expo, axis=0, keepdims=True)
@@ -239,7 +247,7 @@
     remote_ref[...] = d_ext[rows : 2 * rows, :].astype(BF).reshape(remote_ref.shape)
     part_ref[...] = back + d_ext[0:rows, :]
     weight_partials(ids, h_ref, agg, d_pre, keep_ref, send_ref)
-    copy.wait()
+    last.wait()
 
 
 def chunk_sum(block):
@@ -295,20 +303,31 @@
 
 
 def last_spread_kernel(
-    ids, cols, dpre_ref, vals_ref, w_ref, keep_a, recv_a, keep_b, recv_b,
-    out_ref, part_ref, d_ext, local, sem,
+    ids, cols, dpre_ref, vals_ref, w_ref, keep_a, recv_a, keep_b, recv_b, c_in,
+    out_ref, part_ref, c_ref, d_ext, part, carried, local, sems,
 ):
     rows, feat = dpre_ref.shape
-    peers, used = local.shape[0], local.shape[1]
-    slots, size = rows // peers, keep_a.shape[0] // peers
-    put_carry(keep_a, recv_a, local, slots)
-    put_carry(keep_b, recv_b, local, slots + size)
+    peers, slots = local.shape[0], local.shape[1]
+    size = keep_a.shape[0] // peers
+    copies = [
+        pltpu.make_async_copy(c_in, c_ref.at[3], sems.at[0]),
+        pltpu.make_async_copy(
+            carried, out_ref.at[:, pl.ds(slots, 2 * size), :], sems.at[1]
+        ),
+        pltpu.make_async_copy(local, out_ref.at[:, pl.ds(0, slots), :], sems.at[2]),
+        pltpu.make_async_copy(part, part_ref, sems.at[3]),
+    ]
+    copies[0].start()
+    put_carry(keep_a, recv_a, carried, 0)
+    put_carry(keep_b, recv_b, carried, size)
+    copies[1].start()
     back = backward_math(ids, cols, dpre_ref[...], vals_ref, w_ref, d_ext)
-    local[:, 0:slots, :] = d_ext[rows : 2 * rows, :].astype(BF).reshape(peers, slots, feat)
-    away = pltpu.make_async_copy(local, out_ref.at[:, pl.ds(0, used), :], sem)
-    away.start()
-    part_ref[...] = back + d_ext[0:rows, :]
-    away.wait()
+    local[...] = d_ext[rows : 2 * rows, :].astype(BF).reshape(local.shape)
+    copies[2].start()
+    part[...] = back + d_ext[0:rows, :]
+    copies[3].start()
+    for copy in copies:
+        copy.wait()
 
 
 def put_carry(keep_ref, recv_ref, out_ref, first):
@@ -327,13 +346,15 @@
     copy.wait()
 
 
-def chunk_kernel(ids, cols, ret_ref, c_3, out_ref):
-    size = c_3.shape[1]
+def chunk_kernel(ids, cols, ret_ref, buf_in, out_ref, sums, sem):
+    size = sums.shape[2]
     slots = ret_ref.shape[1] - 3 * size
-    out_ref[3] = c_3[...]
     for n, layer in enumerate((2, 1, 0)):
         first = slots + n * size
-        out_ref[layer] = chunk_sum(ret_ref[:, first : first + size, :]).astype(BF)
+        sums[layer] = chunk_sum(ret_ref[:, first : first + size, :]).astype(BF)
+    copy = pltpu.make_async_copy(sums, out_ref.at[pl.ds(0, 3)], sem)
+    copy.start()
+    copy.wait()
 
 
 def end_kernel(ids, cols, ret_ref, part_in, pick_ref, buf_in, buf_ref, dout_ref, buf_sem):
@@ -354,13 +375,7 @@
         out_ref[n : n + 2] = total
 
 
-def final_kernel(scale, ids, cols, mine_ref, other_ref, own, one, two, three, late, home_ref, self_ref, neigh_ref):
-    home_kernel(ids, cols, own, one, two, three, home_ref)
-
-    @pl.when(ids[0] == 0)
-    def _():
-        home_ref[0, 2] = late[...]
-
+def scale_kernel(scale, ids, cols, mine_ref, other_ref, self_ref, neigh_ref):
     mine = mine_ref[...].astype(F32) * scale
     other = other_ref[...].astype(F32) * scale
 
@@ -433,7 +448,7 @@
     )
     arrived = exchange(outgoing.reshape(peers, slots, feat))
     arrived, left, right, far = tie(arrived, left, right, far)
-    sources = [(w_self[0], FAR), (w_neigh[0], FAR), left, sibling(left), right, sibling(right)]
+    sources = [w_self[0], w_neigh[0], left, sibling(left), right, sibling(right)]
     sources += [far, sibling(far)]
     weight = near((2, feat, feat))
 
@@ -445,22 +460,28 @@
     for layer in range(top):
         ins = [hidden[layer], arrived.reshape(rows, feat), vals, pick, *sources]
         if layer:
-            ins += [weights[layer], (acts_buf, FAR)]
-        agg, pre, hid, outgoing, acts_buf, *arranged = run(
+            ins.append(weights[layer])
+        if layer > 1:
+            ins.append((acts_buf, FAR))
+        agg, pre, hid, outgoing, arranged, last = run(
             functools.partial(forward_kernel, layer),
             f"layer_forward_{layer}",
             scalars,
             ins,
-            [act, wide, act, act, stack] + [weight] * (2 if layer == 0 else 1),
+            [act, wide, act, act, weight, stack if layer else weight],
             [ext_scratch, buf_sem, pltpu.SemaphoreType.DMA((2, 2))],
-            {len(ins) - 1: 4} if layer else None,
+            {len(ins) - 1: 5} if layer > 1 else None,
             flops=6 * 10**8,
             moved=4 * 10**6,
         )
+        if layer:
+            acts_buf = last
+        else:
+            weights.append(last)
+        weights.append(arranged)
         hidden.append(hid)
         aggs.append(agg)
         pres.append(pre)
-        weights += arranged[::-1]
         arrived = exchange(outgoing.reshape(peers, slots, feat))
 
     ins = [
@@ -493,14 +514,15 @@
     def travel(buf):
         return [shift(buf[s], "layer", s) for s in all_shifts]
 
+    first_block = pl.BlockSpec((None, rows, feat), lambda i, ids, cols: (0, 0, 0))
+
     def put_home(buf, *pieces):
-        block = pl.BlockSpec((None, rows, feat), lambda i, ids, cols: (0, 0, 0))
         shape = (1, spans, rows, feat)
         return run(
             home_kernel,
             "put_home",
             scalars,
-            [(buf, block), *pieces],
+            [(buf, first_block), *pieces],
             [far_block(shape)],
             moved=2 * 10**6,
         )[0]
@@ -542,12 +564,13 @@
 
     returned, send = tie(exchange(remote), send)
     recv_1, keep_1 = sibling(send), keep
+    chunk_shape = (2, chunk_rows, feat)
     d_pre, grads_buf, keep, send, c_3 = run(
         last_slope_kernel,
         "last_slope",
         scalars,
         [returned, part, pres[0], hidden[0], aggs[0], pick, (grads_buf, FAR)],
-        [act, stack, square, square, far_block((2, chunk_rows, feat))],
+        [act, stack, square, square, near(chunk_shape)],
         [pltpu.VMEM((rows, feat), BF), buf_sem],
         {6: 1},
         flops=4 * 10**8,
@@ -557,13 +580,20 @@
     recv = sibling(send)
     width = slots + 3 * chunk_rows
     operand = (pltpu.HBM((peers, width, feat), BF), FAR)
-    remote, part = run(
+    sums_out = (pltpu.HBM((spans, *chunk_shape), BF), FAR)
+    remote, part, sums = run(
         last_spread_kernel,
         "last_spread",
         scalars,
-        [d_pre, vals, weights[0], *pairs[-1], keep_1, recv_1],
-        [operand, far_block((rows, feat), F32)],
-        [d_ext_scratch, pltpu.VMEM((peers, width - chunk_rows, feat), BF), buf_sem],
+        [d_pre, vals, weights[0], *pairs[-1], keep_1, recv_1, c_3],
+        [operand, (pltpu.HBM((rows, feat), F32), FAR), sums_out],
+        [
+            d_ext_scratch,
+            pltpu.VMEM((rows, feat), F32),
+            pltpu.VMEM((peers, 2 * chunk_rows, feat), BF),
+            pltpu.VMEM((peers, slots, feat), BF),
+            pltpu.SemaphoreType.DMA((4,)),
+        ],
         flops=5 * 10**8,
         moved=4 * 10**6,
     )
@@ -578,20 +608,22 @@
         aliases={2: 0},
         moved=2 * 10**6,
     )[0]
-    joined, acts_buf, grads_buf = tie(joined, acts_buf, grads_buf)
+    joined, acts_buf = tie(joined, acts_buf)
     acts = travel(acts_buf)
-    early = lax.ppermute(grads_buf[2], "layer", [(0, 2), (1, 3), (3, 1)])
-    returned, early, *acts = tie(exchange(joined), early, *acts)
+    layer_acts = put_home(acts_buf, *acts)
+    returned, layer_acts = tie(exchange(joined), layer_acts)
     sums = run(
         chunk_kernel,
         "sum_chunks",
         scalars,
-        [returned, (c_3, whole(c_3.shape))],
-        [far_block((spans, 2, chunk_rows, feat))],
+        [returned, (sums, FAR)],
+        [sums_out],
+        [pltpu.VMEM((3, *chunk_shape), BF), buf_sem],
+        aliases={1: 0},
         moved=10**6,
     )[0]
     sums = lax.all_to_all(sums, "layer", split_axis=0, concat_axis=0, tiled=True)
-    grads_buf, d_out = run(
+    grads_buf = run(
         end_kernel,
         "input_grads",
         scalars,
@@ -601,13 +633,13 @@
             (pick_far, whole(pick_far.shape)),
             (grads_buf, FAR),
         ],
-        [stack, far_block((rows, feat))],
-        [buf_sem],
+        [stack],
+        [pltpu.VMEM((rows, feat), BF), buf_sem],
         {3: 0},
         flops=10**8,
         moved=10**6,
-    )
-    sums, grads_buf, d_out = tie(sums, grads_buf, d_out)
+    )[0]
+    sums, *to_send = tie(sums, *[grads_buf[s] for s in all_shifts])
     spread = run(
         layer_sum_kernel,
         "sum_over_layer",
@@ -616,27 +648,19 @@
         [far_block((peers, chunk_rows, feat))],
         moved=10**6,
     )[0]
-    layer_acts = put_home(acts_buf, *acts)
-    grads = [shift(grads_buf[s], "layer", s) for s in (1, 3)]
-    late = lax.ppermute(d_out, "layer", [(2, 0)])
-    gathered, layer_acts, late, *grads = tie(exchange(spread), layer_acts, late, *grads)
+    grads = [shift(v, "layer", s) for s, v in zip(all_shifts, to_send)]
+    gathered, *grads = tie(exchange(spread), *grads)
     gathered = gathered.reshape(feat, feat)
-    out_square, shape = (1, feat, feat), (1, spans, rows, feat)
-    act_grads, grad_self, grad_neigh = run(
-        functools.partial(final_kernel, scale),
-        "final_outputs",
-        scalars,
-        [
-            gathered,
-            sibling(gathered),
-            (grads_buf, pl.BlockSpec((None, rows, feat), lambda i, ids, cols: (0, 0, 0))),
-            grads[0],
-            early,
-            grads[1],
-            late,
-        ],
-        [far_block(shape), far_block(out_square, F32), far_block(out_square, F32)],
-        moved=6 * 10**6,
+    other = sibling(gathered)
+    act_grads = put_home(grads_buf, *grads)
+    out_square = (1, feat, feat)
+    grad_self, grad_neigh = run(
+        functools.partial(scale_kernel, scale),
+        "scale_grads",
+        scalars,
+        [gathered, other],
+        [(pltpu.HBM(out_square, F32), whole(out_square))] * 2,
+        moved=3 * 10**6,
     )
     return (layer_acts, act_grads, grad_self, grad_neigh)
 

time: 215 us -> 208 us (0.967)
  Pallas kernels: 39.7 us -> 36.2 us
  starting transfers between devices: 30.2 us -> 27.8 us
    ppermute x8 -> x9, waiting for transfers between devices: 16.8 us -> 26.5 us  [shift(): lax.ppermute(value, axis, [(i, (i + steps) % count) for i in range(count)])]
    ppermute x2 -> x0, waiting for transfers between devices: 9.5 us -> none  [the longest x1 6.74 us: body(): late = lax.ppermute(d_out, 'layer', [(2, 0)])]
    ppermute x2 -> x0, starting transfers between devices: 5.38 us -> none  [the longest x1 4.08 us: body(): early = lax.ppermute(grads_buf[2], 'layer', [(0, 2), (1, 3), (3, 1)])]
    ppermute x8 -> x9, starting transfers between devices: 10 us -> 13.7 us  [shift(): lax.ppermute(value, axis, [(i, (i + steps) % count) for i in range(count)])]
    pallas_call x15 -> x16, Pallas kernels: 39.7 us -> 36.2 us  [run(): pl.pallas_call(kernel, name=name, grid_spec=pltpu.PrefetchScalarGridSpec(...]
  transfers between devices with their start and end apart: 21 -> 20, of which waited for: 12 -> 10; matrix products, arithmetic and copies ran while one was open for 1% -> 1% of each run, Pallas kernels for 9% -> 10%
where the time goes in v7:
time: 208 us; the launch traced here: 206 us
  blocking collectives  101 us (49%)
  waiting for transfers between devices  36.9 us (18%)
  Pallas kernels  36.2 us (17%)
  starting transfers between devices  27.8 us (13%)
    all_to_all x7, blocking collectives, exchange(): lax.all_to_all(value, 'node', split_axis=0, concat_axis=0, tiled=True)  101 us
    pallas_call x16, Pallas kernels, run(): pl.pallas_call(kernel, name=name, grid_spec=pltpu.PrefetchScalarGridSpec(...  36.2 us
    ppermute x9, waiting for transfers between devices, shift(): lax.ppermute(value, axis, [(i, (i + steps) % count) for i in range(count)])  26.5 us
    ppermute x9, starting transfers between devices, shift(): lax.ppermute(value, axis, [(i, (i + steps) % count) for i in range(count)])  13.7 us
    all_to_all x2, starting transfers between devices, exchange(): lax.all_to_all(value, 'node', split_axis=0, concat_axis=0, tiled=True)  8.08 us
    all_to_all x2, waiting for transfers between devices, exchange(): lax.all_to_all(value, 'node', split_axis=0, concat_axis=0, tiled=True)  5.34 us
    all_to_all x1, starting transfers between devices, body(): lax.all_to_all(sums, 'layer', split_axis=0, concat_axis=0, tiled=True)  4.18 us
  transfers between devices with their start and end apart: 20, of which 10 were waited for; matrix products, arithmetic and copies ran while one was open for 1% of the time, Pallas kernels for 10%

profile of v7, /device:TPU:0, one launch (start us, length us, event | category | flops | bytes accessed | tf_op | source)
XLA Modules:
  0.0 206.1 jit_solution(4677459324570177711)
XLA Ops:
  0.7 1.3 broadcast_select_fusion
  2.0 3.2 %collective-permute-start.2 = (bf16[512,512]{1,0:T(8,128)(2,1)S(1)}, bf16[512,512]{1,0:T(8,128)(2,1)S(1)}, u32[]{:S(2)}, u32[]{:S(2)}) collective-permute-start(bf16[512,512]{1,0:T(8,128)(2,1)S(1)} %broadcast_select_fusion), channel_id=1, source_target_pairs={{0,64},{32,96},{64,0},{96,32},{1,65},{33,97},{65,1},{97,33},{2,66}... | collective-permute-start | bytes 1572872 | tf_op jit(solution)/shard_map/ppermute | solution.py:26
  5.2 1.1 collective-permute-start.1
  6.3 0.9 collective-permute-start
  7.3 0.7 copy-done.2
  8.0 2.6 %gather_rows.1 = (bf16[256,256]{1,0:T(8,128)(2,1)S(1)}, bf16[256,512]{1,0:T(8,128)(2,1)S(1)}, bf16[256,512]{1,0:T(8,128)(2,1)S(1)}, bf16[2,4,128,128]{3,2,1,0:T(8,128)(2,1)S(1)}, bf16[256,256]{1,0:T(8,128)(2,1)}) custom-call(s32[2]{0:T(128)S(1)} %pad_add_fusion.ids, s32[4,2,4]{2,1,0:T(2,128)S(1)} %bitcast.44, bf16[4,256,512]{2,1,0:T(8,128)(2,1)} %h_ref.1, ...), custom_call_target="tpu_custom_call" | custom-call | flops 100000000 | bytes 1000000 | tf_op jit(solution)/shard_map/gather_rows/pallas_call | solution.py:60
  10.6 17.1 %all_to_all.50 = bf16[32,8,512]{2,1,0:T(8,128)(2,1)S(1)} all-to-all(bf16[32,8,512]{2,1,0:T(8,128)(2,1)S(1)} %bitcast.64), channel_id=1, replica_groups=mesh['layer'=4,'node'=32] {'node'}, dimensions={0} | all-to-all | bytes 524288 | tf_op jit(solution)/shard_map/all_to_all | solution.py:35
  27.7 1.0 collective-permute-done.1.rest_4_
  29.2 1.4 collective-permute-done.3.rest_3_
  30.6 0.7 collective-permute-done.4.rest_5_
  31.4 0.7 collective-permute-done.5.rest_7_
  32.1 1.9 layer_forward_0.1
  34.1 17.1 %all_to_all.51 = bf16[32,8,512]{2,1,0:T(8,128)(2,1)S(1)} all-to-all(bf16[32,8,512]{2,1,0:T(8,128)(2,1)S(1)} %bitcast.62), channel_id=1, replica_groups=mesh['layer'=4,'node'=32] {'node'}, dimensions={0} | all-to-all | bytes 524288 | tf_op jit(solution)/shard_map/all_to_all | solution.py:35
  51.1 1.7 layer_forward_1.1
  52.9 12.5 %all_to_all.52 = bf16[32,8,512]{2,1,0:T(8,128)(2,1)S(1)} all-to-all(bf16[32,8,512]{2,1,0:T(8,128)(2,1)S(1)} %bitcast.63), channel_id=1, replica_groups=mesh['layer'=4,'node'=32] {'node'}, dimensions={0} | all-to-all | bytes 524288 | tf_op jit(solution)/shard_map/all_to_all | solution.py:35
  65.3 1.7 layer_forward_2.1
  67.1 12.5 %all_to_all.53 = bf16[32,8,512]{2,1,0:T(8,128)(2,1)S(1)} all-to-all(bf16[32,8,512]{2,1,0:T(8,128)(2,1)S(1)} %bitcast.60), channel_id=1, replica_groups=mesh['layer'=4,'node'=32] {'node'}, dimensions={0} | all-to-all | bytes 524288 | tf_op jit(solution)/shard_map/all_to_all | solution.py:35
  79.5 3.6 %top_layer.1 = (bf16[32,8,512]{2,1,0:T(8,128)(2,1)S(1)}, f32[256,512]{1,0:T(8,128)S(1)}, bf16[512,512]{1,0:T(8,128)(2,1)S(1)}, bf16[512,512]{1,0:T(8,128)(2,1)S(1)}, bf16[4,256,512]{2,1,0:T(8,128)(2,1)}) custom-call(s32[2]{0:T(128)S(1)} %pad_add_fusion.ids, s32[4,2,4]{2,1,0:T(2,128)S(1)} %bitcast.48, ...), custom_call_target="tpu_custom_call", output_to_operand_aliasing={{4}: (9, {})} | custom-call | flops 1000000000 | bytes 5000000 | tf_op jit(solution)/shard_map/top_layer/pallas_call | solution.py:60
  83.1 12.5 %all_to_all.54.ret_ref = bf16[32,8,512]{2,1,0:T(8,128)(2,1)S(1)} all-to-all(bf16[32,8,512]{2,1,0:T(8,128)(2,1)S(1)} %get-tuple-element.102), channel_id=1, replica_groups=mesh['layer'=4,'node'=32] {'node'}, dimensions={0} | all-to-all | bytes 524288 | tf_op jit(solution)/shard_map/all_to_all | solution.py:35
  95.9 2.4 %layer_backward_2.1 = (bf16[32,8,512]{2,1,0:T(8,128)(2,1)S(1)}, f32[256,512]{1,0:T(8,128)S(1)}, bf16[4,256,512]{2,1,0:T(8,128)(2,1)}, bf16[512,512]{1,0:T(8,128)(2,1)S(1)}, bf16[512,512]{1,0:T(8,128)(2,1)S(1)}) custom-call(s32[2]{0:T(128)S(1)} %pad_add_fusion.ids, s32[4,2,4]{2,1,0:T(2,128)S(1)} %bitcast.49, bf16[32,8,512]{2,1,0:T(8,128)(2,1)S(1)} %all_to_all.54.ret_ref, ...), custom_call_target="tpu_custom_call" | custom-call | flops 1000000000 | bytes 5000000 | tf_op jit(solution)/shard_map/layer_backward_2/pallas_call | solution.py:60
  98.3 12.3 %all_to_all.55.ret_ref = bf16[32,8,512]{2,1,0:T(8,128)(2,1)S(1)} all-to-all(bf16[32,8,512]{2,1,0:T(8,128)(2,1)S(1)} %get-tuple-element.110), channel_id=1, replica_groups=mesh['layer'=4,'node'=32] {'node'}, dimensions={0} | all-to-all | bytes 524288 | tf_op jit(solution)/shard_map/all_to_all | solution.py:35
  110.9 2.6 %layer_backward_1.1 = (bf16[32,24,512]{2,1,0:T(8,128)(2,1)S(1)}, f32[256,512]{1,0:T(8,128)S(1)}, bf16[4,256,512]{2,1,0:T(8,128)(2,1)}, bf16[512,512]{1,0:T(8,128)(2,1)S(1)}, bf16[512,512]{1,0:T(8,128)(2,1)S(1)}) custom-call(s32[2]{0:T(128)S(1)} %pad_add_fusion.ids, s32[4,2,4]{2,1,0:T(2,128)S(1)} %bitcast.50, ...), custom_call_target="tpu_custom_call", output_to_operand_aliasing={{2}: (12, {})} | custom-call | flops 1000000000 | bytes 5000000 | tf_op jit(solution)/shard_map/layer_backward_1/pallas_call | solution.py:60
  113.5 17.2 %all_to_all.56.ret_ref = bf16[32,24,512]{2,1,0:T(8,128)(2,1)S(1)} all-to-all(bf16[32,24,512]{2,1,0:T(8,128)(2,1)S(1)} %get-tuple-element.121), channel_id=1, replica_groups=mesh['layer'=4,'node'=32] {'node'}, dimensions={0} | all-to-all | bytes 1572864 | tf_op jit(solution)/shard_map/all_to_all | solution.py:35
  130.7 0.7 collective-permute-start.8
  131.4 1.8 last_slope.1
  133.3 3.2 %last_spread.1 = (bf16[32,56,512]{2,1,0:T(8,128)(2,1)}, f32[256,512]{1,0:T(8,128)}, bf16[4,2,16,512]{3,2,1,0:T(8,128)(2,1)}) custom-call(s32[2]{0:T(128)S(1)} %pad_add_fusion.ids, s32[4,2,4]{2,1,0:T(2,128)S(1)} %bitcast.52, bf16[256,512]{1,0:T(8,128)(2,1)S(1)} %get-tuple-element.132.dpre_ref, ...), custom_call_target="tpu_custom_call" | custom-call | flops 500000000 | bytes 4000000 | tf_op jit(solution)/shard_map/last_spread/pallas_call | solution.py:60
  136.5 1.6 join_rows.1
  138.1 4.2 %all-to-all-start.7 = ((bf16[32,56,512]{2,1,0:T(8,128)(2,1)}), bf16[32,56,512]{2,1,0:T(8,128)(2,1)S(1)}, u32[]{:S(2)}, u32[]{:S(2)}) async-start(bf16[32,56,512]{2,1,0:T(8,128)(2,1)} %join_rows.1), calls=%async_computation.7 | async-start | bytes 3670016 | tf_op jit(solution)/shard_map/all_to_all | solution.py:35
  142.4 2.7 %collective-permute-start.12 = (bf16[256,512]{1,0:T(8,128)(2,1)S(1)}, bf16[256,512]{1,0:T(8,128)(2,1)S(1)}, u32[]{:S(2)}, u32[]{:S(2)}) collective-permute-start(bf16[256,512]{1,0:T(8,128)(2,1)S(1)} %get-tuple-element.165), channel_id=1, source_target_pairs={{0,96},{32,0},{64,32},{96,64},{1,97},{33,1},{65,33},{97,65},{2,98}... | collective-permute-start | bytes 786440 | tf_op jit(solution)/shard_map/ppermute | solution.py:26
  145.1 0.9 collective-permute-start.11
  146.0 0.8 collective-permute-start.10
  146.8 10.0 %collective-permute-done.12.refs_3_ = bf16[256,512]{1,0:T(8,128)(2,1)S(1)} collective-permute-done((bf16[256,512]{1,0:T(8,128)(2,1)S(1)}, bf16[256,512]{1,0:T(8,128)(2,1)S(1)}, u32[]{:S(2)}, u32[]{:S(2)}) %collective-permute-start.12) | collective-permute-done | bytes 262176 | tf_op jit(solution)/shard_map/ppermute | solution.py:26
  156.8 3.7 %collective-permute-done.10.refs_1_ = bf16[256,512]{1,0:T(8,128)(2,1)S(1)} collective-permute-done((bf16[256,512]{1,0:T(8,128)(2,1)S(1)}, bf16[256,512]{1,0:T(8,128)(2,1)S(1)}, u32[]{:S(2)}, u32[]{:S(2)}) %collective-permute-start.10) | collective-permute-done | bytes 262176 | tf_op jit(solution)/shard_map/ppermute | solution.py:26
  160.4 2.6 %put_home.2 = bf16[1,4,256,512]{3,2,1,0:T(8,128)(2,1)} custom-call(s32[2]{0:T(128)S(1)} %pad_add_fusion.ids, s32[4,2,4]{2,1,0:T(2,128)S(1)} %bitcast.54, bf16[4,256,512]{2,1,0:T(8,128)(2,1)} %get-tuple-element.145.refs_0_, bf16[256,512]{1,0:T(8,128)(2,1)S(1)} %collective-permute-done.10.refs_1_, bf16[256,512]{1,0:T(8,128)(2,1)S(1)} %collective-permute-done.11.refs_2_, ...), custom_call_target="tpu_custom_call" | custom-call | bytes 2000000 | tf_op jit(solution)/shard_map/put_home/pallas_call | solution.py:60
  163.0 5.3 %all-to-all-done.7.ret_ref = bf16[32,56,512]{2,1,0:T(8,128)(2,1)S(1)} async-done(((bf16[32,56,512]{2,1,0:T(8,128)(2,1)}), bf16[32,56,512]{2,1,0:T(8,128)(2,1)S(1)}, u32[]{:S(2)}, u32[]{:S(2)}) %all-to-all-start.7) | async-done | bytes 1835040 | tf_op jit(solution)/shard_map/all_to_all | solution.py:35
  168.4 1.5 sum_chunks.1
  169.8 4.2 %all-to-all-start.8 = ((bf16[4,2,16,512]{3,2,1,0:T(8,128)(2,1)}), bf16[4,2,16,512]{3,2,1,0:T(8,128)(2,1)S(1)}, u32[]{:S(2)}, u32[]{:S(2)}) async-start(bf16[4,2,16,512]{3,2,1,0:T(8,128)(2,1)} %sum_chunks.1), calls=%async_computation.8 | async-start | bytes 262144 | tf_op jit(solution)/shard_map/all_to_all | solution.py:625
  174.0 2.6 %input_grads.1.refs_0_ = bf16[4,256,512]{2,1,0:T(8,128)(2,1)} custom-call(s32[2]{0:T(128)S(1)} %pad_add_fusion.ids, s32[4,2,4]{2,1,0:T(2,128)S(1)} %bitcast.56, bf16[32,56,512]{2,1,0:T(8,128)(2,1)S(1)} %all-to-all-done.7.ret_ref, f32[256,512]{1,0:T(8,128)} %get-tuple-element.148.part_in, ...), custom_call_target="tpu_custom_call", output_to_operand_aliasing={{}: (5, {})} | custom-call | flops 100000000 | bytes 1000000 | tf_op jit(solution)/shard_map/input_grads/pallas_call | solution.py:60
  176.6 1.2 slice_bitcast_fusion
  177.8 2.2 %all-to-all-done.8.sums_ref = bf16[4,2,16,512]{3,2,1,0:T(8,128)(2,1)S(1)} async-done(((bf16[4,2,16,512]{3,2,1,0:T(8,128)(2,1)}), bf16[4,2,16,512]{3,2,1,0:T(8,128)(2,1)S(1)}, u32[]{:S(2)}, u32[]{:S(2)}) %all-to-all-start.8) | async-done | bytes 131104 | tf_op jit(solution)/shard_map/all_to_all | solution.py:625
  180.0 1.4 sum_over_layer.1
  181.4 3.9 %all-to-all-start.9 = ((bf16[32,16,512]{2,1,0:T(8,128)(2,1)}), bf16[32,16,512]{2,1,0:T(8,128)(2,1)S(1)}, u32[]{:S(2)}, u32[]{:S(2)}) async-start(bf16[32,16,512]{2,1,0:T(8,128)(2,1)} %sum_over_layer.1), calls=%async_computation.9 | async-start | bytes 1048576 | tf_op jit(solution)/shard_map/all_to_all | solution.py:35
  185.3 0.6 collective-permute-start.13
  186.0 2.1 %collective-permute-start.14 = (bf16[256,512]{1,0:T(8,128)(2,1)S(1)}, bf16[256,512]{1,0:T(8,128)(2,1)S(1)}, u32[]{:S(2)}, u32[]{:S(2)}) collective-permute-start(bf16[256,512]{1,0:T(8,128)(2,1)S(1)} %get-tuple-element.154), channel_id=1, source_target_pairs={{0,64},{32,96},{64,0},{96,32},{1,65},{33,97},{65,1},{97,33},{2,66}... | collective-permute-start | bytes 786440 | tf_op jit(solution)/shard_map/ppermute | solution.py:26
  188.0 1.4 collective-permute-start.15
  189.4 11.2 %collective-permute-done.13.refs_1_ = bf16[256,512]{1,0:T(8,128)(2,1)S(1)} collective-permute-done((bf16[256,512]{1,0:T(8,128)(2,1)S(1)}, bf16[256,512]{1,0:T(8,128)(2,1)S(1)}, u32[]{:S(2)}, u32[]{:S(2)}) %collective-permute-start.13) | collective-permute-done | bytes 262176 | tf_op jit(solution)/shard_map/ppermute | solution.py:26
  201.2 2.6 %put_home.3 = bf16[1,4,256,512]{3,2,1,0:T(8,128)(2,1)} custom-call(s32[2]{0:T(128)S(1)} %pad_add_fusion.ids, s32[4,2,4]{2,1,0:T(2,128)S(1)} %bitcast.58, bf16[4,256,512]{2,1,0:T(8,128)(2,1)} %input_grads.1.refs_0_, bf16[256,512]{1,0:T(8,128)(2,1)S(1)} %collective-permute-done.13.refs_1_, bf16[256,512]{1,0:T(8,128)(2,1)S(1)} %collective-permute-done.14.refs_2_, ...), custom_call_target="tpu_custom_call" | custom-call | bytes 2000000 | tf_op jit(solution)/shard_map/put_home/pallas_call | solution.py:60
  203.8 2.3 %scale_grads.1 = (f32[1,512,512]{2,1,0:T(8,128)}, f32[1,512,512]{2,1,0:T(8,128)}) custom-call(s32[2]{0:T(128)S(1)} %pad_add_fusion.ids, s32[4,2,4]{2,1,0:T(2,128)S(1)} %bitcast.59, bf16[512,512]{1,0:T(8,128)(2,1)S(1)} %bitcast.40, bf16[512,512]{1,0:T(8,128)(2,1)S(1)} %collective-permute-done.16.other_ref), custom_call_target="tpu_custom_call" | custom-call | bytes 3000000 | tf_op jit(solution)/shard_map/scale_grads/pallas_call | solution.py:60
  (35 shorter events, 2.1 us)
Async XLA Ops:
  0.6 31.5 %copy-start = (bf16[1,512,512]{2,1,0:T(8,128)(2,1)S(1)}, bf16[1,512,512]{2,1,0:T(8,128)(2,1)}, u32[]{:S(2)}) copy-start(bf16[1,512,512]{2,1,0:T(8,128)(2,1)} %param.11) | copy-start | bytes 1572868
  0.6 31.5 %copy-start.1 = (bf16[1,512,512]{2,1,0:T(8,128)(2,1)S(1)}, bf16[1,512,512]{2,1,0:T(8,128)(2,1)}, u32[]{:S(2)}) copy-start(bf16[1,512,512]{2,1,0:T(8,128)(2,1)} %param.12) | copy-start | bytes 1572868
  2.0 25.7 %collective-permute-start.2 = (bf16[512,512]{1,0:T(8,128)(2,1)S(1)}, bf16[512,512]{1,0:T(8,128)(2,1)S(1)}, u32[]{:S(2)}, u32[]{:S(2)}) collective-permute-start(bf16[512,512]{1,0:T(8,128)(2,1)S(1)} %broadcast_select_fusion), channel_id=1, source_target_pairs={{0,64},{32,96},{64,0},{96,32},{1,65},{33,97},{65,1},{97,33},{2,66}... | collective-permute-start | bytes 1572872 | tf_op jit(solution)/shard_map/ppermute | solution.py:26
  5.2 23.5 %collective-permute-start.1 = (bf16[512,512]{1,0:T(8,128)(2,1)S(1)}, bf16[512,512]{1,0:T(8,128)(2,1)S(1)}, u32[]{:S(2)}, u32[]{:S(2)}) collective-permute-start(bf16[512,512]{1,0:T(8,128)(2,1)S(1)} %broadcast_select_fusion), channel_id=1, source_target_pairs={{0,96},{32,0},{64,32},{96,64},{1,97},{33,1},{65,33},{97,65},{2,98}... | collective-permute-start | bytes 1572872 | tf_op jit(solution)/shard_map/ppermute | solution.py:26
  6.3 22.4 %collective-permute-start = (bf16[512,512]{1,0:T(8,128)(2,1)S(1)}, bf16[512,512]{1,0:T(8,128)(2,1)S(1)}, u32[]{:S(2)}, u32[]{:S(2)}) collective-permute-start(bf16[512,512]{1,0:T(8,128)(2,1)S(1)} %broadcast_select_fusion), channel_id=1, source_target_pairs={{0,32},{32,64},{64,96},{96,0},{1,33},{33,65},{65,97},{97,1},{2,34}... | collective-permute-start | bytes 1572872 | tf_op jit(solution)/shard_map/ppermute | solution.py:26
  7.3 0.7 copy-start.2
  28.7 1.9 collective-permute-start.3
  28.7 2.7 %collective-permute-start.4 = (bf16[512,512]{1,0:T(8,128)(2,1)S(1)}, bf16[512,512]{1,0:T(8,128)(2,1)S(1)}, u32[]{:S(2)}, u32[]{:S(2)}) collective-permute-start(bf16[512,512]{1,0:T(8,128)(2,1)S(1)} %collective-permute-done.1.rest_4_), channel_id=1, source_target_pairs={{0,1},{1,0},{2,3},{3,2},{4,5},{5,4},{6,7},{7,6},{8,9},{9,8},{10,11... | collective-permute-start | bytes 1572872 | tf_op jit(solution)/shard_map/ppermute | solution.py:31
  29.2 2.9 %collective-permute-start.5 = (bf16[512,512]{1,0:T(8,128)(2,1)S(1)}, bf16[512,512]{1,0:T(8,128)(2,1)S(1)}, u32[]{:S(2)}, u32[]{:S(2)}) collective-permute-start(bf16[512,512]{1,0:T(8,128)(2,1)S(1)} %collective-permute-done.2.rest_6_), channel_id=1, source_target_pairs={{0,1},{1,0},{2,3},{3,2},{4,5},{5,4},{6,7},{7,6},{8,9},{9,8},{10,11... | collective-permute-start | bytes 1572872 | tf_op jit(solution)/shard_map/ppermute | solution.py:31
  65.3 14.2 %copy-start.4 = (bf16[512,172]{0,1:T(8,128)(2,1)S(1)}, bf16[512,172]{0,1:T(8,128)(2,1)}, u32[]{:S(2)}) copy-start(bf16[512,172]{0,1:T(8,128)(2,1)} %param.13) | copy-start | bytes 528388
  65.3 14.2 %copy-start.5 = (s32[4,256]{1,0:T(4,128)S(1)}, s32[4,256]{1,0:T(4,128)}, u32[]{:S(2)}) copy-start(s32[4,256]{1,0:T(4,128)} %lab_ref.1) | copy-start | bytes 12292
  65.3 14.2 %copy-start.6 = (s32[4,256]{1,0:T(4,128)S(1)}, s32[4,256]{1,0:T(4,128)}, u32[]{:S(2)}) copy-start(s32[4,256]{1,0:T(4,128)} %mask_ref.1) | copy-start | bytes 12292
  95.6 2.7 %collective-permute-start.6 = (bf16[512,512]{1,0:T(8,128)(2,1)S(1)}, bf16[512,512]{1,0:T(8,128)(2,1)S(1)}, u32[]{:S(2)}, u32[]{:S(2)}) collective-permute-start(bf16[512,512]{1,0:T(8,128)(2,1)S(1)} %get-tuple-element.109), channel_id=1, source_target_pairs={{0,1},{1,0},{2,3},{3,2},{4,5},{5,4},{6,7},{7,6},{8,9},{9,8},{10,11... | collective-permute-start | bytes 1572872 | tf_op jit(solution)/shard_map/ppermute | solution.py:31
  110.6 3.0 %collective-permute-start.7 = (bf16[512,512]{1,0:T(8,128)(2,1)S(1)}, bf16[512,512]{1,0:T(8,128)(2,1)S(1)}, u32[]{:S(2)}, u32[]{:S(2)}) collective-permute-start(bf16[512,512]{1,0:T(8,128)(2,1)S(1)} %get-tuple-element.120), channel_id=1, source_target_pairs={{0,1},{1,0},{2,3},{3,2},{4,5},{5,4},{6,7},{7,6},{8,9},{9,8},{10,11... | collective-permute-start | bytes 1572872 | tf_op jit(solution)/shard_map/ppermute | solution.py:31
  130.7 2.5 %collective-permute-start.8 = (bf16[512,512]{1,0:T(8,128)(2,1)S(1)}, bf16[512,512]{1,0:T(8,128)(2,1)S(1)}, u32[]{:S(2)}, u32[]{:S(2)}) collective-permute-start(bf16[512,512]{1,0:T(8,128)(2,1)S(1)} %get-tuple-element.130), channel_id=1, source_target_pairs={{0,1},{1,0},{2,3},{3,2},{4,5},{5,4},{6,7},{7,6},{8,9},{9,8},{10,11... | collective-permute-start | bytes 1572872 | tf_op jit(solution)/shard_map/ppermute | solution.py:31
  133.2 3.3 %collective-permute-start.9 = (bf16[512,512]{1,0:T(8,128)(2,1)S(1)}, bf16[512,512]{1,0:T(8,128)(2,1)S(1)}, u32[]{:S(2)}, u32[]{:S(2)}) collective-permute-start(bf16[512,512]{1,0:T(8,128)(2,1)S(1)} %get-tuple-element.140), channel_id=1, source_target_pairs={{0,1},{1,0},{2,3},{3,2},{4,5},{5,4},{6,7},{7,6},{8,9},{9,8},{10,11... | collective-permute-start | bytes 1572872 | tf_op jit(solution)/shard_map/ppermute | solution.py:31
  138.1 4.2 %copy-start.7 = (bf16[4,256,512]{2,1,0:T(8,128)(2,1)S(1)}, bf16[4,256,512]{2,1,0:T(8,128)(2,1)}, u32[]{:S(2)}) copy-start(bf16[4,256,512]{2,1,0:T(8,128)(2,1)} %get-tuple-element.145.refs_0_) | copy-start | bytes 3145732
  138.1 22.3 %copy-start.3 = (s32[4,1,2,4]{3,2,1,0:T(2,128)S(1)}, s32[4,1,2,4]{3,2,1,0:T(2,128)}, u32[]{:S(2)}) copy-start(s32[4,1,2,4]{3,2,1,0:T(2,128)} %param.16) | copy-start | bytes 388
  138.1 30.2 %all-to-all-start.7 = ((bf16[32,56,512]{2,1,0:T(8,128)(2,1)}), bf16[32,56,512]{2,1,0:T(8,128)(2,1)S(1)}, u32[]{:S(2)}, u32[]{:S(2)}) async-start(bf16[32,56,512]{2,1,0:T(8,128)(2,1)} %join_rows.1), calls=%async_computation.7 | async-start | bytes 3670016 | tf_op jit(solution)/shard_map/all_to_all | solution.py:35
  142.4 14.4 %collective-permute-start.12 = (bf16[256,512]{1,0:T(8,128)(2,1)S(1)}, bf16[256,512]{1,0:T(8,128)(2,1)S(1)}, u32[]{:S(2)}, u32[]{:S(2)}) collective-permute-start(bf16[256,512]{1,0:T(8,128)(2,1)S(1)} %get-tuple-element.165), channel_id=1, source_target_pairs={{0,96},{32,0},{64,32},{96,64},{1,97},{33,1},{65,33},{97,65},{2,98}... | collective-permute-start | bytes 786440 | tf_op jit(solution)/shard_map/ppermute | solution.py:26
  145.1 11.7 %collective-permute-start.11 = (bf16[256,512]{1,0:T(8,128)(2,1)S(1)}, bf16[256,512]{1,0:T(8,128)(2,1)S(1)}, u32[]{:S(2)}, u32[]{:S(2)}) collective-permute-start(bf16[256,512]{1,0:T(8,128)(2,1)S(1)} %get-tuple-element.166), channel_id=1, source_target_pairs={{0,64},{32,96},{64,0},{96,32},{1,65},{33,97},{65,1},{97,33},{2,66}... | collective-permute-start | bytes 786440 | tf_op jit(solution)/shard_map/ppermute | solution.py:26
  146.0 14.5 %collective-permute-start.10 = (bf16[256,512]{1,0:T(8,128)(2,1)S(1)}, bf16[256,512]{1,0:T(8,128)(2,1)S(1)}, u32[]{:S(2)}, u32[]{:S(2)}) collective-permute-start(bf16[256,512]{1,0:T(8,128)(2,1)S(1)} %get-tuple-element.167), channel_id=1, source_target_pairs={{0,32},{32,64},{64,96},{96,0},{1,33},{33,65},{65,97},{97,1},{2,34}... | collective-permute-start | bytes 786440 | tf_op jit(solution)/shard_map/ppermute | solution.py:26
  169.8 10.2 %all-to-all-start.8 = ((bf16[4,2,16,512]{3,2,1,0:T(8,128)(2,1)}), bf16[4,2,16,512]{3,2,1,0:T(8,128)(2,1)S(1)}, u32[]{:S(2)}, u32[]{:S(2)}) async-start(bf16[4,2,16,512]{3,2,1,0:T(8,128)(2,1)} %sum_chunks.1), calls=%async_computation.8 | async-start | bytes 262144 | tf_op jit(solution)/shard_map/all_to_all | solution.py:625
  181.4 19.8 %all-to-all-start.9 = ((bf16[32,16,512]{2,1,0:T(8,128)(2,1)}), bf16[32,16,512]{2,1,0:T(8,128)(2,1)S(1)}, u32[]{:S(2)}, u32[]{:S(2)}) async-start(bf16[32,16,512]{2,1,0:T(8,128)(2,1)} %sum_over_layer.1), calls=%async_computation.9 | async-start | bytes 1048576 | tf_op jit(solution)/shard_map/all_to_all | solution.py:35
  185.3 15.3 %collective-permute-start.13 = (bf16[256,512]{1,0:T(8,128)(2,1)S(1)}, bf16[256,512]{1,0:T(8,128)(2,1)S(1)}, u32[]{:S(2)}, u32[]{:S(2)}) collective-permute-start(bf16[256,512]{1,0:T(8,128)(2,1)S(1)} %get-tuple-element.153), channel_id=1, source_target_pairs={{0,32},{32,64},{64,96},{96,0},{1,33},{33,65},{65,97},{97,1},{2,34}... | collective-permute-start | bytes 786440 | tf_op jit(solution)/shard_map/ppermute | solution.py:26
  186.0 14.6 %collective-permute-start.14 = (bf16[256,512]{1,0:T(8,128)(2,1)S(1)}, bf16[256,512]{1,0:T(8,128)(2,1)S(1)}, u32[]{:S(2)}, u32[]{:S(2)}) collective-permute-start(bf16[256,512]{1,0:T(8,128)(2,1)S(1)} %get-tuple-element.154), channel_id=1, source_target_pairs={{0,64},{32,96},{64,0},{96,32},{1,65},{33,97},{65,1},{97,33},{2,66}... | collective-permute-start | bytes 786440 | tf_op jit(solution)/shard_map/ppermute | solution.py:26
  188.0 13.2 %collective-permute-start.15 = (bf16[256,512]{1,0:T(8,128)(2,1)S(1)}, bf16[256,512]{1,0:T(8,128)(2,1)S(1)}, u32[]{:S(2)}, u32[]{:S(2)}) collective-permute-start(bf16[256,512]{1,0:T(8,128)(2,1)S(1)} %get-tuple-element.155), channel_id=1, source_target_pairs={{0,96},{32,0},{64,32},{96,64},{1,97},{33,1},{65,33},{97,65},{2,98}... | collective-permute-start | bytes 786440 | tf_op jit(solution)/shard_map/ppermute | solution.py:26
  201.2 2.6 %collective-permute-start.16 = (bf16[512,512]{1,0:T(8,128)(2,1)S(1)}, bf16[512,512]{1,0:T(8,128)(2,1)S(1)}, u32[]{:S(2)}, u32[]{:S(2)}) collective-permute-start(bf16[512,512]{1,0:T(8,128)(2,1)S(1)} %bitcast.39), channel_id=1, source_target_pairs={{0,1},{1,0},{2,3},{3,2},{4,5},{5,4},{6,7},{7,6},{8,9},{9,8},{10,11... | collective-permute-start | bytes 1572872 | tf_op jit(solution)/shard_map/ppermute | solution.py:31

commit v8 on v7

--- a/solution.py
+++ b/solution.py
@@ -36,11 +36,11 @@
 
 
 def of_span(shape):
-    return pl.BlockSpec((None, *shape), lambda i, ids, cols: (ids[0], *((0,) * len(shape))))
+    return pl.BlockSpec((None, *shape), lambda i, ids: (ids[0], *((0,) * len(shape))))
 
 
 def whole(shape):
-    return pl.BlockSpec(shape, lambda i, ids, cols: (0,) * len(shape))
+    return pl.BlockSpec(shape, lambda i, ids: (0,) * len(shape))
 
 
 def near(shape, dtype=BF):
@@ -61,17 +61,17 @@
         kernel,
         name=name,
         grid_spec=pltpu.PrefetchScalarGridSpec(
-            num_scalar_prefetch=2,
+            num_scalar_prefetch=1,
             grid=(1,),
             in_specs=[s for _, s in ins],
             out_specs=[s for _, s in outs],
             scratch_shapes=list(scratch),
         ),
         out_shape=[o for o, _ in outs],
-        input_output_aliases={} if aliases is None else {k + 2: v for k, v in aliases.items()},
+        input_output_aliases={} if aliases is None else {k + 1: v for k, v in aliases.items()},
         compiler_params=pltpu.CompilerParams(vmem_limit_bytes=VMEM_BYTES),
         cost_estimate=pl.CostEstimate(flops=flops, bytes_accessed=moved, transcendentals=0),
-    )(*scalars, *arrays)
+    )(scalars, *arrays)
 
 
 def tie(*values):
@@ -108,25 +108,25 @@
     return jnp.concatenate([vals_ref[r, j] for j in range(degree)], axis=1)
 
 
-def aggregate_rows(ids, cols, vals_ref, ext):
+def aggregate_rows(ids, vals_ref, ext):
     tiles, degree, size = vals_ref.shape[0], vals_ref.shape[1], vals_ref.shape[2]
     parts = []
     for r in range(tiles):
         picked = jnp.concatenate(
-            [ext[pl.ds(pl.multiple_of(cols[ids[0], r, j] * size, size), size), :] for j in range(degree)],
+            [ext[pl.ds(pl.multiple_of(ids[2 + r * degree + j] * size, size), size), :] for j in range(degree)],
             axis=0,
         )
         parts.append(dot(side_by_side(vals_ref, r, degree), picked))
     return jnp.concatenate(parts, axis=0).astype(BF)
 
 
-def spread_rows(ids, cols, vals_ref, d_agg, d_ext):
+def spread_rows(ids, vals_ref, d_agg, d_ext):
     tiles, degree, size = vals_ref.shape[0], vals_ref.shape[1], vals_ref.shape[2]
     d_ext[...] = jnp.zeros_like(d_ext)
     for r in range(tiles):
         pieces = dot(side_by_side(vals_ref, r, degree), d_agg[r * size : (r + 1) * size], TN)
         for j in range(degree):
-            rows = pl.ds(pl.multiple_of(cols[ids[0], r, j] * size, size), size)
+            rows = pl.ds(pl.multiple_of(ids[2 + r * degree + j] * size, size), size)
             d_ext[rows, :] += pieces[j * size : (j + 1) * size]
 
 
@@ -138,7 +138,7 @@
     return 1.0 / (1.0 + jnp.exp(-v))
 
 
-def pre_kernel(ids, cols, h_ref, rows_ref, counts_ref, vals_ref, pick_ref, out_ref, h_out, vals_out, pick_far):
+def pre_kernel(ids, h_ref, rows_ref, counts_ref, vals_ref, pick_ref, out_ref, h_out, vals_out, pick_far):
     slots, peers = rows_ref.shape
     total, node_rows = pick_ref.shape
     bits = slots.bit_length() - 1
@@ -162,11 +162,11 @@
     vals_out[...] = vals_ref[...]
 
 
-def forward_math(ids, cols, h_ref, arr_ref, vals_ref, w_ref, ext, ready=None):
+def forward_math(ids, h_ref, arr_ref, vals_ref, w_ref, ext, ready=None):
     rows = h_ref.shape[0]
     ext[0:rows, :] = h_ref[...]
     ext[rows : 2 * rows, :] = arr_ref[...]
-    agg = aggregate_rows(ids, cols, vals_ref, ext)
+    agg = aggregate_rows(ids, vals_ref, ext)
     if ready is not None:
         ready()
     pre = dot(h_ref[...], w_ref[0]) + dot(agg, w_ref[1])
@@ -174,7 +174,7 @@
     return agg, pre, sig, (pre * sig).astype(BF)
 
 
-def forward_kernel(layer, ids, cols, h_ref, arr_ref, vals_ref, pick_ref, *rest):
+def forward_kernel(layer, ids, h_ref, arr_ref, vals_ref, pick_ref, *rest):
     w_refs, rest = rest[:8], rest[8:]
     first = layer == 0
     if first:
@@ -193,7 +193,7 @@
         ready = lambda: wait_weights(*here)
     ahead = (layer + 1, ids, w_refs, next_ref, sems.at[1])
     start_weights(*ahead)
-    agg, pre, _, hid = forward_math(ids, cols, h_ref, arr_ref, vals_ref, w_ref, ext, ready)
+    agg, pre, _, hid = forward_math(ids, h_ref, arr_ref, vals_ref, w_ref, ext, ready)
     hid_ref[...] = hid
     out_ref[...] = dot(pick_ref[...], hid).astype(BF)
     agg_ref[...] = agg
@@ -203,9 +203,9 @@
     wait_weights(*ahead)
 
 
-def backward_math(ids, cols, d_pre, vals_ref, w_ref, d_ext):
+def backward_math(ids, d_pre, vals_ref, w_ref, d_ext):
     d_agg = dot(d_pre, w_ref[1], NT).astype(BF)
-    spread_rows(ids, cols, vals_ref, d_agg, d_ext)
+    spread_rows(ids, vals_ref, d_agg, d_ext)
     return dot(d_pre, w_ref[0], NT)
 
 
@@ -224,12 +224,12 @@
         send_ref[...] = on_rows
 
 
-def top_kernel(layer, ids, cols, h_ref, arr_ref, vals_ref, wout_ref, lab_ref, mask_ref, w_ref, *rest):
+def top_kernel(layer, ids, h_ref, arr_ref, vals_ref, wout_ref, lab_ref, mask_ref, w_ref, *rest):
     remote_ref, part_ref, keep_ref, send_ref, buf_ref, hid_ref, ext, d_ext, buf_sem = rest[1:]
     copy = to_slot(h_ref, layer - 1, ids, buf_ref, buf_sem)
     copy.start()
     rows = h_ref.shape[0]
-    agg, pre, sig, hid = forward_math(ids, cols, h_ref, arr_ref, vals_ref, w_ref, ext)
+    agg, pre, sig, hid = forward_math(ids, h_ref, arr_ref, vals_ref, w_ref, ext)
     hid_ref[...] = hid
     last = to_slot(hid_ref, layer, ids, buf_ref, buf_sem)
     copy.wait()
@@ -243,7 +243,7 @@
     g_logits = (live * (probs - onehot)).astype(BF)
     d_out = dot(g_logits, wout_ref[...], TN).astype(BF)
     d_pre = (d_out.astype(F32) * (sig * (1.0 + pre * (1.0 - sig)))).astype(BF)
-    back = backward_math(ids, cols, d_pre, vals_ref, w_ref, d_ext)
+    back = backward_math(ids, d_pre, vals_ref, w_ref, d_ext)
     remote_ref[...] = d_ext[rows : 2 * rows, :].astype(BF).reshape(remote_ref.shape)
     part_ref[...] = back + d_ext[0:rows, :]
     weight_partials(ids, h_ref, agg, d_pre, keep_ref, send_ref)
@@ -269,7 +269,7 @@
     return (d_out.astype(F32) * (sig * (1.0 + pre * (1.0 - sig)))).astype(BF), copy
 
 
-def backward_kernel(layer, carry, ids, cols, ret_ref, part_in, pre_ref, h_ref, agg_ref, *rest):
+def backward_kernel(layer, carry, ids, ret_ref, part_in, pre_ref, h_ref, agg_ref, *rest):
     (vals_ref, pick_ref, w_ref), rest = rest[:3], rest[3:]
     if carry:
         keep_in, recv_in, rest = rest[0], rest[1], rest[3:]
@@ -278,7 +278,7 @@
     d_pre, copy = slope_math(
         ids, layer, ret_ref, part_in, pre_ref, pick_ref, dout_ref, buf_ref, buf_sem
     )
-    back = backward_math(ids, cols, d_pre, vals_ref, w_ref, d_ext)
+    back = backward_math(ids, d_pre, vals_ref, w_ref, d_ext)
     peers, slots = out_ref.shape[0], rows // out_ref.shape[0]
     out_ref[:, 0:slots, :] = d_ext[rows : 2 * rows, :].astype(BF).reshape(peers, slots, feat)
     if carry:
@@ -289,7 +289,7 @@
 
 
 def last_slope_kernel(
-    ids, cols, ret_ref, part_in, pre_ref, h_ref, agg_ref, pick_ref, buf_in,
+    ids, ret_ref, part_in, pre_ref, h_ref, agg_ref, pick_ref, buf_in,
     dpre_ref, buf_ref, keep_ref, send_ref, chunk_ref, dout_ref, buf_sem,
 ):
     d_pre, copy = slope_math(
@@ -303,29 +303,25 @@
 
 
 def last_spread_kernel(
-    ids, cols, dpre_ref, vals_ref, w_ref, keep_a, recv_a, keep_b, recv_b, c_in,
-    out_ref, part_ref, c_ref, d_ext, part, carried, local, sems,
+    ids, dpre_ref, vals_ref, w_ref, keep_a, recv_a, keep_b, recv_b, c_in,
+    out_ref, part_ref, local_ref, c_ref, d_ext, carried, sems,
 ):
     rows, feat = dpre_ref.shape
-    peers, slots = local.shape[0], local.shape[1]
+    peers, slots = local_ref.shape[0], local_ref.shape[1]
     size = keep_a.shape[0] // peers
     copies = [
         pltpu.make_async_copy(c_in, c_ref.at[3], sems.at[0]),
         pltpu.make_async_copy(
             carried, out_ref.at[:, pl.ds(slots, 2 * size), :], sems.at[1]
         ),
-        pltpu.make_async_copy(local, out_ref.at[:, pl.ds(0, slots), :], sems.at[2]),
-        pltpu.make_async_copy(part, part_ref, sems.at[3]),
     ]
     copies[0].start()
     put_carry(keep_a, recv_a, carried, 0)
     put_carry(keep_b, recv_b, carried, size)
     copies[1].start()
-    back = backward_math(ids, cols, dpre_ref[...], vals_ref, w_ref, d_ext)
-    local[...] = d_ext[rows : 2 * rows, :].astype(BF).reshape(local.shape)
-    copies[2].start()
-    part[...] = back + d_ext[0:rows, :]
-    copies[3].start()
+    back = backward_math(ids, dpre_ref[...], vals_ref, w_ref, d_ext)
+    local_ref[...] = d_ext[rows : 2 * rows, :].astype(BF).reshape(local_ref.shape)
+    part_ref[...] = back + d_ext[0:rows, :]
     for copy in copies:
         copy.wait()
 
@@ -337,16 +333,23 @@
     out_ref[:, first : first + size, :] = total.reshape(peers, size, feat)
 
 
-def join_kernel(ids, cols, keep_ref, recv_ref, buf_in, out_ref, local, sem):
-    size = local.shape[1]
-    put_carry(keep_ref, recv_ref, local, 0)
+def join_kernel(ids, keep_ref, recv_ref, local_ref, part_ref, buf_in, out_ref, part_out, both, sems):
+    size, slots = both.shape[1], local_ref.shape[1]
     first = out_ref.shape[1] - size
-    copy = pltpu.make_async_copy(local, out_ref.at[:, pl.ds(first, size), :], sem)
-    copy.start()
-    copy.wait()
-
-
-def chunk_kernel(ids, cols, ret_ref, buf_in, out_ref, sums, sem):
+    copies = [
+        pltpu.make_async_copy(part_ref, part_out, sems.at[0]),
+        pltpu.make_async_copy(local_ref, out_ref.at[:, pl.ds(0, slots), :], sems.at[1]),
+        pltpu.make_async_copy(both, out_ref.at[:, pl.ds(first, size), :], sems.at[2]),
+    ]
+    copies[0].start()
+    copies[1].start()
+    put_carry(keep_ref, recv_ref, both, 0)
+    copies[2].start()
+    for copy in copies:
+        copy.wait()
+
+
+def chunk_kernel(ids, ret_ref, buf_in, out_ref, sums, sem):
     size = sums.shape[2]
     slots = ret_ref.shape[1] - 3 * size
     for n, layer in enumerate((2, 1, 0)):
@@ -357,7 +360,7 @@
     copy.wait()
 
 
-def end_kernel(ids, cols, ret_ref, part_in, pick_ref, buf_in, buf_ref, dout_ref, buf_sem):
+def end_kernel(ids, ret_ref, part_in, pick_ref, buf_in, buf_ref, dout_ref, buf_sem):
     rows, feat = part_in.shape
     returned = ret_ref[:, 0 : rows // ret_ref.shape[0], :].reshape(rows, feat)
     dout_ref[...] = (part_in[...] + dot(pick_ref[...], returned, TN)).astype(BF)
@@ -366,7 +369,7 @@
     copy.wait()
 
 
-def layer_sum_kernel(ids, cols, sums_ref, out_ref):
+def layer_sum_kernel(ids, sums_ref, out_ref):
     total = sums_ref[0].astype(F32)
     for span in range(1, sums_ref.shape[0]):
         total = total + sums_ref[span].astype(F32)
@@ -375,22 +378,29 @@
         out_ref[n : n + 2] = total
 
 
-def scale_kernel(scale, ids, cols, mine_ref, other_ref, self_ref, neigh_ref):
-    mine = mine_ref[...].astype(F32) * scale
-    other = other_ref[...].astype(F32) * scale
-
-    @pl.when(ids[1] == 0)
-    def _():
-        self_ref[0] = mine
-        neigh_ref[0] = other
-
-    @pl.when(ids[1] != 0)
-    def _():
-        self_ref[0] = other
-        neigh_ref[0] = mine
-
-
-def home_kernel(ids, cols, *refs):
+def scale_kernel(scale, ids, mine_ref, other_ref, self_ref, neigh_ref, mine, other, sems):
+    core = ids[1]
+    size = mine_ref.shape[0] // 4
+    for step in range(4):
+        rows = pl.ds(step * size, size)
+        mine[rows, :] = mine_ref[rows, :].astype(F32) * scale
+        other[rows, :] = other_ref[rows, :].astype(F32) * scale
+        for value, place, sem in ((mine, core, 0), (other, 1 - core, 1)):
+            for target, out_ref in enumerate((self_ref, neigh_ref)):
+
+                @pl.when(place == target)
+                def _():
+                    pltpu.make_async_copy(
+                        value.at[rows], out_ref.at[0, rows], sems.at[sem, step]
+                    ).start()
+
+    for step in range(4):
+        rows = pl.ds(step * size, size)
+        for value, sem in ((mine, 0), (other, 1)):
+            pltpu.make_async_copy(value.at[rows], self_ref.at[0, rows], sems.at[sem, step]).wait()
+
+
+def home_kernel(ids, *refs):
     pieces, out_ref = refs[:-1], refs[-1]
     for s, piece in enumerate(pieces):
         out_ref[0, lax.rem(ids[0] + 4 - s, 4)] = piece[...]
@@ -415,7 +425,8 @@
     peers, slots = send_rows.shape[2], send_rows.shape[3]
     tiles, degree, size = tile_vals.shape[2], tile_vals.shape[3], tile_vals.shape[4]
     scale = 1.0 / (spans * rows * peers)
-    scalars = (jnp.stack([home, core]).astype(jnp.int32), tile_cols.reshape(spans, tiles, degree))
+    own_cols = lax.dynamic_index_in_dim(tile_cols.reshape(spans, tiles * degree), home, 0, False)
+    scalars = jnp.concatenate([jnp.stack([home, core]).astype(jnp.int32), own_cols])
     act, wide, square = near((rows, feat)), near((rows, feat), F32), near((feat, feat))
     ext_scratch = pltpu.VMEM((2 * rows, feat), BF)
     d_ext_scratch = pltpu.VMEM((2 * rows, feat), F32)
@@ -514,7 +525,7 @@
     def travel(buf):
         return [shift(buf[s], "layer", s) for s in all_shifts]
 
-    first_block = pl.BlockSpec((None, rows, feat), lambda i, ids, cols: (0, 0, 0))
+    first_block = pl.BlockSpec((None, rows, feat), lambda i, ids: (0, 0, 0))
 
     def put_home(buf, *pieces):
         shape = (1, spans, rows, feat)
@@ -581,33 +592,31 @@
     width = slots + 3 * chunk_rows
     operand = (pltpu.HBM((peers, width, feat), BF), FAR)
     sums_out = (pltpu.HBM((spans, *chunk_shape), BF), FAR)
-    remote, part, sums = run(
+    remote, part, local, sums = run(
         last_spread_kernel,
         "last_spread",
         scalars,
         [d_pre, vals, weights[0], *pairs[-1], keep_1, recv_1, c_3],
-        [operand, (pltpu.HBM((rows, feat), F32), FAR), sums_out],
+        [operand, wide, near((peers, slots, feat)), sums_out],
         [
             d_ext_scratch,
-            pltpu.VMEM((rows, feat), F32),
             pltpu.VMEM((peers, 2 * chunk_rows, feat), BF),
-            pltpu.VMEM((peers, slots, feat), BF),
-            pltpu.SemaphoreType.DMA((4,)),
+            pltpu.SemaphoreType.DMA((2,)),
         ],
         flops=5 * 10**8,
         moved=4 * 10**6,
     )
     remote, recv = tie(remote, recv)
-    joined = run(
+    joined, part = run(
         join_kernel,
         "join_rows",
         scalars,
-        [keep, recv, (remote, FAR)],
-        [operand],
-        [pltpu.VMEM((peers, chunk_rows, feat), BF), buf_sem],
-        aliases={2: 0},
+        [keep, recv, local, part, (remote, FAR)],
+        [operand, (pltpu.HBM((rows, feat), F32), FAR)],
+        [pltpu.VMEM((peers, chunk_rows, feat), BF), pltpu.SemaphoreType.DMA((3,))],
+        aliases={4: 0},
         moved=2 * 10**6,
-    )[0]
+    )
     joined, acts_buf = tie(joined, acts_buf)
     acts = travel(acts_buf)
     layer_acts = put_home(acts_buf, *acts)
@@ -659,7 +668,8 @@
         "scale_grads",
         scalars,
         [gathered, other],
-        [(pltpu.HBM(out_square, F32), whole(out_square))] * 2,
+        [(pltpu.HBM(out_square, F32), FAR)] * 2,
+        [pltpu.VMEM((feat, feat), F32)] * 2 + [pltpu.SemaphoreType.DMA((2, 4))],
         moved=3 * 10**6,
     )
     return (layer_acts, act_grads, grad_self, grad_neigh)

time: 208 us -> 207 us (level)
  no operation moved by 1% of the time
where the time goes in v8:
time: 207 us; the launch traced here: 205 us
  blocking collectives  101 us (49%)
  waiting for transfers between devices  37.1 us (18%)
  Pallas kernels  34.9 us (17%)
  starting transfers between devices  27.7 us (13%)
    all_to_all x7, blocking collectives, exchange(): lax.all_to_all(value, 'node', split_axis=0, concat_axis=0, tiled=True)  101 us
    pallas_call x16, Pallas kernels, run(): pl.pallas_call(kernel, name=name, grid_spec=pltpu.PrefetchScalarGridSpec(...  34.9 us
    ppermute x9, waiting for transfers between devices, shift(): lax.ppermute(value, axis, [(i, (i + steps) % count) for i in range(count)])  26.5 us
    ppermute x9, starting transfers between devices, shift(): lax.ppermute(value, axis, [(i, (i + steps) % count) for i in range(count)])  13.6 us
    all_to_all x2, starting transfers between devices, exchange(): lax.all_to_all(value, 'node', split_axis=0, concat_axis=0, tiled=True)  8.05 us
    all_to_all x2, waiting for transfers between devices, exchange(): lax.all_to_all(value, 'node', split_axis=0, concat_axis=0, tiled=True)  5.42 us
    all_to_all x1, starting transfers between devices, body(): lax.all_to_all(sums, 'layer', split_axis=0, concat_axis=0, tiled=True)  4.17 us
  transfers between devices with their start and end apart: 20, of which 10 were waited for; matrix products, arithmetic and copies ran while one was open for 1% of the time, Pallas kernels for 10%

profile of v8, /device:TPU:0, one launch (start us, length us, event | category | flops | bytes accessed | tf_op | source)
XLA Modules:
  0.0 205.1 jit_solution(14928960678646156700)
XLA Ops:
  0.7 1.3 broadcast_select_fusion
  2.0 3.2 %collective-permute-start.2 = (bf16[512,512]{1,0:T(8,128)(2,1)S(1)}, bf16[512,512]{1,0:T(8,128)(2,1)S(1)}, u32[]{:S(2)}, u32[]{:S(2)}) collective-permute-start(bf16[512,512]{1,0:T(8,128)(2,1)S(1)} %broadcast_select_fusion), channel_id=1, source_target_pairs={{0,64},{32,96},{64,0},{96,32},{1,65},{33,97},{65,1},{97,33},{2,66}... | collective-permute-start | bytes 1572872 | tf_op jit(solution)/shard_map/ppermute | solution.py:26
  5.2 1.1 collective-permute-start.1
  6.3 0.9 collective-permute-start
  7.2 0.8 reshape.44
  8.1 2.6 %gather_rows.1 = (bf16[256,256]{1,0:T(8,128)(2,1)S(1)}, bf16[256,512]{1,0:T(8,128)(2,1)S(1)}, bf16[256,512]{1,0:T(8,128)(2,1)S(1)}, bf16[2,4,128,128]{3,2,1,0:T(8,128)(2,1)S(1)}, bf16[256,256]{1,0:T(8,128)(2,1)}) custom-call(s32[10]{0:T(128)S(1)} %pad_add_fusion.ids, bf16[4,256,512]{2,1,0:T(8,128)(2,1)} %h_ref.1, s32[4,8,32]{2,1,0:T(8,128)} %bitcast.52, ...), custom_call_target="tpu_custom_call" | custom-call | flops 100000000 | bytes 1000000 | tf_op jit(solution)/shard_map/gather_rows/pallas_call | solution.py:60
  10.7 17.1 %all_to_all.50 = bf16[32,8,512]{2,1,0:T(8,128)(2,1)S(1)} all-to-all(bf16[32,8,512]{2,1,0:T(8,128)(2,1)S(1)} %bitcast.49), channel_id=1, replica_groups=mesh['layer'=4,'node'=32] {'node'}, dimensions={0} | all-to-all | bytes 524288 | tf_op jit(solution)/shard_map/all_to_all | solution.py:35
  27.7 1.0 collective-permute-done.1.rest_4_
  29.2 1.4 collective-permute-done.3.rest_3_
  30.6 0.7 collective-permute-done.4.rest_5_
  31.4 0.7 collective-permute-done.5.rest_7_
  32.1 1.9 layer_forward_0.1
  34.0 17.1 %all_to_all.51 = bf16[32,8,512]{2,1,0:T(8,128)(2,1)S(1)} all-to-all(bf16[32,8,512]{2,1,0:T(8,128)(2,1)S(1)} %bitcast.47), channel_id=1, replica_groups=mesh['layer'=4,'node'=32] {'node'}, dimensions={0} | all-to-all | bytes 524288 | tf_op jit(solution)/shard_map/all_to_all | solution.py:35
  51.1 1.7 layer_forward_1.1
  52.8 12.5 %all_to_all.52 = bf16[32,8,512]{2,1,0:T(8,128)(2,1)S(1)} all-to-all(bf16[32,8,512]{2,1,0:T(8,128)(2,1)S(1)} %bitcast.48), channel_id=1, replica_groups=mesh['layer'=4,'node'=32] {'node'}, dimensions={0} | all-to-all | bytes 524288 | tf_op jit(solution)/shard_map/all_to_all | solution.py:35
  65.2 1.7 layer_forward_2.1
  66.9 12.5 %all_to_all.53 = bf16[32,8,512]{2,1,0:T(8,128)(2,1)S(1)} all-to-all(bf16[32,8,512]{2,1,0:T(8,128)(2,1)S(1)} %bitcast.45), channel_id=1, replica_groups=mesh['layer'=4,'node'=32] {'node'}, dimensions={0} | all-to-all | bytes 524288 | tf_op jit(solution)/shard_map/all_to_all | solution.py:35
  79.4 3.5 %top_layer.1 = (bf16[32,8,512]{2,1,0:T(8,128)(2,1)S(1)}, f32[256,512]{1,0:T(8,128)S(1)}, bf16[512,512]{1,0:T(8,128)(2,1)S(1)}, bf16[512,512]{1,0:T(8,128)(2,1)S(1)}, bf16[4,256,512]{2,1,0:T(8,128)(2,1)}) custom-call(s32[10]{0:T(128)S(1)} %pad_add_fusion.ids, bf16[256,512]{1,0:T(8,128)(2,1)S(1)} %get-tuple-element.101.h_ref, ...), custom_call_target="tpu_custom_call", output_to_operand_aliasing={{4}: (8, {})} | custom-call | flops 1000000000 | bytes 5000000 | tf_op jit(solution)/shard_map/top_layer/pallas_call | solution.py:60
  82.9 12.5 %all_to_all.54.ret_ref = bf16[32,8,512]{2,1,0:T(8,128)(2,1)S(1)} all-to-all(bf16[32,8,512]{2,1,0:T(8,128)(2,1)S(1)} %get-tuple-element.105), channel_id=1, replica_groups=mesh['layer'=4,'node'=32] {'node'}, dimensions={0} | all-to-all | bytes 524288 | tf_op jit(solution)/shard_map/all_to_all | solution.py:35
  95.7 2.3 %layer_backward_2.1 = (bf16[32,8,512]{2,1,0:T(8,128)(2,1)S(1)}, f32[256,512]{1,0:T(8,128)S(1)}, bf16[4,256,512]{2,1,0:T(8,128)(2,1)}, bf16[512,512]{1,0:T(8,128)(2,1)S(1)}, bf16[512,512]{1,0:T(8,128)(2,1)S(1)}) custom-call(s32[10]{0:T(128)S(1)} %pad_add_fusion.ids, bf16[32,8,512]{2,1,0:T(8,128)(2,1)S(1)} %all_to_all.54.ret_ref, ...), custom_call_target="tpu_custom_call" | custom-call | flops 1000000000 | bytes 5000000 | tf_op jit(solution)/shard_map/layer_backward_2/pallas_call | solution.py:60
  98.0 12.3 %all_to_all.55.ret_ref = bf16[32,8,512]{2,1,0:T(8,128)(2,1)S(1)} all-to-all(bf16[32,8,512]{2,1,0:T(8,128)(2,1)S(1)} %get-tuple-element.113), channel_id=1, replica_groups=mesh['layer'=4,'node'=32] {'node'}, dimensions={0} | all-to-all | bytes 524288 | tf_op jit(solution)/shard_map/all_to_all | solution.py:35
  110.6 2.6 %layer_backward_1.1 = (bf16[32,24,512]{2,1,0:T(8,128)(2,1)S(1)}, f32[256,512]{1,0:T(8,128)S(1)}, bf16[4,256,512]{2,1,0:T(8,128)(2,1)}, bf16[512,512]{1,0:T(8,128)(2,1)S(1)}, bf16[512,512]{1,0:T(8,128)(2,1)S(1)}) custom-call(s32[10]{0:T(128)S(1)} %pad_add_fusion.ids, bf16[32,8,512]{2,1,0:T(8,128)(2,1)S(1)} %all_to_all.55.ret_ref, ...), custom_call_target="tpu_custom_call", output_to_operand_aliasing={{2}: (11, {})} | custom-call | flops 1000000000 | bytes 5000000 | tf_op jit(solution)/shard_map/layer_backward_1/pallas_call | solution.py:60
  113.2 17.2 %all_to_all.56.ret_ref = bf16[32,24,512]{2,1,0:T(8,128)(2,1)S(1)} all-to-all(bf16[32,24,512]{2,1,0:T(8,128)(2,1)S(1)} %get-tuple-element.124), channel_id=1, replica_groups=mesh['layer'=4,'node'=32] {'node'}, dimensions={0} | all-to-all | bytes 1572864 | tf_op jit(solution)/shard_map/all_to_all | solution.py:35
  130.4 0.7 collective-permute-start.8
  131.0 1.8 last_slope.1
  132.9 2.9 %last_spread.1 = (bf16[32,56,512]{2,1,0:T(8,128)(2,1)}, f32[256,512]{1,0:T(8,128)S(1)}, bf16[32,8,512]{2,1,0:T(8,128)(2,1)S(1)}, bf16[4,2,16,512]{3,2,1,0:T(8,128)(2,1)}) custom-call(s32[10]{0:T(128)S(1)} %pad_add_fusion.ids, bf16[256,512]{1,0:T(8,128)(2,1)S(1)} %get-tuple-element.135.dpre_ref, ...), custom_call_target="tpu_custom_call" | custom-call | flops 500000000 | bytes 4000000 | tf_op jit(solution)/shard_map/last_spread/pallas_call | solution.py:60
  135.9 1.6 join_rows.1
  137.5 4.2 %all-to-all-start.7 = ((bf16[32,56,512]{2,1,0:T(8,128)(2,1)}), bf16[32,56,512]{2,1,0:T(8,128)(2,1)S(1)}, u32[]{:S(2)}, u32[]{:S(2)}) async-start(bf16[32,56,512]{2,1,0:T(8,128)(2,1)} %get-tuple-element.150), calls=%async_computation.7 | async-start | bytes 3670016 | tf_op jit(solution)/shard_map/all_to_all | solution.py:35
  141.8 2.7 %collective-permute-start.12 = (bf16[256,512]{1,0:T(8,128)(2,1)S(1)}, bf16[256,512]{1,0:T(8,128)(2,1)S(1)}, u32[]{:S(2)}, u32[]{:S(2)}) collective-permute-start(bf16[256,512]{1,0:T(8,128)(2,1)S(1)} %get-tuple-element.171), channel_id=1, source_target_pairs={{0,96},{32,0},{64,32},{96,64},{1,97},{33,1},{65,33},{97,65},{2,98}... | collective-permute-start | bytes 786440 | tf_op jit(solution)/shard_map/ppermute | solution.py:26
  144.5 0.9 collective-permute-start.11
  145.3 0.8 collective-permute-start.10
  146.2 10.0 %collective-permute-done.12.refs_3_ = bf16[256,512]{1,0:T(8,128)(2,1)S(1)} collective-permute-done((bf16[256,512]{1,0:T(8,128)(2,1)S(1)}, bf16[256,512]{1,0:T(8,128)(2,1)S(1)}, u32[]{:S(2)}, u32[]{:S(2)}) %collective-permute-start.12) | collective-permute-done | bytes 262176 | tf_op jit(solution)/shard_map/ppermute | solution.py:26
  156.1 3.7 %collective-permute-done.10.refs_1_ = bf16[256,512]{1,0:T(8,128)(2,1)S(1)} collective-permute-done((bf16[256,512]{1,0:T(8,128)(2,1)S(1)}, bf16[256,512]{1,0:T(8,128)(2,1)S(1)}, u32[]{:S(2)}, u32[]{:S(2)}) %collective-permute-start.10) | collective-permute-done | bytes 262176 | tf_op jit(solution)/shard_map/ppermute | solution.py:26
  159.8 2.5 %put_home.2 = bf16[1,4,256,512]{3,2,1,0:T(8,128)(2,1)} custom-call(s32[10]{0:T(128)S(1)} %pad_add_fusion.ids, bf16[4,256,512]{2,1,0:T(8,128)(2,1)} %get-tuple-element.151.refs_0_, bf16[256,512]{1,0:T(8,128)(2,1)S(1)} %collective-permute-done.10.refs_1_, bf16[256,512]{1,0:T(8,128)(2,1)S(1)} %collective-permute-done.11.refs_2_, ...), custom_call_target="tpu_custom_call" | custom-call | bytes 2000000 | tf_op jit(solution)/shard_map/put_home/pallas_call | solution.py:60
  162.3 5.4 %all-to-all-done.7.ret_ref = bf16[32,56,512]{2,1,0:T(8,128)(2,1)S(1)} async-done(((bf16[32,56,512]{2,1,0:T(8,128)(2,1)}), bf16[32,56,512]{2,1,0:T(8,128)(2,1)S(1)}, u32[]{:S(2)}, u32[]{:S(2)}) %all-to-all-start.7) | async-done | bytes 1835040 | tf_op jit(solution)/shard_map/all_to_all | solution.py:35
  167.7 1.4 sum_chunks.1
  169.1 4.2 %all-to-all-start.8 = ((bf16[4,2,16,512]{3,2,1,0:T(8,128)(2,1)}), bf16[4,2,16,512]{3,2,1,0:T(8,128)(2,1)S(1)}, u32[]{:S(2)}, u32[]{:S(2)}) async-start(bf16[4,2,16,512]{3,2,1,0:T(8,128)(2,1)} %sum_chunks.1), calls=%async_computation.8 | async-start | bytes 262144 | tf_op jit(solution)/shard_map/all_to_all | solution.py:634
  173.3 2.6 %input_grads.1.refs_0_ = bf16[4,256,512]{2,1,0:T(8,128)(2,1)} custom-call(s32[10]{0:T(128)S(1)} %pad_add_fusion.ids, bf16[32,56,512]{2,1,0:T(8,128)(2,1)S(1)} %all-to-all-done.7.ret_ref, f32[256,512]{1,0:T(8,128)} %get-tuple-element.154.part_in, bf16[256,256]{1,0:T(8,128)(2,1)} %get-tuple-element.155.pick_ref, ...), custom_call_target="tpu_custom_call", output_to_operand_aliasing={{}: (4, {})} | custom-call | flops 100000000 | bytes 1000000 | tf_op jit(solution)/shard_map/input_grads/pallas_call | solution.py:60
  175.9 1.2 slice_bitcast_fusion
  177.0 2.2 %all-to-all-done.8.sums_ref = bf16[4,2,16,512]{3,2,1,0:T(8,128)(2,1)S(1)} async-done(((bf16[4,2,16,512]{3,2,1,0:T(8,128)(2,1)}), bf16[4,2,16,512]{3,2,1,0:T(8,128)(2,1)S(1)}, u32[]{:S(2)}, u32[]{:S(2)}) %all-to-all-start.8) | async-done | bytes 131104 | tf_op jit(solution)/shard_map/all_to_all | solution.py:634
  179.3 1.4 sum_over_layer.1
  180.7 3.9 %all-to-all-start.9 = ((bf16[32,16,512]{2,1,0:T(8,128)(2,1)}), bf16[32,16,512]{2,1,0:T(8,128)(2,1)S(1)}, u32[]{:S(2)}, u32[]{:S(2)}) async-start(bf16[32,16,512]{2,1,0:T(8,128)(2,1)} %sum_over_layer.1), calls=%async_computation.9 | async-start | bytes 1048576 | tf_op jit(solution)/shard_map/all_to_all | solution.py:35
  184.6 0.6 collective-permute-start.13
  185.2 2.1 %collective-permute-start.14 = (bf16[256,512]{1,0:T(8,128)(2,1)S(1)}, bf16[256,512]{1,0:T(8,128)(2,1)S(1)}, u32[]{:S(2)}, u32[]{:S(2)}) collective-permute-start(bf16[256,512]{1,0:T(8,128)(2,1)S(1)} %get-tuple-element.160), channel_id=1, source_target_pairs={{0,64},{32,96},{64,0},{96,32},{1,65},{33,97},{65,1},{97,33},{2,66}... | collective-permute-start | bytes 786440 | tf_op jit(solution)/shard_map/ppermute | solution.py:26
  187.3 1.3 collective-permute-start.15
  188.6 11.3 %collective-permute-done.13.refs_1_ = bf16[256,512]{1,0:T(8,128)(2,1)S(1)} collective-permute-done((bf16[256,512]{1,0:T(8,128)(2,1)S(1)}, bf16[256,512]{1,0:T(8,128)(2,1)S(1)}, u32[]{:S(2)}, u32[]{:S(2)}) %collective-permute-start.13) | collective-permute-done | bytes 262176 | tf_op jit(solution)/shard_map/ppermute | solution.py:26
  200.5 2.5 %put_home.3 = bf16[1,4,256,512]{3,2,1,0:T(8,128)(2,1)} custom-call(s32[10]{0:T(128)S(1)} %pad_add_fusion.ids, bf16[4,256,512]{2,1,0:T(8,128)(2,1)} %input_grads.1.refs_0_, bf16[256,512]{1,0:T(8,128)(2,1)S(1)} %collective-permute-done.13.refs_1_, bf16[256,512]{1,0:T(8,128)(2,1)S(1)} %collective-permute-done.14.refs_2_, ...), custom_call_target="tpu_custom_call" | custom-call | bytes 2000000 | tf_op jit(solution)/shard_map/put_home/pallas_call | solution.py:60
  203.0 1.9 scale_grads.1
  (33 shorter events, 2.1 us)
Async XLA Ops:
  0.6 31.5 %copy-start = (bf16[1,512,512]{2,1,0:T(8,128)(2,1)S(1)}, bf16[1,512,512]{2,1,0:T(8,128)(2,1)}, u32[]{:S(2)}) copy-start(bf16[1,512,512]{2,1,0:T(8,128)(2,1)} %param.11) | copy-start | bytes 1572868
  0.6 31.5 %copy-start.1 = (bf16[1,512,512]{2,1,0:T(8,128)(2,1)S(1)}, bf16[1,512,512]{2,1,0:T(8,128)(2,1)}, u32[]{:S(2)}) copy-start(bf16[1,512,512]{2,1,0:T(8,128)(2,1)} %param.12) | copy-start | bytes 1572868
  2.0 25.7 %collective-permute-start.2 = (bf16[512,512]{1,0:T(8,128)(2,1)S(1)}, bf16[512,512]{1,0:T(8,128)(2,1)S(1)}, u32[]{:S(2)}, u32[]{:S(2)}) collective-permute-start(bf16[512,512]{1,0:T(8,128)(2,1)S(1)} %broadcast_select_fusion), channel_id=1, source_target_pairs={{0,64},{32,96},{64,0},{96,32},{1,65},{33,97},{65,1},{97,33},{2,66}... | collective-permute-start | bytes 1572872 | tf_op jit(solution)/shard_map/ppermute | solution.py:26
  5.2 23.5 %collective-permute-start.1 = (bf16[512,512]{1,0:T(8,128)(2,1)S(1)}, bf16[512,512]{1,0:T(8,128)(2,1)S(1)}, u32[]{:S(2)}, u32[]{:S(2)}) collective-permute-start(bf16[512,512]{1,0:T(8,128)(2,1)S(1)} %broadcast_select_fusion), channel_id=1, source_target_pairs={{0,96},{32,0},{64,32},{96,64},{1,97},{33,1},{65,33},{97,65},{2,98}... | collective-permute-start | bytes 1572872 | tf_op jit(solution)/shard_map/ppermute | solution.py:26
  6.3 22.4 %collective-permute-start = (bf16[512,512]{1,0:T(8,128)(2,1)S(1)}, bf16[512,512]{1,0:T(8,128)(2,1)S(1)}, u32[]{:S(2)}, u32[]{:S(2)}) collective-permute-start(bf16[512,512]{1,0:T(8,128)(2,1)S(1)} %broadcast_select_fusion), channel_id=1, source_target_pairs={{0,32},{32,64},{64,96},{96,0},{1,33},{33,65},{65,97},{97,1},{2,34}... | collective-permute-start | bytes 1572872 | tf_op jit(solution)/shard_map/ppermute | solution.py:26
  28.7 1.9 collective-permute-start.3
  28.7 2.7 %collective-permute-start.4 = (bf16[512,512]{1,0:T(8,128)(2,1)S(1)}, bf16[512,512]{1,0:T(8,128)(2,1)S(1)}, u32[]{:S(2)}, u32[]{:S(2)}) collective-permute-start(bf16[512,512]{1,0:T(8,128)(2,1)S(1)} %collective-permute-done.1.rest_4_), channel_id=1, source_target_pairs={{0,1},{1,0},{2,3},{3,2},{4,5},{5,4},{6,7},{7,6},{8,9},{9,8},{10,11... | collective-permute-start | bytes 1572872 | tf_op jit(solution)/shard_map/ppermute | solution.py:31
  29.2 2.9 %collective-permute-start.5 = (bf16[512,512]{1,0:T(8,128)(2,1)S(1)}, bf16[512,512]{1,0:T(8,128)(2,1)S(1)}, u32[]{:S(2)}, u32[]{:S(2)}) collective-permute-start(bf16[512,512]{1,0:T(8,128)(2,1)S(1)} %collective-permute-done.2.rest_6_), channel_id=1, source_target_pairs={{0,1},{1,0},{2,3},{3,2},{4,5},{5,4},{6,7},{7,6},{8,9},{9,8},{10,11... | collective-permute-start | bytes 1572872 | tf_op jit(solution)/shard_map/ppermute | solution.py:31
  65.2 14.1 %copy-start.2 = (bf16[512,172]{0,1:T(8,128)(2,1)S(1)}, bf16[512,172]{0,1:T(8,128)(2,1)}, u32[]{:S(2)}) copy-start(bf16[512,172]{0,1:T(8,128)(2,1)} %param.13) | copy-start | bytes 528388
  65.2 14.1 %copy-start.3 = (s32[4,256]{1,0:T(4,128)S(1)}, s32[4,256]{1,0:T(4,128)}, u32[]{:S(2)}) copy-start(s32[4,256]{1,0:T(4,128)} %lab_ref.1) | copy-start | bytes 12292
  65.2 14.1 %copy-start.4 = (s32[4,256]{1,0:T(4,128)S(1)}, s32[4,256]{1,0:T(4,128)}, u32[]{:S(2)}) copy-start(s32[4,256]{1,0:T(4,128)} %mask_ref.1) | copy-start | bytes 12292
  95.3 2.7 %collective-permute-start.6 = (bf16[512,512]{1,0:T(8,128)(2,1)S(1)}, bf16[512,512]{1,0:T(8,128)(2,1)S(1)}, u32[]{:S(2)}, u32[]{:S(2)}) collective-permute-start(bf16[512,512]{1,0:T(8,128)(2,1)S(1)} %get-tuple-element.112), channel_id=1, source_target_pairs={{0,1},{1,0},{2,3},{3,2},{4,5},{5,4},{6,7},{7,6},{8,9},{9,8},{10,11... | collective-permute-start | bytes 1572872 | tf_op jit(solution)/shard_map/ppermute | solution.py:31
  110.3 2.9 %collective-permute-start.7 = (bf16[512,512]{1,0:T(8,128)(2,1)S(1)}, bf16[512,512]{1,0:T(8,128)(2,1)S(1)}, u32[]{:S(2)}, u32[]{:S(2)}) collective-permute-start(bf16[512,512]{1,0:T(8,128)(2,1)S(1)} %get-tuple-element.123), channel_id=1, source_target_pairs={{0,1},{1,0},{2,3},{3,2},{4,5},{5,4},{6,7},{7,6},{8,9},{9,8},{10,11... | collective-permute-start | bytes 1572872 | tf_op jit(solution)/shard_map/ppermute | solution.py:31
  130.4 2.4 %collective-permute-start.8 = (bf16[512,512]{1,0:T(8,128)(2,1)S(1)}, bf16[512,512]{1,0:T(8,128)(2,1)S(1)}, u32[]{:S(2)}, u32[]{:S(2)}) collective-permute-start(bf16[512,512]{1,0:T(8,128)(2,1)S(1)} %get-tuple-element.133), channel_id=1, source_target_pairs={{0,1},{1,0},{2,3},{3,2},{4,5},{5,4},{6,7},{7,6},{8,9},{9,8},{10,11... | collective-permute-start | bytes 1572872 | tf_op jit(solution)/shard_map/ppermute | solution.py:31
  132.8 3.1 %collective-permute-start.9 = (bf16[512,512]{1,0:T(8,128)(2,1)S(1)}, bf16[512,512]{1,0:T(8,128)(2,1)S(1)}, u32[]{:S(2)}, u32[]{:S(2)}) collective-permute-start(bf16[512,512]{1,0:T(8,128)(2,1)S(1)} %get-tuple-element.143), channel_id=1, source_target_pairs={{0,1},{1,0},{2,3},{3,2},{4,5},{5,4},{6,7},{7,6},{8,9},{9,8},{10,11... | collective-permute-start | bytes 1572872 | tf_op jit(solution)/shard_map/ppermute | solution.py:31
  137.5 4.2 %copy-start.5 = (bf16[4,256,512]{2,1,0:T(8,128)(2,1)S(1)}, bf16[4,256,512]{2,1,0:T(8,128)(2,1)}, u32[]{:S(2)}) copy-start(bf16[4,256,512]{2,1,0:T(8,128)(2,1)} %get-tuple-element.151.refs_0_) | copy-start | bytes 3145732
  137.5 30.2 %all-to-all-start.7 = ((bf16[32,56,512]{2,1,0:T(8,128)(2,1)}), bf16[32,56,512]{2,1,0:T(8,128)(2,1)S(1)}, u32[]{:S(2)}, u32[]{:S(2)}) async-start(bf16[32,56,512]{2,1,0:T(8,128)(2,1)} %get-tuple-element.150), calls=%async_computation.7 | async-start | bytes 3670016 | tf_op jit(solution)/shard_map/all_to_all | solution.py:35
  141.8 14.3 %collective-permute-start.12 = (bf16[256,512]{1,0:T(8,128)(2,1)S(1)}, bf16[256,512]{1,0:T(8,128)(2,1)S(1)}, u32[]{:S(2)}, u32[]{:S(2)}) collective-permute-start(bf16[256,512]{1,0:T(8,128)(2,1)S(1)} %get-tuple-element.171), channel_id=1, source_target_pairs={{0,96},{32,0},{64,32},{96,64},{1,97},{33,1},{65,33},{97,65},{2,98}... | collective-permute-start | bytes 786440 | tf_op jit(solution)/shard_map/ppermute | solution.py:26
  144.5 11.7 %collective-permute-start.11 = (bf16[256,512]{1,0:T(8,128)(2,1)S(1)}, bf16[256,512]{1,0:T(8,128)(2,1)S(1)}, u32[]{:S(2)}, u32[]{:S(2)}) collective-permute-start(bf16[256,512]{1,0:T(8,128)(2,1)S(1)} %get-tuple-element.172), channel_id=1, source_target_pairs={{0,64},{32,96},{64,0},{96,32},{1,65},{33,97},{65,1},{97,33},{2,66}... | collective-permute-start | bytes 786440 | tf_op jit(solution)/shard_map/ppermute | solution.py:26
  145.3 14.5 %collective-permute-start.10 = (bf16[256,512]{1,0:T(8,128)(2,1)S(1)}, bf16[256,512]{1,0:T(8,128)(2,1)S(1)}, u32[]{:S(2)}, u32[]{:S(2)}) collective-permute-start(bf16[256,512]{1,0:T(8,128)(2,1)S(1)} %get-tuple-element.173), channel_id=1, source_target_pairs={{0,32},{32,64},{64,96},{96,0},{1,33},{33,65},{65,97},{97,1},{2,34}... | collective-permute-start | bytes 786440 | tf_op jit(solution)/shard_map/ppermute | solution.py:26
  169.1 10.1 %all-to-all-start.8 = ((bf16[4,2,16,512]{3,2,1,0:T(8,128)(2,1)}), bf16[4,2,16,512]{3,2,1,0:T(8,128)(2,1)S(1)}, u32[]{:S(2)}, u32[]{:S(2)}) async-start(bf16[4,2,16,512]{3,2,1,0:T(8,128)(2,1)} %sum_chunks.1), calls=%async_computation.8 | async-start | bytes 262144 | tf_op jit(solution)/shard_map/all_to_all | solution.py:634
  180.7 19.8 %all-to-all-start.9 = ((bf16[32,16,512]{2,1,0:T(8,128)(2,1)}), bf16[32,16,512]{2,1,0:T(8,128)(2,1)S(1)}, u32[]{:S(2)}, u32[]{:S(2)}) async-start(bf16[32,16,512]{2,1,0:T(8,128)(2,1)} %sum_over_layer.1), calls=%async_computation.9 | async-start | bytes 1048576 | tf_op jit(solution)/shard_map/all_to_all | solution.py:35
  184.6 15.3 %collective-permute-start.13 = (bf16[256,512]{1,0:T(8,128)(2,1)S(1)}, bf16[256,512]{1,0:T(8,128)(2,1)S(1)}, u32[]{:S(2)}, u32[]{:S(2)}) collective-permute-start(bf16[256,512]{1,0:T(8,128)(2,1)S(1)} %get-tuple-element.159), channel_id=1, source_target_pairs={{0,32},{32,64},{64,96},{96,0},{1,33},{33,65},{65,97},{97,1},{2,34}... | collective-permute-start | bytes 786440 | tf_op jit(solution)/shard_map/ppermute | solution.py:26
  185.2 14.6 %collective-permute-start.14 = (bf16[256,512]{1,0:T(8,128)(2,1)S(1)}, bf16[256,512]{1,0:T(8,128)(2,1)S(1)}, u32[]{:S(2)}, u32[]{:S(2)}) collective-permute-start(bf16[256,512]{1,0:T(8,128)(2,1)S(1)} %get-tuple-element.160), channel_id=1, source_target_pairs={{0,64},{32,96},{64,0},{96,32},{1,65},{33,97},{65,1},{97,33},{2,66}... | collective-permute-start | bytes 786440 | tf_op jit(solution)/shard_map/ppermute | solution.py:26
  187.3 13.2 %collective-permute-start.15 = (bf16[256,512]{1,0:T(8,128)(2,1)S(1)}, bf16[256,512]{1,0:T(8,128)(2,1)S(1)}, u32[]{:S(2)}, u32[]{:S(2)}) collective-permute-start(bf16[256,512]{1,0:T(8,128)(2,1)S(1)} %get-tuple-element.161), channel_id=1, source_target_pairs={{0,96},{32,0},{64,32},{96,64},{1,97},{33,1},{65,33},{97,65},{2,98}... | collective-permute-start | bytes 786440 | tf_op jit(solution)/shard_map/ppermute | solution.py:26
  200.5 2.5 %collective-permute-start.16 = (bf16[512,512]{1,0:T(8,128)(2,1)S(1)}, bf16[512,512]{1,0:T(8,128)(2,1)S(1)}, u32[]{:S(2)}, u32[]{:S(2)}) collective-permute-start(bf16[512,512]{1,0:T(8,128)(2,1)S(1)} %bitcast.40), channel_id=1, source_target_pairs={{0,1},{1,0},{2,3},{3,2},{4,5},{5,4},{6,7},{7,6},{8,9},{9,8},{10,11... | collective-permute-start | bytes 1572872 | tf_op jit(solution)/shard_map/ppermute | solution.py:31

commit v9 on v8

--- a/solution.py
+++ b/solution.py
@@ -458,9 +458,9 @@
         moved=10**6,
     )
     arrived = exchange(outgoing.reshape(peers, slots, feat))
-    arrived, left, right, far = tie(arrived, left, right, far)
-    sources = [w_self[0], w_neigh[0], left, sibling(left), right, sibling(right)]
-    sources += [far, sibling(far)]
+    arrived, left, right = tie(arrived, left, right)
+    left_x, right_x, far = tie(sibling(left), sibling(right), far)
+    sources = [w_self[0], w_neigh[0], left, left_x, right, right_x, far, sibling(far)]
     weight = near((2, feat, feat))
 
     hidden, aggs, pres, weights = [features_0], [], [], []

time: 207 us -> 210 us (1.014)
  blocking collectives: 101 us -> 82.8 us
  waiting for transfers between devices: 37.1 us -> 48.3 us
  starting transfers between devices: 27.7 us -> 36.3 us
    all_to_all x7 -> x6, blocking collectives: 101 us -> 82.8 us  [exchange(): lax.all_to_all(value, 'node', split_axis=0, concat_axis=0, tiled=True)]
    all_to_all x2 -> x3, starting transfers between devices: 8.05 us -> 16.4 us  [exchange(): lax.all_to_all(value, 'node', split_axis=0, concat_axis=0, tiled=True)]
    all_to_all x2 -> x3, waiting for transfers between devices: 5.42 us -> 11.7 us  [exchange(): lax.all_to_all(value, 'node', split_axis=0, concat_axis=0, tiled=True)]
    ppermute x9, waiting for transfers between devices: 26.5 us -> 32.4 us  [shift(): lax.ppermute(value, axis, [(i, (i + steps) % count) for i in range(count)])]
  transfers between devices with their start and end apart: 20 -> 21, of which waited for: 10 -> 9; matrix products, arithmetic and copies ran while one was open for 1% -> 1% of each run, Pallas kernels for 10% -> 10%
where the time goes in v9:
time: 210 us; the launch traced here: 208 us
  blocking collectives  82.8 us (39%)
  waiting for transfers between devices  48.3 us (23%)
  starting transfers between devices  36.3 us (17%)
  Pallas kernels  35 us (17%)
  other arithmetic  2.21 us (1%)
    all_to_all x6, blocking collectives, exchange(): lax.all_to_all(value, 'node', split_axis=0, concat_axis=0, tiled=True)  82.8 us
    pallas_call x16, Pallas kernels, run(): pl.pallas_call(kernel, name=name, grid_spec=pltpu.PrefetchScalarGridSpec(...  35 us
    ppermute x9, waiting for transfers between devices, shift(): lax.ppermute(value, axis, [(i, (i + steps) % count) for i in range(count)])  32.4 us
    all_to_all x3, starting transfers between devices, exchange(): lax.all_to_all(value, 'node', split_axis=0, concat_axis=0, tiled=True)  16.4 us
    ppermute x9, starting transfers between devices, shift(): lax.ppermute(value, axis, [(i, (i + steps) % count) for i in range(count)])  13.5 us
    all_to_all x3, waiting for transfers between devices, exchange(): lax.all_to_all(value, 'node', split_axis=0, concat_axis=0, tiled=True)  11.7 us
    all_to_all x1, starting transfers between devices, body(): lax.all_to_all(sums, 'layer', split_axis=0, concat_axis=0, tiled=True)  4.5 us
  transfers between devices with their start and end apart: 21, of which 9 were waited for; matrix products, arithmetic and copies ran while one was open for 1% of the time, Pallas kernels for 10%

profile of v9, /device:TPU:0, one launch (start us, length us, event | category | flops | bytes accessed | tf_op | source)
XLA Modules:
  0.0 207.6 jit_solution(10118142973875468761)
XLA Ops:
  0.7 2.1 %broadcast_select_fusion = bf16[512,512]{1,0:T(8,128)(2,1)} fusion(pred[]{:T(512)S(6)} %eq.3, bf16[1,512,512]{2,1,0:T(8,128)(2,1)} %param.12, bf16[1,512,512]{2,1,0:T(8,128)(2,1)} %param.11), kind=kLoop, calls=%fused_computation | loop fusion | flops 262144 | bytes 1572865 | tf_op jit(solution)/shard_map/jit(_where)/select_n | solution.py:435
  2.8 2.8 %collective-permute-start.1 = (bf16[512,512]{1,0:T(8,128)(2,1)}, bf16[512,512]{1,0:T(8,128)(2,1)S(1)}, u32[]{:S(2)}, u32[]{:S(2)}) collective-permute-start(bf16[512,512]{1,0:T(8,128)(2,1)} %broadcast_select_fusion), channel_id=1, source_target_pairs={{0,96},{32,0},{64,32},{96,64},{1,97},{33,1},{65,33},{97,65},{2,98}... | collective-permute-start | bytes 1572872 | tf_op jit(solution)/shard_map/ppermute | solution.py:26
  5.6 0.8 reshape.44
  6.5 2.7 %gather_rows.1 = (bf16[256,256]{1,0:T(8,128)(2,1)S(1)}, bf16[256,512]{1,0:T(8,128)(2,1)}, bf16[256,512]{1,0:T(8,128)(2,1)S(1)}, bf16[2,4,128,128]{3,2,1,0:T(8,128)(2,1)S(1)}, bf16[256,256]{1,0:T(8,128)(2,1)}) custom-call(s32[10]{0:T(128)S(1)} %pad_add_fusion.ids, bf16[4,256,512]{2,1,0:T(8,128)(2,1)} %h_ref.1, s32[4,8,32]{2,1,0:T(8,128)} %bitcast.51, ...), custom_call_target="tpu_custom_call" | custom-call | flops 100000000 | bytes 1000000 | tf_op jit(solution)/shard_map/gather_rows/pallas_call | solution.py:60
  9.2 8.3 %all-to-all-start = ((bf16[32,8,512]{2,1,0:T(8,128)(2,1)}), bf16[32,8,512]{2,1,0:T(8,128)(2,1)S(1)}, u32[]{:S(2)}, u32[]{:S(2)}) async-start(bf16[32,8,512]{2,1,0:T(8,128)(2,1)} %bitcast.6), calls=%async_computation | async-start | bytes 524288 | tf_op jit(solution)/shard_map/all_to_all | solution.py:35
  17.6 2.4 %collective-permute-start.4 = (bf16[512,512]{1,0:T(8,128)(2,1)}, bf16[512,512]{1,0:T(8,128)(2,1)S(1)}, u32[]{:S(2)}, u32[]{:S(2)}) collective-permute-start(bf16[512,512]{1,0:T(8,128)(2,1)} %broadcast_select_fusion), channel_id=1, source_target_pairs={{0,64},{32,96},{64,0},{96,32},{1,65},{33,97},{65,1},{97,33},{2,66}... | collective-permute-start | bytes 1572872 | tf_op jit(solution)/shard_map/ppermute | solution.py:26
  20.0 6.6 %all-to-all-done = bf16[32,8,512]{2,1,0:T(8,128)(2,1)S(1)} async-done(((bf16[32,8,512]{2,1,0:T(8,128)(2,1)}), bf16[32,8,512]{2,1,0:T(8,128)(2,1)S(1)}, u32[]{:S(2)}, u32[]{:S(2)}) %all-to-all-start) | async-done | bytes 262176 | tf_op jit(solution)/shard_map/all_to_all | solution.py:35
  26.5 0.3 collective-permute-start.2
  27.0 6.4 %collective-permute-done.4.rest_6_ = bf16[512,512]{1,0:T(8,128)(2,1)S(1)} collective-permute-done((bf16[512,512]{1,0:T(8,128)(2,1)}, bf16[512,512]{1,0:T(8,128)(2,1)S(1)}, u32[]{:S(2)}, u32[]{:S(2)}) %collective-permute-start.4) | collective-permute-done | bytes 524320 | tf_op jit(solution)/shard_map/ppermute | solution.py:26
  33.5 1.9 collective-permute-done.5.rest_7_
  35.4 1.9 layer_forward_0.1
  37.3 16.0 %all_to_all.50 = bf16[32,8,512]{2,1,0:T(8,128)(2,1)S(1)} all-to-all(bf16[32,8,512]{2,1,0:T(8,128)(2,1)S(1)} %bitcast.47), channel_id=1, replica_groups=mesh['layer'=4,'node'=32] {'node'}, dimensions={0} | all-to-all | bytes 524288 | tf_op jit(solution)/shard_map/all_to_all | solution.py:35
  53.3 1.7 layer_forward_1.1
  55.0 12.5 %all_to_all.51 = bf16[32,8,512]{2,1,0:T(8,128)(2,1)S(1)} all-to-all(bf16[32,8,512]{2,1,0:T(8,128)(2,1)S(1)} %bitcast.48), channel_id=1, replica_groups=mesh['layer'=4,'node'=32] {'node'}, dimensions={0} | all-to-all | bytes 524288 | tf_op jit(solution)/shard_map/all_to_all | solution.py:35
  67.4 1.7 layer_forward_2.1
  69.1 12.5 %all_to_all.52 = bf16[32,8,512]{2,1,0:T(8,128)(2,1)S(1)} all-to-all(bf16[32,8,512]{2,1,0:T(8,128)(2,1)S(1)} %bitcast.45), channel_id=1, replica_groups=mesh['layer'=4,'node'=32] {'node'}, dimensions={0} | all-to-all | bytes 524288 | tf_op jit(solution)/shard_map/all_to_all | solution.py:35
  81.6 3.5 %top_layer.1 = (bf16[32,8,512]{2,1,0:T(8,128)(2,1)S(1)}, f32[256,512]{1,0:T(8,128)S(1)}, bf16[512,512]{1,0:T(8,128)(2,1)S(1)}, bf16[512,512]{1,0:T(8,128)(2,1)S(1)}, bf16[4,256,512]{2,1,0:T(8,128)(2,1)}) custom-call(s32[10]{0:T(128)S(1)} %pad_add_fusion.ids, bf16[256,512]{1,0:T(8,128)(2,1)S(1)} %get-tuple-element.105.h_ref, ...), custom_call_target="tpu_custom_call", output_to_operand_aliasing={{4}: (8, {})} | custom-call | flops 1000000000 | bytes 5000000 | tf_op jit(solution)/shard_map/top_layer/pallas_call | solution.py:60
  85.1 12.5 %all_to_all.53.ret_ref = bf16[32,8,512]{2,1,0:T(8,128)(2,1)S(1)} all-to-all(bf16[32,8,512]{2,1,0:T(8,128)(2,1)S(1)} %get-tuple-element.109), channel_id=1, replica_groups=mesh['layer'=4,'node'=32] {'node'}, dimensions={0} | all-to-all | bytes 524288 | tf_op jit(solution)/shard_map/all_to_all | solution.py:35
  97.9 2.3 %layer_backward_2.1 = (bf16[32,8,512]{2,1,0:T(8,128)(2,1)S(1)}, f32[256,512]{1,0:T(8,128)S(1)}, bf16[4,256,512]{2,1,0:T(8,128)(2,1)}, bf16[512,512]{1,0:T(8,128)(2,1)S(1)}, bf16[512,512]{1,0:T(8,128)(2,1)S(1)}) custom-call(s32[10]{0:T(128)S(1)} %pad_add_fusion.ids, bf16[32,8,512]{2,1,0:T(8,128)(2,1)S(1)} %all_to_all.53.ret_ref, ...), custom_call_target="tpu_custom_call" | custom-call | flops 1000000000 | bytes 5000000 | tf_op jit(solution)/shard_map/layer_backward_2/pallas_call | solution.py:60
  100.2 12.3 %all_to_all.54.ret_ref = bf16[32,8,512]{2,1,0:T(8,128)(2,1)S(1)} all-to-all(bf16[32,8,512]{2,1,0:T(8,128)(2,1)S(1)} %get-tuple-element.117), channel_id=1, replica_groups=mesh['layer'=4,'node'=32] {'node'}, dimensions={0} | all-to-all | bytes 524288 | tf_op jit(solution)/shard_map/all_to_all | solution.py:35
  112.5 0.3 collective-permute-start.7
  112.8 2.6 %layer_backward_1.1 = (bf16[32,24,512]{2,1,0:T(8,128)(2,1)S(1)}, f32[256,512]{1,0:T(8,128)S(1)}, bf16[4,256,512]{2,1,0:T(8,128)(2,1)}, bf16[512,512]{1,0:T(8,128)(2,1)S(1)}, bf16[512,512]{1,0:T(8,128)(2,1)S(1)}) custom-call(s32[10]{0:T(128)S(1)} %pad_add_fusion.ids, bf16[32,8,512]{2,1,0:T(8,128)(2,1)S(1)} %all_to_all.54.ret_ref, ...), custom_call_target="tpu_custom_call", output_to_operand_aliasing={{2}: (11, {})} | custom-call | flops 1000000000 | bytes 5000000 | tf_op jit(solution)/shard_map/layer_backward_1/pallas_call | solution.py:60
  115.4 17.2 %all_to_all.55.ret_ref = bf16[32,24,512]{2,1,0:T(8,128)(2,1)S(1)} all-to-all(bf16[32,24,512]{2,1,0:T(8,128)(2,1)S(1)} %get-tuple-element.128), channel_id=1, replica_groups=mesh['layer'=4,'node'=32] {'node'}, dimensions={0} | all-to-all | bytes 1572864 | tf_op jit(solution)/shard_map/all_to_all | solution.py:35
  132.6 0.7 collective-permute-start.8
  133.2 1.8 last_slope.1
  135.1 2.9 %last_spread.1 = (bf16[32,56,512]{2,1,0:T(8,128)(2,1)}, f32[256,512]{1,0:T(8,128)S(1)}, bf16[32,8,512]{2,1,0:T(8,128)(2,1)S(1)}, bf16[4,2,16,512]{3,2,1,0:T(8,128)(2,1)}) custom-call(s32[10]{0:T(128)S(1)} %pad_add_fusion.ids, bf16[256,512]{1,0:T(8,128)(2,1)S(1)} %get-tuple-element.139.dpre_ref, ...), custom_call_target="tpu_custom_call" | custom-call | flops 500000000 | bytes 4000000 | tf_op jit(solution)/shard_map/last_spread/pallas_call | solution.py:60
  138.0 1.6 join_rows.1
  139.7 4.2 %all-to-all-start.7 = ((bf16[32,56,512]{2,1,0:T(8,128)(2,1)}), bf16[32,56,512]{2,1,0:T(8,128)(2,1)S(1)}, u32[]{:S(2)}, u32[]{:S(2)}) async-start(bf16[32,56,512]{2,1,0:T(8,128)(2,1)} %get-tuple-element.154), calls=%async_computation.7 | async-start | bytes 3670016 | tf_op jit(solution)/shard_map/all_to_all | solution.py:35
  143.9 3.3 %collective-permute-start.12 = (bf16[256,512]{1,0:T(8,128)(2,1)S(1)}, bf16[256,512]{1,0:T(8,128)(2,1)S(1)}, u32[]{:S(2)}, u32[]{:S(2)}) collective-permute-start(bf16[256,512]{1,0:T(8,128)(2,1)S(1)} %get-tuple-element.175), channel_id=1, source_target_pairs={{0,96},{32,0},{64,32},{96,64},{1,97},{33,1},{65,33},{97,65},{2,98}... | collective-permute-start | bytes 786440 | tf_op jit(solution)/shard_map/ppermute | solution.py:26
  147.2 0.9 collective-permute-start.10
  148.2 10.7 %collective-permute-done.12.refs_3_ = bf16[256,512]{1,0:T(8,128)(2,1)S(1)} collective-permute-done((bf16[256,512]{1,0:T(8,128)(2,1)S(1)}, bf16[256,512]{1,0:T(8,128)(2,1)S(1)}, u32[]{:S(2)}, u32[]{:S(2)}) %collective-permute-start.12) | collective-permute-done | bytes 262176 | tf_op jit(solution)/shard_map/ppermute | solution.py:26
  158.9 3.4 %collective-permute-done.10.refs_1_ = bf16[256,512]{1,0:T(8,128)(2,1)S(1)} collective-permute-done((bf16[256,512]{1,0:T(8,128)(2,1)S(1)}, bf16[256,512]{1,0:T(8,128)(2,1)S(1)}, u32[]{:S(2)}, u32[]{:S(2)}) %collective-permute-start.10) | collective-permute-done | bytes 262176 | tf_op jit(solution)/shard_map/ppermute | solution.py:26
  162.3 2.5 %put_home.2 = bf16[1,4,256,512]{3,2,1,0:T(8,128)(2,1)} custom-call(s32[10]{0:T(128)S(1)} %pad_add_fusion.ids, bf16[4,256,512]{2,1,0:T(8,128)(2,1)} %get-tuple-element.155.refs_0_, bf16[256,512]{1,0:T(8,128)(2,1)S(1)} %collective-permute-done.10.refs_1_, bf16[256,512]{1,0:T(8,128)(2,1)S(1)} %collective-permute-done.11.refs_2_, ...), custom_call_target="tpu_custom_call" | custom-call | bytes 2000000 | tf_op jit(solution)/shard_map/put_home/pallas_call | solution.py:60
  164.8 5.1 %all-to-all-done.7.ret_ref = bf16[32,56,512]{2,1,0:T(8,128)(2,1)S(1)} async-done(((bf16[32,56,512]{2,1,0:T(8,128)(2,1)}), bf16[32,56,512]{2,1,0:T(8,128)(2,1)S(1)}, u32[]{:S(2)}, u32[]{:S(2)}) %all-to-all-start.7) | async-done | bytes 1835040 | tf_op jit(solution)/shard_map/all_to_all | solution.py:35
  169.9 1.4 sum_chunks.1
  171.3 4.5 %all-to-all-start.8 = ((bf16[4,2,16,512]{3,2,1,0:T(8,128)(2,1)}), bf16[4,2,16,512]{3,2,1,0:T(8,128)(2,1)S(1)}, u32[]{:S(2)}, u32[]{:S(2)}) async-start(bf16[4,2,16,512]{3,2,1,0:T(8,128)(2,1)} %sum_chunks.1), calls=%async_computation.8 | async-start | bytes 262144 | tf_op jit(solution)/shard_map/all_to_all | solution.py:634
  175.8 2.6 %input_grads.1.refs_0_ = bf16[4,256,512]{2,1,0:T(8,128)(2,1)} custom-call(s32[10]{0:T(128)S(1)} %pad_add_fusion.ids, bf16[32,56,512]{2,1,0:T(8,128)(2,1)S(1)} %all-to-all-done.7.ret_ref, f32[256,512]{1,0:T(8,128)} %get-tuple-element.158.part_in, bf16[256,256]{1,0:T(8,128)(2,1)} %get-tuple-element.159.pick_ref, ...), custom_call_target="tpu_custom_call", output_to_operand_aliasing={{}: (4, {})} | custom-call | flops 100000000 | bytes 1000000 | tf_op jit(solution)/shard_map/input_grads/pallas_call | solution.py:60
  178.4 1.2 slice_bitcast_fusion
  179.5 2.2 %all-to-all-done.8.sums_ref = bf16[4,2,16,512]{3,2,1,0:T(8,128)(2,1)S(1)} async-done(((bf16[4,2,16,512]{3,2,1,0:T(8,128)(2,1)}), bf16[4,2,16,512]{3,2,1,0:T(8,128)(2,1)S(1)}, u32[]{:S(2)}, u32[]{:S(2)}) %all-to-all-start.8) | async-done | bytes 131104 | tf_op jit(solution)/shard_map/all_to_all | solution.py:634
  181.8 1.4 sum_over_layer.1
  183.2 3.9 %all-to-all-start.9 = ((bf16[32,16,512]{2,1,0:T(8,128)(2,1)}), bf16[32,16,512]{2,1,0:T(8,128)(2,1)S(1)}, u32[]{:S(2)}, u32[]{:S(2)}) async-start(bf16[32,16,512]{2,1,0:T(8,128)(2,1)} %sum_over_layer.1), calls=%async_computation.9 | async-start | bytes 1048576 | tf_op jit(solution)/shard_map/all_to_all | solution.py:35
  187.1 0.6 collective-permute-start.13
  187.7 2.1 collective-permute-start.14
  189.8 1.3 collective-permute-start.15
  191.1 11.3 %collective-permute-done.13.refs_1_ = bf16[256,512]{1,0:T(8,128)(2,1)S(1)} collective-permute-done((bf16[256,512]{1,0:T(8,128)(2,1)S(1)}, bf16[256,512]{1,0:T(8,128)(2,1)S(1)}, u32[]{:S(2)}, u32[]{:S(2)}) %collective-permute-start.13) | collective-permute-done | bytes 262176 | tf_op jit(solution)/shard_map/ppermute | solution.py:26
  202.3 0.6 collective-permute-done.15.refs_3_
  203.0 2.5 %put_home.3 = bf16[1,4,256,512]{3,2,1,0:T(8,128)(2,1)} custom-call(s32[10]{0:T(128)S(1)} %pad_add_fusion.ids, bf16[4,256,512]{2,1,0:T(8,128)(2,1)} %input_grads.1.refs_0_, bf16[256,512]{1,0:T(8,128)(2,1)S(1)} %collective-permute-done.13.refs_1_, bf16[256,512]{1,0:T(8,128)(2,1)S(1)} %collective-permute-done.14.refs_2_, ...), custom_call_target="tpu_custom_call" | custom-call | bytes 2000000 | tf_op jit(solution)/shard_map/put_home/pallas_call | solution.py:60
  205.5 1.9 scale_grads.1
  (34 shorter events, 0.8 us)
Async XLA Ops:
  0.6 34.8 %copy-start = (bf16[1,512,512]{2,1,0:T(8,128)(2,1)S(1)}, bf16[1,512,512]{2,1,0:T(8,128)(2,1)}, u32[]{:S(2)}) copy-start(bf16[1,512,512]{2,1,0:T(8,128)(2,1)} %param.11) | copy-start | bytes 1572868
  0.6 34.8 %copy-start.1 = (bf16[1,512,512]{2,1,0:T(8,128)(2,1)S(1)}, bf16[1,512,512]{2,1,0:T(8,128)(2,1)}, u32[]{:S(2)}) copy-start(bf16[1,512,512]{2,1,0:T(8,128)(2,1)} %param.12) | copy-start | bytes 1572868
  2.8 23.7 %collective-permute-start.1 = (bf16[512,512]{1,0:T(8,128)(2,1)}, bf16[512,512]{1,0:T(8,128)(2,1)S(1)}, u32[]{:S(2)}, u32[]{:S(2)}) collective-permute-start(bf16[512,512]{1,0:T(8,128)(2,1)} %broadcast_select_fusion), channel_id=1, source_target_pairs={{0,96},{32,0},{64,32},{96,64},{1,97},{33,1},{65,33},{97,65},{2,98}... | collective-permute-start | bytes 1572872 | tf_op jit(solution)/shard_map/ppermute | solution.py:26
  5.6 20.9 %collective-permute-start = (bf16[512,512]{1,0:T(8,128)(2,1)}, bf16[512,512]{1,0:T(8,128)(2,1)S(1)}, u32[]{:S(2)}, u32[]{:S(2)}) collective-permute-start(bf16[512,512]{1,0:T(8,128)(2,1)} %broadcast_select_fusion), channel_id=1, source_target_pairs={{0,32},{32,64},{64,96},{96,0},{1,33},{33,65},{65,97},{97,1},{2,34}... | collective-permute-start | bytes 1572872 | tf_op jit(solution)/shard_map/ppermute | solution.py:26
  9.2 17.3 %all-to-all-start = ((bf16[32,8,512]{2,1,0:T(8,128)(2,1)}), bf16[32,8,512]{2,1,0:T(8,128)(2,1)S(1)}, u32[]{:S(2)}, u32[]{:S(2)}) async-start(bf16[32,8,512]{2,1,0:T(8,128)(2,1)} %bitcast.6), calls=%async_computation | async-start | bytes 524288 | tf_op jit(solution)/shard_map/all_to_all | solution.py:35
  17.6 15.9 %collective-permute-start.4 = (bf16[512,512]{1,0:T(8,128)(2,1)}, bf16[512,512]{1,0:T(8,128)(2,1)S(1)}, u32[]{:S(2)}, u32[]{:S(2)}) collective-permute-start(bf16[512,512]{1,0:T(8,128)(2,1)} %broadcast_select_fusion), channel_id=1, source_target_pairs={{0,64},{32,96},{64,0},{96,32},{1,65},{33,97},{65,1},{97,33},{2,66}... | collective-permute-start | bytes 1572872 | tf_op jit(solution)/shard_map/ppermute | solution.py:26
  26.5 7.0 %collective-permute-start.2 = (bf16[512,512]{1,0:T(8,128)(2,1)S(1)}, bf16[512,512]{1,0:T(8,128)(2,1)S(1)}, u32[]{:S(2)}, u32[]{:S(2)}) collective-permute-start(bf16[512,512]{1,0:T(8,128)(2,1)S(1)} %collective-permute-done.rest_2_), channel_id=1, source_target_pairs={{0,1},{1,0},{2,3},{3,2},{4,5},{5,4},{6,7},{7,6},{8,9},{9,8},{10,11... | collective-permute-start | bytes 1572872 | tf_op jit(solution)/shard_map/ppermute | solution.py:31
  26.9 6.6 %collective-permute-start.3 = (bf16[512,512]{1,0:T(8,128)(2,1)S(1)}, bf16[512,512]{1,0:T(8,128)(2,1)S(1)}, u32[]{:S(2)}, u32[]{:S(2)}) collective-permute-start(bf16[512,512]{1,0:T(8,128)(2,1)S(1)} %collective-permute-done.1.rest_4_), channel_id=1, source_target_pairs={{0,1},{1,0},{2,3},{3,2},{4,5},{5,4},{6,7},{7,6},{8,9},{9,8},{10,11... | collective-permute-start | bytes 1572872 | tf_op jit(solution)/shard_map/ppermute | solution.py:31
  33.5 1.9 collective-permute-start.5
  67.4 14.1 %copy-start.2 = (bf16[512,172]{0,1:T(8,128)(2,1)S(1)}, bf16[512,172]{0,1:T(8,128)(2,1)}, u32[]{:S(2)}) copy-start(bf16[512,172]{0,1:T(8,128)(2,1)} %param.13) | copy-start | bytes 528388
  67.4 14.1 %copy-start.3 = (s32[4,256]{1,0:T(4,128)S(1)}, s32[4,256]{1,0:T(4,128)}, u32[]{:S(2)}) copy-start(s32[4,256]{1,0:T(4,128)} %lab_ref.1) | copy-start | bytes 12292
  67.4 14.1 %copy-start.4 = (s32[4,256]{1,0:T(4,128)S(1)}, s32[4,256]{1,0:T(4,128)}, u32[]{:S(2)}) copy-start(s32[4,256]{1,0:T(4,128)} %mask_ref.1) | copy-start | bytes 12292
  97.5 2.7 %collective-permute-start.6 = (bf16[512,512]{1,0:T(8,128)(2,1)S(1)}, bf16[512,512]{1,0:T(8,128)(2,1)S(1)}, u32[]{:S(2)}, u32[]{:S(2)}) collective-permute-start(bf16[512,512]{1,0:T(8,128)(2,1)S(1)} %get-tuple-element.116), channel_id=1, source_target_pairs={{0,1},{1,0},{2,3},{3,2},{4,5},{5,4},{6,7},{7,6},{8,9},{9,8},{10,11... | collective-permute-start | bytes 1572872 | tf_op jit(solution)/shard_map/ppermute | solution.py:31
  112.5 2.9 %collective-permute-start.7 = (bf16[512,512]{1,0:T(8,128)(2,1)S(1)}, bf16[512,512]{1,0:T(8,128)(2,1)S(1)}, u32[]{:S(2)}, u32[]{:S(2)}) collective-permute-start(bf16[512,512]{1,0:T(8,128)(2,1)S(1)} %get-tuple-element.127), channel_id=1, source_target_pairs={{0,1},{1,0},{2,3},{3,2},{4,5},{5,4},{6,7},{7,6},{8,9},{9,8},{10,11... | collective-permute-start | bytes 1572872 | tf_op jit(solution)/shard_map/ppermute | solution.py:31
  132.6 2.4 %collective-permute-start.8 = (bf16[512,512]{1,0:T(8,128)(2,1)S(1)}, bf16[512,512]{1,0:T(8,128)(2,1)S(1)}, u32[]{:S(2)}, u32[]{:S(2)}) collective-permute-start(bf16[512,512]{1,0:T(8,128)(2,1)S(1)} %get-tuple-element.137), channel_id=1, source_target_pairs={{0,1},{1,0},{2,3},{3,2},{4,5},{5,4},{6,7},{7,6},{8,9},{9,8},{10,11... | collective-permute-start | bytes 1572872 | tf_op jit(solution)/shard_map/ppermute | solution.py:31
  135.0 3.0 %collective-permute-start.9 = (bf16[512,512]{1,0:T(8,128)(2,1)S(1)}, bf16[512,512]{1,0:T(8,128)(2,1)S(1)}, u32[]{:S(2)}, u32[]{:S(2)}) collective-permute-start(bf16[512,512]{1,0:T(8,128)(2,1)S(1)} %get-tuple-element.147), channel_id=1, source_target_pairs={{0,1},{1,0},{2,3},{3,2},{4,5},{5,4},{6,7},{7,6},{8,9},{9,8},{10,11... | collective-permute-start | bytes 1572872 | tf_op jit(solution)/shard_map/ppermute | solution.py:31
  139.7 4.2 %copy-start.5 = (bf16[4,256,512]{2,1,0:T(8,128)(2,1)S(1)}, bf16[4,256,512]{2,1,0:T(8,128)(2,1)}, u32[]{:S(2)}) copy-start(bf16[4,256,512]{2,1,0:T(8,128)(2,1)} %get-tuple-element.155.refs_0_) | copy-start | bytes 3145732
  139.7 30.2 %all-to-all-start.7 = ((bf16[32,56,512]{2,1,0:T(8,128)(2,1)}), bf16[32,56,512]{2,1,0:T(8,128)(2,1)S(1)}, u32[]{:S(2)}, u32[]{:S(2)}) async-start(bf16[32,56,512]{2,1,0:T(8,128)(2,1)} %get-tuple-element.154), calls=%async_computation.7 | async-start | bytes 3670016 | tf_op jit(solution)/shard_map/all_to_all | solution.py:35
  143.9 14.9 %collective-permute-start.12 = (bf16[256,512]{1,0:T(8,128)(2,1)S(1)}, bf16[256,512]{1,0:T(8,128)(2,1)S(1)}, u32[]{:S(2)}, u32[]{:S(2)}) collective-permute-start(bf16[256,512]{1,0:T(8,128)(2,1)S(1)} %get-tuple-element.175), channel_id=1, source_target_pairs={{0,96},{32,0},{64,32},{96,64},{1,97},{33,1},{65,33},{97,65},{2,98}... | collective-permute-start | bytes 786440 | tf_op jit(solution)/shard_map/ppermute | solution.py:26
  147.2 11.6 %collective-permute-start.11 = (bf16[256,512]{1,0:T(8,128)(2,1)S(1)}, bf16[256,512]{1,0:T(8,128)(2,1)S(1)}, u32[]{:S(2)}, u32[]{:S(2)}) collective-permute-start(bf16[256,512]{1,0:T(8,128)(2,1)S(1)} %get-tuple-element.176), channel_id=1, source_target_pairs={{0,64},{32,96},{64,0},{96,32},{1,65},{33,97},{65,1},{97,33},{2,66}... | collective-permute-start | bytes 786440 | tf_op jit(solution)/shard_map/ppermute | solution.py:26
  147.2 15.0 %collective-permute-start.10 = (bf16[256,512]{1,0:T(8,128)(2,1)S(1)}, bf16[256,512]{1,0:T(8,128)(2,1)S(1)}, u32[]{:S(2)}, u32[]{:S(2)}) collective-permute-start(bf16[256,512]{1,0:T(8,128)(2,1)S(1)} %get-tuple-element.177), channel_id=1, source_target_pairs={{0,32},{32,64},{64,96},{96,0},{1,33},{33,65},{65,97},{97,1},{2,34}... | collective-permute-start | bytes 786440 | tf_op jit(solution)/shard_map/ppermute | solution.py:26
  171.3 10.5 %all-to-all-start.8 = ((bf16[4,2,16,512]{3,2,1,0:T(8,128)(2,1)}), bf16[4,2,16,512]{3,2,1,0:T(8,128)(2,1)S(1)}, u32[]{:S(2)}, u32[]{:S(2)}) async-start(bf16[4,2,16,512]{3,2,1,0:T(8,128)(2,1)} %sum_chunks.1), calls=%async_computation.8 | async-start | bytes 262144 | tf_op jit(solution)/shard_map/all_to_all | solution.py:634
  183.2 19.8 %all-to-all-start.9 = ((bf16[32,16,512]{2,1,0:T(8,128)(2,1)}), bf16[32,16,512]{2,1,0:T(8,128)(2,1)S(1)}, u32[]{:S(2)}, u32[]{:S(2)}) async-start(bf16[32,16,512]{2,1,0:T(8,128)(2,1)} %sum_over_layer.1), calls=%async_computation.9 | async-start | bytes 1048576 | tf_op jit(solution)/shard_map/all_to_all | solution.py:35
  187.1 15.3 %collective-permute-start.13 = (bf16[256,512]{1,0:T(8,128)(2,1)S(1)}, bf16[256,512]{1,0:T(8,128)(2,1)S(1)}, u32[]{:S(2)}, u32[]{:S(2)}) collective-permute-start(bf16[256,512]{1,0:T(8,128)(2,1)S(1)} %get-tuple-element.163), channel_id=1, source_target_pairs={{0,32},{32,64},{64,96},{96,0},{1,33},{33,65},{65,97},{97,1},{2,34}... | collective-permute-start | bytes 786440 | tf_op jit(solution)/shard_map/ppermute | solution.py:26
  187.7 14.6 %collective-permute-start.14 = (bf16[256,512]{1,0:T(8,128)(2,1)S(1)}, bf16[256,512]{1,0:T(8,128)(2,1)S(1)}, u32[]{:S(2)}, u32[]{:S(2)}) collective-permute-start(bf16[256,512]{1,0:T(8,128)(2,1)S(1)} %get-tuple-element.164), channel_id=1, source_target_pairs={{0,64},{32,96},{64,0},{96,32},{1,65},{33,97},{65,1},{97,33},{2,66}... | collective-permute-start | bytes 786440 | tf_op jit(solution)/shard_map/ppermute | solution.py:26
  189.8 13.2 %collective-permute-start.15 = (bf16[256,512]{1,0:T(8,128)(2,1)S(1)}, bf16[256,512]{1,0:T(8,128)(2,1)S(1)}, u32[]{:S(2)}, u32[]{:S(2)}) collective-permute-start(bf16[256,512]{1,0:T(8,128)(2,1)S(1)} %get-tuple-element.165), channel_id=1, source_target_pairs={{0,96},{32,0},{64,32},{96,64},{1,97},{33,1},{65,33},{97,65},{2,98}... | collective-permute-start | bytes 786440 | tf_op jit(solution)/shard_map/ppermute | solution.py:26
  203.0 2.5 %collective-permute-start.16 = (bf16[512,512]{1,0:T(8,128)(2,1)S(1)}, bf16[512,512]{1,0:T(8,128)(2,1)S(1)}, u32[]{:S(2)}, u32[]{:S(2)}) collective-permute-start(bf16[512,512]{1,0:T(8,128)(2,1)S(1)} %bitcast.40), channel_id=1, source_target_pairs={{0,1},{1,0},{2,3},{3,2},{4,5},{5,4},{6,7},{7,6},{8,9},{9,8},{10,11... | collective-permute-start | bytes 1572872 | tf_op jit(solution)/shard_map/ppermute | solution.py:31

commit v10 on v8

--- a/solution.py
+++ b/solution.py
@@ -120,11 +120,12 @@
     return jnp.concatenate(parts, axis=0).astype(BF)
 
 
-def spread_rows(ids, vals_ref, d_agg, d_ext):
-    tiles, degree, size = vals_ref.shape[0], vals_ref.shape[1], vals_ref.shape[2]
+def spread_rows(ids, vals_t, d_agg, d_ext):
+    tiles, size = vals_t.shape[0], vals_t.shape[2]
+    degree = vals_t.shape[1] // size
     d_ext[...] = jnp.zeros_like(d_ext)
     for r in range(tiles):
-        pieces = dot(side_by_side(vals_ref, r, degree), d_agg[r * size : (r + 1) * size], TN)
+        pieces = dot(vals_t[r], d_agg[r * size : (r + 1) * size])
         for j in range(degree):
             rows = pl.ds(pl.multiple_of(ids[2 + r * degree + j] * size, size), size)
             d_ext[rows, :] += pieces[j * size : (j + 1) * size]
@@ -138,7 +139,7 @@
     return 1.0 / (1.0 + jnp.exp(-v))
 
 
-def pre_kernel(ids, h_ref, rows_ref, counts_ref, vals_ref, pick_ref, out_ref, h_out, vals_out, pick_far):
+def pre_kernel(ids, h_ref, rows_ref, counts_ref, vals_ref, pick_ref, out_ref, h_out, vals_out, vals_t, pick_t, pick_far):
     slots, peers = rows_ref.shape
     total, node_rows = pick_ref.shape
     bits = slots.bit_length() - 1
@@ -156,10 +157,14 @@
     place = lax.broadcasted_iota(jnp.int32, (total, node_rows), 1).astype(F32)
     pick = (place == row).astype(F32).astype(BF)
     pick_ref[...] = pick
-    pick_far[...] = pick
+    turned = jnp.transpose(pick)
+    pick_t[...] = turned
+    pick_far[...] = turned
     out_ref[...] = dot(pick, h_ref[...]).astype(BF)
     h_out[...] = h_ref[...]
     vals_out[...] = vals_ref[...]
+    for r in range(vals_ref.shape[0]):
+        vals_t[r] = jnp.transpose(side_by_side(vals_ref, r, vals_ref.shape[1]))
 
 
 def forward_math(ids, h_ref, arr_ref, vals_ref, w_ref, ext, ready=None):
@@ -224,7 +229,7 @@
         send_ref[...] = on_rows
 
 
-def top_kernel(layer, ids, h_ref, arr_ref, vals_ref, wout_ref, lab_ref, mask_ref, w_ref, *rest):
+def top_kernel(layer, ids, h_ref, arr_ref, vals_ref, vals_t, wout_ref, lab_ref, mask_ref, w_ref, *rest):
     remote_ref, part_ref, keep_ref, send_ref, buf_ref, hid_ref, ext, d_ext, buf_sem = rest[1:]
     copy = to_slot(h_ref, layer - 1, ids, buf_ref, buf_sem)
     copy.start()
@@ -243,7 +248,7 @@
     g_logits = (live * (probs - onehot)).astype(BF)
     d_out = dot(g_logits, wout_ref[...], TN).astype(BF)
     d_pre = (d_out.astype(F32) * (sig * (1.0 + pre * (1.0 - sig)))).astype(BF)
-    back = backward_math(ids, d_pre, vals_ref, w_ref, d_ext)
+    back = backward_math(ids, d_pre, vals_t, w_ref, d_ext)
     remote_ref[...] = d_ext[rows : 2 * rows, :].astype(BF).reshape(remote_ref.shape)
     part_ref[...] = back + d_ext[0:rows, :]
     weight_partials(ids, h_ref, agg, d_pre, keep_ref, send_ref)
@@ -260,7 +265,7 @@
 def slope_math(ids, layer, ret_ref, part_in, pre_ref, pick_ref, dout_ref, buf_ref, buf_sem):
     rows, feat = part_in.shape
     returned = ret_ref[:, 0 : rows // ret_ref.shape[0], :].reshape(rows, feat)
-    d_out = (part_in[...] + dot(pick_ref[...], returned, TN)).astype(BF)
+    d_out = (part_in[...] + dot(pick_ref[...], returned)).astype(BF)
     dout_ref[...] = d_out
     copy = to_slot(dout_ref, layer + 1, ids, buf_ref, buf_sem)
     copy.start()
@@ -363,7 +368,7 @@
 def end_kernel(ids, ret_ref, part_in, pick_ref, buf_in, buf_ref, dout_ref, buf_sem):
     rows, feat = part_in.shape
     returned = ret_ref[:, 0 : rows // ret_ref.shape[0], :].reshape(rows, feat)
-    dout_ref[...] = (part_in[...] + dot(pick_ref[...], returned, TN)).astype(BF)
+    dout_ref[...] = (part_in[...] + dot(pick_ref[...], returned)).astype(BF)
     copy = to_slot(dout_ref, 0, ids, buf_ref, buf_sem)
     copy.start()
     copy.wait()
@@ -434,7 +439,7 @@
 
     mine = jnp.where(core == 0, w_self[0], w_neigh[0])
     left, right, far = (shift(mine, "layer", s) for s in (1, -1, 2))
-    pick, outgoing, features_0, vals, pick_far = run(
+    pick, outgoing, features_0, vals, vals_t, pick_t, pick_far = run(
         pre_kernel,
         "gather_rows",
         scalars,
@@ -452,7 +457,9 @@
             act,
             act,
             near((tiles, degree, size, size)),
-            far_block((peers * slots, rows)),
+            near((tiles, degree * size, size)),
+            near((rows, peers * slots)),
+            far_block((rows, peers * slots)),
         ],
         flops=10**8,
         moved=10**6,
@@ -499,6 +506,7 @@
         hidden[top],
         arrived.reshape(rows, feat),
         vals,
+        vals_t,
         w_out.T,
         labels,
         train_mask,
@@ -551,8 +559,8 @@
             pres[layer],
             hidden[layer],
             aggs[layer],
-            vals,
-            pick,
+            vals_t,
+            pick_t,
             weights[layer],
         ]
         aliases = None
@@ -580,7 +588,7 @@
         last_slope_kernel,
         "last_slope",
         scalars,
-        [returned, part, pres[0], hidden[0], aggs[0], pick, (grads_buf, FAR)],
+        [returned, part, pres[0], hidden[0], aggs[0], pick_t, (grads_buf, FAR)],
         [act, stack, square, square, near(chunk_shape)],
         [pltpu.VMEM((rows, feat), BF), buf_sem],
         {6: 1},
@@ -596,7 +604,7 @@
         last_spread_kernel,
         "last_spread",
         scalars,
-        [d_pre, vals, weights[0], *pairs[-1], keep_1, recv_1, c_3],
+        [d_pre, vals_t, weights[0], *pairs[-1], keep_1, recv_1, c_3],
         [operand, wide, near((peers, slots, feat)), sums_out],
         [
             d_ext_scratch,

time: 207 us -> 207 us (level)
  no operation moved by 1% of the time
where the time goes in v10:
time: 207 us; the launch traced here: 205 us
  blocking collectives  101 us (49%)
  waiting for transfers between devices  37 us (18%)
  Pallas kernels  34.9 us (17%)
  starting transfers between devices  27.7 us (13%)
    all_to_all x7, blocking collectives, exchange(): lax.all_to_all(value, 'node', split_axis=0, concat_axis=0, tiled=True)  101 us
    pallas_call x16, Pallas kernels, run(): pl.pallas_call(kernel, name=name, grid_spec=pltpu.PrefetchScalarGridSpec(...  34.9 us
    ppermute x9, waiting for transfers between devices, shift(): lax.ppermute(value, axis, [(i, (i + steps) % count) for i in range(count)])  26.4 us
    ppermute x9, starting transfers between devices, shift(): lax.ppermute(value, axis, [(i, (i + steps) % count) for i in range(count)])  13.5 us
    all_to_all x2, starting transfers between devices, exchange(): lax.all_to_all(value, 'node', split_axis=0, concat_axis=0, tiled=True)  8.03 us
    all_to_all x2, waiting for transfers between devices, exchange(): lax.all_to_all(value, 'node', split_axis=0, concat_axis=0, tiled=True)  5.43 us
    all_to_all x1, starting transfers between devices, body(): lax.all_to_all(sums, 'layer', split_axis=0, concat_axis=0, tiled=True)  4.15 us
  transfers between devices with their start and end apart: 20, of which 10 were waited for; matrix products, arithmetic and copies ran while one was open for 1% of the time, Pallas kernels for 10%

profile of v10, /device:TPU:0, one launch (start us, length us, event | category | flops | bytes accessed | tf_op | source)
XLA Modules:
  0.0 205.0 jit_solution(7207374717092608562)
XLA Ops:
  0.7 1.3 broadcast_select_fusion
  2.0 3.2 %collective-permute-start.2 = (bf16[512,512]{1,0:T(8,128)(2,1)S(1)}, bf16[512,512]{1,0:T(8,128)(2,1)S(1)}, u32[]{:S(2)}, u32[]{:S(2)}) collective-permute-start(bf16[512,512]{1,0:T(8,128)(2,1)S(1)} %broadcast_select_fusion), channel_id=1, source_target_pairs={{0,64},{32,96},{64,0},{96,32},{1,65},{33,97},{65,1},{97,33},{2,66}... | collective-permute-start | bytes 1572872 | tf_op jit(solution)/shard_map/ppermute | solution.py:26
  5.2 1.1 collective-permute-start.1
  6.3 0.9 collective-permute-start
  7.2 0.8 reshape.44
  8.1 2.7 %gather_rows.1 = (bf16[256,256]{1,0:T(8,128)(2,1)S(1)}, bf16[256,512]{1,0:T(8,128)(2,1)S(1)}, bf16[256,512]{1,0:T(8,128)(2,1)S(1)}, bf16[2,4,128,128]{3,2,1,0:T(...) custom-call(s32[10]{0:T(128)S(1)} %pad_add_fusion.ids, ...), custom_call_target="tpu_custom_call" | custom-call | flops 100000000 | bytes 1000000 | tf_op jit(solution)/shard_map/gather_rows/pallas_call | solution.py:60
  10.8 17.1 %all_to_all.50 = bf16[32,8,512]{2,1,0:T(8,128)(2,1)S(1)} all-to-all(bf16[32,8,512]{2,1,0:T(8,128)(2,1)S(1)} %bitcast.47), channel_id=1, replica_groups=mesh['layer'=4,'node'=32] {'node'}, dimensions={0} | all-to-all | bytes 524288 | tf_op jit(solution)/shard_map/all_to_all | solution.py:35
  27.8 0.9 collective-permute-done.1.rest_4_
  29.2 1.4 collective-permute-done.3.rest_3_
  30.6 0.7 collective-permute-done.4.rest_5_
  31.4 0.7 collective-permute-done.5.rest_7_
  32.1 1.9 layer_forward_0.1
  34.0 17.1 %all_to_all.51 = bf16[32,8,512]{2,1,0:T(8,128)(2,1)S(1)} all-to-all(bf16[32,8,512]{2,1,0:T(8,128)(2,1)S(1)} %bitcast.48), channel_id=1, replica_groups=mesh['layer'=4,'node'=32] {'node'}, dimensions={0} | all-to-all | bytes 524288 | tf_op jit(solution)/shard_map/all_to_all | solution.py:35
  51.1 1.7 layer_forward_1.1
  52.8 12.5 %all_to_all.52 = bf16[32,8,512]{2,1,0:T(8,128)(2,1)S(1)} all-to-all(bf16[32,8,512]{2,1,0:T(8,128)(2,1)S(1)} %bitcast.49), channel_id=1, replica_groups=mesh['layer'=4,'node'=32] {'node'}, dimensions={0} | all-to-all | bytes 524288 | tf_op jit(solution)/shard_map/all_to_all | solution.py:35
  65.2 1.7 layer_forward_2.1
  66.9 12.5 %all_to_all.53 = bf16[32,8,512]{2,1,0:T(8,128)(2,1)S(1)} all-to-all(bf16[32,8,512]{2,1,0:T(8,128)(2,1)S(1)} %bitcast.45), channel_id=1, replica_groups=mesh['layer'=4,'node'=32] {'node'}, dimensions={0} | all-to-all | bytes 524288 | tf_op jit(solution)/shard_map/all_to_all | solution.py:35
  79.4 3.5 %top_layer.1 = (bf16[32,8,512]{2,1,0:T(8,128)(2,1)S(1)}, f32[256,512]{1,0:T(8,128)S(1)}, bf16[512,512]{1,0:T(8,128)(2,1)S(1)}, bf16[512,512]{1,0:T(8,128)(2,1)S(1)}, bf16[4,256,512]{2,1,0:T(8,128)(2,1)}) custom-call(s32[10]{0:T(128)S(1)} %pad_add_fusion.ids, bf16[256,512]{1,0:T(8,128)(2,1)S(1)} %get-tuple-element.103.h_ref, ...), custom_call_target="tpu_custom_call", output_to_operand_aliasing={{4}: (9, {})} | custom-call | flops 1000000000 | bytes 5000000 | tf_op jit(solution)/shard_map/top_layer/pallas_call | solution.py:60
  82.9 12.5 %all_to_all.54.ret_ref = bf16[32,8,512]{2,1,0:T(8,128)(2,1)S(1)} all-to-all(bf16[32,8,512]{2,1,0:T(8,128)(2,1)S(1)} %get-tuple-element.108), channel_id=1, replica_groups=mesh['layer'=4,'node'=32] {'node'}, dimensions={0} | all-to-all | bytes 524288 | tf_op jit(solution)/shard_map/all_to_all | solution.py:35
  95.7 2.3 %layer_backward_2.1 = (bf16[32,8,512]{2,1,0:T(8,128)(2,1)S(1)}, f32[256,512]{1,0:T(8,128)S(1)}, bf16[4,256,512]{2,1,0:T(8,128)(2,1)}, bf16[512,512]{1,0:T(8,128)(2,1)S(1)}, bf16[512,512]{1,0:T(8,128)(2,1)S(1)}) custom-call(s32[10]{0:T(128)S(1)} %pad_add_fusion.ids, bf16[32,8,512]{2,1,0:T(8,128)(2,1)S(1)} %all_to_all.54.ret_ref, ...), custom_call_target="tpu_custom_call" | custom-call | flops 1000000000 | bytes 5000000 | tf_op jit(solution)/shard_map/layer_backward_2/pallas_call | solution.py:60
  98.0 12.3 %all_to_all.55.ret_ref = bf16[32,8,512]{2,1,0:T(8,128)(2,1)S(1)} all-to-all(bf16[32,8,512]{2,1,0:T(8,128)(2,1)S(1)} %get-tuple-element.117), channel_id=1, replica_groups=mesh['layer'=4,'node'=32] {'node'}, dimensions={0} | all-to-all | bytes 524288 | tf_op jit(solution)/shard_map/all_to_all | solution.py:35
  110.6 2.6 %layer_backward_1.1 = (bf16[32,24,512]{2,1,0:T(8,128)(2,1)S(1)}, f32[256,512]{1,0:T(8,128)S(1)}, bf16[4,256,512]{2,1,0:T(8,128)(2,1)}, bf16[512,512]{1,0:T(8,128)(2,1)S(1)}, bf16[512,512]{1,0:T(8,128)(2,1)S(1)}) custom-call(s32[10]{0:T(128)S(1)} %pad_add_fusion.ids, bf16[32,8,512]{2,1,0:T(8,128)(2,1)S(1)} %all_to_all.55.ret_ref, ...), custom_call_target="tpu_custom_call", output_to_operand_aliasing={{2}: (11, {})} | custom-call | flops 1000000000 | bytes 5000000 | tf_op jit(solution)/shard_map/layer_backward_1/pallas_call | solution.py:60
  113.2 17.2 %all_to_all.56.ret_ref = bf16[32,24,512]{2,1,0:T(8,128)(2,1)S(1)} all-to-all(bf16[32,24,512]{2,1,0:T(8,128)(2,1)S(1)} %get-tuple-element.128), channel_id=1, replica_groups=mesh['layer'=4,'node'=32] {'node'}, dimensions={0} | all-to-all | bytes 1572864 | tf_op jit(solution)/shard_map/all_to_all | solution.py:35
  130.4 0.7 collective-permute-start.8
  131.0 1.7 last_slope.1
  132.9 2.9 %last_spread.1 = (bf16[32,56,512]{2,1,0:T(8,128)(2,1)}, f32[256,512]{1,0:T(8,128)S(1)}, bf16[32,8,512]{2,1,0:T(8,128)(2,1)S(1)}, bf16[4,2,16,512]{3,2,1,0:T(8,128)(2,1)}) custom-call(s32[10]{0:T(128)S(1)} %pad_add_fusion.ids, bf16[256,512]{1,0:T(8,128)(2,1)S(1)} %get-tuple-element.139.dpre_ref, ...), custom_call_target="tpu_custom_call" | custom-call | flops 500000000 | bytes 4000000 | tf_op jit(solution)/shard_map/last_spread/pallas_call | solution.py:60
  135.9 1.6 join_rows.1
  137.5 4.1 %all-to-all-start.7 = ((bf16[32,56,512]{2,1,0:T(8,128)(2,1)}), bf16[32,56,512]{2,1,0:T(8,128)(2,1)S(1)}, u32[]{:S(2)}, u32[]{:S(2)}) async-start(bf16[32,56,512]{2,1,0:T(8,128)(2,1)} %get-tuple-element.154), calls=%async_computation.7 | async-start | bytes 3670016 | tf_op jit(solution)/shard_map/all_to_all | solution.py:35
  141.7 2.7 %collective-permute-start.12 = (bf16[256,512]{1,0:T(8,128)(2,1)S(1)}, bf16[256,512]{1,0:T(8,128)(2,1)S(1)}, u32[]{:S(2)}, u32[]{:S(2)}) collective-permute-start(bf16[256,512]{1,0:T(8,128)(2,1)S(1)} %get-tuple-element.175), channel_id=1, source_target_pairs={{0,96},{32,0},{64,32},{96,64},{1,97},{33,1},{65,33},{97,65},{2,98}... | collective-permute-start | bytes 786440 | tf_op jit(solution)/shard_map/ppermute | solution.py:26
  144.4 0.9 collective-permute-start.11
  145.3 0.8 collective-permute-start.10
  146.1 10.0 %collective-permute-done.12.refs_3_ = bf16[256,512]{1,0:T(8,128)(2,1)S(1)} collective-permute-done((bf16[256,512]{1,0:T(8,128)(2,1)S(1)}, bf16[256,512]{1,0:T(8,128)(2,1)S(1)}, u32[]{:S(2)}, u32[]{:S(2)}) %collective-permute-start.12) | collective-permute-done | bytes 262176 | tf_op jit(solution)/shard_map/ppermute | solution.py:26
  156.1 3.7 %collective-permute-done.10.refs_1_ = bf16[256,512]{1,0:T(8,128)(2,1)S(1)} collective-permute-done((bf16[256,512]{1,0:T(8,128)(2,1)S(1)}, bf16[256,512]{1,0:T(8,128)(2,1)S(1)}, u32[]{:S(2)}, u32[]{:S(2)}) %collective-permute-start.10) | collective-permute-done | bytes 262176 | tf_op jit(solution)/shard_map/ppermute | solution.py:26
  159.7 2.5 %put_home.2 = bf16[1,4,256,512]{3,2,1,0:T(8,128)(2,1)} custom-call(s32[10]{0:T(128)S(1)} %pad_add_fusion.ids, bf16[4,256,512]{2,1,0:T(8,128)(2,1)} %get-tuple-element.155.refs_0_, bf16[256,512]{1,0:T(8,128)(2,1)S(1)} %collective-permute-done.10.refs_1_, bf16[256,512]{1,0:T(8,128)(2,1)S(1)} %collective-permute-done.11.refs_2_, ...), custom_call_target="tpu_custom_call" | custom-call | bytes 2000000 | tf_op jit(solution)/shard_map/put_home/pallas_call | solution.py:60
  162.3 5.4 %all-to-all-done.7.ret_ref = bf16[32,56,512]{2,1,0:T(8,128)(2,1)S(1)} async-done(((bf16[32,56,512]{2,1,0:T(8,128)(2,1)}), bf16[32,56,512]{2,1,0:T(8,128)(2,1)S(1)}, u32[]{:S(2)}, u32[]{:S(2)}) %all-to-all-start.7) | async-done | bytes 1835040 | tf_op jit(solution)/shard_map/all_to_all | solution.py:35
  167.7 1.4 sum_chunks.1
  169.1 4.1 %all-to-all-start.8 = ((bf16[4,2,16,512]{3,2,1,0:T(8,128)(2,1)}), bf16[4,2,16,512]{3,2,1,0:T(8,128)(2,1)S(1)}, u32[]{:S(2)}, u32[]{:S(2)}) async-start(bf16[4,2,16,512]{3,2,1,0:T(8,128)(2,1)} %sum_chunks.1), calls=%async_computation.8 | async-start | bytes 262144 | tf_op jit(solution)/shard_map/all_to_all | solution.py:642
  173.2 2.5 %input_grads.1.refs_0_ = bf16[4,256,512]{2,1,0:T(8,128)(2,1)} custom-call(s32[10]{0:T(128)S(1)} %pad_add_fusion.ids, bf16[32,56,512]{2,1,0:T(8,128)(2,1)S(1)} %all-to-all-done.7.ret_ref, f32[256,512]{1,0:T(8,128)} %get-tuple-element.158.part_in, bf16[256,256]{1,0:T(8,128)(2,1)} %get-tuple-element.159.pick_ref, ...), custom_call_target="tpu_custom_call", output_to_operand_aliasing={{}: (4, {})} | custom-call | flops 100000000 | bytes 1000000 | tf_op jit(solution)/shard_map/input_grads/pallas_call | solution.py:60
  175.8 1.2 slice_bitcast_fusion
  177.0 2.3 %all-to-all-done.8.sums_ref = bf16[4,2,16,512]{3,2,1,0:T(8,128)(2,1)S(1)} async-done(((bf16[4,2,16,512]{3,2,1,0:T(8,128)(2,1)}), bf16[4,2,16,512]{3,2,1,0:T(8,128)(2,1)S(1)}, u32[]{:S(2)}, u32[]{:S(2)}) %all-to-all-start.8) | async-done | bytes 131104 | tf_op jit(solution)/shard_map/all_to_all | solution.py:642
  179.2 1.4 sum_over_layer.1
  180.6 3.9 %all-to-all-start.9 = ((bf16[32,16,512]{2,1,0:T(8,128)(2,1)}), bf16[32,16,512]{2,1,0:T(8,128)(2,1)S(1)}, u32[]{:S(2)}, u32[]{:S(2)}) async-start(bf16[32,16,512]{2,1,0:T(8,128)(2,1)} %sum_over_layer.1), calls=%async_computation.9 | async-start | bytes 1048576 | tf_op jit(solution)/shard_map/all_to_all | solution.py:35
  184.5 0.6 collective-permute-start.13
  185.1 2.1 %collective-permute-start.14 = (bf16[256,512]{1,0:T(8,128)(2,1)S(1)}, bf16[256,512]{1,0:T(8,128)(2,1)S(1)}, u32[]{:S(2)}, u32[]{:S(2)}) collective-permute-start(bf16[256,512]{1,0:T(8,128)(2,1)S(1)} %get-tuple-element.164), channel_id=1, source_target_pairs={{0,64},{32,96},{64,0},{96,32},{1,65},{33,97},{65,1},{97,33},{2,66}... | collective-permute-start | bytes 786440 | tf_op jit(solution)/shard_map/ppermute | solution.py:26
  187.2 1.3 collective-permute-start.15
  188.5 11.3 %collective-permute-done.13.refs_1_ = bf16[256,512]{1,0:T(8,128)(2,1)S(1)} collective-permute-done((bf16[256,512]{1,0:T(8,128)(2,1)S(1)}, bf16[256,512]{1,0:T(8,128)(2,1)S(1)}, u32[]{:S(2)}, u32[]{:S(2)}) %collective-permute-start.13) | collective-permute-done | bytes 262176 | tf_op jit(solution)/shard_map/ppermute | solution.py:26
  200.4 2.5 %put_home.3 = bf16[1,4,256,512]{3,2,1,0:T(8,128)(2,1)} custom-call(s32[10]{0:T(128)S(1)} %pad_add_fusion.ids, bf16[4,256,512]{2,1,0:T(8,128)(2,1)} %input_grads.1.refs_0_, bf16[256,512]{1,0:T(8,128)(2,1)S(1)} %collective-permute-done.13.refs_1_, bf16[256,512]{1,0:T(8,128)(2,1)S(1)} %collective-permute-done.14.refs_2_, ...), custom_call_target="tpu_custom_call" | custom-call | bytes 2000000 | tf_op jit(solution)/shard_map/put_home/pallas_call | solution.py:60
  202.9 1.9 scale_grads.1
  (33 shorter events, 2.1 us)
Async XLA Ops:
  0.6 31.5 %copy-start = (bf16[1,512,512]{2,1,0:T(8,128)(2,1)S(1)}, bf16[1,512,512]{2,1,0:T(8,128)(2,1)}, u32[]{:S(2)}) copy-start(bf16[1,512,512]{2,1,0:T(8,128)(2,1)} %param.11) | copy-start | bytes 1572868
  0.6 31.5 %copy-start.1 = (bf16[1,512,512]{2,1,0:T(8,128)(2,1)S(1)}, bf16[1,512,512]{2,1,0:T(8,128)(2,1)}, u32[]{:S(2)}) copy-start(bf16[1,512,512]{2,1,0:T(8,128)(2,1)} %param.12) | copy-start | bytes 1572868
  2.0 25.8 %collective-permute-start.2 = (bf16[512,512]{1,0:T(8,128)(2,1)S(1)}, bf16[512,512]{1,0:T(8,128)(2,1)S(1)}, u32[]{:S(2)}, u32[]{:S(2)}) collective-permute-start(bf16[512,512]{1,0:T(8,128)(2,1)S(1)} %broadcast_select_fusion), channel_id=1, source_target_pairs={{0,64},{32,96},{64,0},{96,32},{1,65},{33,97},{65,1},{97,33},{2,66}... | collective-permute-start | bytes 1572872 | tf_op jit(solution)/shard_map/ppermute | solution.py:26
  5.2 23.5 %collective-permute-start.1 = (bf16[512,512]{1,0:T(8,128)(2,1)S(1)}, bf16[512,512]{1,0:T(8,128)(2,1)S(1)}, u32[]{:S(2)}, u32[]{:S(2)}) collective-permute-start(bf16[512,512]{1,0:T(8,128)(2,1)S(1)} %broadcast_select_fusion), channel_id=1, source_target_pairs={{0,96},{32,0},{64,32},{96,64},{1,97},{33,1},{65,33},{97,65},{2,98}... | collective-permute-start | bytes 1572872 | tf_op jit(solution)/shard_map/ppermute | solution.py:26
  6.3 22.4 %collective-permute-start = (bf16[512,512]{1,0:T(8,128)(2,1)S(1)}, bf16[512,512]{1,0:T(8,128)(2,1)S(1)}, u32[]{:S(2)}, u32[]{:S(2)}) collective-permute-start(bf16[512,512]{1,0:T(8,128)(2,1)S(1)} %broadcast_select_fusion), channel_id=1, source_target_pairs={{0,32},{32,64},{64,96},{96,0},{1,33},{33,65},{65,97},{97,1},{2,34}... | collective-permute-start | bytes 1572872 | tf_op jit(solution)/shard_map/ppermute | solution.py:26
  28.7 1.9 collective-permute-start.3
  28.7 2.7 %collective-permute-start.4 = (bf16[512,512]{1,0:T(8,128)(2,1)S(1)}, bf16[512,512]{1,0:T(8,128)(2,1)S(1)}, u32[]{:S(2)}, u32[]{:S(2)}) collective-permute-start(bf16[512,512]{1,0:T(8,128)(2,1)S(1)} %collective-permute-done.1.rest_4_), channel_id=1, source_target_pairs={{0,1},{1,0},{2,3},{3,2},{4,5},{5,4},{6,7},{7,6},{8,9},{9,8},{10,11... | collective-permute-start | bytes 1572872 | tf_op jit(solution)/shard_map/ppermute | solution.py:31
  29.2 2.9 %collective-permute-start.5 = (bf16[512,512]{1,0:T(8,128)(2,1)S(1)}, bf16[512,512]{1,0:T(8,128)(2,1)S(1)}, u32[]{:S(2)}, u32[]{:S(2)}) collective-permute-start(bf16[512,512]{1,0:T(8,128)(2,1)S(1)} %collective-permute-done.2.rest_6_), channel_id=1, source_target_pairs={{0,1},{1,0},{2,3},{3,2},{4,5},{5,4},{6,7},{7,6},{8,9},{9,8},{10,11... | collective-permute-start | bytes 1572872 | tf_op jit(solution)/shard_map/ppermute | solution.py:31
  65.2 14.1 %copy-start.2 = (bf16[512,172]{0,1:T(8,128)(2,1)S(1)}, bf16[512,172]{0,1:T(8,128)(2,1)}, u32[]{:S(2)}) copy-start(bf16[512,172]{0,1:T(8,128)(2,1)} %param.13) | copy-start | bytes 528388
  65.2 14.1 %copy-start.3 = (s32[4,256]{1,0:T(4,128)S(1)}, s32[4,256]{1,0:T(4,128)}, u32[]{:S(2)}) copy-start(s32[4,256]{1,0:T(4,128)} %lab_ref.1) | copy-start | bytes 12292
  65.2 14.1 %copy-start.4 = (s32[4,256]{1,0:T(4,128)S(1)}, s32[4,256]{1,0:T(4,128)}, u32[]{:S(2)}) copy-start(s32[4,256]{1,0:T(4,128)} %mask_ref.1) | copy-start | bytes 12292
  95.4 2.6 %collective-permute-start.6 = (bf16[512,512]{1,0:T(8,128)(2,1)S(1)}, bf16[512,512]{1,0:T(8,128)(2,1)S(1)}, u32[]{:S(2)}, u32[]{:S(2)}) collective-permute-start(bf16[512,512]{1,0:T(8,128)(2,1)S(1)} %get-tuple-element.116), channel_id=1, source_target_pairs={{0,1},{1,0},{2,3},{3,2},{4,5},{5,4},{6,7},{7,6},{8,9},{9,8},{10,11... | collective-permute-start | bytes 1572872 | tf_op jit(solution)/shard_map/ppermute | solution.py:31
  110.3 2.9 %collective-permute-start.7 = (bf16[512,512]{1,0:T(8,128)(2,1)S(1)}, bf16[512,512]{1,0:T(8,128)(2,1)S(1)}, u32[]{:S(2)}, u32[]{:S(2)}) collective-permute-start(bf16[512,512]{1,0:T(8,128)(2,1)S(1)} %get-tuple-element.127), channel_id=1, source_target_pairs={{0,1},{1,0},{2,3},{3,2},{4,5},{5,4},{6,7},{7,6},{8,9},{9,8},{10,11... | collective-permute-start | bytes 1572872 | tf_op jit(solution)/shard_map/ppermute | solution.py:31
  130.4 2.4 %collective-permute-start.8 = (bf16[512,512]{1,0:T(8,128)(2,1)S(1)}, bf16[512,512]{1,0:T(8,128)(2,1)S(1)}, u32[]{:S(2)}, u32[]{:S(2)}) collective-permute-start(bf16[512,512]{1,0:T(8,128)(2,1)S(1)} %get-tuple-element.137), channel_id=1, source_target_pairs={{0,1},{1,0},{2,3},{3,2},{4,5},{5,4},{6,7},{7,6},{8,9},{9,8},{10,11... | collective-permute-start | bytes 1572872 | tf_op jit(solution)/shard_map/ppermute | solution.py:31
  132.8 3.1 %collective-permute-start.9 = (bf16[512,512]{1,0:T(8,128)(2,1)S(1)}, bf16[512,512]{1,0:T(8,128)(2,1)S(1)}, u32[]{:S(2)}, u32[]{:S(2)}) collective-permute-start(bf16[512,512]{1,0:T(8,128)(2,1)S(1)} %get-tuple-element.147), channel_id=1, source_target_pairs={{0,1},{1,0},{2,3},{3,2},{4,5},{5,4},{6,7},{7,6},{8,9},{9,8},{10,11... | collective-permute-start | bytes 1572872 | tf_op jit(solution)/shard_map/ppermute | solution.py:31
  137.5 4.2 %copy-start.5 = (bf16[4,256,512]{2,1,0:T(8,128)(2,1)S(1)}, bf16[4,256,512]{2,1,0:T(8,128)(2,1)}, u32[]{:S(2)}) copy-start(bf16[4,256,512]{2,1,0:T(8,128)(2,1)} %get-tuple-element.155.refs_0_) | copy-start | bytes 3145732
  137.5 30.2 %all-to-all-start.7 = ((bf16[32,56,512]{2,1,0:T(8,128)(2,1)}), bf16[32,56,512]{2,1,0:T(8,128)(2,1)S(1)}, u32[]{:S(2)}, u32[]{:S(2)}) async-start(bf16[32,56,512]{2,1,0:T(8,128)(2,1)} %get-tuple-element.154), calls=%async_computation.7 | async-start | bytes 3670016 | tf_op jit(solution)/shard_map/all_to_all | solution.py:35
  141.7 14.3 %collective-permute-start.12 = (bf16[256,512]{1,0:T(8,128)(2,1)S(1)}, bf16[256,512]{1,0:T(8,128)(2,1)S(1)}, u32[]{:S(2)}, u32[]{:S(2)}) collective-permute-start(bf16[256,512]{1,0:T(8,128)(2,1)S(1)} %get-tuple-element.175), channel_id=1, source_target_pairs={{0,96},{32,0},{64,32},{96,64},{1,97},{33,1},{65,33},{97,65},{2,98}... | collective-permute-start | bytes 786440 | tf_op jit(solution)/shard_map/ppermute | solution.py:26
  144.4 11.7 %collective-permute-start.11 = (bf16[256,512]{1,0:T(8,128)(2,1)S(1)}, bf16[256,512]{1,0:T(8,128)(2,1)S(1)}, u32[]{:S(2)}, u32[]{:S(2)}) collective-permute-start(bf16[256,512]{1,0:T(8,128)(2,1)S(1)} %get-tuple-element.176), channel_id=1, source_target_pairs={{0,64},{32,96},{64,0},{96,32},{1,65},{33,97},{65,1},{97,33},{2,66}... | collective-permute-start | bytes 786440 | tf_op jit(solution)/shard_map/ppermute | solution.py:26
  145.3 14.5 %collective-permute-start.10 = (bf16[256,512]{1,0:T(8,128)(2,1)S(1)}, bf16[256,512]{1,0:T(8,128)(2,1)S(1)}, u32[]{:S(2)}, u32[]{:S(2)}) collective-permute-start(bf16[256,512]{1,0:T(8,128)(2,1)S(1)} %get-tuple-element.177), channel_id=1, source_target_pairs={{0,32},{32,64},{64,96},{96,0},{1,33},{33,65},{65,97},{97,1},{2,34}... | collective-permute-start | bytes 786440 | tf_op jit(solution)/shard_map/ppermute | solution.py:26
  169.1 10.1 %all-to-all-start.8 = ((bf16[4,2,16,512]{3,2,1,0:T(8,128)(2,1)}), bf16[4,2,16,512]{3,2,1,0:T(8,128)(2,1)S(1)}, u32[]{:S(2)}, u32[]{:S(2)}) async-start(bf16[4,2,16,512]{3,2,1,0:T(8,128)(2,1)} %sum_chunks.1), calls=%async_computation.8 | async-start | bytes 262144 | tf_op jit(solution)/shard_map/all_to_all | solution.py:642
  180.6 19.8 %all-to-all-start.9 = ((bf16[32,16,512]{2,1,0:T(8,128)(2,1)}), bf16[32,16,512]{2,1,0:T(8,128)(2,1)S(1)}, u32[]{:S(2)}, u32[]{:S(2)}) async-start(bf16[32,16,512]{2,1,0:T(8,128)(2,1)} %sum_over_layer.1), calls=%async_computation.9 | async-start | bytes 1048576 | tf_op jit(solution)/shard_map/all_to_all | solution.py:35
  184.5 15.3 %collective-permute-start.13 = (bf16[256,512]{1,0:T(8,128)(2,1)S(1)}, bf16[256,512]{1,0:T(8,128)(2,1)S(1)}, u32[]{:S(2)}, u32[]{:S(2)}) collective-permute-start(bf16[256,512]{1,0:T(8,128)(2,1)S(1)} %get-tuple-element.163), channel_id=1, source_target_pairs={{0,32},{32,64},{64,96},{96,0},{1,33},{33,65},{65,97},{97,1},{2,34}... | collective-permute-start | bytes 786440 | tf_op jit(solution)/shard_map/ppermute | solution.py:26
  185.1 14.6 %collective-permute-start.14 = (bf16[256,512]{1,0:T(8,128)(2,1)S(1)}, bf16[256,512]{1,0:T(8,128)(2,1)S(1)}, u32[]{:S(2)}, u32[]{:S(2)}) collective-permute-start(bf16[256,512]{1,0:T(8,128)(2,1)S(1)} %get-tuple-element.164), channel_id=1, source_target_pairs={{0,64},{32,96},{64,0},{96,32},{1,65},{33,97},{65,1},{97,33},{2,66}... | collective-permute-start | bytes 786440 | tf_op jit(solution)/shard_map/ppermute | solution.py:26
  187.2 13.2 %collective-permute-start.15 = (bf16[256,512]{1,0:T(8,128)(2,1)S(1)}, bf16[256,512]{1,0:T(8,128)(2,1)S(1)}, u32[]{:S(2)}, u32[]{:S(2)}) collective-permute-start(bf16[256,512]{1,0:T(8,128)(2,1)S(1)} %get-tuple-element.165), channel_id=1, source_target_pairs={{0,96},{32,0},{64,32},{96,64},{1,97},{33,1},{65,33},{97,65},{2,98}... | collective-permute-start | bytes 786440 | tf_op jit(solution)/shard_map/ppermute | solution.py:26
  200.4 2.5 %collective-permute-start.16 = (bf16[512,512]{1,0:T(8,128)(2,1)S(1)}, bf16[512,512]{1,0:T(8,128)(2,1)S(1)}, u32[]{:S(2)}, u32[]{:S(2)}) collective-permute-start(bf16[512,512]{1,0:T(8,128)(2,1)S(1)} %bitcast.40), channel_id=1, source_target_pairs={{0,1},{1,0},{2,3},{3,2},{4,5},{5,4},{6,7},{7,6},{8,9},{9,8},{10,11... | collective-permute-start | bytes 1572872 | tf_op jit(solution)/shard_map/ppermute | solution.py:31

commit v11 on v10

--- a/solution.py
+++ b/solution.py
@@ -315,7 +315,7 @@
     peers, slots = local_ref.shape[0], local_ref.shape[1]
     size = keep_a.shape[0] // peers
     copies = [
-        pltpu.make_async_copy(c_in, c_ref.at[3], sems.at[0]),
+        pltpu.make_async_copy(c_in, c_ref, sems.at[0]),
         pltpu.make_async_copy(
             carried, out_ref.at[:, pl.ds(slots, 2 * size), :], sems.at[1]
         ),
@@ -354,15 +354,17 @@
         copy.wait()
 
 
-def chunk_kernel(ids, ret_ref, buf_in, out_ref, sums, sem):
+def chunk_kernel(ids, ret_ref, c_in, o_0, o_1, o_2, o_3, sums, sem):
+    copy = pltpu.make_async_copy(c_in, sums.at[3], sem)
+    copy.start()
     size = sums.shape[2]
     slots = ret_ref.shape[1] - 3 * size
     for n, layer in enumerate((2, 1, 0)):
         first = slots + n * size
         sums[layer] = chunk_sum(ret_ref[:, first : first + size, :]).astype(BF)
-    copy = pltpu.make_async_copy(sums, out_ref.at[pl.ds(0, 3)], sem)
-    copy.start()
     copy.wait()
+    for s, out_ref in enumerate((o_0, o_1, o_2, o_3)):
+        out_ref[...] = sums[lax.rem(ids[0] + s, 4)]
 
 
 def end_kernel(ids, ret_ref, part_in, pick_ref, buf_in, buf_ref, dout_ref, buf_sem):
@@ -374,11 +376,9 @@
     copy.wait()
 
 
-def layer_sum_kernel(ids, sums_ref, out_ref):
-    total = sums_ref[0].astype(F32)
-    for span in range(1, sums_ref.shape[0]):
-        total = total + sums_ref[span].astype(F32)
-    total = total.astype(BF)
+def layer_sum_kernel(ids, own_ref, a_ref, b_ref, c_ref, out_ref):
+    total = own_ref[...].astype(F32) + a_ref[...].astype(F32)
+    total = (total + b_ref[...].astype(F32) + c_ref[...].astype(F32)).astype(BF)
     for n in range(0, out_ref.shape[0], 2):
         out_ref[n : n + 2] = total
 
@@ -599,7 +599,7 @@
     recv = sibling(send)
     width = slots + 3 * chunk_rows
     operand = (pltpu.HBM((peers, width, feat), BF), FAR)
-    sums_out = (pltpu.HBM((spans, *chunk_shape), BF), FAR)
+    sums_out = (pltpu.HBM(chunk_shape, BF), FAR)
     remote, part, local, sums = run(
         last_spread_kernel,
         "last_spread",
@@ -629,17 +629,16 @@
     acts = travel(acts_buf)
     layer_acts = put_home(acts_buf, *acts)
     returned, layer_acts = tie(exchange(joined), layer_acts)
-    sums = run(
+    own_sum, *sums = run(
         chunk_kernel,
         "sum_chunks",
         scalars,
         [returned, (sums, FAR)],
-        [sums_out],
-        [pltpu.VMEM((3, *chunk_shape), BF), buf_sem],
-        aliases={1: 0},
+        [near(chunk_shape)] * spans,
+        [pltpu.VMEM((spans, *chunk_shape), BF), buf_sem],
         moved=10**6,
-    )[0]
-    sums = lax.all_to_all(sums, "layer", split_axis=0, concat_axis=0, tiled=True)
+    )
+    sums = [shift(v, "layer", s) for s, v in zip(all_shifts, sums)]
     grads_buf = run(
         end_kernel,
         "input_grads",
@@ -656,12 +655,13 @@
         flops=10**8,
         moved=10**6,
     )[0]
-    sums, *to_send = tie(sums, *[grads_buf[s] for s in all_shifts])
+    pieces = tie(*sums, *[grads_buf[s] for s in all_shifts])
+    sums, to_send = pieces[:3], pieces[3:]
     spread = run(
         layer_sum_kernel,
         "sum_over_layer",
         scalars,
-        [sums],
+        [own_sum, *sums],
         [far_block((peers, chunk_rows, feat))],
         moved=10**6,
     )[0]

time: 207 us -> 206 us (level)
    ppermute x9 -> x12, starting transfers between devices: 13.5 us -> 18.6 us  [shift(): lax.ppermute(value, axis, [(i, (i + steps) % count) for i in range(count)])]
    all_to_all x1 -> x0, starting transfers between devices: 4.15 us -> none  [body(): lax.all_to_all(sums, 'layer', split_axis=0, concat_axis=0, tiled=True)]
    all_to_all x1 -> x0, waiting for transfers between devices: 2.27 us -> none  [body(): lax.all_to_all(sums, 'layer', split_axis=0, concat_axis=0, tiled=True)]
    ppermute x9 -> x12, waiting for transfers between devices: 26.4 us -> 27 us  [shift(): lax.ppermute(value, axis, [(i, (i + steps) % count) for i in range(count)])]
  transfers between devices with their start and end apart: 20 -> 22, of which waited for: 10 -> 9; matrix products, arithmetic and copies ran while one was open for 1% -> 1% of each run, Pallas kernels for 10% -> 10%
where the time goes in v11:
time: 206 us; the launch traced here: 204 us
  blocking collectives  101 us (49%)
  waiting for transfers between devices  35.4 us (17%)
  Pallas kernels  34.8 us (17%)
  starting transfers between devices  28.6 us (14%)
    all_to_all x7, blocking collectives, exchange(): lax.all_to_all(value, 'node', split_axis=0, concat_axis=0, tiled=True)  101 us
    pallas_call x16, Pallas kernels, run(): pl.pallas_call(kernel, name=name, grid_spec=pltpu.PrefetchScalarGridSpec(...  34.8 us
    ppermute x12, waiting for transfers between devices, shift(): lax.ppermute(value, axis, [(i, (i + steps) % count) for i in range(count)])  27 us
    ppermute x12, starting transfers between devices, shift(): lax.ppermute(value, axis, [(i, (i + steps) % count) for i in range(count)])  18.6 us
    all_to_all x2, starting transfers between devices, exchange(): lax.all_to_all(value, 'node', split_axis=0, concat_axis=0, tiled=True)  8.03 us
    all_to_all x2, waiting for transfers between devices, exchange(): lax.all_to_all(value, 'node', split_axis=0, concat_axis=0, tiled=True)  5.43 us
  transfers between devices with their start and end apart: 22, of which 9 were waited for; matrix products, arithmetic and copies ran while one was open for 1% of the time, Pallas kernels for 10%

profile of v11, /device:TPU:0, one launch (start us, length us, event | category | flops | bytes accessed | tf_op | source)
XLA Modules:
  0.0 204.1 jit_solution(12194498268081495686)
XLA Ops:
  0.7 1.3 broadcast_select_fusion
  2.0 3.2 %collective-permute-start.2 = (bf16[512,512]{1,0:T(8,128)(2,1)S(1)}, bf16[512,512]{1,0:T(8,128)(2,1)S(1)}, u32[]{:S(2)}, u32[]{:S(2)}) collective-permute-start(bf16[512,512]{1,0:T(8,128)(2,1)S(1)} %broadcast_select_fusion), channel_id=1, source_target_pairs={{0,64},{32,96},{64,0},{96,32},{1,65},{33,97},{65,1},{97,33},{2,66}... | collective-permute-start | bytes 1572872 | tf_op jit(solution)/shard_map/ppermute | solution.py:26
  5.2 1.1 collective-permute-start.1
  6.3 0.9 collective-permute-start
  7.2 0.8 reshape.44
  8.1 2.7 %gather_rows.1 = (bf16[256,256]{1,0:T(8,128)(2,1)S(1)}, bf16[256,512]{1,0:T(8,128)(2,1)S(1)}, bf16[256,512]{1,0:T(8,128)(2,1)S(1)}, bf16[2,4,128,128]{3,2,1,0:T(...) custom-call(s32[10]{0:T(128)S(1)} %pad_add_fusion.ids, ...), custom_call_target="tpu_custom_call" | custom-call | flops 100000000 | bytes 1000000 | tf_op jit(solution)/shard_map/gather_rows/pallas_call | solution.py:60
  10.7 17.1 %all_to_all.45 = bf16[32,8,512]{2,1,0:T(8,128)(2,1)S(1)} all-to-all(bf16[32,8,512]{2,1,0:T(8,128)(2,1)S(1)} %bitcast.47), channel_id=1, replica_groups=mesh['layer'=4,'node'=32] {'node'}, dimensions={0} | all-to-all | bytes 524288 | tf_op jit(solution)/shard_map/all_to_all | solution.py:35
  27.8 0.9 collective-permute-done.1.rest_4_
  29.2 1.4 collective-permute-done.3.rest_3_
  30.6 0.7 collective-permute-done.4.rest_5_
  31.4 0.7 collective-permute-done.5.rest_7_
  32.1 1.9 layer_forward_0.1
  34.0 17.1 %all_to_all.46 = bf16[32,8,512]{2,1,0:T(8,128)(2,1)S(1)} all-to-all(bf16[32,8,512]{2,1,0:T(8,128)(2,1)S(1)} %bitcast.48), channel_id=1, replica_groups=mesh['layer'=4,'node'=32] {'node'}, dimensions={0} | all-to-all | bytes 524288 | tf_op jit(solution)/shard_map/all_to_all | solution.py:35
  51.1 1.7 layer_forward_1.1
  52.8 12.5 %all_to_all.47 = bf16[32,8,512]{2,1,0:T(8,128)(2,1)S(1)} all-to-all(bf16[32,8,512]{2,1,0:T(8,128)(2,1)S(1)} %bitcast.49), channel_id=1, replica_groups=mesh['layer'=4,'node'=32] {'node'}, dimensions={0} | all-to-all | bytes 524288 | tf_op jit(solution)/shard_map/all_to_all | solution.py:35
  65.2 1.7 layer_forward_2.1
  66.9 12.5 %all_to_all.48 = bf16[32,8,512]{2,1,0:T(8,128)(2,1)S(1)} all-to-all(bf16[32,8,512]{2,1,0:T(8,128)(2,1)S(1)} %bitcast.45), channel_id=1, replica_groups=mesh['layer'=4,'node'=32] {'node'}, dimensions={0} | all-to-all | bytes 524288 | tf_op jit(solution)/shard_map/all_to_all | solution.py:35
  79.4 3.5 %top_layer.1 = (bf16[32,8,512]{2,1,0:T(8,128)(2,1)S(1)}, f32[256,512]{1,0:T(8,128)S(1)}, bf16[512,512]{1,0:T(8,128)(2,1)S(1)}, bf16[512,512]{1,0:T(8,128)(2,1)S(1)}, bf16[4,256,512]{2,1,0:T(8,128)(2,1)}) custom-call(s32[10]{0:T(128)S(1)} %pad_add_fusion.ids, bf16[256,512]{1,0:T(8,128)(2,1)S(1)} %get-tuple-element.109.h_ref, ...), custom_call_target="tpu_custom_call", output_to_operand_aliasing={{4}: (9, {})} | custom-call | flops 1000000000 | bytes 5000000 | tf_op jit(solution)/shard_map/top_layer/pallas_call | solution.py:60
  82.9 12.5 %all_to_all.49.ret_ref = bf16[32,8,512]{2,1,0:T(8,128)(2,1)S(1)} all-to-all(bf16[32,8,512]{2,1,0:T(8,128)(2,1)S(1)} %get-tuple-element.114), channel_id=1, replica_groups=mesh['layer'=4,'node'=32] {'node'}, dimensions={0} | all-to-all | bytes 524288 | tf_op jit(solution)/shard_map/all_to_all | solution.py:35
  95.7 2.3 %layer_backward_2.1 = (bf16[32,8,512]{2,1,0:T(8,128)(2,1)S(1)}, f32[256,512]{1,0:T(8,128)S(1)}, bf16[4,256,512]{2,1,0:T(8,128)(2,1)}, bf16[512,512]{1,0:T(8,128)(2,1)S(1)}, bf16[512,512]{1,0:T(8,128)(2,1)S(1)}) custom-call(s32[10]{0:T(128)S(1)} %pad_add_fusion.ids, bf16[32,8,512]{2,1,0:T(8,128)(2,1)S(1)} %all_to_all.49.ret_ref, ...), custom_call_target="tpu_custom_call" | custom-call | flops 1000000000 | bytes 5000000 | tf_op jit(solution)/shard_map/layer_backward_2/pallas_call | solution.py:60
  98.0 12.3 %all_to_all.50.ret_ref = bf16[32,8,512]{2,1,0:T(8,128)(2,1)S(1)} all-to-all(bf16[32,8,512]{2,1,0:T(8,128)(2,1)S(1)} %get-tuple-element.123), channel_id=1, replica_groups=mesh['layer'=4,'node'=32] {'node'}, dimensions={0} | all-to-all | bytes 524288 | tf_op jit(solution)/shard_map/all_to_all | solution.py:35
  110.6 2.6 %layer_backward_1.1 = (bf16[32,24,512]{2,1,0:T(8,128)(2,1)S(1)}, f32[256,512]{1,0:T(8,128)S(1)}, bf16[4,256,512]{2,1,0:T(8,128)(2,1)}, bf16[512,512]{1,0:T(8,128)(2,1)S(1)}, bf16[512,512]{1,0:T(8,128)(2,1)S(1)}) custom-call(s32[10]{0:T(128)S(1)} %pad_add_fusion.ids, bf16[32,8,512]{2,1,0:T(8,128)(2,1)S(1)} %all_to_all.50.ret_ref, ...), custom_call_target="tpu_custom_call", output_to_operand_aliasing={{2}: (11, {})} | custom-call | flops 1000000000 | bytes 5000000 | tf_op jit(solution)/shard_map/layer_backward_1/pallas_call | solution.py:60
  113.2 17.2 %all_to_all.51.ret_ref = bf16[32,24,512]{2,1,0:T(8,128)(2,1)S(1)} all-to-all(bf16[32,24,512]{2,1,0:T(8,128)(2,1)S(1)} %get-tuple-element.134), channel_id=1, replica_groups=mesh['layer'=4,'node'=32] {'node'}, dimensions={0} | all-to-all | bytes 1572864 | tf_op jit(solution)/shard_map/all_to_all | solution.py:35
  130.4 0.7 collective-permute-start.8
  131.0 1.7 last_slope.1
  132.9 2.9 %last_spread.1 = (bf16[32,56,512]{2,1,0:T(8,128)(2,1)}, f32[256,512]{1,0:T(8,128)S(1)}, bf16[32,8,512]{2,1,0:T(8,128)(2,1)S(1)}, bf16[2,16,512]{2,1,0:T(8,128)(2,1)}) custom-call(s32[10]{0:T(128)S(1)} %pad_add_fusion.ids, bf16[256,512]{1,0:T(8,128)(2,1)S(1)} %get-tuple-element.145.dpre_ref, ...), custom_call_target="tpu_custom_call" | custom-call | flops 500000000 | bytes 4000000 | tf_op jit(solution)/shard_map/last_spread/pallas_call | solution.py:60
  135.8 1.6 join_rows.1
  137.5 4.1 %all-to-all-start.7 = ((bf16[32,56,512]{2,1,0:T(8,128)(2,1)}), bf16[32,56,512]{2,1,0:T(8,128)(2,1)S(1)}, u32[]{:S(2)}, u32[]{:S(2)}) async-start(bf16[32,56,512]{2,1,0:T(8,128)(2,1)} %get-tuple-element.160), calls=%async_computation.7 | async-start | bytes 3670016 | tf_op jit(solution)/shard_map/all_to_all | solution.py:35
  141.7 2.7 %collective-permute-start.12 = (bf16[256,512]{1,0:T(8,128)(2,1)S(1)}, bf16[256,512]{1,0:T(8,128)(2,1)S(1)}, u32[]{:S(2)}, u32[]{:S(2)}) collective-permute-start(bf16[256,512]{1,0:T(8,128)(2,1)S(1)} %get-tuple-element.187), channel_id=1, source_target_pairs={{0,96},{32,0},{64,32},{96,64},{1,97},{33,1},{65,33},{97,65},{2,98}... | collective-permute-start | bytes 786440 | tf_op jit(solution)/shard_map/ppermute | solution.py:26
  144.4 0.9 collective-permute-start.11
  145.2 0.8 collective-permute-start.10
  146.1 10.0 %collective-permute-done.12.refs_3_ = bf16[256,512]{1,0:T(8,128)(2,1)S(1)} collective-permute-done((bf16[256,512]{1,0:T(8,128)(2,1)S(1)}, bf16[256,512]{1,0:T(8,128)(2,1)S(1)}, u32[]{:S(2)}, u32[]{:S(2)}) %collective-permute-start.12) | collective-permute-done | bytes 262176 | tf_op jit(solution)/shard_map/ppermute | solution.py:26
  156.0 3.7 %collective-permute-done.10.refs_1_ = bf16[256,512]{1,0:T(8,128)(2,1)S(1)} collective-permute-done((bf16[256,512]{1,0:T(8,128)(2,1)S(1)}, bf16[256,512]{1,0:T(8,128)(2,1)S(1)}, u32[]{:S(2)}, u32[]{:S(2)}) %collective-permute-start.10) | collective-permute-done | bytes 262176 | tf_op jit(solution)/shard_map/ppermute | solution.py:26
  159.7 2.5 %put_home.2 = bf16[1,4,256,512]{3,2,1,0:T(8,128)(2,1)} custom-call(s32[10]{0:T(128)S(1)} %pad_add_fusion.ids, bf16[4,256,512]{2,1,0:T(8,128)(2,1)} %get-tuple-element.161.refs_0_, bf16[256,512]{1,0:T(8,128)(2,1)S(1)} %collective-permute-done.10.refs_1_, bf16[256,512]{1,0:T(8,128)(2,1)S(1)} %collective-permute-done.11.refs_2_, ...), custom_call_target="tpu_custom_call" | custom-call | bytes 2000000 | tf_op jit(solution)/shard_map/put_home/pallas_call | solution.py:60
  162.2 5.4 %all-to-all-done.7.ret_ref = bf16[32,56,512]{2,1,0:T(8,128)(2,1)S(1)} async-done(((bf16[32,56,512]{2,1,0:T(8,128)(2,1)}), bf16[32,56,512]{2,1,0:T(8,128)(2,1)S(1)}, u32[]{:S(2)}, u32[]{:S(2)}) %all-to-all-start.7) | async-done | bytes 1835040 | tf_op jit(solution)/shard_map/all_to_all | solution.py:35
  167.7 1.3 sum_chunks.1
  169.0 1.5 collective-permute-start.13
  170.5 2.7 %collective-permute-start.14 = (bf16[2,16,512]{2,1,0:T(8,128)(2,1)S(1)}, bf16[2,16,512]{2,1,0:T(8,128)(2,1)S(1)}, u32[]{:S(2)}, u32[]{:S(2)}) collective-permute-start(bf16[2,16,512]{2,1,0:T(8,128)(2,1)S(1)} %get-tuple-element.170), channel_id=1, source_target_pairs={{0,64},{32,96},{64,0},{96,32},{1,65},{33,97},{65,1},{97,33},{2,66}... | collective-permute-start | bytes 98312 | tf_op jit(solution)/shard_map/ppermute | solution.py:26
  173.1 1.4 collective-permute-start.15
  174.5 2.5 %input_grads.1.refs_0_ = bf16[4,256,512]{2,1,0:T(8,128)(2,1)} custom-call(s32[10]{0:T(128)S(1)} %pad_add_fusion.ids, bf16[32,56,512]{2,1,0:T(8,128)(2,1)S(1)} %all-to-all-done.7.ret_ref, f32[256,512]{1,0:T(8,128)} %get-tuple-element.164.part_in, bf16[256,256]{1,0:T(8,128)(2,1)} %get-tuple-element.165.pick_ref, ...), custom_call_target="tpu_custom_call", output_to_operand_aliasing={{}: (4, {})} | custom-call | flops 100000000 | bytes 1000000 | tf_op jit(solution)/shard_map/input_grads/pallas_call | solution.py:60
  177.1 1.2 slice_bitcast_fusion
  178.3 1.4 sum_over_layer.1
  179.7 3.9 %all-to-all-start.8 = ((bf16[32,16,512]{2,1,0:T(8,128)(2,1)}), bf16[32,16,512]{2,1,0:T(8,128)(2,1)S(1)}, u32[]{:S(2)}, u32[]{:S(2)}) async-start(bf16[32,16,512]{2,1,0:T(8,128)(2,1)} %sum_over_layer.1), calls=%async_computation.8 | async-start | bytes 1048576 | tf_op jit(solution)/shard_map/all_to_all | solution.py:35
  183.6 0.7 collective-permute-start.16
  184.2 2.2 %collective-permute-start.17 = (bf16[256,512]{1,0:T(8,128)(2,1)S(1)}, bf16[256,512]{1,0:T(8,128)(2,1)S(1)}, u32[]{:S(2)}, u32[]{:S(2)}) collective-permute-start(bf16[256,512]{1,0:T(8,128)(2,1)S(1)} %get-tuple-element.176), channel_id=1, source_target_pairs={{0,64},{32,96},{64,0},{96,32},{1,65},{33,97},{65,1},{97,33},{2,66}... | collective-permute-start | bytes 786440 | tf_op jit(solution)/shard_map/ppermute | solution.py:26
  187.0 11.8 %collective-permute-done.16.refs_1_ = bf16[256,512]{1,0:T(8,128)(2,1)S(1)} collective-permute-done((bf16[256,512]{1,0:T(8,128)(2,1)S(1)}, bf16[256,512]{1,0:T(8,128)(2,1)S(1)}, u32[]{:S(2)}, u32[]{:S(2)}) %collective-permute-start.16) | collective-permute-done | bytes 262176 | tf_op jit(solution)/shard_map/ppermute | solution.py:26
  199.5 2.5 %put_home.3 = bf16[1,4,256,512]{3,2,1,0:T(8,128)(2,1)} custom-call(s32[10]{0:T(128)S(1)} %pad_add_fusion.ids, bf16[4,256,512]{2,1,0:T(8,128)(2,1)} %input_grads.1.refs_0_, bf16[256,512]{1,0:T(8,128)(2,1)S(1)} %collective-permute-done.16.refs_1_, bf16[256,512]{1,0:T(8,128)(2,1)S(1)} %collective-permute-done.17.refs_2_, ...), custom_call_target="tpu_custom_call" | custom-call | bytes 2000000 | tf_op jit(solution)/shard_map/put_home/pallas_call | solution.py:60
  202.0 1.9 scale_grads.1
  (37 shorter events, 2.6 us)
Async XLA Ops:
  0.6 31.5 %copy-start = (bf16[1,512,512]{2,1,0:T(8,128)(2,1)S(1)}, bf16[1,512,512]{2,1,0:T(8,128)(2,1)}, u32[]{:S(2)}) copy-start(bf16[1,512,512]{2,1,0:T(8,128)(2,1)} %param.11) | copy-start | bytes 1572868
  0.6 31.5 %copy-start.1 = (bf16[1,512,512]{2,1,0:T(8,128)(2,1)S(1)}, bf16[1,512,512]{2,1,0:T(8,128)(2,1)}, u32[]{:S(2)}) copy-start(bf16[1,512,512]{2,1,0:T(8,128)(2,1)} %param.12) | copy-start | bytes 1572868
  2.0 25.8 %collective-permute-start.2 = (bf16[512,512]{1,0:T(8,128)(2,1)S(1)}, bf16[512,512]{1,0:T(8,128)(2,1)S(1)}, u32[]{:S(2)}, u32[]{:S(2)}) collective-permute-start(bf16[512,512]{1,0:T(8,128)(2,1)S(1)} %broadcast_select_fusion), channel_id=1, source_target_pairs={{0,64},{32,96},{64,0},{96,32},{1,65},{33,97},{65,1},{97,33},{2,66}... | collective-permute-start | bytes 1572872 | tf_op jit(solution)/shard_map/ppermute | solution.py:26
  5.2 23.5 %collective-permute-start.1 = (bf16[512,512]{1,0:T(8,128)(2,1)S(1)}, bf16[512,512]{1,0:T(8,128)(2,1)S(1)}, u32[]{:S(2)}, u32[]{:S(2)}) collective-permute-start(bf16[512,512]{1,0:T(8,128)(2,1)S(1)} %broadcast_select_fusion), channel_id=1, source_target_pairs={{0,96},{32,0},{64,32},{96,64},{1,97},{33,1},{65,33},{97,65},{2,98}... | collective-permute-start | bytes 1572872 | tf_op jit(solution)/shard_map/ppermute | solution.py:26
  6.3 22.4 %collective-permute-start = (bf16[512,512]{1,0:T(8,128)(2,1)S(1)}, bf16[512,512]{1,0:T(8,128)(2,1)S(1)}, u32[]{:S(2)}, u32[]{:S(2)}) collective-permute-start(bf16[512,512]{1,0:T(8,128)(2,1)S(1)} %broadcast_select_fusion), channel_id=1, source_target_pairs={{0,32},{32,64},{64,96},{96,0},{1,33},{33,65},{65,97},{97,1},{2,34}... | collective-permute-start | bytes 1572872 | tf_op jit(solution)/shard_map/ppermute | solution.py:26
  28.7 1.9 collective-permute-start.3
  28.7 2.7 %collective-permute-start.4 = (bf16[512,512]{1,0:T(8,128)(2,1)S(1)}, bf16[512,512]{1,0:T(8,128)(2,1)S(1)}, u32[]{:S(2)}, u32[]{:S(2)}) collective-permute-start(bf16[512,512]{1,0:T(8,128)(2,1)S(1)} %collective-permute-done.1.rest_4_), channel_id=1, source_target_pairs={{0,1},{1,0},{2,3},{3,2},{4,5},{5,4},{6,7},{7,6},{8,9},{9,8},{10,11... | collective-permute-start | bytes 1572872 | tf_op jit(solution)/shard_map/ppermute | solution.py:31
  29.2 2.9 %collective-permute-start.5 = (bf16[512,512]{1,0:T(8,128)(2,1)S(1)}, bf16[512,512]{1,0:T(8,128)(2,1)S(1)}, u32[]{:S(2)}, u32[]{:S(2)}) collective-permute-start(bf16[512,512]{1,0:T(8,128)(2,1)S(1)} %collective-permute-done.2.rest_6_), channel_id=1, source_target_pairs={{0,1},{1,0},{2,3},{3,2},{4,5},{5,4},{6,7},{7,6},{8,9},{9,8},{10,11... | collective-permute-start | bytes 1572872 | tf_op jit(solution)/shard_map/ppermute | solution.py:31
  65.2 14.1 %copy-start.2 = (bf16[512,172]{0,1:T(8,128)(2,1)S(1)}, bf16[512,172]{0,1:T(8,128)(2,1)}, u32[]{:S(2)}) copy-start(bf16[512,172]{0,1:T(8,128)(2,1)} %param.13) | copy-start | bytes 528388
  65.2 14.1 %copy-start.3 = (s32[4,256]{1,0:T(4,128)S(1)}, s32[4,256]{1,0:T(4,128)}, u32[]{:S(2)}) copy-start(s32[4,256]{1,0:T(4,128)} %lab_ref.1) | copy-start | bytes 12292
  65.2 14.1 %copy-start.4 = (s32[4,256]{1,0:T(4,128)S(1)}, s32[4,256]{1,0:T(4,128)}, u32[]{:S(2)}) copy-start(s32[4,256]{1,0:T(4,128)} %mask_ref.1) | copy-start | bytes 12292
  95.4 2.6 %collective-permute-start.6 = (bf16[512,512]{1,0:T(8,128)(2,1)S(1)}, bf16[512,512]{1,0:T(8,128)(2,1)S(1)}, u32[]{:S(2)}, u32[]{:S(2)}) collective-permute-start(bf16[512,512]{1,0:T(8,128)(2,1)S(1)} %get-tuple-element.122), channel_id=1, source_target_pairs={{0,1},{1,0},{2,3},{3,2},{4,5},{5,4},{6,7},{7,6},{8,9},{9,8},{10,11... | collective-permute-start | bytes 1572872 | tf_op jit(solution)/shard_map/ppermute | solution.py:31
  110.3 2.9 %collective-permute-start.7 = (bf16[512,512]{1,0:T(8,128)(2,1)S(1)}, bf16[512,512]{1,0:T(8,128)(2,1)S(1)}, u32[]{:S(2)}, u32[]{:S(2)}) collective-permute-start(bf16[512,512]{1,0:T(8,128)(2,1)S(1)} %get-tuple-element.133), channel_id=1, source_target_pairs={{0,1},{1,0},{2,3},{3,2},{4,5},{5,4},{6,7},{7,6},{8,9},{9,8},{10,11... | collective-permute-start | bytes 1572872 | tf_op jit(solution)/shard_map/ppermute | solution.py:31
  130.4 2.4 %collective-permute-start.8 = (bf16[512,512]{1,0:T(8,128)(2,1)S(1)}, bf16[512,512]{1,0:T(8,128)(2,1)S(1)}, u32[]{:S(2)}, u32[]{:S(2)}) collective-permute-start(bf16[512,512]{1,0:T(8,128)(2,1)S(1)} %get-tuple-element.143), channel_id=1, source_target_pairs={{0,1},{1,0},{2,3},{3,2},{4,5},{5,4},{6,7},{7,6},{8,9},{9,8},{10,11... | collective-permute-start | bytes 1572872 | tf_op jit(solution)/shard_map/ppermute | solution.py:31
  132.8 3.0 %collective-permute-start.9 = (bf16[512,512]{1,0:T(8,128)(2,1)S(1)}, bf16[512,512]{1,0:T(8,128)(2,1)S(1)}, u32[]{:S(2)}, u32[]{:S(2)}) collective-permute-start(bf16[512,512]{1,0:T(8,128)(2,1)S(1)} %get-tuple-element.153), channel_id=1, source_target_pairs={{0,1},{1,0},{2,3},{3,2},{4,5},{5,4},{6,7},{7,6},{8,9},{9,8},{10,11... | collective-permute-start | bytes 1572872 | tf_op jit(solution)/shard_map/ppermute | solution.py:31
  137.5 4.2 %copy-start.5 = (bf16[4,256,512]{2,1,0:T(8,128)(2,1)S(1)}, bf16[4,256,512]{2,1,0:T(8,128)(2,1)}, u32[]{:S(2)}) copy-start(bf16[4,256,512]{2,1,0:T(8,128)(2,1)} %get-tuple-element.161.refs_0_) | copy-start | bytes 3145732
  137.5 30.2 %all-to-all-start.7 = ((bf16[32,56,512]{2,1,0:T(8,128)(2,1)}), bf16[32,56,512]{2,1,0:T(8,128)(2,1)S(1)}, u32[]{:S(2)}, u32[]{:S(2)}) async-start(bf16[32,56,512]{2,1,0:T(8,128)(2,1)} %get-tuple-element.160), calls=%async_computation.7 | async-start | bytes 3670016 | tf_op jit(solution)/shard_map/all_to_all | solution.py:35
  141.7 14.3 %collective-permute-start.12 = (bf16[256,512]{1,0:T(8,128)(2,1)S(1)}, bf16[256,512]{1,0:T(8,128)(2,1)S(1)}, u32[]{:S(2)}, u32[]{:S(2)}) collective-permute-start(bf16[256,512]{1,0:T(8,128)(2,1)S(1)} %get-tuple-element.187), channel_id=1, source_target_pairs={{0,96},{32,0},{64,32},{96,64},{1,97},{33,1},{65,33},{97,65},{2,98}... | collective-permute-start | bytes 786440 | tf_op jit(solution)/shard_map/ppermute | solution.py:26
  144.4 11.7 %collective-permute-start.11 = (bf16[256,512]{1,0:T(8,128)(2,1)S(1)}, bf16[256,512]{1,0:T(8,128)(2,1)S(1)}, u32[]{:S(2)}, u32[]{:S(2)}) collective-permute-start(bf16[256,512]{1,0:T(8,128)(2,1)S(1)} %get-tuple-element.188), channel_id=1, source_target_pairs={{0,64},{32,96},{64,0},{96,32},{1,65},{33,97},{65,1},{97,33},{2,66}... | collective-permute-start | bytes 786440 | tf_op jit(solution)/shard_map/ppermute | solution.py:26
  145.2 14.5 %collective-permute-start.10 = (bf16[256,512]{1,0:T(8,128)(2,1)S(1)}, bf16[256,512]{1,0:T(8,128)(2,1)S(1)}, u32[]{:S(2)}, u32[]{:S(2)}) collective-permute-start(bf16[256,512]{1,0:T(8,128)(2,1)S(1)} %get-tuple-element.189), channel_id=1, source_target_pairs={{0,32},{32,64},{64,96},{96,0},{1,33},{33,65},{65,97},{97,1},{2,34}... | collective-permute-start | bytes 786440 | tf_op jit(solution)/shard_map/ppermute | solution.py:26
  169.0 9.3 %collective-permute-start.13 = (bf16[2,16,512]{2,1,0:T(8,128)(2,1)S(1)}, bf16[2,16,512]{2,1,0:T(8,128)(2,1)S(1)}, u32[]{:S(2)}, u32[]{:S(2)}) collective-permute-start(bf16[2,16,512]{2,1,0:T(8,128)(2,1)S(1)} %get-tuple-element.169), channel_id=1, source_target_pairs={{0,32},{32,64},{64,96},{96,0},{1,33},{33,65},{65,97},{97,1},{2,34}... | collective-permute-start | bytes 98312 | tf_op jit(solution)/shard_map/ppermute | solution.py:26
  170.5 7.8 %collective-permute-start.14 = (bf16[2,16,512]{2,1,0:T(8,128)(2,1)S(1)}, bf16[2,16,512]{2,1,0:T(8,128)(2,1)S(1)}, u32[]{:S(2)}, u32[]{:S(2)}) collective-permute-start(bf16[2,16,512]{2,1,0:T(8,128)(2,1)S(1)} %get-tuple-element.170), channel_id=1, source_target_pairs={{0,64},{32,96},{64,0},{96,32},{1,65},{33,97},{65,1},{97,33},{2,66}... | collective-permute-start | bytes 98312 | tf_op jit(solution)/shard_map/ppermute | solution.py:26
  173.1 5.2 %collective-permute-start.15 = (bf16[2,16,512]{2,1,0:T(8,128)(2,1)S(1)}, bf16[2,16,512]{2,1,0:T(8,128)(2,1)S(1)}, u32[]{:S(2)}, u32[]{:S(2)}) collective-permute-start(bf16[2,16,512]{2,1,0:T(8,128)(2,1)S(1)} %get-tuple-element.171), channel_id=1, source_target_pairs={{0,96},{32,0},{64,32},{96,64},{1,97},{33,1},{65,33},{97,65},{2,98}... | collective-permute-start | bytes 98312 | tf_op jit(solution)/shard_map/ppermute | solution.py:26
  179.7 19.8 %all-to-all-start.8 = ((bf16[32,16,512]{2,1,0:T(8,128)(2,1)}), bf16[32,16,512]{2,1,0:T(8,128)(2,1)S(1)}, u32[]{:S(2)}, u32[]{:S(2)}) async-start(bf16[32,16,512]{2,1,0:T(8,128)(2,1)} %sum_over_layer.1), calls=%async_computation.8 | async-start | bytes 1048576 | tf_op jit(solution)/shard_map/all_to_all | solution.py:35
  183.6 15.3 %collective-permute-start.16 = (bf16[256,512]{1,0:T(8,128)(2,1)S(1)}, bf16[256,512]{1,0:T(8,128)(2,1)S(1)}, u32[]{:S(2)}, u32[]{:S(2)}) collective-permute-start(bf16[256,512]{1,0:T(8,128)(2,1)S(1)} %get-tuple-element.175), channel_id=1, source_target_pairs={{0,32},{32,64},{64,96},{96,0},{1,33},{33,65},{65,97},{97,1},{2,34}... | collective-permute-start | bytes 786440 | tf_op jit(solution)/shard_map/ppermute | solution.py:26
  184.2 14.6 %collective-permute-start.17 = (bf16[256,512]{1,0:T(8,128)(2,1)S(1)}, bf16[256,512]{1,0:T(8,128)(2,1)S(1)}, u32[]{:S(2)}, u32[]{:S(2)}) collective-permute-start(bf16[256,512]{1,0:T(8,128)(2,1)S(1)} %get-tuple-element.176), channel_id=1, source_target_pairs={{0,64},{32,96},{64,0},{96,32},{1,65},{33,97},{65,1},{97,33},{2,66}... | collective-permute-start | bytes 786440 | tf_op jit(solution)/shard_map/ppermute | solution.py:26
  186.5 13.0 %collective-permute-start.18 = (bf16[256,512]{1,0:T(8,128)(2,1)S(1)}, bf16[256,512]{1,0:T(8,128)(2,1)S(1)}, u32[]{:S(2)}, u32[]{:S(2)}) collective-permute-start(bf16[256,512]{1,0:T(8,128)(2,1)S(1)} %get-tuple-element.177), channel_id=1, source_target_pairs={{0,96},{32,0},{64,32},{96,64},{1,97},{33,1},{65,33},{97,65},{2,98}... | collective-permute-start | bytes 786440 | tf_op jit(solution)/shard_map/ppermute | solution.py:26
  199.5 2.5 %collective-permute-start.19 = (bf16[512,512]{1,0:T(8,128)(2,1)S(1)}, bf16[512,512]{1,0:T(8,128)(2,1)S(1)}, u32[]{:S(2)}, u32[]{:S(2)}) collective-permute-start(bf16[512,512]{1,0:T(8,128)(2,1)S(1)} %bitcast.40), channel_id=1, source_target_pairs={{0,1},{1,0},{2,3},{3,2},{4,5},{5,4},{6,7},{7,6},{8,9},{9,8},{10,11... | collective-permute-start | bytes 1572872 | tf_op jit(solution)/shard_map/ppermute | solution.py:31

commit v12 on v11

--- a/solution.py
+++ b/solution.py
@@ -367,13 +367,30 @@
         out_ref[...] = sums[lax.rem(ids[0] + s, 4)]
 
 
-def end_kernel(ids, ret_ref, part_in, pick_ref, buf_in, buf_ref, dout_ref, buf_sem):
+def end_kernel(ids, ret_ref, part_in, pick_ref, buf_in, buf_ref, o_1, o_2, o_3, dout_ref, sems):
     rows, feat = part_in.shape
+    outs = (o_1, o_2, o_3)
+    copies = [
+        pltpu.make_async_copy(buf_in.at[s + 1], out_ref, sems.at[s])
+        for s, out_ref in enumerate(outs)
+    ]
+    for copy in copies:
+        copy.start()
     returned = ret_ref[:, 0 : rows // ret_ref.shape[0], :].reshape(rows, feat)
     dout_ref[...] = (part_in[...] + dot(pick_ref[...], returned)).astype(BF)
-    copy = to_slot(dout_ref, 0, ids, buf_ref, buf_sem)
-    copy.start()
-    copy.wait()
+    for copy in copies:
+        copy.wait()
+    for s, out_ref in enumerate(outs):
+
+        @pl.when(lax.rem(ids[0] + s + 1, 4) == 0)
+        def _():
+            out_ref[...] = dout_ref[...]
+
+    @pl.when(ids[0] == 0)
+    def _():
+        home = pltpu.make_async_copy(dout_ref, buf_ref.at[0], sems.at[3])
+        home.start()
+        home.wait()
 
 
 def layer_sum_kernel(ids, own_ref, a_ref, b_ref, c_ref, out_ref):
@@ -639,7 +656,7 @@
         moved=10**6,
     )
     sums = [shift(v, "layer", s) for s, v in zip(all_shifts, sums)]
-    grads_buf = run(
+    grads_buf, *to_send = run(
         end_kernel,
         "input_grads",
         scalars,
@@ -649,13 +666,13 @@
             (pick_far, whole(pick_far.shape)),
             (grads_buf, FAR),
         ],
-        [stack],
-        [pltpu.VMEM((rows, feat), BF), buf_sem],
+        [stack, act, act, act],
+        [pltpu.VMEM((rows, feat), BF), pltpu.SemaphoreType.DMA((4,))],
         {3: 0},
         flops=10**8,
         moved=10**6,
-    )[0]
-    pieces = tie(*sums, *[grads_buf[s] for s in all_shifts])
+    )
+    pieces = tie(*sums, *to_send)
     sums, to_send = pieces[:3], pieces[3:]
     spread = run(
         layer_sum_kernel,

time: 206 us -> 206 us (level)
  transfers between devices with their start and end apart: 22 -> 22, of which waited for: 9 -> 9; matrix products, arithmetic and copies ran while one was open for 1% -> 0% of each run, Pallas kernels for 10% -> 10%
where the time goes in v12:
time: 206 us; the launch traced here: 204 us
  blocking collectives  101 us (49%)
  Pallas kernels  35.7 us (17%)
  waiting for transfers between devices  35.5 us (17%)
  starting transfers between devices  28.4 us (14%)
    all_to_all x7, blocking collectives, exchange(): lax.all_to_all(value, 'node', split_axis=0, concat_axis=0, tiled=True)  101 us
    pallas_call x16, Pallas kernels, run(): pl.pallas_call(kernel, name=name, grid_spec=pltpu.PrefetchScalarGridSpec(...  35.7 us
    ppermute x12, waiting for transfers between devices, shift(): lax.ppermute(value, axis, [(i, (i + steps) % count) for i in range(count)])  27.1 us
    ppermute x12, starting transfers between devices, shift(): lax.ppermute(value, axis, [(i, (i + steps) % count) for i in range(count)])  18.4 us
    all_to_all x2, starting transfers between devices, exchange(): lax.all_to_all(value, 'node', split_axis=0, concat_axis=0, tiled=True)  8.04 us
    all_to_all x2, waiting for transfers between devices, exchange(): lax.all_to_all(value, 'node', split_axis=0, concat_axis=0, tiled=True)  5.43 us
  transfers between devices with their start and end apart: 22, of which 9 were waited for; matrix products, arithmetic and copies ran while one was open for 0% of the time, Pallas kernels for 10%

profile of v12, /device:TPU:0, one launch (start us, length us, event | category | flops | bytes accessed | tf_op | source)
XLA Modules:
  0.0 203.9 jit_solution(15571183849745469628)
XLA Ops:
  0.7 1.3 broadcast_select_fusion
  2.0 3.2 %collective-permute-start.2 = (bf16[512,512]{1,0:T(8,128)(2,1)S(1)}, bf16[512,512]{1,0:T(8,128)(2,1)S(1)}, u32[]{:S(2)}, u32[]{:S(2)}) collective-permute-start(bf16[512,512]{1,0:T(8,128)(2,1)S(1)} %broadcast_select_fusion), channel_id=1, source_target_pairs={{0,64},{32,96},{64,0},{96,32},{1,65},{33,97},{65,1},{97,33},{2,66}... | collective-permute-start | bytes 1572872 | tf_op jit(solution)/shard_map/ppermute | solution.py:26
  5.2 1.1 collective-permute-start.1
  6.3 0.9 collective-permute-start
  7.2 0.8 reshape.44
  8.1 2.7 %gather_rows.1 = (bf16[256,256]{1,0:T(8,128)(2,1)S(1)}, bf16[256,512]{1,0:T(8,128)(2,1)S(1)}, bf16[256,512]{1,0:T(8,128)(2,1)S(1)}, bf16[2,4,128,128]{3,2,1,0:T(...) custom-call(s32[10]{0:T(128)S(1)} %pad_add_fusion.ids, ...), custom_call_target="tpu_custom_call" | custom-call | flops 100000000 | bytes 1000000 | tf_op jit(solution)/shard_map/gather_rows/pallas_call | solution.py:60
  10.7 17.1 %all_to_all.45 = bf16[32,8,512]{2,1,0:T(8,128)(2,1)S(1)} all-to-all(bf16[32,8,512]{2,1,0:T(8,128)(2,1)S(1)} %bitcast.41), channel_id=1, replica_groups=mesh['layer'=4,'node'=32] {'node'}, dimensions={0} | all-to-all | bytes 524288 | tf_op jit(solution)/shard_map/all_to_all | solution.py:35
  27.8 0.9 collective-permute-done.1.rest_4_
  28.7 0.5 collective-permute-start.4
  29.2 1.4 collective-permute-done.3.rest_3_
  30.6 0.7 collective-permute-done.4.rest_5_
  31.4 0.7 collective-permute-done.5.rest_7_
  32.1 1.9 layer_forward_0.1
  34.0 17.1 %all_to_all.46 = bf16[32,8,512]{2,1,0:T(8,128)(2,1)S(1)} all-to-all(bf16[32,8,512]{2,1,0:T(8,128)(2,1)S(1)} %bitcast.42), channel_id=1, replica_groups=mesh['layer'=4,'node'=32] {'node'}, dimensions={0} | all-to-all | bytes 524288 | tf_op jit(solution)/shard_map/all_to_all | solution.py:35
  51.1 1.7 layer_forward_1.1
  52.8 12.5 %all_to_all.47 = bf16[32,8,512]{2,1,0:T(8,128)(2,1)S(1)} all-to-all(bf16[32,8,512]{2,1,0:T(8,128)(2,1)S(1)} %bitcast.43), channel_id=1, replica_groups=mesh['layer'=4,'node'=32] {'node'}, dimensions={0} | all-to-all | bytes 524288 | tf_op jit(solution)/shard_map/all_to_all | solution.py:35
  65.2 1.7 layer_forward_2.1
  66.9 12.5 %all_to_all.48 = bf16[32,8,512]{2,1,0:T(8,128)(2,1)S(1)} all-to-all(bf16[32,8,512]{2,1,0:T(8,128)(2,1)S(1)} %bitcast.39), channel_id=1, replica_groups=mesh['layer'=4,'node'=32] {'node'}, dimensions={0} | all-to-all | bytes 524288 | tf_op jit(solution)/shard_map/all_to_all | solution.py:35
  79.4 3.5 %top_layer.1 = (bf16[32,8,512]{2,1,0:T(8,128)(2,1)S(1)}, f32[256,512]{1,0:T(8,128)S(1)}, bf16[512,512]{1,0:T(8,128)(2,1)S(1)}, bf16[512,512]{1,0:T(8,128)(2,1)S(1)}, bf16[4,256,512]{2,1,0:T(8,128)(2,1)}) custom-call(s32[10]{0:T(128)S(1)} %pad_add_fusion.ids, bf16[256,512]{1,0:T(8,128)(2,1)S(1)} %get-tuple-element.113.h_ref, ...), custom_call_target="tpu_custom_call", output_to_operand_aliasing={{4}: (9, {})} | custom-call | flops 1000000000 | bytes 5000000 | tf_op jit(solution)/shard_map/top_layer/pallas_call | solution.py:60
  82.9 12.5 %all_to_all.49.ret_ref = bf16[32,8,512]{2,1,0:T(8,128)(2,1)S(1)} all-to-all(bf16[32,8,512]{2,1,0:T(8,128)(2,1)S(1)} %get-tuple-element.118), channel_id=1, replica_groups=mesh['layer'=4,'node'=32] {'node'}, dimensions={0} | all-to-all | bytes 524288 | tf_op jit(solution)/shard_map/all_to_all | solution.py:35
  95.7 2.3 %layer_backward_2.1 = (bf16[32,8,512]{2,1,0:T(8,128)(2,1)S(1)}, f32[256,512]{1,0:T(8,128)S(1)}, bf16[4,256,512]{2,1,0:T(8,128)(2,1)}, bf16[512,512]{1,0:T(8,128)(2,1)S(1)}, bf16[512,512]{1,0:T(8,128)(2,1)S(1)}) custom-call(s32[10]{0:T(128)S(1)} %pad_add_fusion.ids, bf16[32,8,512]{2,1,0:T(8,128)(2,1)S(1)} %all_to_all.49.ret_ref, ...), custom_call_target="tpu_custom_call" | custom-call | flops 1000000000 | bytes 5000000 | tf_op jit(solution)/shard_map/layer_backward_2/pallas_call | solution.py:60
  98.0 12.3 %all_to_all.50.ret_ref = bf16[32,8,512]{2,1,0:T(8,128)(2,1)S(1)} all-to-all(bf16[32,8,512]{2,1,0:T(8,128)(2,1)S(1)} %get-tuple-element.127), channel_id=1, replica_groups=mesh['layer'=4,'node'=32] {'node'}, dimensions={0} | all-to-all | bytes 524288 | tf_op jit(solution)/shard_map/all_to_all | solution.py:35
  110.6 2.6 %layer_backward_1.1 = (bf16[32,24,512]{2,1,0:T(8,128)(2,1)S(1)}, f32[256,512]{1,0:T(8,128)S(1)}, bf16[4,256,512]{2,1,0:T(8,128)(2,1)}, bf16[512,512]{1,0:T(8,128)(2,1)S(1)}, bf16[512,512]{1,0:T(8,128)(2,1)S(1)}) custom-call(s32[10]{0:T(128)S(1)} %pad_add_fusion.ids, bf16[32,8,512]{2,1,0:T(8,128)(2,1)S(1)} %all_to_all.50.ret_ref, ...), custom_call_target="tpu_custom_call", output_to_operand_aliasing={{2}: (11, {})} | custom-call | flops 1000000000 | bytes 5000000 | tf_op jit(solution)/shard_map/layer_backward_1/pallas_call | solution.py:60
  113.2 17.2 %all_to_all.51.ret_ref = bf16[32,24,512]{2,1,0:T(8,128)(2,1)S(1)} all-to-all(bf16[32,24,512]{2,1,0:T(8,128)(2,1)S(1)} %get-tuple-element.138), channel_id=1, replica_groups=mesh['layer'=4,'node'=32] {'node'}, dimensions={0} | all-to-all | bytes 1572864 | tf_op jit(solution)/shard_map/all_to_all | solution.py:35
  130.4 0.7 collective-permute-start.8
  131.0 1.7 last_slope.1
  132.9 2.9 %last_spread.1 = (bf16[32,56,512]{2,1,0:T(8,128)(2,1)}, f32[256,512]{1,0:T(8,128)S(1)}, bf16[32,8,512]{2,1,0:T(8,128)(2,1)S(1)}, bf16[2,16,512]{2,1,0:T(8,128)(2,1)}) custom-call(s32[10]{0:T(128)S(1)} %pad_add_fusion.ids, bf16[256,512]{1,0:T(8,128)(2,1)S(1)} %get-tuple-element.149.dpre_ref, ...), custom_call_target="tpu_custom_call" | custom-call | flops 500000000 | bytes 4000000 | tf_op jit(solution)/shard_map/last_spread/pallas_call | solution.py:60
  135.8 1.6 join_rows.1
  137.5 4.1 %all-to-all-start.7 = ((bf16[32,56,512]{2,1,0:T(8,128)(2,1)}), bf16[32,56,512]{2,1,0:T(8,128)(2,1)S(1)}, u32[]{:S(2)}, u32[]{:S(2)}) async-start(bf16[32,56,512]{2,1,0:T(8,128)(2,1)} %get-tuple-element.164), calls=%async_computation.7 | async-start | bytes 3670016 | tf_op jit(solution)/shard_map/all_to_all | solution.py:35
  141.7 2.7 %collective-permute-start.12 = (bf16[256,512]{1,0:T(8,128)(2,1)S(1)}, bf16[256,512]{1,0:T(8,128)(2,1)S(1)}, u32[]{:S(2)}, u32[]{:S(2)}) collective-permute-start(bf16[256,512]{1,0:T(8,128)(2,1)S(1)} %get-tuple-element.192), channel_id=1, source_target_pairs={{0,96},{32,0},{64,32},{96,64},{1,97},{33,1},{65,33},{97,65},{2,98}... | collective-permute-start | bytes 786440 | tf_op jit(solution)/shard_map/ppermute | solution.py:26
  144.4 0.9 collective-permute-start.11
  145.2 0.8 collective-permute-start.10
  146.1 10.0 %collective-permute-done.12.refs_3_ = bf16[256,512]{1,0:T(8,128)(2,1)S(1)} collective-permute-done((bf16[256,512]{1,0:T(8,128)(2,1)S(1)}, bf16[256,512]{1,0:T(8,128)(2,1)S(1)}, u32[]{:S(2)}, u32[]{:S(2)}) %collective-permute-start.12) | collective-permute-done | bytes 262176 | tf_op jit(solution)/shard_map/ppermute | solution.py:26
  156.0 3.7 %collective-permute-done.10.refs_1_ = bf16[256,512]{1,0:T(8,128)(2,1)S(1)} collective-permute-done((bf16[256,512]{1,0:T(8,128)(2,1)S(1)}, bf16[256,512]{1,0:T(8,128)(2,1)S(1)}, u32[]{:S(2)}, u32[]{:S(2)}) %collective-permute-start.10) | collective-permute-done | bytes 262176 | tf_op jit(solution)/shard_map/ppermute | solution.py:26
  159.7 2.5 %put_home.2 = bf16[1,4,256,512]{3,2,1,0:T(8,128)(2,1)} custom-call(s32[10]{0:T(128)S(1)} %pad_add_fusion.ids, bf16[4,256,512]{2,1,0:T(8,128)(2,1)} %get-tuple-element.165.refs_0_, bf16[256,512]{1,0:T(8,128)(2,1)S(1)} %collective-permute-done.10.refs_1_, bf16[256,512]{1,0:T(8,128)(2,1)S(1)} %collective-permute-done.11.refs_2_, ...), custom_call_target="tpu_custom_call" | custom-call | bytes 2000000 | tf_op jit(solution)/shard_map/put_home/pallas_call | solution.py:60
  162.2 5.4 %all-to-all-done.7.ret_ref = bf16[32,56,512]{2,1,0:T(8,128)(2,1)S(1)} async-done(((bf16[32,56,512]{2,1,0:T(8,128)(2,1)}), bf16[32,56,512]{2,1,0:T(8,128)(2,1)S(1)}, u32[]{:S(2)}, u32[]{:S(2)}) %all-to-all-start.7) | async-done | bytes 1835040 | tf_op jit(solution)/shard_map/all_to_all | solution.py:35
  167.7 1.3 sum_chunks.1
  169.0 1.5 collective-permute-start.13
  170.5 2.7 %collective-permute-start.14 = (bf16[2,16,512]{2,1,0:T(8,128)(2,1)S(1)}, bf16[2,16,512]{2,1,0:T(8,128)(2,1)S(1)}, u32[]{:S(2)}, u32[]{:S(2)}) collective-permute-start(bf16[2,16,512]{2,1,0:T(8,128)(2,1)S(1)} %get-tuple-element.175), channel_id=1, source_target_pairs={{0,64},{32,96},{64,0},{96,32},{1,65},{33,97},{65,1},{97,33},{2,66}... | collective-permute-start | bytes 98312 | tf_op jit(solution)/shard_map/ppermute | solution.py:26
  173.1 1.4 collective-permute-start.15
  174.5 3.5 %input_grads.1 = (bf16[4,256,512]{2,1,0:T(8,128)(2,1)}, bf16[256,512]{1,0:T(8,128)(2,1)S(1)}, bf16[256,512]{1,0:T(8,128)(2,1)S(1)}, bf16[256,512]{1,0:T(8,128)(2,1)S(1)}) custom-call(s32[10]{0:T(128)S(1)} %pad_add_fusion.ids, bf16[32,56,512]{2,1,0:T(8,128)(2,1)S(1)} %all-to-all-done.7.ret_ref, ...), custom_call_target="tpu_custom_call", output_to_operand_aliasing={{0}: (4, {})} | custom-call | flops 100000000 | bytes 1000000 | tf_op jit(solution)/shard_map/input_grads/pallas_call | solution.py:60
  178.0 1.4 sum_over_layer.1
  179.4 3.9 %all-to-all-start.8 = ((bf16[32,16,512]{2,1,0:T(8,128)(2,1)}), bf16[32,16,512]{2,1,0:T(8,128)(2,1)S(1)}, u32[]{:S(2)}, u32[]{:S(2)}) async-start(bf16[32,16,512]{2,1,0:T(8,128)(2,1)} %sum_over_layer.1), calls=%async_computation.8 | async-start | bytes 1048576 | tf_op jit(solution)/shard_map/all_to_all | solution.py:35
  183.4 3.1 %collective-permute-start.17 = (bf16[256,512]{1,0:T(8,128)(2,1)S(1)}, bf16[256,512]{1,0:T(8,128)(2,1)S(1)}, u32[]{:S(2)}, u32[]{:S(2)}) collective-permute-start(bf16[256,512]{1,0:T(8,128)(2,1)S(1)} %get-tuple-element.184), channel_id=1, source_target_pairs={{0,64},{32,96},{64,0},{96,32},{1,65},{33,97},{65,1},{97,33},{2,66}... | collective-permute-start | bytes 786440 | tf_op jit(solution)/shard_map/ppermute | solution.py:26
  186.7 12.0 %collective-permute-done.16.refs_1_ = bf16[256,512]{1,0:T(8,128)(2,1)S(1)} collective-permute-done((bf16[256,512]{1,0:T(8,128)(2,1)S(1)}, bf16[256,512]{1,0:T(8,128)(2,1)S(1)}, u32[]{:S(2)}, u32[]{:S(2)}) %collective-permute-start.16) | collective-permute-done | bytes 262176 | tf_op jit(solution)/shard_map/ppermute | solution.py:26
  198.6 0.6 collective-permute-done.18.refs_3_
  199.2 2.5 %put_home.3 = bf16[1,4,256,512]{3,2,1,0:T(8,128)(2,1)} custom-call(s32[10]{0:T(128)S(1)} %pad_add_fusion.ids, bf16[4,256,512]{2,1,0:T(8,128)(2,1)} %get-tuple-element.171.refs_0_, bf16[256,512]{1,0:T(8,128)(2,1)S(1)} %collective-permute-done.16.refs_1_, bf16[256,512]{1,0:T(8,128)(2,1)S(1)} %collective-permute-done.17.refs_2_, ...), custom_call_target="tpu_custom_call" | custom-call | bytes 2000000 | tf_op jit(solution)/shard_map/put_home/pallas_call | solution.py:60
  201.8 1.9 scale_grads.1
  (36 shorter events, 1.2 us)
Async XLA Ops:
  0.6 31.5 %copy-start = (bf16[1,512,512]{2,1,0:T(8,128)(2,1)S(1)}, bf16[1,512,512]{2,1,0:T(8,128)(2,1)}, u32[]{:S(2)}) copy-start(bf16[1,512,512]{2,1,0:T(8,128)(2,1)} %param.11) | copy-start | bytes 1572868
  0.6 31.5 %copy-start.1 = (bf16[1,512,512]{2,1,0:T(8,128)(2,1)S(1)}, bf16[1,512,512]{2,1,0:T(8,128)(2,1)}, u32[]{:S(2)}) copy-start(bf16[1,512,512]{2,1,0:T(8,128)(2,1)} %param.12) | copy-start | bytes 1572868
  2.0 25.8 %collective-permute-start.2 = (bf16[512,512]{1,0:T(8,128)(2,1)S(1)}, bf16[512,512]{1,0:T(8,128)(2,1)S(1)}, u32[]{:S(2)}, u32[]{:S(2)}) collective-permute-start(bf16[512,512]{1,0:T(8,128)(2,1)S(1)} %broadcast_select_fusion), channel_id=1, source_target_pairs={{0,64},{32,96},{64,0},{96,32},{1,65},{33,97},{65,1},{97,33},{2,66}... | collective-permute-start | bytes 1572872 | tf_op jit(solution)/shard_map/ppermute | solution.py:26
  5.2 23.5 %collective-permute-start.1 = (bf16[512,512]{1,0:T(8,128)(2,1)S(1)}, bf16[512,512]{1,0:T(8,128)(2,1)S(1)}, u32[]{:S(2)}, u32[]{:S(2)}) collective-permute-start(bf16[512,512]{1,0:T(8,128)(2,1)S(1)} %broadcast_select_fusion), channel_id=1, source_target_pairs={{0,96},{32,0},{64,32},{96,64},{1,97},{33,1},{65,33},{97,65},{2,98}... | collective-permute-start | bytes 1572872 | tf_op jit(solution)/shard_map/ppermute | solution.py:26
  6.3 22.4 %collective-permute-start = (bf16[512,512]{1,0:T(8,128)(2,1)S(1)}, bf16[512,512]{1,0:T(8,128)(2,1)S(1)}, u32[]{:S(2)}, u32[]{:S(2)}) collective-permute-start(bf16[512,512]{1,0:T(8,128)(2,1)S(1)} %broadcast_select_fusion), channel_id=1, source_target_pairs={{0,32},{32,64},{64,96},{96,0},{1,33},{33,65},{65,97},{97,1},{2,34}... | collective-permute-start | bytes 1572872 | tf_op jit(solution)/shard_map/ppermute | solution.py:26
  28.7 1.9 collective-permute-start.3
  28.7 2.7 %collective-permute-start.4 = (bf16[512,512]{1,0:T(8,128)(2,1)S(1)}, bf16[512,512]{1,0:T(8,128)(2,1)S(1)}, u32[]{:S(2)}, u32[]{:S(2)}) collective-permute-start(bf16[512,512]{1,0:T(8,128)(2,1)S(1)} %collective-permute-done.1.rest_4_), channel_id=1, source_target_pairs={{0,1},{1,0},{2,3},{3,2},{4,5},{5,4},{6,7},{7,6},{8,9},{9,8},{10,11... | collective-permute-start | bytes 1572872 | tf_op jit(solution)/shard_map/ppermute | solution.py:31
  29.2 2.9 %collective-permute-start.5 = (bf16[512,512]{1,0:T(8,128)(2,1)S(1)}, bf16[512,512]{1,0:T(8,128)(2,1)S(1)}, u32[]{:S(2)}, u32[]{:S(2)}) collective-permute-start(bf16[512,512]{1,0:T(8,128)(2,1)S(1)} %collective-permute-done.2.rest_6_), channel_id=1, source_target_pairs={{0,1},{1,0},{2,3},{3,2},{4,5},{5,4},{6,7},{7,6},{8,9},{9,8},{10,11... | collective-permute-start | bytes 1572872 | tf_op jit(solution)/shard_map/ppermute | solution.py:31
  65.2 14.1 %copy-start.2 = (bf16[512,172]{0,1:T(8,128)(2,1)S(1)}, bf16[512,172]{0,1:T(8,128)(2,1)}, u32[]{:S(2)}) copy-start(bf16[512,172]{0,1:T(8,128)(2,1)} %param.13) | copy-start | bytes 528388
  65.2 14.1 %copy-start.3 = (s32[4,256]{1,0:T(4,128)S(1)}, s32[4,256]{1,0:T(4,128)}, u32[]{:S(2)}) copy-start(s32[4,256]{1,0:T(4,128)} %lab_ref.1) | copy-start | bytes 12292
  65.2 14.1 %copy-start.4 = (s32[4,256]{1,0:T(4,128)S(1)}, s32[4,256]{1,0:T(4,128)}, u32[]{:S(2)}) copy-start(s32[4,256]{1,0:T(4,128)} %mask_ref.1) | copy-start | bytes 12292
  95.4 2.6 %collective-permute-start.6 = (bf16[512,512]{1,0:T(8,128)(2,1)S(1)}, bf16[512,512]{1,0:T(8,128)(2,1)S(1)}, u32[]{:S(2)}, u32[]{:S(2)}) collective-permute-start(bf16[512,512]{1,0:T(8,128)(2,1)S(1)} %get-tuple-element.126), channel_id=1, source_target_pairs={{0,1},{1,0},{2,3},{3,2},{4,5},{5,4},{6,7},{7,6},{8,9},{9,8},{10,11... | collective-permute-start | bytes 1572872 | tf_op jit(solution)/shard_map/ppermute | solution.py:31
  110.3 2.9 %collective-permute-start.7 = (bf16[512,512]{1,0:T(8,128)(2,1)S(1)}, bf16[512,512]{1,0:T(8,128)(2,1)S(1)}, u32[]{:S(2)}, u32[]{:S(2)}) collective-permute-start(bf16[512,512]{1,0:T(8,128)(2,1)S(1)} %get-tuple-element.137), channel_id=1, source_target_pairs={{0,1},{1,0},{2,3},{3,2},{4,5},{5,4},{6,7},{7,6},{8,9},{9,8},{10,11... | collective-permute-start | bytes 1572872 | tf_op jit(solution)/shard_map/ppermute | solution.py:31
  130.4 2.4 %collective-permute-start.8 = (bf16[512,512]{1,0:T(8,128)(2,1)S(1)}, bf16[512,512]{1,0:T(8,128)(2,1)S(1)}, u32[]{:S(2)}, u32[]{:S(2)}) collective-permute-start(bf16[512,512]{1,0:T(8,128)(2,1)S(1)} %get-tuple-element.147), channel_id=1, source_target_pairs={{0,1},{1,0},{2,3},{3,2},{4,5},{5,4},{6,7},{7,6},{8,9},{9,8},{10,11... | collective-permute-start | bytes 1572872 | tf_op jit(solution)/shard_map/ppermute | solution.py:31
  132.8 3.0 %collective-permute-start.9 = (bf16[512,512]{1,0:T(8,128)(2,1)S(1)}, bf16[512,512]{1,0:T(8,128)(2,1)S(1)}, u32[]{:S(2)}, u32[]{:S(2)}) collective-permute-start(bf16[512,512]{1,0:T(8,128)(2,1)S(1)} %get-tuple-element.157), channel_id=1, source_target_pairs={{0,1},{1,0},{2,3},{3,2},{4,5},{5,4},{6,7},{7,6},{8,9},{9,8},{10,11... | collective-permute-start | bytes 1572872 | tf_op jit(solution)/shard_map/ppermute | solution.py:31
  137.5 4.2 %copy-start.5 = (bf16[4,256,512]{2,1,0:T(8,128)(2,1)S(1)}, bf16[4,256,512]{2,1,0:T(8,128)(2,1)}, u32[]{:S(2)}) copy-start(bf16[4,256,512]{2,1,0:T(8,128)(2,1)} %get-tuple-element.165.refs_0_) | copy-start | bytes 3145732
  137.5 30.2 %all-to-all-start.7 = ((bf16[32,56,512]{2,1,0:T(8,128)(2,1)}), bf16[32,56,512]{2,1,0:T(8,128)(2,1)S(1)}, u32[]{:S(2)}, u32[]{:S(2)}) async-start(bf16[32,56,512]{2,1,0:T(8,128)(2,1)} %get-tuple-element.164), calls=%async_computation.7 | async-start | bytes 3670016 | tf_op jit(solution)/shard_map/all_to_all | solution.py:35
  141.7 14.3 %collective-permute-start.12 = (bf16[256,512]{1,0:T(8,128)(2,1)S(1)}, bf16[256,512]{1,0:T(8,128)(2,1)S(1)}, u32[]{:S(2)}, u32[]{:S(2)}) collective-permute-start(bf16[256,512]{1,0:T(8,128)(2,1)S(1)} %get-tuple-element.192), channel_id=1, source_target_pairs={{0,96},{32,0},{64,32},{96,64},{1,97},{33,1},{65,33},{97,65},{2,98}... | collective-permute-start | bytes 786440 | tf_op jit(solution)/shard_map/ppermute | solution.py:26
  144.4 11.7 %collective-permute-start.11 = (bf16[256,512]{1,0:T(8,128)(2,1)S(1)}, bf16[256,512]{1,0:T(8,128)(2,1)S(1)}, u32[]{:S(2)}, u32[]{:S(2)}) collective-permute-start(bf16[256,512]{1,0:T(8,128)(2,1)S(1)} %get-tuple-element.193), channel_id=1, source_target_pairs={{0,64},{32,96},{64,0},{96,32},{1,65},{33,97},{65,1},{97,33},{2,66}... | collective-permute-start | bytes 786440 | tf_op jit(solution)/shard_map/ppermute | solution.py:26
  145.2 14.5 %collective-permute-start.10 = (bf16[256,512]{1,0:T(8,128)(2,1)S(1)}, bf16[256,512]{1,0:T(8,128)(2,1)S(1)}, u32[]{:S(2)}, u32[]{:S(2)}) collective-permute-start(bf16[256,512]{1,0:T(8,128)(2,1)S(1)} %get-tuple-element.194), channel_id=1, source_target_pairs={{0,32},{32,64},{64,96},{96,0},{1,33},{33,65},{65,97},{97,1},{2,34}... | collective-permute-start | bytes 786440 | tf_op jit(solution)/shard_map/ppermute | solution.py:26
  169.0 9.0 %collective-permute-start.13 = (bf16[2,16,512]{2,1,0:T(8,128)(2,1)S(1)}, bf16[2,16,512]{2,1,0:T(8,128)(2,1)S(1)}, u32[]{:S(2)}, u32[]{:S(2)}) collective-permute-start(bf16[2,16,512]{2,1,0:T(8,128)(2,1)S(1)} %get-tuple-element.174), channel_id=1, source_target_pairs={{0,32},{32,64},{64,96},{96,0},{1,33},{33,65},{65,97},{97,1},{2,34}... | collective-permute-start | bytes 98312 | tf_op jit(solution)/shard_map/ppermute | solution.py:26
  170.5 7.6 %collective-permute-start.14 = (bf16[2,16,512]{2,1,0:T(8,128)(2,1)S(1)}, bf16[2,16,512]{2,1,0:T(8,128)(2,1)S(1)}, u32[]{:S(2)}, u32[]{:S(2)}) collective-permute-start(bf16[2,16,512]{2,1,0:T(8,128)(2,1)S(1)} %get-tuple-element.175), channel_id=1, source_target_pairs={{0,64},{32,96},{64,0},{96,32},{1,65},{33,97},{65,1},{97,33},{2,66}... | collective-permute-start | bytes 98312 | tf_op jit(solution)/shard_map/ppermute | solution.py:26
  173.1 4.9 %collective-permute-start.15 = (bf16[2,16,512]{2,1,0:T(8,128)(2,1)S(1)}, bf16[2,16,512]{2,1,0:T(8,128)(2,1)S(1)}, u32[]{:S(2)}, u32[]{:S(2)}) collective-permute-start(bf16[2,16,512]{2,1,0:T(8,128)(2,1)S(1)} %get-tuple-element.176), channel_id=1, source_target_pairs={{0,96},{32,0},{64,32},{96,64},{1,97},{33,1},{65,33},{97,65},{2,98}... | collective-permute-start | bytes 98312 | tf_op jit(solution)/shard_map/ppermute | solution.py:26
  179.4 19.8 %all-to-all-start.8 = ((bf16[32,16,512]{2,1,0:T(8,128)(2,1)}), bf16[32,16,512]{2,1,0:T(8,128)(2,1)S(1)}, u32[]{:S(2)}, u32[]{:S(2)}) async-start(bf16[32,16,512]{2,1,0:T(8,128)(2,1)} %sum_over_layer.1), calls=%async_computation.8 | async-start | bytes 1048576 | tf_op jit(solution)/shard_map/all_to_all | solution.py:35
  183.3 15.3 %collective-permute-start.16 = (bf16[256,512]{1,0:T(8,128)(2,1)S(1)}, bf16[256,512]{1,0:T(8,128)(2,1)S(1)}, u32[]{:S(2)}, u32[]{:S(2)}) collective-permute-start(bf16[256,512]{1,0:T(8,128)(2,1)S(1)} %get-tuple-element.183), channel_id=1, source_target_pairs={{0,32},{32,64},{64,96},{96,0},{1,33},{33,65},{65,97},{97,1},{2,34}... | collective-permute-start | bytes 786440 | tf_op jit(solution)/shard_map/ppermute | solution.py:26
  183.4 15.2 %collective-permute-start.17 = (bf16[256,512]{1,0:T(8,128)(2,1)S(1)}, bf16[256,512]{1,0:T(8,128)(2,1)S(1)}, u32[]{:S(2)}, u32[]{:S(2)}) collective-permute-start(bf16[256,512]{1,0:T(8,128)(2,1)S(1)} %get-tuple-element.184), channel_id=1, source_target_pairs={{0,64},{32,96},{64,0},{96,32},{1,65},{33,97},{65,1},{97,33},{2,66}... | collective-permute-start | bytes 786440 | tf_op jit(solution)/shard_map/ppermute | solution.py:26
  186.5 12.7 %collective-permute-start.18 = (bf16[256,512]{1,0:T(8,128)(2,1)S(1)}, bf16[256,512]{1,0:T(8,128)(2,1)S(1)}, u32[]{:S(2)}, u32[]{:S(2)}) collective-permute-start(bf16[256,512]{1,0:T(8,128)(2,1)S(1)} %get-tuple-element.185), channel_id=1, source_target_pairs={{0,96},{32,0},{64,32},{96,64},{1,97},{33,1},{65,33},{97,65},{2,98}... | collective-permute-start | bytes 786440 | tf_op jit(solution)/shard_map/ppermute | solution.py:26
  199.2 2.5 %collective-permute-start.19 = (bf16[512,512]{1,0:T(8,128)(2,1)S(1)}, bf16[512,512]{1,0:T(8,128)(2,1)S(1)}, u32[]{:S(2)}, u32[]{:S(2)}) collective-permute-start(bf16[512,512]{1,0:T(8,128)(2,1)S(1)} %bitcast.34), channel_id=1, source_target_pairs={{0,1},{1,0},{2,3},{3,2},{4,5},{5,4},{6,7},{7,6},{8,9},{9,8},{10,11... | collective-permute-start | bytes 1572872 | tf_op jit(solution)/shard_map/ppermute | solution.py:31

commit v13 on v12

--- a/solution.py
+++ b/solution.py
@@ -378,6 +378,12 @@
         copy.start()
     returned = ret_ref[:, 0 : rows // ret_ref.shape[0], :].reshape(rows, feat)
     dout_ref[...] = (part_in[...] + dot(pick_ref[...], returned)).astype(BF)
+    home = pltpu.make_async_copy(dout_ref, buf_ref.at[0], sems.at[3])
+
+    @pl.when(ids[0] == 0)
+    def _():
+        home.start()
+
     for copy in copies:
         copy.wait()
     for s, out_ref in enumerate(outs):
@@ -388,8 +394,6 @@
 
     @pl.when(ids[0] == 0)
     def _():
-        home = pltpu.make_async_copy(dout_ref, buf_ref.at[0], sems.at[3])
-        home.start()
         home.wait()
 
 
@@ -422,10 +426,19 @@
             pltpu.make_async_copy(value.at[rows], self_ref.at[0, rows], sems.at[sem, step]).wait()
 
 
-def home_kernel(ids, *refs):
-    pieces, out_ref = refs[:-1], refs[-1]
-    for s, piece in enumerate(pieces):
-        out_ref[0, lax.rem(ids[0] + 4 - s, 4)] = piece[...]
+def home_kernel(ids, own_ref, a_ref, b_ref, c_ref, out_ref, own, sems):
+    load = pltpu.make_async_copy(own_ref.at[0], own, sems.at[4])
+    load.start()
+    copies = [
+        pltpu.make_async_copy(piece, out_ref.at[0, lax.rem(ids[0] + 4 - s, 4)], sems.at[s])
+        for s, piece in enumerate((own, a_ref, b_ref, c_ref))
+    ]
+    for copy in copies[1:]:
+        copy.start()
+    load.wait()
+    copies[0].start()
+    for copy in copies:
+        copy.wait()
 
 
 def body(
@@ -558,8 +571,9 @@
             home_kernel,
             "put_home",
             scalars,
-            [(buf, first_block), *pieces],
-            [far_block(shape)],
+            [(buf, FAR), *pieces],
+            [(pltpu.HBM(shape, BF), FAR)],
+            [pltpu.VMEM((rows, feat), BF), pltpu.SemaphoreType.DMA((5,))],
             moved=2 * 10**6,
         )[0]
 

time: 206 us -> 205 us (level)
  transfers between devices with their start and end apart: 22 -> 22, of which waited for: 9 -> 10; matrix products, arithmetic and copies ran while one was open for 0% -> 0% of each run, Pallas kernels for 10% -> 10%
where the time goes in v13:
time: 205 us; the launch traced here: 203 us
  blocking collectives  101 us (49%)
  waiting for transfers between devices  35 us (17%)
  Pallas kernels  34.7 us (17%)
  starting transfers between devices  29 us (14%)
    all_to_all x7, blocking collectives, exchange(): lax.all_to_all(value, 'node', split_axis=0, concat_axis=0, tiled=True)  101 us
    pallas_call x16, Pallas kernels, run(): pl.pallas_call(kernel, name=name, grid_spec=pltpu.PrefetchScalarGridSpec(...  34.7 us
    ppermute x12, waiting for transfers between devices, shift(): lax.ppermute(value, axis, [(i, (i + steps) % count) for i in range(count)])  26.6 us
    ppermute x12, starting transfers between devices, shift(): lax.ppermute(value, axis, [(i, (i + steps) % count) for i in range(count)])  19 us
    all_to_all x2, starting transfers between devices, exchange(): lax.all_to_all(value, 'node', split_axis=0, concat_axis=0, tiled=True)  8.04 us
    all_to_all x2, waiting for transfers between devices, exchange(): lax.all_to_all(value, 'node', split_axis=0, concat_axis=0, tiled=True)  5.58 us
  transfers between devices with their start and end apart: 22, of which 10 were waited for; matrix products, arithmetic and copies ran while one was open for 0% of the time, Pallas kernels for 10%

profile of v13, /device:TPU:0, one launch (start us, length us, event | category | flops | bytes accessed | tf_op | source)
XLA Modules:
  0.0 203.0 jit_solution(1409249287599937121)
XLA Ops:
  0.7 1.3 broadcast_select_fusion
  2.0 3.2 %collective-permute-start.2 = (bf16[512,512]{1,0:T(8,128)(2,1)S(1)}, bf16[512,512]{1,0:T(8,128)(2,1)S(1)}, u32[]{:S(2)}, u32[]{:S(2)}) collective-permute-start(bf16[512,512]{1,0:T(8,128)(2,1)S(1)} %broadcast_select_fusion), channel_id=1, source_target_pairs={{0,64},{32,96},{64,0},{96,32},{1,65},{33,97},{65,1},{97,33},{2,66}... | collective-permute-start | bytes 1572872 | tf_op jit(solution)/shard_map/ppermute | solution.py:26
  5.2 1.1 collective-permute-start.1
  6.3 0.9 collective-permute-start
  7.2 0.8 reshape.44
  8.1 2.7 %gather_rows.1 = (bf16[256,256]{1,0:T(8,128)(2,1)S(1)}, bf16[256,512]{1,0:T(8,128)(2,1)S(1)}, bf16[256,512]{1,0:T(8,128)(2,1)S(1)}, bf16[2,4,128,128]{3,2,1,0:T(...) custom-call(s32[10]{0:T(128)S(1)} %pad_add_fusion.ids, ...), custom_call_target="tpu_custom_call" | custom-call | flops 100000000 | bytes 1000000 | tf_op jit(solution)/shard_map/gather_rows/pallas_call | solution.py:60
  10.7 17.1 %all_to_all.45 = bf16[32,8,512]{2,1,0:T(8,128)(2,1)S(1)} all-to-all(bf16[32,8,512]{2,1,0:T(8,128)(2,1)S(1)} %bitcast.41), channel_id=1, replica_groups=mesh['layer'=4,'node'=32] {'node'}, dimensions={0} | all-to-all | bytes 524288 | tf_op jit(solution)/shard_map/all_to_all | solution.py:35
  27.8 0.9 collective-permute-done.1.rest_4_
  29.2 1.4 collective-permute-done.3.rest_3_
  30.6 0.7 collective-permute-done.4.rest_5_
  31.4 0.7 collective-permute-done.5.rest_7_
  32.1 1.9 layer_forward_0.1
  34.0 17.1 %all_to_all.46 = bf16[32,8,512]{2,1,0:T(8,128)(2,1)S(1)} all-to-all(bf16[32,8,512]{2,1,0:T(8,128)(2,1)S(1)} %bitcast.42), channel_id=1, replica_groups=mesh['layer'=4,'node'=32] {'node'}, dimensions={0} | all-to-all | bytes 524288 | tf_op jit(solution)/shard_map/all_to_all | solution.py:35
  51.1 1.7 layer_forward_1.1
  52.8 12.5 %all_to_all.47 = bf16[32,8,512]{2,1,0:T(8,128)(2,1)S(1)} all-to-all(bf16[32,8,512]{2,1,0:T(8,128)(2,1)S(1)} %bitcast.43), channel_id=1, replica_groups=mesh['layer'=4,'node'=32] {'node'}, dimensions={0} | all-to-all | bytes 524288 | tf_op jit(solution)/shard_map/all_to_all | solution.py:35
  65.2 1.7 layer_forward_2.1
  66.9 12.5 %all_to_all.48 = bf16[32,8,512]{2,1,0:T(8,128)(2,1)S(1)} all-to-all(bf16[32,8,512]{2,1,0:T(8,128)(2,1)S(1)} %bitcast.39), channel_id=1, replica_groups=mesh['layer'=4,'node'=32] {'node'}, dimensions={0} | all-to-all | bytes 524288 | tf_op jit(solution)/shard_map/all_to_all | solution.py:35
  79.4 3.5 %top_layer.1 = (bf16[32,8,512]{2,1,0:T(8,128)(2,1)S(1)}, f32[256,512]{1,0:T(8,128)S(1)}, bf16[512,512]{1,0:T(8,128)(2,1)S(1)}, bf16[512,512]{1,0:T(8,128)(2,1)S(1)}, bf16[4,256,512]{2,1,0:T(8,128)(2,1)}) custom-call(s32[10]{0:T(128)S(1)} %pad_add_fusion.ids, bf16[256,512]{1,0:T(8,128)(2,1)S(1)} %get-tuple-element.113.h_ref, ...), custom_call_target="tpu_custom_call", output_to_operand_aliasing={{4}: (9, {})} | custom-call | flops 1000000000 | bytes 5000000 | tf_op jit(solution)/shard_map/top_layer/pallas_call | solution.py:60
  82.9 12.5 %all_to_all.49.ret_ref = bf16[32,8,512]{2,1,0:T(8,128)(2,1)S(1)} all-to-all(bf16[32,8,512]{2,1,0:T(8,128)(2,1)S(1)} %get-tuple-element.118), channel_id=1, replica_groups=mesh['layer'=4,'node'=32] {'node'}, dimensions={0} | all-to-all | bytes 524288 | tf_op jit(solution)/shard_map/all_to_all | solution.py:35
  95.7 2.3 %layer_backward_2.1 = (bf16[32,8,512]{2,1,0:T(8,128)(2,1)S(1)}, f32[256,512]{1,0:T(8,128)S(1)}, bf16[4,256,512]{2,1,0:T(8,128)(2,1)}, bf16[512,512]{1,0:T(8,128)(2,1)S(1)}, bf16[512,512]{1,0:T(8,128)(2,1)S(1)}) custom-call(s32[10]{0:T(128)S(1)} %pad_add_fusion.ids, bf16[32,8,512]{2,1,0:T(8,128)(2,1)S(1)} %all_to_all.49.ret_ref, ...), custom_call_target="tpu_custom_call" | custom-call | flops 1000000000 | bytes 5000000 | tf_op jit(solution)/shard_map/layer_backward_2/pallas_call | solution.py:60
  98.0 12.3 %all_to_all.50.ret_ref = bf16[32,8,512]{2,1,0:T(8,128)(2,1)S(1)} all-to-all(bf16[32,8,512]{2,1,0:T(8,128)(2,1)S(1)} %get-tuple-element.127), channel_id=1, replica_groups=mesh['layer'=4,'node'=32] {'node'}, dimensions={0} | all-to-all | bytes 524288 | tf_op jit(solution)/shard_map/all_to_all | solution.py:35
  110.6 2.6 %layer_backward_1.1 = (bf16[32,24,512]{2,1,0:T(8,128)(2,1)S(1)}, f32[256,512]{1,0:T(8,128)S(1)}, bf16[4,256,512]{2,1,0:T(8,128)(2,1)}, bf16[512,512]{1,0:T(8,128)(2,1)S(1)}, bf16[512,512]{1,0:T(8,128)(2,1)S(1)}) custom-call(s32[10]{0:T(128)S(1)} %pad_add_fusion.ids, bf16[32,8,512]{2,1,0:T(8,128)(2,1)S(1)} %all_to_all.50.ret_ref, ...), custom_call_target="tpu_custom_call", output_to_operand_aliasing={{2}: (11, {})} | custom-call | flops 1000000000 | bytes 5000000 | tf_op jit(solution)/shard_map/layer_backward_1/pallas_call | solution.py:60
  113.2 17.2 %all_to_all.51.ret_ref = bf16[32,24,512]{2,1,0:T(8,128)(2,1)S(1)} all-to-all(bf16[32,24,512]{2,1,0:T(8,128)(2,1)S(1)} %get-tuple-element.138), channel_id=1, replica_groups=mesh['layer'=4,'node'=32] {'node'}, dimensions={0} | all-to-all | bytes 1572864 | tf_op jit(solution)/shard_map/all_to_all | solution.py:35
  130.4 0.7 collective-permute-start.8
  131.0 1.7 last_slope.1
  132.9 2.9 %last_spread.1 = (bf16[32,56,512]{2,1,0:T(8,128)(2,1)}, f32[256,512]{1,0:T(8,128)S(1)}, bf16[32,8,512]{2,1,0:T(8,128)(2,1)S(1)}, bf16[2,16,512]{2,1,0:T(8,128)(2,1)}) custom-call(s32[10]{0:T(128)S(1)} %pad_add_fusion.ids, bf16[256,512]{1,0:T(8,128)(2,1)S(1)} %get-tuple-element.149.dpre_ref, ...), custom_call_target="tpu_custom_call" | custom-call | flops 500000000 | bytes 4000000 | tf_op jit(solution)/shard_map/last_spread/pallas_call | solution.py:60
  135.8 1.6 join_rows.1
  137.5 4.1 %all-to-all-start.7 = ((bf16[32,56,512]{2,1,0:T(8,128)(2,1)}), bf16[32,56,512]{2,1,0:T(8,128)(2,1)S(1)}, u32[]{:S(2)}, u32[]{:S(2)}) async-start(bf16[32,56,512]{2,1,0:T(8,128)(2,1)} %get-tuple-element.164), calls=%async_computation.7 | async-start | bytes 3670016 | tf_op jit(solution)/shard_map/all_to_all | solution.py:35
  141.7 2.7 %collective-permute-start.12 = (bf16[256,512]{1,0:T(8,128)(2,1)S(1)}, bf16[256,512]{1,0:T(8,128)(2,1)S(1)}, u32[]{:S(2)}, u32[]{:S(2)}) collective-permute-start(bf16[256,512]{1,0:T(8,128)(2,1)S(1)} %get-tuple-element.192), channel_id=1, source_target_pairs={{0,96},{32,0},{64,32},{96,64},{1,97},{33,1},{65,33},{97,65},{2,98}... | collective-permute-start | bytes 786440 | tf_op jit(solution)/shard_map/ppermute | solution.py:26
  144.4 0.9 collective-permute-start.11
  145.2 0.8 collective-permute-start.10
  146.1 10.0 %collective-permute-done.12.c_ref = bf16[256,512]{1,0:T(8,128)(2,1)S(1)} collective-permute-done((bf16[256,512]{1,0:T(8,128)(2,1)S(1)}, bf16[256,512]{1,0:T(8,128)(2,1)S(1)}, u32[]{:S(2)}, u32[]{:S(2)}) %collective-permute-start.12) | collective-permute-done | bytes 262176 | tf_op jit(solution)/shard_map/ppermute | solution.py:26
  156.0 3.7 %collective-permute-done.10.a_ref = bf16[256,512]{1,0:T(8,128)(2,1)S(1)} collective-permute-done((bf16[256,512]{1,0:T(8,128)(2,1)S(1)}, bf16[256,512]{1,0:T(8,128)(2,1)S(1)}, u32[]{:S(2)}, u32[]{:S(2)}) %collective-permute-start.10) | collective-permute-done | bytes 262176 | tf_op jit(solution)/shard_map/ppermute | solution.py:26
  159.7 2.4 %put_home.2 = bf16[1,4,256,512]{3,2,1,0:T(8,128)(2,1)} custom-call(s32[10]{0:T(128)S(1)} %pad_add_fusion.ids, bf16[4,256,512]{2,1,0:T(8,128)(2,1)} %get-tuple-element.165.own_ref, bf16[256,512]{1,0:T(8,128)(2,1)S(1)} %collective-permute-done.10.a_ref, bf16[256,512]{1,0:T(8,128)(2,1)S(1)} %collective-permute-done.11.b_ref, ...), custom_call_target="tpu_custom_call" | custom-call | bytes 2000000 | tf_op jit(solution)/shard_map/put_home/pallas_call | solution.py:60
  162.1 5.6 %all-to-all-done.7.ret_ref = bf16[32,56,512]{2,1,0:T(8,128)(2,1)S(1)} async-done(((bf16[32,56,512]{2,1,0:T(8,128)(2,1)}), bf16[32,56,512]{2,1,0:T(8,128)(2,1)S(1)}, u32[]{:S(2)}, u32[]{:S(2)}) %all-to-all-start.7) | async-done | bytes 1835040 | tf_op jit(solution)/shard_map/all_to_all | solution.py:35
  167.7 1.3 sum_chunks.1
  169.0 1.5 collective-permute-start.13
  170.5 2.7 %collective-permute-start.14 = (bf16[2,16,512]{2,1,0:T(8,128)(2,1)S(1)}, bf16[2,16,512]{2,1,0:T(8,128)(2,1)S(1)}, u32[]{:S(2)}, u32[]{:S(2)}) collective-permute-start(bf16[2,16,512]{2,1,0:T(8,128)(2,1)S(1)} %get-tuple-element.175), channel_id=1, source_target_pairs={{0,64},{32,96},{64,0},{96,32},{1,65},{33,97},{65,1},{97,33},{2,66}... | collective-permute-start | bytes 98312 | tf_op jit(solution)/shard_map/ppermute | solution.py:26
  173.1 1.4 collective-permute-start.15
  174.5 2.8 %input_grads.1 = (bf16[4,256,512]{2,1,0:T(8,128)(2,1)}, bf16[256,512]{1,0:T(8,128)(2,1)S(1)}, bf16[256,512]{1,0:T(8,128)(2,1)S(1)}, bf16[256,512]{1,0:T(8,128)(2,1)S(1)}) custom-call(s32[10]{0:T(128)S(1)} %pad_add_fusion.ids, bf16[32,56,512]{2,1,0:T(8,128)(2,1)S(1)} %all-to-all-done.7.ret_ref, ...), custom_call_target="tpu_custom_call", output_to_operand_aliasing={{0}: (4, {})} | custom-call | flops 100000000 | bytes 1000000 | tf_op jit(solution)/shard_map/input_grads/pallas_call | solution.py:60
  177.3 1.4 sum_over_layer.1
  178.7 3.9 %all-to-all-start.8 = ((bf16[32,16,512]{2,1,0:T(8,128)(2,1)}), bf16[32,16,512]{2,1,0:T(8,128)(2,1)S(1)}, u32[]{:S(2)}, u32[]{:S(2)}) async-start(bf16[32,16,512]{2,1,0:T(8,128)(2,1)} %sum_over_layer.1), calls=%async_computation.8 | async-start | bytes 1048576 | tf_op jit(solution)/shard_map/all_to_all | solution.py:35
  182.6 0.7 collective-permute-start.16
  183.3 3.2 %collective-permute-start.17 = (bf16[256,512]{1,0:T(8,128)(2,1)S(1)}, bf16[256,512]{1,0:T(8,128)(2,1)S(1)}, u32[]{:S(2)}, u32[]{:S(2)}) collective-permute-start(bf16[256,512]{1,0:T(8,128)(2,1)S(1)} %get-tuple-element.184), channel_id=1, source_target_pairs={{0,64},{32,96},{64,0},{96,32},{1,65},{33,97},{65,1},{97,33},{2,66}... | collective-permute-start | bytes 786440 | tf_op jit(solution)/shard_map/ppermute | solution.py:26
  186.5 6.0 %collective-permute-done.16.a_ref = bf16[256,512]{1,0:T(8,128)(2,1)S(1)} collective-permute-done((bf16[256,512]{1,0:T(8,128)(2,1)S(1)}, bf16[256,512]{1,0:T(8,128)(2,1)S(1)}, u32[]{:S(2)}, u32[]{:S(2)}) %collective-permute-start.16) | collective-permute-done | bytes 262176 | tf_op jit(solution)/shard_map/ppermute | solution.py:26
  192.5 5.9 %collective-permute-done.17.b_ref = bf16[256,512]{1,0:T(8,128)(2,1)S(1)} collective-permute-done((bf16[256,512]{1,0:T(8,128)(2,1)S(1)}, bf16[256,512]{1,0:T(8,128)(2,1)S(1)}, u32[]{:S(2)}, u32[]{:S(2)}) %collective-permute-start.17) | collective-permute-done | bytes 262176 | tf_op jit(solution)/shard_map/ppermute | solution.py:26
  198.5 2.4 %put_home.3 = bf16[1,4,256,512]{3,2,1,0:T(8,128)(2,1)} custom-call(s32[10]{0:T(128)S(1)} %pad_add_fusion.ids, bf16[4,256,512]{2,1,0:T(8,128)(2,1)} %get-tuple-element.171.own_ref, bf16[256,512]{1,0:T(8,128)(2,1)S(1)} %collective-permute-done.16.a_ref, bf16[256,512]{1,0:T(8,128)(2,1)S(1)} %collective-permute-done.17.b_ref, ...), custom_call_target="tpu_custom_call" | custom-call | bytes 2000000 | tf_op jit(solution)/shard_map/put_home/pallas_call | solution.py:60
  200.9 1.9 scale_grads.1
  (36 shorter events, 1.6 us)
Async XLA Ops:
  0.6 31.5 %copy-start = (bf16[1,512,512]{2,1,0:T(8,128)(2,1)S(1)}, bf16[1,512,512]{2,1,0:T(8,128)(2,1)}, u32[]{:S(2)}) copy-start(bf16[1,512,512]{2,1,0:T(8,128)(2,1)} %param.11) | copy-start | bytes 1572868
  0.6 31.5 %copy-start.1 = (bf16[1,512,512]{2,1,0:T(8,128)(2,1)S(1)}, bf16[1,512,512]{2,1,0:T(8,128)(2,1)}, u32[]{:S(2)}) copy-start(bf16[1,512,512]{2,1,0:T(8,128)(2,1)} %param.12) | copy-start | bytes 1572868
  2.0 25.8 %collective-permute-start.2 = (bf16[512,512]{1,0:T(8,128)(2,1)S(1)}, bf16[512,512]{1,0:T(8,128)(2,1)S(1)}, u32[]{:S(2)}, u32[]{:S(2)}) collective-permute-start(bf16[512,512]{1,0:T(8,128)(2,1)S(1)} %broadcast_select_fusion), channel_id=1, source_target_pairs={{0,64},{32,96},{64,0},{96,32},{1,65},{33,97},{65,1},{97,33},{2,66}... | collective-permute-start | bytes 1572872 | tf_op jit(solution)/shard_map/ppermute | solution.py:26
  5.2 23.5 %collective-permute-start.1 = (bf16[512,512]{1,0:T(8,128)(2,1)S(1)}, bf16[512,512]{1,0:T(8,128)(2,1)S(1)}, u32[]{:S(2)}, u32[]{:S(2)}) collective-permute-start(bf16[512,512]{1,0:T(8,128)(2,1)S(1)} %broadcast_select_fusion), channel_id=1, source_target_pairs={{0,96},{32,0},{64,32},{96,64},{1,97},{33,1},{65,33},{97,65},{2,98}... | collective-permute-start | bytes 1572872 | tf_op jit(solution)/shard_map/ppermute | solution.py:26
  6.3 22.4 %collective-permute-start = (bf16[512,512]{1,0:T(8,128)(2,1)S(1)}, bf16[512,512]{1,0:T(8,128)(2,1)S(1)}, u32[]{:S(2)}, u32[]{:S(2)}) collective-permute-start(bf16[512,512]{1,0:T(8,128)(2,1)S(1)} %broadcast_select_fusion), channel_id=1, source_target_pairs={{0,32},{32,64},{64,96},{96,0},{1,33},{33,65},{65,97},{97,1},{2,34}... | collective-permute-start | bytes 1572872 | tf_op jit(solution)/shard_map/ppermute | solution.py:26
  28.7 1.9 collective-permute-start.3
  28.7 2.7 %collective-permute-start.4 = (bf16[512,512]{1,0:T(8,128)(2,1)S(1)}, bf16[512,512]{1,0:T(8,128)(2,1)S(1)}, u32[]{:S(2)}, u32[]{:S(2)}) collective-permute-start(bf16[512,512]{1,0:T(8,128)(2,1)S(1)} %collective-permute-done.1.rest_4_), channel_id=1, source_target_pairs={{0,1},{1,0},{2,3},{3,2},{4,5},{5,4},{6,7},{7,6},{8,9},{9,8},{10,11... | collective-permute-start | bytes 1572872 | tf_op jit(solution)/shard_map/ppermute | solution.py:31
  29.2 2.9 %collective-permute-start.5 = (bf16[512,512]{1,0:T(8,128)(2,1)S(1)}, bf16[512,512]{1,0:T(8,128)(2,1)S(1)}, u32[]{:S(2)}, u32[]{:S(2)}) collective-permute-start(bf16[512,512]{1,0:T(8,128)(2,1)S(1)} %collective-permute-done.2.rest_6_), channel_id=1, source_target_pairs={{0,1},{1,0},{2,3},{3,2},{4,5},{5,4},{6,7},{7,6},{8,9},{9,8},{10,11... | collective-permute-start | bytes 1572872 | tf_op jit(solution)/shard_map/ppermute | solution.py:31
  65.2 14.1 %copy-start.2 = (bf16[512,172]{0,1:T(8,128)(2,1)S(1)}, bf16[512,172]{0,1:T(8,128)(2,1)}, u32[]{:S(2)}) copy-start(bf16[512,172]{0,1:T(8,128)(2,1)} %param.13) | copy-start | bytes 528388
  65.2 14.1 %copy-start.3 = (s32[4,256]{1,0:T(4,128)S(1)}, s32[4,256]{1,0:T(4,128)}, u32[]{:S(2)}) copy-start(s32[4,256]{1,0:T(4,128)} %lab_ref.1) | copy-start | bytes 12292
  65.2 14.1 %copy-start.4 = (s32[4,256]{1,0:T(4,128)S(1)}, s32[4,256]{1,0:T(4,128)}, u32[]{:S(2)}) copy-start(s32[4,256]{1,0:T(4,128)} %mask_ref.1) | copy-start | bytes 12292
  95.4 2.6 %collective-permute-start.6 = (bf16[512,512]{1,0:T(8,128)(2,1)S(1)}, bf16[512,512]{1,0:T(8,128)(2,1)S(1)}, u32[]{:S(2)}, u32[]{:S(2)}) collective-permute-start(bf16[512,512]{1,0:T(8,128)(2,1)S(1)} %get-tuple-element.126), channel_id=1, source_target_pairs={{0,1},{1,0},{2,3},{3,2},{4,5},{5,4},{6,7},{7,6},{8,9},{9,8},{10,11... | collective-permute-start | bytes 1572872 | tf_op jit(solution)/shard_map/ppermute | solution.py:31
  110.3 2.9 %collective-permute-start.7 = (bf16[512,512]{1,0:T(8,128)(2,1)S(1)}, bf16[512,512]{1,0:T(8,128)(2,1)S(1)}, u32[]{:S(2)}, u32[]{:S(2)}) collective-permute-start(bf16[512,512]{1,0:T(8,128)(2,1)S(1)} %get-tuple-element.137), channel_id=1, source_target_pairs={{0,1},{1,0},{2,3},{3,2},{4,5},{5,4},{6,7},{7,6},{8,9},{9,8},{10,11... | collective-permute-start | bytes 1572872 | tf_op jit(solution)/shard_map/ppermute | solution.py:31
  130.4 2.4 %collective-permute-start.8 = (bf16[512,512]{1,0:T(8,128)(2,1)S(1)}, bf16[512,512]{1,0:T(8,128)(2,1)S(1)}, u32[]{:S(2)}, u32[]{:S(2)}) collective-permute-start(bf16[512,512]{1,0:T(8,128)(2,1)S(1)} %get-tuple-element.147), channel_id=1, source_target_pairs={{0,1},{1,0},{2,3},{3,2},{4,5},{5,4},{6,7},{7,6},{8,9},{9,8},{10,11... | collective-permute-start | bytes 1572872 | tf_op jit(solution)/shard_map/ppermute | solution.py:31
  132.8 3.0 %collective-permute-start.9 = (bf16[512,512]{1,0:T(8,128)(2,1)S(1)}, bf16[512,512]{1,0:T(8,128)(2,1)S(1)}, u32[]{:S(2)}, u32[]{:S(2)}) collective-permute-start(bf16[512,512]{1,0:T(8,128)(2,1)S(1)} %get-tuple-element.157), channel_id=1, source_target_pairs={{0,1},{1,0},{2,3},{3,2},{4,5},{5,4},{6,7},{7,6},{8,9},{9,8},{10,11... | collective-permute-start | bytes 1572872 | tf_op jit(solution)/shard_map/ppermute | solution.py:31
  137.5 4.2 %copy-start.5 = (bf16[4,256,512]{2,1,0:T(8,128)(2,1)S(1)}, bf16[4,256,512]{2,1,0:T(8,128)(2,1)}, u32[]{:S(2)}) copy-start(bf16[4,256,512]{2,1,0:T(8,128)(2,1)} %get-tuple-element.165.own_ref) | copy-start | bytes 3145732
  137.5 30.2 %all-to-all-start.7 = ((bf16[32,56,512]{2,1,0:T(8,128)(2,1)}), bf16[32,56,512]{2,1,0:T(8,128)(2,1)S(1)}, u32[]{:S(2)}, u32[]{:S(2)}) async-start(bf16[32,56,512]{2,1,0:T(8,128)(2,1)} %get-tuple-element.164), calls=%async_computation.7 | async-start | bytes 3670016 | tf_op jit(solution)/shard_map/all_to_all | solution.py:35
  141.7 14.3 %collective-permute-start.12 = (bf16[256,512]{1,0:T(8,128)(2,1)S(1)}, bf16[256,512]{1,0:T(8,128)(2,1)S(1)}, u32[]{:S(2)}, u32[]{:S(2)}) collective-permute-start(bf16[256,512]{1,0:T(8,128)(2,1)S(1)} %get-tuple-element.192), channel_id=1, source_target_pairs={{0,96},{32,0},{64,32},{96,64},{1,97},{33,1},{65,33},{97,65},{2,98}... | collective-permute-start | bytes 786440 | tf_op jit(solution)/shard_map/ppermute | solution.py:26
  144.4 11.7 %collective-permute-start.11 = (bf16[256,512]{1,0:T(8,128)(2,1)S(1)}, bf16[256,512]{1,0:T(8,128)(2,1)S(1)}, u32[]{:S(2)}, u32[]{:S(2)}) collective-permute-start(bf16[256,512]{1,0:T(8,128)(2,1)S(1)} %get-tuple-element.193), channel_id=1, source_target_pairs={{0,64},{32,96},{64,0},{96,32},{1,65},{33,97},{65,1},{97,33},{2,66}... | collective-permute-start | bytes 786440 | tf_op jit(solution)/shard_map/ppermute | solution.py:26
  145.2 14.5 %collective-permute-start.10 = (bf16[256,512]{1,0:T(8,128)(2,1)S(1)}, bf16[256,512]{1,0:T(8,128)(2,1)S(1)}, u32[]{:S(2)}, u32[]{:S(2)}) collective-permute-start(bf16[256,512]{1,0:T(8,128)(2,1)S(1)} %get-tuple-element.194), channel_id=1, source_target_pairs={{0,32},{32,64},{64,96},{96,0},{1,33},{33,65},{65,97},{97,1},{2,34}... | collective-permute-start | bytes 786440 | tf_op jit(solution)/shard_map/ppermute | solution.py:26
  169.0 8.3 %collective-permute-start.13 = (bf16[2,16,512]{2,1,0:T(8,128)(2,1)S(1)}, bf16[2,16,512]{2,1,0:T(8,128)(2,1)S(1)}, u32[]{:S(2)}, u32[]{:S(2)}) collective-permute-start(bf16[2,16,512]{2,1,0:T(8,128)(2,1)S(1)} %get-tuple-element.174), channel_id=1, source_target_pairs={{0,32},{32,64},{64,96},{96,0},{1,33},{33,65},{65,97},{97,1},{2,34}... | collective-permute-start | bytes 98312 | tf_op jit(solution)/shard_map/ppermute | solution.py:26
  170.5 6.9 %collective-permute-start.14 = (bf16[2,16,512]{2,1,0:T(8,128)(2,1)S(1)}, bf16[2,16,512]{2,1,0:T(8,128)(2,1)S(1)}, u32[]{:S(2)}, u32[]{:S(2)}) collective-permute-start(bf16[2,16,512]{2,1,0:T(8,128)(2,1)S(1)} %get-tuple-element.175), channel_id=1, source_target_pairs={{0,64},{32,96},{64,0},{96,32},{1,65},{33,97},{65,1},{97,33},{2,66}... | collective-permute-start | bytes 98312 | tf_op jit(solution)/shard_map/ppermute | solution.py:26
  173.1 4.2 %collective-permute-start.15 = (bf16[2,16,512]{2,1,0:T(8,128)(2,1)S(1)}, bf16[2,16,512]{2,1,0:T(8,128)(2,1)S(1)}, u32[]{:S(2)}, u32[]{:S(2)}) collective-permute-start(bf16[2,16,512]{2,1,0:T(8,128)(2,1)S(1)} %get-tuple-element.176), channel_id=1, source_target_pairs={{0,96},{32,0},{64,32},{96,64},{1,97},{33,1},{65,33},{97,65},{2,98}... | collective-permute-start | bytes 98312 | tf_op jit(solution)/shard_map/ppermute | solution.py:26
  178.7 19.8 %all-to-all-start.8 = ((bf16[32,16,512]{2,1,0:T(8,128)(2,1)}), bf16[32,16,512]{2,1,0:T(8,128)(2,1)S(1)}, u32[]{:S(2)}, u32[]{:S(2)}) async-start(bf16[32,16,512]{2,1,0:T(8,128)(2,1)} %sum_over_layer.1), calls=%async_computation.8 | async-start | bytes 1048576 | tf_op jit(solution)/shard_map/all_to_all | solution.py:35
  182.6 9.9 %collective-permute-start.16 = (bf16[256,512]{1,0:T(8,128)(2,1)S(1)}, bf16[256,512]{1,0:T(8,128)(2,1)S(1)}, u32[]{:S(2)}, u32[]{:S(2)}) collective-permute-start(bf16[256,512]{1,0:T(8,128)(2,1)S(1)} %get-tuple-element.183), channel_id=1, source_target_pairs={{0,32},{32,64},{64,96},{96,0},{1,33},{33,65},{65,97},{97,1},{2,34}... | collective-permute-start | bytes 786440 | tf_op jit(solution)/shard_map/ppermute | solution.py:26
  183.3 15.1 %collective-permute-start.17 = (bf16[256,512]{1,0:T(8,128)(2,1)S(1)}, bf16[256,512]{1,0:T(8,128)(2,1)S(1)}, u32[]{:S(2)}, u32[]{:S(2)}) collective-permute-start(bf16[256,512]{1,0:T(8,128)(2,1)S(1)} %get-tuple-element.184), channel_id=1, source_target_pairs={{0,64},{32,96},{64,0},{96,32},{1,65},{33,97},{65,1},{97,33},{2,66}... | collective-permute-start | bytes 786440 | tf_op jit(solution)/shard_map/ppermute | solution.py:26
  186.5 12.0 %collective-permute-start.18 = (bf16[256,512]{1,0:T(8,128)(2,1)S(1)}, bf16[256,512]{1,0:T(8,128)(2,1)S(1)}, u32[]{:S(2)}, u32[]{:S(2)}) collective-permute-start(bf16[256,512]{1,0:T(8,128)(2,1)S(1)} %get-tuple-element.185), channel_id=1, source_target_pairs={{0,96},{32,0},{64,32},{96,64},{1,97},{33,1},{65,33},{97,65},{2,98}... | collective-permute-start | bytes 786440 | tf_op jit(solution)/shard_map/ppermute | solution.py:26
  198.5 2.4 %collective-permute-start.19 = (bf16[512,512]{1,0:T(8,128)(2,1)S(1)}, bf16[512,512]{1,0:T(8,128)(2,1)S(1)}, u32[]{:S(2)}, u32[]{:S(2)}) collective-permute-start(bf16[512,512]{1,0:T(8,128)(2,1)S(1)} %bitcast.34), channel_id=1, source_target_pairs={{0,1},{1,0},{2,3},{3,2},{4,5},{5,4},{6,7},{7,6},{8,9},{9,8},{10,11... | collective-permute-start | bytes 1572872 | tf_op jit(solution)/shard_map/ppermute | solution.py:31
